TPU v7x, 256 devices: a whole 4x4x8 slice. The times are simulated.
256 devices in a mesh: spec: 16 (over z_lo, x, core), photo: 16 (over y, z_hi).
Axes of the slice: x: 4, y: 4, z: 8 (z_hi: 4, z_lo: 2; z = z_hi * 2 + z_lo), core: 2. Of those that a mesh axis runs over, the one named last changes fastest.
Arguments:
- spec_feat: bfloat16 [131072, 64], P(('spec', 'photo')), may hold values from -2.5 to 2.5
- photo_feat: bfloat16 [16, 16384, 64], P('spec', 'photo'), may hold values from -2.5 to 2.5
- spec_mass: bfloat16 [131072], P(('spec', 'photo')), may hold values from 0.25 to 4
- photo_mass: bfloat16 [16, 16384], P('spec', 'photo'), may hold values from 0.25 to 4
- tile_index: int32 [16, 16, 96], P('spec', 'photo'), may hold values from 0 to 2047, as said below
- tile_count: int32 [16, 16], P('spec', 'photo'), may hold values from 4 to 96, as said below
Outputs:
- grad_spec: float32 [131072, 64], P(('spec', 'photo'))
- grad_photo: float32 [16, 16384, 64], P('spec', 'photo')
Inputs may be any that keep to these rules, and one draw needn't show every extreme that they name: `tile_index`: the first tile_count[s, p] entries of each list are distinct; over all lists, every tile row of every spectroscopic block and every tile column of every photometric block lies in some live tile. Entries past the count are ignored. `tile_count`: some pair of blocks has exactly 96 live tiles.
All inputs are finite; a program needn't handle non-finite values.
Results may differ from a plain program's by a relative error of at most 0.002.
Values may be sent and summed in bfloat16 or wider, within the bound.
No kernel may reach another device: no remote copies, remote signals or barrier semaphores. Data moves between devices by JAX's collectives and lax.ppermute only.
A program may use at most 64 MiB of HBM per device.

v0:
```python
import math

import jax
import jax.numpy as jnp
from jax import lax
from jax.experimental import pallas as pl
from jax.experimental.pallas import tpu as pltpu
from jax.sharding import PartitionSpec as P


TILE = 256
TR = 32
TC = 64
F = 64
TMAX = 96
SB = 512
PB = 1024
EXT = 72
WROWS = 80
SLOTS = 16
GROUP = 8
TURNS = TMAX // GROUP
SCALE = 0.125 * math.log2(math.e)
f32 = jnp.float32
bf16 = jnp.bfloat16


def photo_perm(fy, fz):
    return [(y * 4 + z, fy(y) * 4 + fz(z)) for y in range(4) for z in range(4)]


def spec_perm(fl, fx, fc):
    return [
        (l * 8 + x * 2 + c, fl(l) * 8 + fx(x) * 2 + fc(c))
        for l in range(2)
        for x in range(4)
        for c in range(2)
    ]


def same(i):
    return i


def flip(i):
    return i ^ 1


def mirror(i):
    return 3 - i


def shift(k):
    return lambda i: (i + k) % 4


def shift_y(a, k):
    return lax.ppermute(a, "photo", photo_perm(shift(k), same))


def shift_z(a, k):
    return lax.ppermute(a, "photo", photo_perm(same, shift(k)))


def shift_x(a, k):
    return lax.ppermute(a, "spec", spec_perm(same, shift(k), same))


def swap_core(a):
    return lax.ppermute(a, "spec", spec_perm(same, same, flip))


def swap_low(a):
    return lax.ppermute(a, "spec", spec_perm(flip, same, same))


def sum_photo(a):
    parts = [lax.ppermute(a, "photo", photo_perm(fy, fz)) for fy, fz in ((flip, same), (same, flip), (flip, flip))]
    a = (a + parts[0]) + (parts[1] + parts[2])
    a = a + lax.ppermute(a, "photo", photo_perm(mirror, same))
    return (a, lax.ppermute(a, "photo", photo_perm(same, mirror)))


def sum_spec(a):
    a = a + swap_core(a)
    parts = [
        lax.ppermute(a, "spec", spec_perm(fl, fx, same)) for fl, fx in ((flip, same), (same, flip), (flip, flip))
    ]
    a = (a + parts[0]) + (parts[1] + parts[2])
    return (a, lax.ppermute(a, "spec", spec_perm(same, mirror, same)))


def spec_slot(q, photo_id):
    return (((photo_id >> 2) - (q >> 2)) & 3) * 4 + ((photo_id - q) & 3)


def photo_slot(q, spec_id):
    low = ((spec_id >> 3) - (q >> 3)) & 1
    across = ((spec_id >> 1) - (q >> 1)) & 3
    core = (spec_id - q) & 1
    return core * 8 + across * 2 + low


def entry_of(index_ref, t, last):
    entry = index_ref[jnp.minimum(t, last)]
    return ((entry >> 6) & 31, entry & 63)


def live(value, t, count_ref):
    return value * (t < count_ref[0]).astype(value.dtype)


def contract_last(a, b):
    return lax.dot_general(a, b, (((1,), (1,)), ((), ())), preferred_element_type=f32)


def high_low_rows(value):
    high = value.astype(bf16).astype(f32)
    sub = lax.broadcasted_iota(jnp.int32, value.shape, 0)
    return jnp.where(sub == 0, high, jnp.where(sub == 1, value - high, 0.0)).astype(bf16)


def high_low(value):
    return high_low_rows(jnp.broadcast_to(value, (16, value.shape[1])))


def turns_of(count_ref):
    return (count_ref[0] + GROUP - 1) // GROUP


def over_tiles(index_ref, count_ref, before, step, after):
    last = count_ref[0] - 1

    def turn(i, carry):
        before(i)
        for k in range(GROUP):
            row, column = entry_of(index_ref, i * GROUP + k, last)
            step(i, k, i * GROUP + k, row, column)
        after(i)
        return carry

    lax.fori_loop(0, turns_of(count_ref), turn, 0)


def start_tiles(count_ref, g_hbm, g_ref, sems):
    def turn(i, carry):
        pltpu.make_async_copy(g_hbm.at[i], g_ref.at[i], sems.at[i]).start()
        return carry

    lax.fori_loop(0, turns_of(count_ref), turn, 0)


def wait_tiles(g_hbm, g_ref, sems):
    return lambda i: pltpu.make_async_copy(g_hbm.at[i], g_ref.at[i], sems.at[i]).wait()


def nothing(i):
    pass


def store_pairs(acc_ref, out_ref):
    for i in range(out_ref.shape[0]):
        both = acc_ref[i]
        out_ref[i : i + 1, :] = both[0:1, :] + both[1:2, :]


def piece_copies(xs, ys, xt_ref, yt_ref, sems):
    copies = [pltpu.make_async_copy(xs[k], xt_ref.at[pl.ds(4 * k, 4)], sems.at[k]) for k in range(4)]
    return copies + [
        pltpu.make_async_copy(ys[k], yt_ref.at[pl.ds(2 * k, 2)], sems.at[4 + k]) for k in range(8)
    ]


def first_kernel(index_ref, count_ref, pos_ref, *refs):
    xs, ys = (refs[0:4], refs[4:12])
    out_ref, m_ref, n_ref, g_hbm = refs[12:16]
    xt_ref, yt_ref, xr_ref, w_ref, acc_ref, g_ref, sems, g_sems = refs[16:]
    copies = piece_copies(xs, ys, xt_ref, yt_ref, sems)
    for copy in copies:
        copy.start()
    acc_ref[...] = jnp.zeros_like(acc_ref)
    for copy in copies:
        copy.wait()

    def turn_slot(s, carry):
        for h in range(2):
            x = xt_ref[s, 0:F, h * TILE : (h + 1) * TILE].astype(f32)
            xr_ref[2 * s + h] = jnp.transpose(x).astype(bf16)
        return carry

    lax.fori_loop(0, SLOTS, turn_slot, 0)

    def weigh(q, carry):
        slot = photo_slot(q, pos_ref[1])
        for k in range(4):
            y = yt_ref[slot, 0:F, k * TILE : (k + 1) * TILE].astype(f32)
            norm = jnp.sum(y * y, axis=0, keepdims=True)
            w_ref[4 * q + k] = high_low(jnp.exp(norm * -0.0625))
        return carry

    lax.fori_loop(0, SLOTS, weigh, 0)
    for q in range(SLOTS):
        mass = xt_ref[spec_slot(q, pos_ref[0]), F:EXT, :].astype(f32)
        for k in range(2):
            m_ref[2 * q + k : 2 * q + k + 1, :] = mass[0:1, k * TILE : (k + 1) * TILE]
    for q in range(SLOTS):
        mass = yt_ref[photo_slot(q, pos_ref[1]), F:EXT, :].astype(f32)
        for k in range(4):
            n_ref[4 * q + k : 4 * q + k + 1, :] = mass[0:1, k * TILE : (k + 1) * TILE]

    def step(i, k, t, row, column):
        row_local = spec_slot(row >> 1, pos_ref[0]) * 2 + (row & 1)
        slot = photo_slot(column >> 2, pos_ref[1])
        lane = pl.multiple_of((column & 3) * TILE, TILE)
        y = yt_ref[slot, 0:F, pl.ds(lane, TILE)]
        cross = jnp.dot(xr_ref[row_local], y, preferred_element_type=f32)
        g = jnp.exp2(cross * SCALE).astype(bf16)
        g_ref[i, k] = g
        acc_ref[row] += contract_last(live(w_ref[column], t, count_ref), g)

    def send(i):
        pltpu.make_async_copy(g_ref.at[i], g_hbm.at[i], g_sems.at[i]).start()

    over_tiles(index_ref, count_ref, nothing, step, send)
    store_pairs(acc_ref, out_ref)

    def sent(i, carry):
        pltpu.make_async_copy(g_ref.at[i], g_hbm.at[i], g_sems.at[i]).wait()
        return carry

    lax.fori_loop(0, turns_of(count_ref), sent, 0)


def column_kernel(index_ref, count_ref, ra_ref, rb_ref, m_ref, g_hbm, out_ref, w_ref, acc_ref, g_ref, sems):
    start_tiles(count_ref, g_hbm, g_ref, sems)
    acc_ref[...] = jnp.zeros_like(acc_ref)
    u = m_ref[...] / (ra_ref[...] + rb_ref[...])
    for row in range(TR):
        w_ref[row] = high_low(u[row : row + 1, :])

    def step(i, k, t, row, column):
        acc_ref[column] += jnp.dot(live(w_ref[row], t, count_ref), g_ref[i, k], preferred_element_type=f32)

    over_tiles(index_ref, count_ref, wait_tiles(g_hbm, g_ref, sems), step, nothing)
    store_pairs(acc_ref, out_ref)


def row_kernel(index_ref, count_ref, ca_ref, cb_ref, n_ref, g_hbm, out_ref, w_ref, acc_ref, g_ref, sems):
    start_tiles(count_ref, g_hbm, g_ref, sems)
    acc_ref[...] = jnp.zeros_like(acc_ref)
    v = n_ref[...] / (ca_ref[...] + cb_ref[...])
    for column in range(TC):
        w_ref[column] = high_low(v[column : column + 1, :])

    def step(i, k, t, row, column):
        acc_ref[row] += contract_last(live(w_ref[column], t, count_ref), g_ref[i, k])

    over_tiles(index_ref, count_ref, wait_tiles(g_hbm, g_ref, sems), step, nothing)
    store_pairs(acc_ref, out_ref)


def grad_kernel(index_ref, count_ref, pos_ref, ra_ref, rb_ref, ca_ref, cb_ref, m_ref, n_ref, g_hbm, *refs):
    xs, ys = (refs[0:4], refs[4:12])
    spec_outs, photo_outs, share_ref = (refs[12:16], refs[16:18], refs[18])
    xt_ref, yt_ref, u_ref, v_ref, wy_ref, vx_ref, spec_acc, photo_acc = refs[19:27]
    spec_ref, photo_ref, g_ref, sems, g_sems, out_sems = refs[27:]
    copies = piece_copies(xs, ys, xt_ref, yt_ref, sems)
    for copy in copies:
        copy.start()
    start_tiles(count_ref, g_hbm, g_ref, g_sems)
    u_all = m_ref[...] / (ra_ref[...] + rb_ref[...])
    total = ca_ref[...] + cb_ref[...]
    v_all = n_ref[...] / total
    both_all = v_all * total
    for q in range(SLOTS):
        slot = spec_slot(q, pos_ref[0])
        for k in range(2):
            row = 2 * q + k
            u_ref[2 * slot + k] = jnp.broadcast_to(u_all[row : row + 1, :], (8, TILE))
    for q in range(SLOTS):
        slot = photo_slot(q, pos_ref[1])
        for k in range(4):
            column = 4 * q + k
            v_ref[4 * slot + k] = jnp.broadcast_to(v_all[column : column + 1, :], (8, TILE))

        @pl.when(slot == 0)
        def _():
            for k in range(4):
                share_ref[k] = jnp.broadcast_to(both_all[4 * q + k : 4 * q + k + 1, :], (8, TILE))

    spec_acc[...] = jnp.zeros_like(spec_acc)
    photo_acc[...] = jnp.zeros_like(photo_acc)
    for copy in copies:
        copy.wait()

    def ready_y(s, carry):
        for k in range(4):
            y = yt_ref[s, 0:F, k * TILE : (k + 1) * TILE].astype(f32)
            v = v_ref[4 * s + k][0:1, :]
            wy_ref[4 * s + k, 0:F, :] = (y * v).astype(bf16)
            wy_ref[4 * s + k, F:WROWS, :] = high_low(v)
        return carry

    def ready_x(s, carry):
        for k in range(2):
            x = xt_ref[s, 0:F, k * TILE : (k + 1) * TILE].astype(f32)
            vx_ref[2 * s + k] = (x * u_ref[2 * s + k][0:1, :]).astype(bf16)
        return carry

    lax.fori_loop(0, SLOTS, ready_y, 0)
    lax.fori_loop(0, SLOTS, ready_x, 0)

    def step(i, k, t, row, column):
        row_local = spec_slot(row >> 1, pos_ref[0]) * 2 + (row & 1)
        column_local = photo_slot(column >> 2, pos_ref[1]) * 4 + (column & 3)
        g = g_ref[i, k]
        spec_acc[row_local] += contract_last(live(wy_ref[column_local], t, count_ref), g)
        photo_acc[column_local] += jnp.dot(live(vx_ref[row_local], t, count_ref), g, preferred_element_type=f32)

    over_tiles(index_ref, count_ref, wait_tiles(g_hbm, g_ref, g_sems), step, nothing)

    def store_y(s, carry):
        for k in range(4):
            v = v_ref[4 * s + k][0:1, :]
            photo_ref[s, :, k * TILE : (k + 1) * TILE] = (photo_acc[4 * s + k] * v).astype(bf16)
        return carry

    def store_x(s, carry):
        for k in range(2):
            lanes = slice(k * TILE, (k + 1) * TILE)
            u = u_ref[2 * s + k][0:1, :]
            both = spec_acc[2 * s + k]
            spec_ref[s, 0:F, lanes] = (both[0:F, :] * u).astype(bf16)
            total = jnp.broadcast_to((both[F : F + 1, :] + both[F + 1 : F + 2, :]) * u, (8, TILE))
            spec_ref[s, F:EXT, lanes] = high_low_rows(total)
        return carry

    sends = []
    for h in (1, 0):
        lax.fori_loop(8 * h, 8 * h + 8, store_y, 0)
        sends.append(pltpu.make_async_copy(photo_ref.at[pl.ds(8 * h, 8)], photo_outs[h], out_sems.at[4 + h]))
        sends[-1].start()
    for h in range(4):
        lax.fori_loop(4 * h, 4 * h + 4, store_x, 0)
        sends.append(pltpu.make_async_copy(spec_ref.at[pl.ds(4 * h, 4)], spec_outs[h], out_sems.at[h]))
        sends[-1].start()
    for send in sends:
        send.wait()


def relay_kernel(a_ref, b_ref, c_ref, d_ref, own_ref, *send_refs):
    for k in range(4):
        parts = [ref[k].astype(f32) for ref in (a_ref, b_ref, c_ref, d_ref)]
        part = parts[0] + parts[1] + parts[2] + parts[3]
        if k == 0:
            own_ref[...] = part
            continue
        send_refs[k - 1][0:F, :] = part[0:F, :].astype(bf16)
        total = jnp.broadcast_to(part[F : F + 1, :] + part[F + 1 : F + 2, :], (8, SB))
        send_refs[k - 1][F:EXT, :] = high_low_rows(total)


SMEM = pl.BlockSpec(memory_space=pltpu.SMEM)
VMEM = pl.BlockSpec(memory_space=pltpu.VMEM)
ANY = pl.BlockSpec(memory_space=pl.ANY)


def call(kernel, in_specs, outs, scratch, *args):
    return pl.pallas_call(
        kernel,
        in_specs=in_specs,
        out_specs=[spec for spec, _, _ in outs],
        out_shape=[jax.ShapeDtypeStruct(s, d) for _, s, d in outs],
        scratch_shapes=scratch,
    )(*args)


def in_vmem(arrays):
    return [pltpu.with_memory_space_constraint(a, pltpu.VMEM) for a in arrays]


def per_device(spec_feat, photo_feat, spec_mass, photo_mass, tile_index, tile_count):
    photo_id = lax.axis_index("photo")
    spec_id = lax.axis_index("spec")
    meta = (
        tile_index.reshape(TMAX),
        tile_count.reshape(1),
        jnp.stack([photo_id, spec_id]).astype(jnp.int32),
    )
    x_own = spec_feat.T
    y_own = photo_feat[0].T
    x_pad = jnp.zeros((EXT - F - 1, SB), bf16)
    y_pad = jnp.zeros((EXT - F - 1, PB), bf16)
    x0 = jnp.concatenate([x_own, spec_mass.reshape(1, SB), x_pad])[None]
    y0 = jnp.concatenate([y_own, photo_mass.reshape(1, PB), y_pad])[None]

    x_parts = [shift_z(x0, k) for k in (1, 2, 3)]
    y_low = swap_low(y0)
    y0 = jnp.concatenate([y0, y_low])
    x0 = jnp.concatenate([x0] + x_parts)
    ys = [y0] + [shift_x(y0, k) for k in (1, 2, 3)]
    xs = [x0] + [shift_y(x0, k) for k in (1, 2, 3)]
    ys = ys + [swap_core(y) for y in ys]

    tiles = pltpu.VMEM((TURNS, GROUP, TILE, TILE), bf16)
    tile_sems = pltpu.SemaphoreType.DMA((TURNS,))
    row_acc = [pltpu.VMEM((TC, 16, TILE), bf16), pltpu.VMEM((TR, 16, TILE), f32)]
    column_acc = [pltpu.VMEM((TR, 16, TILE), bf16), pltpu.VMEM((TC, 16, TILE), f32)]
    blocks = [pltpu.VMEM((SLOTS, EXT, SB), bf16), pltpu.VMEM((SLOTS, EXT, PB), bf16)]
    piece_sems = pltpu.SemaphoreType.DMA((12,))
    r, m, n, g = call(
        first_kernel, [SMEM] * 3 + [ANY] * 12,
        [
            (VMEM, (TR, TILE), f32), (VMEM, (TR, TILE), f32), (VMEM, (TC, TILE), f32),
            (ANY, (TURNS, GROUP, TILE, TILE), bf16),
        ],
        blocks + [pltpu.VMEM((TR, TILE, F), bf16)] + row_acc + [tiles, piece_sems, tile_sems],
        *meta, *xs, *ys,
    )
    lists = meta[0:2]

    def columns(ra, rb):
        return call(
            column_kernel, [SMEM] * 2 + [VMEM] * 3 + [ANY], [(VMEM, (TC, TILE), f32)],
            column_acc + [tiles, tile_sems], *lists, ra, rb, m, g,
        )[0]

    ra, rb = in_vmem(sum_photo(r))
    ca, cb = in_vmem(sum_spec(columns(ra, rb)))
    (r,) = call(
        row_kernel, [SMEM] * 2 + [VMEM] * 3 + [ANY], [(VMEM, (TR, TILE), f32)],
        row_acc + [tiles, tile_sems], *lists, ca, cb, n, g,
    )
    ra, rb = in_vmem(sum_photo(r))
    ca, cb = in_vmem(sum_spec(columns(ra, rb)))
    *parts, share = call(
        grad_kernel, [SMEM] * 3 + [VMEM] * 6 + [ANY] * 13,
        [(ANY, (4, EXT, SB), bf16)] * 4 + [(ANY, (8, F, PB), bf16)] * 2 + [(VMEM, (4, 8, TILE), f32)],
        blocks
        + [
            pltpu.VMEM((TR, 8, TILE), f32),
            pltpu.VMEM((TC, 8, TILE), f32),
            pltpu.VMEM((TC, WROWS, TILE), bf16),
            pltpu.VMEM((TR, F, TILE), bf16),
            pltpu.VMEM((TR, WROWS, TILE), f32),
            pltpu.VMEM((TC, F, TILE), f32),
            pltpu.VMEM((SLOTS, EXT, SB), bf16),
            pltpu.VMEM((SLOTS, F, PB), bf16),
            tiles, piece_sems, tile_sems,
            pltpu.SemaphoreType.DMA((6,)),
        ],
        *meta, ra, rb, ca, cb, m, n, g, *xs, *ys,
    )
    share = share[:, 0, :].reshape(1, PB)

    spec_parts, photo_parts = (parts[0:4], parts[4:6])
    far = swap_core(photo_parts[1])
    y_parts = [shift_y(spec_parts[k], -k) for k in (1, 2, 3)]
    photo_sums = [
        photo_parts[0][2 * k : 2 * k + 2].astype(f32) + far[2 * k : 2 * k + 2].astype(f32) for k in range(4)
    ]
    x_parts = [shift_x(photo_sums[k].astype(bf16), -k) for k in (1, 2, 3)]
    y_parts, x_parts = lax.optimization_barrier((y_parts, x_parts))
    spec_sum, *z_parts = call(
        relay_kernel, [VMEM] * 4,
        [(VMEM, (EXT, SB), f32)] + [(VMEM, (EXT, SB), bf16)] * 3, [],
        spec_parts[0], *in_vmem(y_parts),
    )
    z_parts = [shift_z(part, -k) for k, part in zip((1, 2, 3), z_parts)]
    photo_sum = photo_sums[0]
    for part in x_parts:
        photo_sum = photo_sum + part.astype(f32)
    for part in z_parts:
        spec_sum = spec_sum + part.astype(f32)
    photo_sum = photo_sum[0] + swap_low(photo_sum[1].astype(bf16)).astype(f32)
    row_marginal = spec_sum[F : F + 1] + spec_sum[F + 1 : F + 2]
    grad_spec = 2.0 * (row_marginal * x_own.astype(f32) - spec_sum[0:F])
    grad_photo = 2.0 * (share * y_own.astype(f32) - photo_sum)
    return (grad_spec.T, grad_photo.T[None])


def solution(mesh):
    return jax.shard_map(
        per_device,
        mesh=mesh,
        in_specs=(
            P(("spec", "photo"), None),
            P("spec", "photo", None),
            P(("spec", "photo")),
            P("spec", "photo"),
            P("spec", "photo", None),
            P("spec", "photo"),
        ),
        out_specs=(P(("spec", "photo"), None), P("spec", "photo", None)),
        check_vma=False,
    )
```

profile of v0, /device:TPU:8, one launch (start us, length us, event | category | flops | bytes accessed | tf_op | source)
XLA Modules:
  0.0 198.6 jit_solution(11304416325197270230)
XLA Ops:
  2.3 6.4 %collective-permute-start.2 = (bf16[1,72,512]{2,1,0:T(8,128)(2,1)S(1)}, bf16[1,72,512]{2,1,0:T(8,128)(2,1)S(1)}, u32[]{:S(2)}, u32[]{:S(2)}) collective-permute-start(bf16[1,72,512]{2,1,0:T(8,128)(2,1)S(1)} %maximum_bitcast_fusion.1), channel_id=1, source_target_pairs={{0,3},{1,0},{2,1},{3,2},{4,7},{5,4},{6,5},{7,6},{8,11},{9,8},{10,9... | collective-permute-start | bytes 221192 | tf_op jit(solution)/shard_map/ppermute | solution.py:62
  9.7 2.8 %collective-permute-start = (bf16[1,72,512]{2,1,0:T(8,128)(2,1)S(1)}, bf16[1,72,512]{2,1,0:T(8,128)(2,1)S(1)}, u32[]{:S(2)}, u32[]{:S(2)}) collective-permute-start(bf16[1,72,512]{2,1,0:T(8,128)(2,1)S(1)} %maximum_bitcast_fusion.1), channel_id=1, source_target_pairs={{0,1},{1,2},{2,3},{3,0},{4,5},{5,6},{6,7},{7,4},{8,9},{9,10},{10,1... | collective-permute-start | bytes 221192 | tf_op jit(solution)/shard_map/ppermute | solution.py:62
  15.0 3.6 %collective-permute-done.1 = bf16[1,72,512]{2,1,0:T(8,128)(2,1)S(1)} collective-permute-done((bf16[1,72,512]{2,1,0:T(8,128)(2,1)S(1)}, bf16[1,72,512]{2,1,0:T(8,128)(2,1)S(1)}, u32[]{:S(2)}, u32[]{:S(2)}) %collective-permute-start.1) | collective-permute-done | bytes 73760 | tf_op jit(solution)/shard_map/ppermute | solution.py:62
  21.9 2.8 %collective-permute-start.9 = (bf16[2,72,1024]{2,1,0:T(8,128)(2,1)S(1)}, bf16[2,72,1024]{2,1,0:T(8,128)(2,1)S(1)}, u32[]{:S(2)}, u32[]{:S(2)}) collective-permute-start(bf16[2,72,1024]{2,1,0:T(8,128)(2,1)S(1)} %pad_maximum_fusion.1.refs_4_), channel_id=1, source_target_pairs={{0,96},{16,112},{32,0},{48,16},{64,32},{80,48},{96,64},{112,80},{1... | collective-permute-start | bytes 884744 | tf_op jit(solution)/shard_map/ppermute | solution.py:66
  27.6 2.6 %collective-permute-start.3 = (bf16[4,72,512]{2,1,0:T(8,128)(2,1)S(1)}, bf16[4,72,512]{2,1,0:T(8,128)(2,1)S(1)}, u32[]{:S(2)}, u32[]{:S(2)}) collective-permute-start(bf16[4,72,512]{2,1,0:T(8,128)(2,1)S(1)} %pad_maximum_fusion.refs_0_), channel_id=1, source_target_pairs={{0,4},{1,5},{2,6},{3,7},{4,8},{5,9},{6,10},{7,11},{8,12},{9,13},{1... | collective-permute-start | bytes 884744 | tf_op jit(solution)/shard_map/ppermute | solution.py:58
  30.2 2.6 %collective-permute-done.4.refs_2_ = bf16[4,72,512]{2,1,0:T(8,128)(2,1)S(1)} collective-permute-done((bf16[4,72,512]{2,1,0:T(8,128)(2,1)S(1)}, bf16[4,72,512]{2,1,0:T(8,128)(2,1)S(1)}, u32[]{:S(2)}, u32[]{:S(2)}) %collective-permute-start.4) | collective-permute-done | bytes 294944 | tf_op jit(solution)/shard_map/ppermute | solution.py:58
  35.3 3.1 %collective-permute-done.7.refs_5_ = bf16[2,72,1024]{2,1,0:T(8,128)(2,1)S(1)} collective-permute-done((bf16[2,72,1024]{2,1,0:T(8,128)(2,1)S(1)}, bf16[2,72,1024]{2,1,0:T(8,128)(2,1)S(1)}, u32[]{:S(2)}, u32[]{:S(2)}) %collective-permute-start.7) | collective-permute-done | bytes 294944 | tf_op jit(solution)/shard_map/ppermute | solution.py:66
  40.8 9.2 %shard_map.77 = (f32[32,256]{1,0:T(8,128)}, f32[32,256]{1,0:T(8,128)}, f32[64,256]{1,0:T(8,128)}, bf16[12,8,256,256]{3,2,1,0:T(8,128)(2,1)}) custom-call(s32[96]{0:T(128)} %bitcast.42, s32[1]{0:T(128)} %bitcast.34.count_ref, s32[2]{0:T(128)} %pad_add_fusion.pos_ref, bf16[4,72,512]{2,1,0:T(8,128)(2,1)} %copy-done, bf16[4,72,512]{2,1,0:T(8,128)(2,1)} %copy-done.7, ...), custom_call_target="tpu_custom_call" | custom-call | tf_op jit(solution)/shard_map/pallas_call | solution.py:369
  51.9 2.9 %collective-permute-start.15 = (f32[32,256]{1,0:T(8,128)}, f32[32,256]{1,0:T(8,128)S(1)}, u32[]{:S(2)}, u32[]{:S(2)}) collective-permute-start(f32[32,256]{1,0:T(8,128)} %get-tuple-element.23), channel_id=1, source_target_pairs={{0,1},{1,0},{2,3},{3,2},{4,5},{5,4},{6,7},{7,6},{8,9},{9,8},{10,11... | collective-permute-start | bytes 98312 | tf_op jit(solution)/shard_map/ppermute | solution.py:78
  59.7 3.7 %collective-permute-start.17 = (f32[32,256]{1,0:T(8,128)S(1)}, f32[32,256]{1,0:T(8,128)S(1)}, u32[]{:S(2)}, u32[]{:S(2)}) collective-permute-start(f32[32,256]{1,0:T(8,128)S(1)} %add_add_fusion.3), channel_id=1, source_target_pairs={{0,12},{1,13},{2,14},{3,15},{4,8},{5,9},{6,10},{7,11},{8,4},{9,5},... | collective-permute-start | bytes 98312 | tf_op jit(solution)/shard_map/ppermute | solution.py:80
  65.3 7.0 %collective-permute-start.18 = (f32[32,256]{1,0:T(8,128)S(1)}, f32[32,256]{1,0:T(8,128)S(1)}, u32[]{:S(2)}, u32[]{:S(2)}) collective-permute-start(f32[32,256]{1,0:T(8,128)S(1)} %add.87.ra_ref), channel_id=1, source_target_pairs={{0,3},{1,2},{2,1},{3,0},{4,7},{5,6},{6,5},{7,4},{8,11},{9,10},{10,... | collective-permute-start | bytes 98312 | tf_op jit(solution)/shard_map/ppermute | solution.py:81
  74.2 3.7 %shard_map.78 = f32[64,256]{1,0:T(8,128)} custom-call(s32[96]{0:T(128)} %bitcast.43, s32[1]{0:T(128)} %bitcast.35.count_ref, f32[32,256]{1,0:T(8,128)S(1)} %add.87.ra_ref, f32[32,256]{1,0:T(8,128)S(1)} %collective-permute-done.18.rb_ref, f32[32,256]{1,0:T(8,128)} %get-tuple-element.24.m_ref, bf16[12,8,256,256]{3,2,1,0:T(8,128)(2,1)} %get-tuple-element.25.g_hbm), custom_call_target="tpu_custom_call" | custom-call | tf_op jit(solution)/shard_map/pallas_call | solution.py:369
  80.3 2.7 %collective-permute-start.22 = (f32[64,256]{1,0:T(8,128)S(1)}, f32[64,256]{1,0:T(8,128)S(1)}, u32[]{:S(2)}, u32[]{:S(2)}) collective-permute-start(f32[64,256]{1,0:T(8,128)S(1)} %add.88), channel_id=1, source_target_pairs={{0,160},{16,176},{32,128},{48,144},{64,224},{80,240},{96,192},{112... | collective-permute-start | bytes 196616 | tf_op jit(solution)/shard_map/ppermute | solution.py:87
  83.0 3.6 %collective-permute-start.21 = (f32[64,256]{1,0:T(8,128)S(1)}, f32[64,256]{1,0:T(8,128)S(1)}, u32[]{:S(2)}, u32[]{:S(2)}) collective-permute-start(f32[64,256]{1,0:T(8,128)S(1)} %add.88), channel_id=1, source_target_pairs={{0,32},{16,48},{32,0},{48,16},{64,96},{80,112},{96,64},{112,80},{1... | collective-permute-start | bytes 196616 | tf_op jit(solution)/shard_map/ppermute | solution.py:87
  92.2 4.2 %collective-permute-done.23.cb_ref = f32[64,256]{1,0:T(8,128)S(1)} collective-permute-done((f32[64,256]{1,0:T(8,128)S(1)}, f32[64,256]{1,0:T(8,128)S(1)}, u32[]{:S(2)}, u32[]{:S(2)}) %collective-permute-start.23) | collective-permute-done | bytes 65568 | tf_op jit(solution)/shard_map/ppermute | solution.py:90
  96.4 4.0 %shard_map.79 = f32[32,256]{1,0:T(8,128)} custom-call(s32[96]{0:T(128)} %bitcast.44, s32[1]{0:T(128)} %bitcast.36.count_ref, f32[64,256]{1,0:T(8,128)S(1)} %add_add_fusion.1.ca_ref, f32[64,256]{1,0:T(8,128)S(1)} %collective-permute-done.23.cb_ref, f32[64,256]{1,0:T(8,128)} %get-tuple-element.26.n_ref, bf16[12,8,256,256]{3,2,1,0:T(8,128)(2,1)} %get-tuple-element.25.g_hbm), custom_call_target="tpu_custom_call" | custom-call | tf_op jit(solution)/shard_map/pallas_call | solution.py:369
  102.3 4.3 %collective-permute-start.25 = (f32[32,256]{1,0:T(8,128)}, f32[32,256]{1,0:T(8,128)S(1)}, u32[]{:S(2)}, u32[]{:S(2)}) collective-permute-start(f32[32,256]{1,0:T(8,128)} %shard_map.79), channel_id=1, source_target_pairs={{0,1},{1,0},{2,3},{3,2},{4,5},{5,4},{6,7},{7,6},{8,9},{9,8},{10,11... | collective-permute-start | bytes 98312 | tf_op jit(solution)/shard_map/ppermute | solution.py:78
  106.6 2.4 %collective-permute-done.25 = f32[32,256]{1,0:T(8,128)S(1)} collective-permute-done((f32[32,256]{1,0:T(8,128)}, f32[32,256]{1,0:T(8,128)S(1)}, u32[]{:S(2)}, u32[]{:S(2)}) %collective-permute-start.25) | collective-permute-done | bytes 32800 | tf_op jit(solution)/shard_map/ppermute | solution.py:78
  111.5 3.6 %collective-permute-start.27 = (f32[32,256]{1,0:T(8,128)S(1)}, f32[32,256]{1,0:T(8,128)S(1)}, u32[]{:S(2)}, u32[]{:S(2)}) collective-permute-start(f32[32,256]{1,0:T(8,128)S(1)} %add_add_fusion.2), channel_id=1, source_target_pairs={{0,12},{1,13},{2,14},{3,15},{4,8},{5,9},{6,10},{7,11},{8,4},{9,5},... | collective-permute-start | bytes 98312 | tf_op jit(solution)/shard_map/ppermute | solution.py:80
  117.0 3.1 %collective-permute-start.28 = (f32[32,256]{1,0:T(8,128)S(1)}, f32[32,256]{1,0:T(8,128)S(1)}, u32[]{:S(2)}, u32[]{:S(2)}) collective-permute-start(f32[32,256]{1,0:T(8,128)S(1)} %add.95.ra_ref), channel_id=1, source_target_pairs={{0,3},{1,2},{2,1},{3,0},{4,7},{5,6},{6,5},{7,4},{8,11},{9,10},{10,... | collective-permute-start | bytes 98312 | tf_op jit(solution)/shard_map/ppermute | solution.py:81
  120.1 2.9 %collective-permute-done.28.rb_ref = f32[32,256]{1,0:T(8,128)S(1)} collective-permute-done((f32[32,256]{1,0:T(8,128)S(1)}, f32[32,256]{1,0:T(8,128)S(1)}, u32[]{:S(2)}, u32[]{:S(2)}) %collective-permute-start.28) | collective-permute-done | bytes 32800 | tf_op jit(solution)/shard_map/ppermute | solution.py:81
  123.0 3.7 %shard_map.80 = f32[64,256]{1,0:T(8,128)} custom-call(s32[96]{0:T(128)} %bitcast.45, s32[1]{0:T(128)} %bitcast.37.count_ref, f32[32,256]{1,0:T(8,128)S(1)} %add.95.ra_ref, f32[32,256]{1,0:T(8,128)S(1)} %collective-permute-done.28.rb_ref, f32[32,256]{1,0:T(8,128)} %get-tuple-element.24.m_ref, bf16[12,8,256,256]{3,2,1,0:T(8,128)(2,1)} %get-tuple-element.25.g_hbm), custom_call_target="tpu_custom_call" | custom-call | tf_op jit(solution)/shard_map/pallas_call | solution.py:369
  129.2 3.8 %collective-permute-start.31 = (f32[64,256]{1,0:T(8,128)S(1)}, f32[64,256]{1,0:T(8,128)S(1)}, u32[]{:S(2)}, u32[]{:S(2)}) collective-permute-start(f32[64,256]{1,0:T(8,128)S(1)} %add.96), channel_id=1, source_target_pairs={{0,32},{16,48},{32,0},{48,16},{64,96},{80,112},{96,64},{112,80},{1... | collective-permute-start | bytes 196616 | tf_op jit(solution)/shard_map/ppermute | solution.py:87
  138.4 4.5 %collective-permute-done.33.cb_ref = f32[64,256]{1,0:T(8,128)S(1)} collective-permute-done((f32[64,256]{1,0:T(8,128)S(1)}, f32[64,256]{1,0:T(8,128)S(1)}, u32[]{:S(2)}, u32[]{:S(2)}) %collective-permute-start.33) | collective-permute-done | bytes 65568 | tf_op jit(solution)/shard_map/ppermute | solution.py:90
  142.9 8.1 %shard_map.81 = (bf16[4,72,512]{2,1,0:T(8,128)(2,1)}, bf16[4,72,512]{2,1,0:T(8,128)(2,1)}, bf16[4,72,512]{2,1,0:T(8,128)(2,1)}, bf16[4,72,512]{2,1,0:T(8,128)(2,...) custom-call(s32[96]{0:T(128)} %bitcast.46, s32[1]{0:T(128)} %bitcast.38.count_ref, ...), custom_call_target="tpu_custom_call" | custom-call | tf_op jit(solution)/shard_map/pallas_call | solution.py:369
  151.4 4.0 %collective-permute-start.34 = (bf16[4,72,512]{2,1,0:T(8,128)(2,1)}, bf16[4,72,512]{2,1,0:T(8,128)(2,1)S(1)}, u32[]{:S(2)}, u32[]{:S(2)}) collective-permute-start(bf16[4,72,512]{2,1,0:T(8,128)(2,1)} %get-tuple-element.28), channel_id=1, source_target_pairs={{0,12},{1,13},{2,14},{3,15},{4,0},{5,1},{6,2},{7,3},{8,4},{9,5},{1... | collective-permute-start | bytes 884744 | tf_op jit(solution)/shard_map/ppermute | solution.py:58
  158.9 3.6 %collective-permute-start.39 = (bf16[2,64,1024]{2,1,0:T(8,128)(2,1)S(1)}, bf16[2,64,1024]{2,1,0:T(8,128)(2,1)S(1)}, u32[]{:S(2)}, u32[]{:S(2)}) collective-permute-start(bf16[2,64,1024]{2,1,0:T(8,128)(2,1)S(1)} %get-tuple-element.45), channel_id=1, source_target_pairs={{0,64},{16,80},{32,96},{48,112},{64,0},{80,16},{96,32},{112,48},{1... | collective-permute-start | bytes 786440 | tf_op jit(solution)/shard_map/ppermute | solution.py:66
  165.1 5.5 %collective-permute-done.35.c_ref = bf16[4,72,512]{2,1,0:T(8,128)(2,1)S(1)} collective-permute-done((bf16[4,72,512]{2,1,0:T(8,128)(2,1)}, bf16[4,72,512]{2,1,0:T(8,128)(2,1)S(1)}, u32[]{:S(2)}, u32[]{:S(2)}) %collective-permute-start.35) | collective-permute-done | bytes 294944 | tf_op jit(solution)/shard_map/ppermute | solution.py:58
  171.3 2.7 %collective-permute-done.39 = bf16[2,64,1024]{2,1,0:T(8,128)(2,1)S(1)} collective-permute-done((bf16[2,64,1024]{2,1,0:T(8,128)(2,1)S(1)}, bf16[2,64,1024]{2,1,0:T(8,128)(2,1)S(1)}, u32[]{:S(2)}, u32[]{:S(2)}) %collective-permute-start.39) | collective-permute-done | bytes 262176 | tf_op jit(solution)/shard_map/ppermute | solution.py:66
  175.7 9.3 %collective-permute-start.41 = (bf16[72,512]{1,0:T(8,128)(2,1)}, bf16[72,512]{1,0:T(8,128)(2,1)S(1)}, u32[]{:S(2)}, u32[]{:S(2)}) collective-permute-start(bf16[72,512]{1,0:T(8,128)(2,1)} %get-tuple-element.37), channel_id=1, source_target_pairs={{0,3},{1,0},{2,1},{3,2},{4,7},{5,4},{6,5},{7,6},{8,11},{9,8},{10,9... | collective-permute-start | bytes 221192 | tf_op jit(solution)/shard_map/ppermute | solution.py:62
  185.9 2.9 %collective-permute-start.43 = (bf16[72,512]{1,0:T(8,128)(2,1)}, bf16[72,512]{1,0:T(8,128)(2,1)S(1)}, u32[]{:S(2)}, u32[]{:S(2)}) collective-permute-start(bf16[72,512]{1,0:T(8,128)(2,1)} %get-tuple-element.39), channel_id=1, source_target_pairs={{0,1},{1,2},{2,3},{3,0},{4,5},{5,6},{6,7},{7,4},{8,9},{9,10},{10,1... | collective-permute-start | bytes 221192 | tf_op jit(solution)/shard_map/ppermute | solution.py:62
  192.0 4.1 %collective-permute-done.42 = bf16[72,512]{1,0:T(8,128)(2,1)S(1)} collective-permute-done((bf16[72,512]{1,0:T(8,128)(2,1)}, bf16[72,512]{1,0:T(8,128)(2,1)S(1)}, u32[]{:S(2)}, u32[]{:S(2)}) %collective-permute-start.42) | collective-permute-done | bytes 73760 | tf_op jit(solution)/shard_map/ppermute | solution.py:62
  (116 shorter events, 63.3 us)
Async XLA Ops:
  2.3 12.7 %collective-permute-start.2 = (bf16[1,72,512]{2,1,0:T(8,128)(2,1)S(1)}, bf16[1,72,512]{2,1,0:T(8,128)(2,1)S(1)}, u32[]{:S(2)}, u32[]{:S(2)}) collective-permute-start(bf16[1,72,512]{2,1,0:T(8,128)(2,1)S(1)} %maximum_bitcast_fusion.1), channel_id=1, source_target_pairs={{0,3},{1,0},{2,1},{3,2},{4,7},{5,4},{6,5},{7,6},{8,11},{9,8},{10,9... | collective-permute-start | bytes 221192 | tf_op jit(solution)/shard_map/ppermute | solution.py:62
  8.7 9.9 %collective-permute-start.1 = (bf16[1,72,512]{2,1,0:T(8,128)(2,1)S(1)}, bf16[1,72,512]{2,1,0:T(8,128)(2,1)S(1)}, u32[]{:S(2)}, u32[]{:S(2)}) collective-permute-start(bf16[1,72,512]{2,1,0:T(8,128)(2,1)S(1)} %maximum_bitcast_fusion.1), channel_id=1, source_target_pairs={{0,2},{1,3},{2,0},{3,1},{4,6},{5,7},{6,4},{7,5},{8,10},{9,11},{10,... | collective-permute-start | bytes 221192 | tf_op jit(solution)/shard_map/ppermute | solution.py:62
  9.7 9.0 %collective-permute-start = (bf16[1,72,512]{2,1,0:T(8,128)(2,1)S(1)}, bf16[1,72,512]{2,1,0:T(8,128)(2,1)S(1)}, u32[]{:S(2)}, u32[]{:S(2)}) collective-permute-start(bf16[1,72,512]{2,1,0:T(8,128)(2,1)S(1)} %maximum_bitcast_fusion.1), channel_id=1, source_target_pairs={{0,1},{1,2},{2,3},{3,0},{4,5},{5,6},{6,7},{7,4},{8,9},{9,10},{10,1... | collective-permute-start | bytes 221192 | tf_op jit(solution)/shard_map/ppermute | solution.py:62
  13.5 8.3 %collective-permute-start.6 = (bf16[1,72,1024]{2,1,0:T(8,128)(2,1)S(1)}, bf16[1,72,1024]{2,1,0:T(8,128)(2,1)S(1)}, u32[]{:S(2)}, u32[]{:S(2)}) collective-permute-start(bf16[1,72,1024]{2,1,0:T(8,128)(2,1)S(1)} %maximum_bitcast_fusion), channel_id=1, source_target_pairs={{0,128},{16,144},{32,160},{48,176},{64,192},{80,208},{96,224},{112... | collective-permute-start | bytes 442376 | tf_op jit(solution)/shard_map/ppermute | solution.py:74
  18.7 8.9 %collective-permute-start.5 = (bf16[4,72,512]{2,1,0:T(8,128)(2,1)S(1)}, bf16[4,72,512]{2,1,0:T(8,128)(2,1)S(1)}, u32[]{:S(2)}, u32[]{:S(2)}) collective-permute-start(bf16[4,72,512]{2,1,0:T(8,128)(2,1)S(1)} %pad_maximum_fusion.refs_0_), channel_id=1, source_target_pairs={{0,12},{1,13},{2,14},{3,15},{4,0},{5,1},{6,2},{7,3},{8,4},{9,5},{1... | collective-permute-start | bytes 884744 | tf_op jit(solution)/shard_map/ppermute | solution.py:58
  19.7 13.1 %collective-permute-start.4 = (bf16[4,72,512]{2,1,0:T(8,128)(2,1)S(1)}, bf16[4,72,512]{2,1,0:T(8,128)(2,1)S(1)}, u32[]{:S(2)}, u32[]{:S(2)}) collective-permute-start(bf16[4,72,512]{2,1,0:T(8,128)(2,1)S(1)} %pad_maximum_fusion.refs_0_), channel_id=1, source_target_pairs={{0,8},{1,9},{2,10},{3,11},{4,12},{5,13},{6,14},{7,15},{8,0},{9,1},... | collective-permute-start | bytes 884744 | tf_op jit(solution)/shard_map/ppermute | solution.py:58
  21.9 12.9 %collective-permute-start.9 = (bf16[2,72,1024]{2,1,0:T(8,128)(2,1)S(1)}, bf16[2,72,1024]{2,1,0:T(8,128)(2,1)S(1)}, u32[]{:S(2)}, u32[]{:S(2)}) collective-permute-start(bf16[2,72,1024]{2,1,0:T(8,128)(2,1)S(1)} %pad_maximum_fusion.1.refs_4_), channel_id=1, source_target_pairs={{0,96},{16,112},{32,0},{48,16},{64,32},{80,48},{96,64},{112,80},{1... | collective-permute-start | bytes 884744 | tf_op jit(solution)/shard_map/ppermute | solution.py:66
  24.7 10.6 %collective-permute-start.8 = (bf16[2,72,1024]{2,1,0:T(8,128)(2,1)S(1)}, bf16[2,72,1024]{2,1,0:T(8,128)(2,1)S(1)}, u32[]{:S(2)}, u32[]{:S(2)}) collective-permute-start(bf16[2,72,1024]{2,1,0:T(8,128)(2,1)S(1)} %pad_maximum_fusion.1.refs_4_), channel_id=1, source_target_pairs={{0,64},{16,80},{32,96},{48,112},{64,0},{80,16},{96,32},{112,48},{1... | collective-permute-start | bytes 884744 | tf_op jit(solution)/shard_map/ppermute | solution.py:66
  25.5 13.0 %collective-permute-start.7 = (bf16[2,72,1024]{2,1,0:T(8,128)(2,1)S(1)}, bf16[2,72,1024]{2,1,0:T(8,128)(2,1)S(1)}, u32[]{:S(2)}, u32[]{:S(2)}) collective-permute-start(bf16[2,72,1024]{2,1,0:T(8,128)(2,1)S(1)} %pad_maximum_fusion.1.refs_4_), channel_id=1, source_target_pairs={{0,32},{16,48},{32,64},{48,80},{64,96},{80,112},{96,0},{112,16},{1... | collective-permute-start | bytes 884744 | tf_op jit(solution)/shard_map/ppermute | solution.py:66
  27.6 12.1 %collective-permute-start.3 = (bf16[4,72,512]{2,1,0:T(8,128)(2,1)S(1)}, bf16[4,72,512]{2,1,0:T(8,128)(2,1)S(1)}, u32[]{:S(2)}, u32[]{:S(2)}) collective-permute-start(bf16[4,72,512]{2,1,0:T(8,128)(2,1)S(1)} %pad_maximum_fusion.refs_0_), channel_id=1, source_target_pairs={{0,4},{1,5},{2,6},{3,7},{4,8},{5,9},{6,10},{7,11},{8,12},{9,13},{1... | collective-permute-start | bytes 884744 | tf_op jit(solution)/shard_map/ppermute | solution.py:58
  32.9 6.8 %collective-permute-start.10 = (bf16[2,72,1024]{2,1,0:T(8,128)(2,1)S(1)}, bf16[2,72,1024]{2,1,0:T(8,128)(2,1)S(1)}, u32[]{:S(2)}, u32[]{:S(2)}) collective-permute-start(bf16[2,72,1024]{2,1,0:T(8,128)(2,1)S(1)} %pad_maximum_fusion.1.refs_4_), channel_id=1, source_target_pairs={{0,16},{16,0},{32,48},{48,32},{64,80},{80,64},{96,112},{112,96},{1... | collective-permute-start | bytes 884744 | tf_op jit(solution)/shard_map/ppermute | solution.py:70
  50.0 6.0 %collective-permute-start.16 = (f32[32,256]{1,0:T(8,128)}, f32[32,256]{1,0:T(8,128)S(1)}, u32[]{:S(2)}, u32[]{:S(2)}) collective-permute-start(f32[32,256]{1,0:T(8,128)} %get-tuple-element.23), channel_id=1, source_target_pairs={{0,5},{1,4},{2,7},{3,6},{4,1},{5,0},{6,3},{7,2},{8,13},{9,12},{10,... | collective-permute-start | bytes 98312 | tf_op jit(solution)/shard_map/ppermute | solution.py:78
  59.7 5.6 %collective-permute-start.17 = (f32[32,256]{1,0:T(8,128)S(1)}, f32[32,256]{1,0:T(8,128)S(1)}, u32[]{:S(2)}, u32[]{:S(2)}) collective-permute-start(f32[32,256]{1,0:T(8,128)S(1)} %add_add_fusion.3), channel_id=1, source_target_pairs={{0,12},{1,13},{2,14},{3,15},{4,8},{5,9},{6,10},{7,11},{8,4},{9,5},... | collective-permute-start | bytes 98312 | tf_op jit(solution)/shard_map/ppermute | solution.py:80
  65.3 8.9 %collective-permute-start.18 = (f32[32,256]{1,0:T(8,128)S(1)}, f32[32,256]{1,0:T(8,128)S(1)}, u32[]{:S(2)}, u32[]{:S(2)}) collective-permute-start(f32[32,256]{1,0:T(8,128)S(1)} %add.87.ra_ref), channel_id=1, source_target_pairs={{0,3},{1,2},{2,1},{3,0},{4,7},{5,6},{6,5},{7,4},{8,11},{9,10},{10,... | collective-permute-start | bytes 98312 | tf_op jit(solution)/shard_map/ppermute | solution.py:81
  80.3 6.3 %collective-permute-start.22 = (f32[64,256]{1,0:T(8,128)S(1)}, f32[64,256]{1,0:T(8,128)S(1)}, u32[]{:S(2)}, u32[]{:S(2)}) collective-permute-start(f32[64,256]{1,0:T(8,128)S(1)} %add.88), channel_id=1, source_target_pairs={{0,160},{16,176},{32,128},{48,144},{64,224},{80,240},{96,192},{112... | collective-permute-start | bytes 196616 | tf_op jit(solution)/shard_map/ppermute | solution.py:87
  83.0 5.8 %collective-permute-start.21 = (f32[64,256]{1,0:T(8,128)S(1)}, f32[64,256]{1,0:T(8,128)S(1)}, u32[]{:S(2)}, u32[]{:S(2)}) collective-permute-start(f32[64,256]{1,0:T(8,128)S(1)} %add.88), channel_id=1, source_target_pairs={{0,32},{16,48},{32,0},{48,16},{64,96},{80,112},{96,64},{112,80},{1... | collective-permute-start | bytes 196616 | tf_op jit(solution)/shard_map/ppermute | solution.py:87
  90.9 5.6 %collective-permute-start.23 = (f32[64,256]{1,0:T(8,128)S(1)}, f32[64,256]{1,0:T(8,128)S(1)}, u32[]{:S(2)}, u32[]{:S(2)}) collective-permute-start(f32[64,256]{1,0:T(8,128)S(1)} %add_add_fusion.1.ca_ref), channel_id=1, source_target_pairs={{0,96},{16,112},{32,64},{48,80},{64,32},{80,48},{96,0},{112,16},{1... | collective-permute-start | bytes 196616 | tf_op jit(solution)/shard_map/ppermute | solution.py:90
  100.4 6.2 %collective-permute-start.26 = (f32[32,256]{1,0:T(8,128)}, f32[32,256]{1,0:T(8,128)S(1)}, u32[]{:S(2)}, u32[]{:S(2)}) collective-permute-start(f32[32,256]{1,0:T(8,128)} %shard_map.79), channel_id=1, source_target_pairs={{0,5},{1,4},{2,7},{3,6},{4,1},{5,0},{6,3},{7,2},{8,13},{9,12},{10,... | collective-permute-start | bytes 98312 | tf_op jit(solution)/shard_map/ppermute | solution.py:78
  102.3 6.7 %collective-permute-start.25 = (f32[32,256]{1,0:T(8,128)}, f32[32,256]{1,0:T(8,128)S(1)}, u32[]{:S(2)}, u32[]{:S(2)}) collective-permute-start(f32[32,256]{1,0:T(8,128)} %shard_map.79), channel_id=1, source_target_pairs={{0,1},{1,0},{2,3},{3,2},{4,5},{5,4},{6,7},{7,6},{8,9},{9,8},{10,11... | collective-permute-start | bytes 98312 | tf_op jit(solution)/shard_map/ppermute | solution.py:78
  117.0 6.0 %collective-permute-start.28 = (f32[32,256]{1,0:T(8,128)S(1)}, f32[32,256]{1,0:T(8,128)S(1)}, u32[]{:S(2)}, u32[]{:S(2)}) collective-permute-start(f32[32,256]{1,0:T(8,128)S(1)} %add.95.ra_ref), channel_id=1, source_target_pairs={{0,3},{1,2},{2,1},{3,0},{4,7},{5,6},{6,5},{7,4},{8,11},{9,10},{10,... | collective-permute-start | bytes 98312 | tf_op jit(solution)/shard_map/ppermute | solution.py:81
  129.2 6.6 %collective-permute-start.31 = (f32[64,256]{1,0:T(8,128)S(1)}, f32[64,256]{1,0:T(8,128)S(1)}, u32[]{:S(2)}, u32[]{:S(2)}) collective-permute-start(f32[64,256]{1,0:T(8,128)S(1)} %add.96), channel_id=1, source_target_pairs={{0,32},{16,48},{32,0},{48,16},{64,96},{80,112},{96,64},{112,80},{1... | collective-permute-start | bytes 196616 | tf_op jit(solution)/shard_map/ppermute | solution.py:87
  151.1 6.4 %collective-permute-start.37 = (bf16[8,64,1024]{2,1,0:T(8,128)(2,1)}, bf16[8,64,1024]{2,1,0:T(8,128)(2,1)S(1)}, u32[]{:S(2)}, u32[]{:S(2)}) collective-permute-start(bf16[8,64,1024]{2,1,0:T(8,128)(2,1)} %get-tuple-element.32), channel_id=1, source_target_pairs={{0,16},{16,0},{32,48},{48,32},{64,80},{80,64},{96,112},{112,96},{1... | collective-permute-start | bytes 3145736 | tf_op jit(solution)/shard_map/ppermute | solution.py:70
  151.4 11.7 %collective-permute-start.34 = (bf16[4,72,512]{2,1,0:T(8,128)(2,1)}, bf16[4,72,512]{2,1,0:T(8,128)(2,1)S(1)}, u32[]{:S(2)}, u32[]{:S(2)}) collective-permute-start(bf16[4,72,512]{2,1,0:T(8,128)(2,1)} %get-tuple-element.28), channel_id=1, source_target_pairs={{0,12},{1,13},{2,14},{3,15},{4,0},{5,1},{6,2},{7,3},{8,4},{9,5},{1... | collective-permute-start | bytes 884744 | tf_op jit(solution)/shard_map/ppermute | solution.py:58
  155.4 15.2 %collective-permute-start.35 = (bf16[4,72,512]{2,1,0:T(8,128)(2,1)}, bf16[4,72,512]{2,1,0:T(8,128)(2,1)S(1)}, u32[]{:S(2)}, u32[]{:S(2)}) collective-permute-start(bf16[4,72,512]{2,1,0:T(8,128)(2,1)} %get-tuple-element.29), channel_id=1, source_target_pairs={{0,8},{1,9},{2,10},{3,11},{4,12},{5,13},{6,14},{7,15},{8,0},{9,1},... | collective-permute-start | bytes 884744 | tf_op jit(solution)/shard_map/ppermute | solution.py:58
  156.8 14.5 %collective-permute-start.36 = (bf16[4,72,512]{2,1,0:T(8,128)(2,1)}, bf16[4,72,512]{2,1,0:T(8,128)(2,1)S(1)}, u32[]{:S(2)}, u32[]{:S(2)}) collective-permute-start(bf16[4,72,512]{2,1,0:T(8,128)(2,1)} %get-tuple-element.30), channel_id=1, source_target_pairs={{0,4},{1,5},{2,6},{3,7},{4,8},{5,9},{6,10},{7,11},{8,12},{9,13},{1... | collective-permute-start | bytes 884744 | tf_op jit(solution)/shard_map/ppermute | solution.py:58
  158.8 12.4 %collective-permute-start.40 = (bf16[2,64,1024]{2,1,0:T(8,128)(2,1)S(1)}, bf16[2,64,1024]{2,1,0:T(8,128)(2,1)S(1)}, u32[]{:S(2)}, u32[]{:S(2)}) collective-permute-start(bf16[2,64,1024]{2,1,0:T(8,128)(2,1)S(1)} %get-tuple-element.44), channel_id=1, source_target_pairs={{0,32},{16,48},{32,64},{48,80},{64,96},{80,112},{96,0},{112,16},{1... | collective-permute-start | bytes 786440 | tf_op jit(solution)/shard_map/ppermute | solution.py:66
  158.9 15.0 %collective-permute-start.39 = (bf16[2,64,1024]{2,1,0:T(8,128)(2,1)S(1)}, bf16[2,64,1024]{2,1,0:T(8,128)(2,1)S(1)}, u32[]{:S(2)}, u32[]{:S(2)}) collective-permute-start(bf16[2,64,1024]{2,1,0:T(8,128)(2,1)S(1)} %get-tuple-element.45), channel_id=1, source_target_pairs={{0,64},{16,80},{32,96},{48,112},{64,0},{80,16},{96,32},{112,48},{1... | collective-permute-start | bytes 786440 | tf_op jit(solution)/shard_map/ppermute | solution.py:66
  163.1 10.8 %collective-permute-start.38 = (bf16[2,64,1024]{2,1,0:T(8,128)(2,1)S(1)}, bf16[2,64,1024]{2,1,0:T(8,128)(2,1)S(1)}, u32[]{:S(2)}, u32[]{:S(2)}) collective-permute-start(bf16[2,64,1024]{2,1,0:T(8,128)(2,1)S(1)} %get-tuple-element.46), channel_id=1, source_target_pairs={{0,96},{16,112},{32,0},{48,16},{64,32},{80,48},{96,64},{112,80},{1... | collective-permute-start | bytes 786440 | tf_op jit(solution)/shard_map/ppermute | solution.py:66
  175.7 16.3 %collective-permute-start.41 = (bf16[72,512]{1,0:T(8,128)(2,1)}, bf16[72,512]{1,0:T(8,128)(2,1)S(1)}, u32[]{:S(2)}, u32[]{:S(2)}) collective-permute-start(bf16[72,512]{1,0:T(8,128)(2,1)} %get-tuple-element.37), channel_id=1, source_target_pairs={{0,3},{1,0},{2,1},{3,2},{4,7},{5,4},{6,5},{7,6},{8,11},{9,8},{10,9... | collective-permute-start | bytes 221192 | tf_op jit(solution)/shard_map/ppermute | solution.py:62
  185.0 11.2 %collective-permute-start.42 = (bf16[72,512]{1,0:T(8,128)(2,1)}, bf16[72,512]{1,0:T(8,128)(2,1)S(1)}, u32[]{:S(2)}, u32[]{:S(2)}) collective-permute-start(bf16[72,512]{1,0:T(8,128)(2,1)} %get-tuple-element.38), channel_id=1, source_target_pairs={{0,2},{1,3},{2,0},{3,1},{4,6},{5,7},{6,4},{7,5},{8,10},{9,11},{10,... | collective-permute-start | bytes 221192 | tf_op jit(solution)/shard_map/ppermute | solution.py:62
  185.9 10.2 %collective-permute-start.43 = (bf16[72,512]{1,0:T(8,128)(2,1)}, bf16[72,512]{1,0:T(8,128)(2,1)S(1)}, u32[]{:S(2)}, u32[]{:S(2)}) collective-permute-start(bf16[72,512]{1,0:T(8,128)(2,1)} %get-tuple-element.39), channel_id=1, source_target_pairs={{0,1},{1,2},{2,3},{3,0},{4,5},{5,6},{6,7},{7,4},{8,9},{9,10},{10,1... | collective-permute-start | bytes 221192 | tf_op jit(solution)/shard_map/ppermute | solution.py:62
  190.0 7.8 %collective-permute-start.44 = (bf16[64,1024]{1,0:T(8,128)(2,1)S(1)}, bf16[64,1024]{1,0:T(8,128)(2,1)S(1)}, u32[]{:S(2)}, u32[]{:S(2)}) collective-permute-start(bf16[64,1024]{1,0:T(8,128)(2,1)S(1)} %fusion.4), channel_id=1, source_target_pairs={{0,128},{16,144},{32,160},{48,176},{64,192},{80,208},{96,224},{112... | collective-permute-start | bytes 393224 | tf_op jit(solution)/shard_map/ppermute | solution.py:74
  (27 other events, 269.0 us)
where the time goes:
time: 201 us; the launch traced here: 199 us
  starting transfers between devices  89.1 us (44%)
  waiting for transfers between devices  64.2 us (32%)
  Pallas kernels  30.5 us (15%)
  other arithmetic  10.8 us (5%)
  local copies, waits for them, and re-layouts  2.3 us (1%)
    pallas_call x6, Pallas kernels, call(): pl.pallas_call(kernel, in_specs=in_specs, out_specs=[spec for spec, _, _...  30.5 us
    ppermute x6, starting transfers between devices, shift_z(): return lax.ppermute(a, 'photo', photo_perm(same, shift(k)))  23.3 us
    ppermute x6, starting transfers between devices, shift_y(): return lax.ppermute(a, 'photo', photo_perm(shift(k), same))  11.7 us
    ppermute x6, starting transfers between devices, sum_photo(): lax.ppermute(a, 'photo', photo_perm(fy, fz))  11 us
    ppermute x6, waiting for transfers between devices, shift_y(): return lax.ppermute(a, 'photo', photo_perm(shift(k), same))  10.6 us
    ppermute x6, starting transfers between devices, sum_spec(): lax.ppermute(a, 'spec', spec_perm(fl, fx, same))  10.2 us
    ppermute x2, starting transfers between devices, sum_photo(): return (a, lax.ppermute(a, 'photo', photo_perm(same, mirror)))  10.1 us
    ppermute x6, starting transfers between devices, shift_x(): return lax.ppermute(a, 'spec', spec_perm(same, shift(k), same))  9.47 us
  transfers between devices with their start and end apart: 45, of which 31 were waited for; matrix products, arithmetic and copies ran while one was open for 3% of the time, Pallas kernels for 0%

commit v1 on v0

--- a/solution.py
+++ b/solution.py
@@ -58,8 +58,12 @@
     return lax.ppermute(a, "photo", photo_perm(shift(k), same))
 
 
-def shift_z(a, k):
-    return lax.ppermute(a, "photo", photo_perm(same, shift(k)))
+def flip_z(a):
+    return lax.ppermute(a, "photo", photo_perm(same, flip))
+
+
+def mirror_z(a):
+    return lax.ppermute(a, "photo", photo_perm(same, mirror))
 
 
 def shift_x(a, k):
@@ -91,7 +95,8 @@
 
 
 def spec_slot(q, photo_id):
-    return (((photo_id >> 2) - (q >> 2)) & 3) * 4 + ((photo_id - q) & 3)
+    across = (photo_id ^ q) & 3
+    return (((photo_id >> 2) - (q >> 2)) & 3) * 4 + (across ^ (across >> 1))
 
 
 def photo_slot(q, spec_id):
@@ -348,16 +353,19 @@
         send.wait()
 
 
-def relay_kernel(a_ref, b_ref, c_ref, d_ref, own_ref, *send_refs):
-    for k in range(4):
-        parts = [ref[k].astype(f32) for ref in (a_ref, b_ref, c_ref, d_ref)]
-        part = parts[0] + parts[1] + parts[2] + parts[3]
-        if k == 0:
-            own_ref[...] = part
+def relay_kernel(*refs):
+    *in_refs, own_ref, send_ref = refs
+    half = own_ref.shape[0]
+    for k in range(2 * half):
+        part = in_refs[0][k].astype(f32)
+        for ref in in_refs[1:]:
+            part = part + ref[k].astype(f32)
+        if k < half:
+            own_ref[k] = part
             continue
-        send_refs[k - 1][0:F, :] = part[0:F, :].astype(bf16)
+        send_ref[k - half, 0:F, :] = part[0:F, :].astype(bf16)
         total = jnp.broadcast_to(part[F : F + 1, :] + part[F + 1 : F + 2, :], (8, SB))
-        send_refs[k - 1][F:EXT, :] = high_low_rows(total)
+        send_ref[k - half, F:EXT, :] = high_low_rows(total)
 
 
 SMEM = pl.BlockSpec(memory_space=pltpu.SMEM)
@@ -394,10 +402,12 @@
     x0 = jnp.concatenate([x_own, spec_mass.reshape(1, SB), x_pad])[None]
     y0 = jnp.concatenate([y_own, photo_mass.reshape(1, PB), y_pad])[None]
 
-    x_parts = [shift_z(x0, k) for k in (1, 2, 3)]
+    x_flip = flip_z(x0)
     y_low = swap_low(y0)
+    x0 = jnp.concatenate([x0, x_flip])
+    x_mirror = mirror_z(x0)
     y0 = jnp.concatenate([y0, y_low])
-    x0 = jnp.concatenate([x0] + x_parts)
+    x0 = jnp.concatenate([x0, x_mirror])
     ys = [y0] + [shift_x(y0, k) for k in (1, 2, 3)]
     xs = [x0] + [shift_y(x0, k) for k in (1, 2, 3)]
     ys = ys + [swap_core(y) for y in ys]
@@ -456,23 +466,27 @@
     spec_parts, photo_parts = (parts[0:4], parts[4:6])
     far = swap_core(photo_parts[1])
     y_parts = [shift_y(spec_parts[k], -k) for k in (1, 2, 3)]
-    photo_sums = [
-        photo_parts[0][2 * k : 2 * k + 2].astype(f32) + far[2 * k : 2 * k + 2].astype(f32) for k in range(4)
-    ]
-    x_parts = [shift_x(photo_sums[k].astype(bf16), -k) for k in (1, 2, 3)]
-    y_parts, x_parts = lax.optimization_barrier((y_parts, x_parts))
-    spec_sum, *z_parts = call(
-        relay_kernel, [VMEM] * 4,
-        [(VMEM, (EXT, SB), f32)] + [(VMEM, (EXT, SB), bf16)] * 3, [],
-        spec_parts[0], *in_vmem(y_parts),
-    )
-    z_parts = [shift_z(part, -k) for k, part in zip((1, 2, 3), z_parts)]
+    photo_sums = [photo_parts[0][2 * k : 2 * k + 2].astype(f32) + far[2 * k : 2 * k + 2].astype(f32) for k in range(4)]
+    x_parts = [total.astype(bf16) for total in photo_sums[1:]]
+    x_parts = [shift_x(part, -k) for k, part in zip((1, 2, 3), x_parts)]
+
+    def relay(half, first, rest):
+        return call(
+            relay_kernel, [VMEM] * (1 + len(rest)),
+            [(VMEM, (half, EXT, SB), f32), (VMEM, (half, EXT, SB), bf16)], [], first, *in_vmem(rest),
+        )
+
+    spec_sum, send = relay(2, spec_parts[0], y_parts)
+    mirrored = mirror_z(send)
+    spec_sum, send = relay(1, spec_sum, [mirrored])
+    flipped = flip_z(send)
+    spec_sum = spec_sum[0] + flipped[0].astype(f32)
     photo_sum = photo_sums[0]
     for part in x_parts:
         photo_sum = photo_sum + part.astype(f32)
-    for part in z_parts:
-        spec_sum = spec_sum + part.astype(f32)
-    photo_sum = photo_sum[0] + swap_low(photo_sum[1].astype(bf16)).astype(f32)
+    photo_send = photo_sum[1].astype(bf16)
+    lowered = swap_low(photo_send)
+    photo_sum = photo_sum[0] + lowered.astype(f32)
     row_marginal = spec_sum[F : F + 1] + spec_sum[F + 1 : F + 2]
     grad_spec = 2.0 * (row_marginal * x_own.astype(f32) - spec_sum[0:F])
     grad_photo = 2.0 * (share * y_own.astype(f32) - photo_sum)

time: 201 us -> 214 us (1.065)
  waiting for transfers between devices: 64.2 us -> 79.8 us
  starting transfers between devices: 89.1 us -> 83.1 us
    ppermute x6, waiting for transfers between devices: 8.24 us -> 18.7 us  [shift_x(): return lax.ppermute(a, 'spec', spec_perm(same, shift(k), same))]
    ppermute x6 -> x4, starting transfers between devices: 23.3 us -> 15.9 us  [the longest x2 8.56 us: mirror_z(): return lax.ppermute(a, 'photo', photo_perm(same, mirror))]
    ppermute x6, waiting for transfers between devices: 10.6 us -> 17.1 us  [shift_y(): return lax.ppermute(a, 'photo', photo_perm(shift(k), same))]
    ppermute x2, starting transfers between devices: 2.4 us -> 6.6 us  [sum_spec(): return (a, lax.ppermute(a, 'spec', spec_perm(same, mirror, same)))]
    ppermute x2, waiting for transfers between devices: 8.73 us -> 4.82 us  [sum_spec(): return (a, lax.ppermute(a, 'spec', spec_perm(same, mirror, same)))]
    ppermute x2, starting transfers between devices: 7.28 us -> 3.63 us  [sum_photo(): a = a + lax.ppermute(a, 'photo', photo_perm(mirror, same))]
    ppermute x2, waiting for transfers between devices: 0.01 us -> 2.27 us  [swap_low(): return lax.ppermute(a, 'spec', spec_perm(flip, same, same))]
    ppermute x6 -> x4, waiting for transfers between devices: 8.16 us -> 6.14 us  [the longest x2 5.55 us: mirror_z(): return lax.ppermute(a, 'photo', photo_perm(same, mirror))]
  transfers between devices with their start and end apart: 45 -> 43, of which waited for: 31 -> 30; matrix products, arithmetic and copies ran while one was open for 3% -> 3% of each run, Pallas kernels for 0% -> 2%
where the time goes in v1:
time: 214 us; the launch traced here: 210 us
  starting transfers between devices  83.1 us (39%)
  waiting for transfers between devices  79.8 us (37%)
  Pallas kernels  32.2 us (15%)
  other arithmetic  10.8 us (5%)
  local copies, waits for them, and re-layouts  2.49 us (1%)
    pallas_call x7, Pallas kernels, call(): pl.pallas_call(kernel, in_specs=in_specs, out_specs=[spec for spec, _, _...  32.2 us
    ppermute x6, waiting for transfers between devices, shift_x(): return lax.ppermute(a, 'spec', spec_perm(same, shift(k), same))  18.7 us
    ppermute x6, waiting for transfers between devices, shift_y(): return lax.ppermute(a, 'photo', photo_perm(shift(k), same))  17.1 us
    ppermute x6, starting transfers between devices, sum_photo(): lax.ppermute(a, 'photo', photo_perm(fy, fz))  12.1 us
    ppermute x6, starting transfers between devices, sum_spec(): lax.ppermute(a, 'spec', spec_perm(fl, fx, same))  11.5 us
    ppermute x6, starting transfers between devices, shift_y(): return lax.ppermute(a, 'photo', photo_perm(shift(k), same))  11.4 us
    ppermute x2, starting transfers between devices, sum_photo(): return (a, lax.ppermute(a, 'photo', photo_perm(same, mirror)))  8.86 us
    ppermute x2, starting transfers between devices, mirror_z(): return lax.ppermute(a, 'photo', photo_perm(same, mirror))  8.56 us
  transfers between devices with their start and end apart: 43, of which 30 were waited for; matrix products, arithmetic and copies ran while one was open for 3% of the time, Pallas kernels for 2%

profile of v1, /device:TPU:8, one launch (start us, length us, event | category | flops | bytes accessed | tf_op | source)
XLA Modules:
  0.0 210.0 jit_solution(9309876937080194730)
XLA Ops:
  2.3 3.4 %collective-permute-start = (bf16[1,72,512]{2,1,0:T(8,128)(2,1)S(1)}, bf16[1,72,512]{2,1,0:T(8,128)(2,1)S(1)}, u32[]{:S(2)}, u32[]{:S(2)}) collective-permute-start(bf16[1,72,512]{2,1,0:T(8,128)(2,1)S(1)} %maximum_bitcast_fusion.1), channel_id=1, source_target_pairs={{0,1},{1,0},{2,3},{3,2},{4,5},{5,4},{6,7},{7,6},{8,9},{9,8},{10,11... | collective-permute-start | bytes 221192 | tf_op jit(solution)/shard_map/ppermute | solution.py:62
  9.3 4.8 %collective-permute-start.1 = (bf16[2,72,512]{2,1,0:T(8,128)(2,1)S(1)}, bf16[2,72,512]{2,1,0:T(8,128)(2,1)S(1)}, u32[]{:S(2)}, u32[]{:S(2)}) collective-permute-start(bf16[2,72,512]{2,1,0:T(8,128)(2,1)S(1)} %pad_maximum_fusion.2), channel_id=1, source_target_pairs={{0,3},{1,2},{2,1},{3,0},{4,7},{5,6},{6,5},{7,4},{8,11},{9,10},{10,... | collective-permute-start | bytes 442376 | tf_op jit(solution)/shard_map/ppermute | solution.py:66
  14.3 2.8 %collective-permute-start.8 = (bf16[2,72,1024]{2,1,0:T(8,128)(2,1)S(1)}, bf16[2,72,1024]{2,1,0:T(8,128)(2,1)S(1)}, u32[]{:S(2)}, u32[]{:S(2)}) collective-permute-start(bf16[2,72,1024]{2,1,0:T(8,128)(2,1)S(1)} %pad_maximum_fusion.1.refs_4_), channel_id=1, source_target_pairs={{0,96},{16,112},{32,0},{48,16},{64,32},{80,48},{96,64},{112,80},{1... | collective-permute-start | bytes 884744 | tf_op jit(solution)/shard_map/ppermute | solution.py:70
  20.6 2.6 %collective-permute-start.3 = (bf16[4,72,512]{2,1,0:T(8,128)(2,1)S(1)}, bf16[4,72,512]{2,1,0:T(8,128)(2,1)S(1)}, u32[]{:S(2)}, u32[]{:S(2)}) collective-permute-start(bf16[4,72,512]{2,1,0:T(8,128)(2,1)S(1)} %pad_maximum_fusion.refs_0_), channel_id=1, source_target_pairs={{0,8},{1,9},{2,10},{3,11},{4,12},{5,13},{6,14},{7,15},{8,0},{9,1},... | collective-permute-start | bytes 884744 | tf_op jit(solution)/shard_map/ppermute | solution.py:58
  23.1 7.2 %collective-permute-done.8.refs_7_ = bf16[2,72,1024]{2,1,0:T(8,128)(2,1)S(1)} collective-permute-done((bf16[2,72,1024]{2,1,0:T(8,128)(2,1)S(1)}, bf16[2,72,1024]{2,1,0:T(8,128)(2,1)S(1)}, u32[]{:S(2)}, u32[]{:S(2)}) %collective-permute-start.8) | collective-permute-done | bytes 294944 | tf_op jit(solution)/shard_map/ppermute | solution.py:70
  35.8 2.8 %collective-permute-done.2.refs_1_ = bf16[4,72,512]{2,1,0:T(8,128)(2,1)S(1)} collective-permute-done((bf16[4,72,512]{2,1,0:T(8,128)(2,1)S(1)}, bf16[4,72,512]{2,1,0:T(8,128)(2,1)S(1)}, u32[]{:S(2)}, u32[]{:S(2)}) %collective-permute-start.2) | collective-permute-done | bytes 294944 | tf_op jit(solution)/shard_map/ppermute | solution.py:58
  39.7 9.2 %shard_map.77 = (f32[32,256]{1,0:T(8,128)}, f32[32,256]{1,0:T(8,128)}, f32[64,256]{1,0:T(8,128)}, bf16[12,8,256,256]{3,2,1,0:T(8,128)(2,1)}) custom-call(s32[96]{0:T(128)} %bitcast.50, s32[1]{0:T(128)} %bitcast.42.count_ref, s32[2]{0:T(128)} %pad_add_fusion.pos_ref, bf16[4,72,512]{2,1,0:T(8,128)(2,1)} %copy-done.1, bf16[4,72,512]{2,1,0:T(8,128)(2,1)} %copy-done.8, ...), custom_call_target="tpu_custom_call" | custom-call | tf_op jit(solution)/shard_map/pallas_call | solution.py:377
  48.9 3.2 %collective-permute-start.15 = (f32[32,256]{1,0:T(8,128)}, f32[32,256]{1,0:T(8,128)S(1)}, u32[]{:S(2)}, u32[]{:S(2)}) collective-permute-start(f32[32,256]{1,0:T(8,128)} %get-tuple-element.17), channel_id=1, source_target_pairs={{0,5},{1,4},{2,7},{3,6},{4,1},{5,0},{6,3},{7,2},{8,13},{9,12},{10,... | collective-permute-start | bytes 98312 | tf_op jit(solution)/shard_map/ppermute | solution.py:82
  58.7 3.5 %collective-permute-start.16 = (f32[32,256]{1,0:T(8,128)S(1)}, f32[32,256]{1,0:T(8,128)S(1)}, u32[]{:S(2)}, u32[]{:S(2)}) collective-permute-start(f32[32,256]{1,0:T(8,128)S(1)} %add_add_fusion.3), channel_id=1, source_target_pairs={{0,12},{1,13},{2,14},{3,15},{4,8},{5,9},{6,10},{7,11},{8,4},{9,5},... | collective-permute-start | bytes 98312 | tf_op jit(solution)/shard_map/ppermute | solution.py:84
  64.2 6.2 %collective-permute-start.17 = (f32[32,256]{1,0:T(8,128)S(1)}, f32[32,256]{1,0:T(8,128)S(1)}, u32[]{:S(2)}, u32[]{:S(2)}) collective-permute-start(f32[32,256]{1,0:T(8,128)S(1)} %add.83.ra_ref), channel_id=1, source_target_pairs={{0,3},{1,2},{2,1},{3,0},{4,7},{5,6},{6,5},{7,4},{8,11},{9,10},{10,... | collective-permute-start | bytes 98312 | tf_op jit(solution)/shard_map/ppermute | solution.py:85
  72.3 3.7 %shard_map.78 = f32[64,256]{1,0:T(8,128)} custom-call(s32[96]{0:T(128)} %bitcast.51, s32[1]{0:T(128)} %bitcast.43.count_ref, f32[32,256]{1,0:T(8,128)S(1)} %add.83.ra_ref, f32[32,256]{1,0:T(8,128)S(1)} %collective-permute-done.17.rb_ref, f32[32,256]{1,0:T(8,128)} %get-tuple-element.18.m_ref, bf16[12,8,256,256]{3,2,1,0:T(8,128)(2,1)} %get-tuple-element.19.g_hbm), custom_call_target="tpu_custom_call" | custom-call | tf_op jit(solution)/shard_map/pallas_call | solution.py:377
  78.4 2.6 %collective-permute-start.21 = (f32[64,256]{1,0:T(8,128)S(1)}, f32[64,256]{1,0:T(8,128)S(1)}, u32[]{:S(2)}, u32[]{:S(2)}) collective-permute-start(f32[64,256]{1,0:T(8,128)S(1)} %add.84), channel_id=1, source_target_pairs={{0,160},{16,176},{32,128},{48,144},{64,224},{80,240},{96,192},{112... | collective-permute-start | bytes 196616 | tf_op jit(solution)/shard_map/ppermute | solution.py:91
  81.0 4.2 %collective-permute-start.20 = (f32[64,256]{1,0:T(8,128)S(1)}, f32[64,256]{1,0:T(8,128)S(1)}, u32[]{:S(2)}, u32[]{:S(2)}) collective-permute-start(f32[64,256]{1,0:T(8,128)S(1)} %add.84), channel_id=1, source_target_pairs={{0,32},{16,48},{32,0},{48,16},{64,96},{80,112},{96,64},{112,80},{1... | collective-permute-start | bytes 196616 | tf_op jit(solution)/shard_map/ppermute | solution.py:91
  89.5 3.6 %collective-permute-start.22 = (f32[64,256]{1,0:T(8,128)S(1)}, f32[64,256]{1,0:T(8,128)S(1)}, u32[]{:S(2)}, u32[]{:S(2)}) collective-permute-start(f32[64,256]{1,0:T(8,128)S(1)} %add_add_fusion.1.ca_ref), channel_id=1, source_target_pairs={{0,96},{16,112},{32,64},{48,80},{64,32},{80,48},{96,0},{112,16},{1... | collective-permute-start | bytes 196616 | tf_op jit(solution)/shard_map/ppermute | solution.py:94
  95.3 4.0 %shard_map.79 = f32[32,256]{1,0:T(8,128)} custom-call(s32[96]{0:T(128)} %bitcast.52, s32[1]{0:T(128)} %bitcast.44.count_ref, f32[64,256]{1,0:T(8,128)S(1)} %add_add_fusion.1.ca_ref, f32[64,256]{1,0:T(8,128)S(1)} %collective-permute-done.22.cb_ref, f32[64,256]{1,0:T(8,128)} %get-tuple-element.20.n_ref, bf16[12,8,256,256]{3,2,1,0:T(8,128)(2,1)} %get-tuple-element.19.g_hbm), custom_call_target="tpu_custom_call" | custom-call | tf_op jit(solution)/shard_map/pallas_call | solution.py:377
  100.1 6.4 %collective-permute-start.24 = (f32[32,256]{1,0:T(8,128)}, f32[32,256]{1,0:T(8,128)S(1)}, u32[]{:S(2)}, u32[]{:S(2)}) collective-permute-start(f32[32,256]{1,0:T(8,128)} %shard_map.79), channel_id=1, source_target_pairs={{0,1},{1,0},{2,3},{3,2},{4,5},{5,4},{6,7},{7,6},{8,9},{9,8},{10,11... | collective-permute-start | bytes 98312 | tf_op jit(solution)/shard_map/ppermute | solution.py:82
  111.5 3.9 %collective-permute-done.26 = f32[32,256]{1,0:T(8,128)S(1)} collective-permute-done((f32[32,256]{1,0:T(8,128)S(1)}, f32[32,256]{1,0:T(8,128)S(1)}, u32[]{:S(2)}, u32[]{:S(2)}) %collective-permute-start.26) | collective-permute-done | bytes 32800 | tf_op jit(solution)/shard_map/ppermute | solution.py:84
  115.4 2.6 %collective-permute-start.27 = (f32[32,256]{1,0:T(8,128)S(1)}, f32[32,256]{1,0:T(8,128)S(1)}, u32[]{:S(2)}, u32[]{:S(2)}) collective-permute-start(f32[32,256]{1,0:T(8,128)S(1)} %add.91.ra_ref), channel_id=1, source_target_pairs={{0,3},{1,2},{2,1},{3,0},{4,7},{5,6},{6,5},{7,4},{8,11},{9,10},{10,... | collective-permute-start | bytes 98312 | tf_op jit(solution)/shard_map/ppermute | solution.py:85
  118.1 3.4 %collective-permute-done.27.rb_ref = f32[32,256]{1,0:T(8,128)S(1)} collective-permute-done((f32[32,256]{1,0:T(8,128)S(1)}, f32[32,256]{1,0:T(8,128)S(1)}, u32[]{:S(2)}, u32[]{:S(2)}) %collective-permute-start.27) | collective-permute-done | bytes 32800 | tf_op jit(solution)/shard_map/ppermute | solution.py:85
  121.4 3.7 %shard_map.80 = f32[64,256]{1,0:T(8,128)} custom-call(s32[96]{0:T(128)} %bitcast.53, s32[1]{0:T(128)} %bitcast.45.count_ref, f32[32,256]{1,0:T(8,128)S(1)} %add.91.ra_ref, f32[32,256]{1,0:T(8,128)S(1)} %collective-permute-done.27.rb_ref, f32[32,256]{1,0:T(8,128)} %get-tuple-element.18.m_ref, bf16[12,8,256,256]{3,2,1,0:T(8,128)(2,1)} %get-tuple-element.19.g_hbm), custom_call_target="tpu_custom_call" | custom-call | tf_op jit(solution)/shard_map/pallas_call | solution.py:377
  128.3 4.1 %collective-permute-start.30 = (f32[64,256]{1,0:T(8,128)S(1)}, f32[64,256]{1,0:T(8,128)S(1)}, u32[]{:S(2)}, u32[]{:S(2)}) collective-permute-start(f32[64,256]{1,0:T(8,128)S(1)} %add.92), channel_id=1, source_target_pairs={{0,32},{16,48},{32,0},{48,16},{64,96},{80,112},{96,64},{112,80},{1... | collective-permute-start | bytes 196616 | tf_op jit(solution)/shard_map/ppermute | solution.py:91
  136.6 3.0 %collective-permute-start.32 = (f32[64,256]{1,0:T(8,128)S(1)}, f32[64,256]{1,0:T(8,128)S(1)}, u32[]{:S(2)}, u32[]{:S(2)}) collective-permute-start(f32[64,256]{1,0:T(8,128)S(1)} %add_add_fusion.ca_ref), channel_id=1, source_target_pairs={{0,96},{16,112},{32,64},{48,80},{64,32},{80,48},{96,0},{112,16},{1... | collective-permute-start | bytes 196616 | tf_op jit(solution)/shard_map/ppermute | solution.py:94
  139.6 2.6 %collective-permute-done.32.cb_ref = f32[64,256]{1,0:T(8,128)S(1)} collective-permute-done((f32[64,256]{1,0:T(8,128)S(1)}, f32[64,256]{1,0:T(8,128)S(1)}, u32[]{:S(2)}, u32[]{:S(2)}) %collective-permute-start.32) | collective-permute-done | bytes 65568 | tf_op jit(solution)/shard_map/ppermute | solution.py:94
  142.2 8.1 %shard_map.81 = (bf16[4,72,512]{2,1,0:T(8,128)(2,1)}, bf16[4,72,512]{2,1,0:T(8,128)(2,1)}, bf16[4,72,512]{2,1,0:T(8,128)(2,1)}, bf16[4,72,512]{2,1,0:T(8,128)(2,...) custom-call(s32[96]{0:T(128)} %bitcast.54, s32[1]{0:T(128)} %bitcast.46.count_ref, ...), custom_call_target="tpu_custom_call" | custom-call | tf_op jit(solution)/shard_map/pallas_call | solution.py:377
  150.4 4.9 %collective-permute-start.33 = (bf16[4,72,512]{2,1,0:T(8,128)(2,1)}, bf16[4,72,512]{2,1,0:T(8,128)(2,1)S(1)}, u32[]{:S(2)}, u32[]{:S(2)}) collective-permute-start(bf16[4,72,512]{2,1,0:T(8,128)(2,1)} %get-tuple-element.22), channel_id=1, source_target_pairs={{0,12},{1,13},{2,14},{3,15},{4,0},{5,1},{6,2},{7,3},{8,4},{9,5},{1... | collective-permute-start | bytes 884744 | tf_op jit(solution)/shard_map/ppermute | solution.py:58
  157.1 6.1 %collective-permute-done.33.refs_1_ = bf16[4,72,512]{2,1,0:T(8,128)(2,1)S(1)} collective-permute-done((bf16[4,72,512]{2,1,0:T(8,128)(2,1)}, bf16[4,72,512]{2,1,0:T(8,128)(2,1)S(1)}, u32[]{:S(2)}, u32[]{:S(2)}) %collective-permute-start.33) | collective-permute-done | bytes 294944 | tf_op jit(solution)/shard_map/ppermute | solution.py:58
  163.2 7.5 %collective-permute-done.34.refs_2_ = bf16[4,72,512]{2,1,0:T(8,128)(2,1)S(1)} collective-permute-done((bf16[4,72,512]{2,1,0:T(8,128)(2,1)}, bf16[4,72,512]{2,1,0:T(8,128)(2,1)S(1)}, u32[]{:S(2)}, u32[]{:S(2)}) %collective-permute-start.34) | collective-permute-done | bytes 294944 | tf_op jit(solution)/shard_map/ppermute | solution.py:58
  173.1 3.7 %collective-permute-start.36 = (bf16[2,72,512]{2,1,0:T(8,128)(2,1)}, bf16[2,72,512]{2,1,0:T(8,128)(2,1)S(1)}, u32[]{:S(2)}, u32[]{:S(2)}) collective-permute-start(bf16[2,72,512]{2,1,0:T(8,128)(2,1)} %get-tuple-element.26), channel_id=1, source_target_pairs={{0,3},{1,2},{2,1},{3,0},{4,7},{5,6},{6,5},{7,4},{8,11},{9,10},{10,... | collective-permute-start | bytes 442376 | tf_op jit(solution)/shard_map/ppermute | solution.py:66
  177.6 4.4 %collective-permute-done.36.refs_1_ = bf16[2,72,512]{2,1,0:T(8,128)(2,1)S(1)} collective-permute-done((bf16[2,72,512]{2,1,0:T(8,128)(2,1)}, bf16[2,72,512]{2,1,0:T(8,128)(2,1)S(1)}, u32[]{:S(2)}, u32[]{:S(2)}) %collective-permute-start.36) | collective-permute-done | bytes 147488 | tf_op jit(solution)/shard_map/ppermute | solution.py:66
  183.7 3.9 %collective-permute-start.37 = (bf16[1,72,512]{2,1,0:T(8,128)(2,1)}, bf16[1,72,512]{2,1,0:T(8,128)(2,1)S(1)}, u32[]{:S(2)}, u32[]{:S(2)}) collective-permute-start(bf16[1,72,512]{2,1,0:T(8,128)(2,1)} %get-tuple-element.28), channel_id=1, source_target_pairs={{0,1},{1,0},{2,3},{3,2},{4,5},{5,4},{6,7},{7,6},{8,9},{9,8},{10,11... | collective-permute-start | bytes 221192 | tf_op jit(solution)/shard_map/ppermute | solution.py:62
  193.4 4.8 %collective-permute-done.39 = bf16[2,64,1024]{2,1,0:T(8,128)(2,1)S(1)} collective-permute-done((bf16[2,64,1024]{2,1,0:T(8,128)(2,1)S(1)}, bf16[2,64,1024]{2,1,0:T(8,128)(2,1)S(1)}, u32[]{:S(2)}, u32[]{:S(2)}) %collective-permute-start.39) | collective-permute-done | bytes 262176 | tf_op jit(solution)/shard_map/ppermute | solution.py:70
  198.3 4.6 %collective-permute-done.41 = bf16[2,64,1024]{2,1,0:T(8,128)(2,1)S(1)} collective-permute-done((bf16[2,64,1024]{2,1,0:T(8,128)(2,1)S(1)}, bf16[2,64,1024]{2,1,0:T(8,128)(2,1)S(1)}, u32[]{:S(2)}, u32[]{:S(2)}) %collective-permute-start.41) | collective-permute-done | bytes 262176 | tf_op jit(solution)/shard_map/ppermute | solution.py:70
  (114 shorter events, 66.7 us)
Async XLA Ops:
  2.3 7.0 %collective-permute-start = (bf16[1,72,512]{2,1,0:T(8,128)(2,1)S(1)}, bf16[1,72,512]{2,1,0:T(8,128)(2,1)S(1)}, u32[]{:S(2)}, u32[]{:S(2)}) collective-permute-start(bf16[1,72,512]{2,1,0:T(8,128)(2,1)S(1)} %maximum_bitcast_fusion.1), channel_id=1, source_target_pairs={{0,1},{1,0},{2,3},{3,2},{4,5},{5,4},{6,7},{7,6},{8,9},{9,8},{10,11... | collective-permute-start | bytes 221192 | tf_op jit(solution)/shard_map/ppermute | solution.py:62
  6.7 7.5 %collective-permute-start.5 = (bf16[1,72,1024]{2,1,0:T(8,128)(2,1)S(1)}, bf16[1,72,1024]{2,1,0:T(8,128)(2,1)S(1)}, u32[]{:S(2)}, u32[]{:S(2)}) collective-permute-start(bf16[1,72,1024]{2,1,0:T(8,128)(2,1)S(1)} %maximum_bitcast_fusion), channel_id=1, source_target_pairs={{0,128},{16,144},{32,160},{48,176},{64,192},{80,208},{96,224},{112... | collective-permute-start | bytes 442376 | tf_op jit(solution)/shard_map/ppermute | solution.py:78
  9.3 10.7 %collective-permute-start.1 = (bf16[2,72,512]{2,1,0:T(8,128)(2,1)S(1)}, bf16[2,72,512]{2,1,0:T(8,128)(2,1)S(1)}, u32[]{:S(2)}, u32[]{:S(2)}) collective-permute-start(bf16[2,72,512]{2,1,0:T(8,128)(2,1)S(1)} %pad_maximum_fusion.2), channel_id=1, source_target_pairs={{0,3},{1,2},{2,1},{3,0},{4,7},{5,6},{6,5},{7,4},{8,11},{9,10},{10,... | collective-permute-start | bytes 442376 | tf_op jit(solution)/shard_map/ppermute | solution.py:66
  14.2 6.3 %collective-permute-start.9 = (bf16[2,72,1024]{2,1,0:T(8,128)(2,1)S(1)}, bf16[2,72,1024]{2,1,0:T(8,128)(2,1)S(1)}, u32[]{:S(2)}, u32[]{:S(2)}) collective-permute-start(bf16[2,72,1024]{2,1,0:T(8,128)(2,1)S(1)} %pad_maximum_fusion.1.refs_4_), channel_id=1, source_target_pairs={{0,16},{16,0},{32,48},{48,32},{64,80},{80,64},{96,112},{112,96},{1... | collective-permute-start | bytes 884744 | tf_op jit(solution)/shard_map/ppermute | solution.py:74
  14.3 16.0 %collective-permute-start.8 = (bf16[2,72,1024]{2,1,0:T(8,128)(2,1)S(1)}, bf16[2,72,1024]{2,1,0:T(8,128)(2,1)S(1)}, u32[]{:S(2)}, u32[]{:S(2)}) collective-permute-start(bf16[2,72,1024]{2,1,0:T(8,128)(2,1)S(1)} %pad_maximum_fusion.1.refs_4_), channel_id=1, source_target_pairs={{0,96},{16,112},{32,0},{48,16},{64,32},{80,48},{96,64},{112,80},{1... | collective-permute-start | bytes 884744 | tf_op jit(solution)/shard_map/ppermute | solution.py:70
  17.1 14.8 %collective-permute-start.7 = (bf16[2,72,1024]{2,1,0:T(8,128)(2,1)S(1)}, bf16[2,72,1024]{2,1,0:T(8,128)(2,1)S(1)}, u32[]{:S(2)}, u32[]{:S(2)}) collective-permute-start(bf16[2,72,1024]{2,1,0:T(8,128)(2,1)S(1)} %pad_maximum_fusion.1.refs_4_), channel_id=1, source_target_pairs={{0,64},{16,80},{32,96},{48,112},{64,0},{80,16},{96,32},{112,48},{1... | collective-permute-start | bytes 884744 | tf_op jit(solution)/shard_map/ppermute | solution.py:70
  17.9 16.1 %collective-permute-start.6 = (bf16[2,72,1024]{2,1,0:T(8,128)(2,1)S(1)}, bf16[2,72,1024]{2,1,0:T(8,128)(2,1)S(1)}, u32[]{:S(2)}, u32[]{:S(2)}) collective-permute-start(bf16[2,72,1024]{2,1,0:T(8,128)(2,1)S(1)} %pad_maximum_fusion.1.refs_4_), channel_id=1, source_target_pairs={{0,32},{16,48},{32,64},{48,80},{64,96},{80,112},{96,0},{112,16},{1... | collective-permute-start | bytes 884744 | tf_op jit(solution)/shard_map/ppermute | solution.py:70
  20.0 14.0 %collective-permute-start.4 = (bf16[4,72,512]{2,1,0:T(8,128)(2,1)S(1)}, bf16[4,72,512]{2,1,0:T(8,128)(2,1)S(1)}, u32[]{:S(2)}, u32[]{:S(2)}) collective-permute-start(bf16[4,72,512]{2,1,0:T(8,128)(2,1)S(1)} %pad_maximum_fusion.refs_0_), channel_id=1, source_target_pairs={{0,12},{1,13},{2,14},{3,15},{4,0},{5,1},{6,2},{7,3},{8,4},{9,5},{1... | collective-permute-start | bytes 884744 | tf_op jit(solution)/shard_map/ppermute | solution.py:58
  20.6 15.3 %collective-permute-start.3 = (bf16[4,72,512]{2,1,0:T(8,128)(2,1)S(1)}, bf16[4,72,512]{2,1,0:T(8,128)(2,1)S(1)}, u32[]{:S(2)}, u32[]{:S(2)}) collective-permute-start(bf16[4,72,512]{2,1,0:T(8,128)(2,1)S(1)} %pad_maximum_fusion.refs_0_), channel_id=1, source_target_pairs={{0,8},{1,9},{2,10},{3,11},{4,12},{5,13},{6,14},{7,15},{8,0},{9,1},... | collective-permute-start | bytes 884744 | tf_op jit(solution)/shard_map/ppermute | solution.py:58
  30.3 8.3 %collective-permute-start.2 = (bf16[4,72,512]{2,1,0:T(8,128)(2,1)S(1)}, bf16[4,72,512]{2,1,0:T(8,128)(2,1)S(1)}, u32[]{:S(2)}, u32[]{:S(2)}) collective-permute-start(bf16[4,72,512]{2,1,0:T(8,128)(2,1)S(1)} %pad_maximum_fusion.refs_0_), channel_id=1, source_target_pairs={{0,4},{1,5},{2,6},{3,7},{4,8},{5,9},{6,10},{7,11},{8,12},{9,13},{1... | collective-permute-start | bytes 884744 | tf_op jit(solution)/shard_map/ppermute | solution.py:58
  31.9 6.7 %collective-permute-start.12 = (bf16[2,72,1024]{2,1,0:T(8,128)(2,1)S(1)}, bf16[2,72,1024]{2,1,0:T(8,128)(2,1)S(1)}, u32[]{:S(2)}, u32[]{:S(2)}) collective-permute-start(bf16[2,72,1024]{2,1,0:T(8,128)(2,1)S(1)} %collective-permute-done.8.refs_7_), channel_id=1, source_target_pairs={{0,16},{16,0},{32,48},{48,32},{64,80},{80,64},{96,112},{112,96},{1... | collective-permute-start | bytes 884744 | tf_op jit(solution)/shard_map/ppermute | solution.py:74
  48.9 6.3 %collective-permute-start.15 = (f32[32,256]{1,0:T(8,128)}, f32[32,256]{1,0:T(8,128)S(1)}, u32[]{:S(2)}, u32[]{:S(2)}) collective-permute-start(f32[32,256]{1,0:T(8,128)} %get-tuple-element.17), channel_id=1, source_target_pairs={{0,5},{1,4},{2,7},{3,6},{4,1},{5,0},{6,3},{7,2},{8,13},{9,12},{10,... | collective-permute-start | bytes 98312 | tf_op jit(solution)/shard_map/ppermute | solution.py:82
  58.7 5.4 %collective-permute-start.16 = (f32[32,256]{1,0:T(8,128)S(1)}, f32[32,256]{1,0:T(8,128)S(1)}, u32[]{:S(2)}, u32[]{:S(2)}) collective-permute-start(f32[32,256]{1,0:T(8,128)S(1)} %add_add_fusion.3), channel_id=1, source_target_pairs={{0,12},{1,13},{2,14},{3,15},{4,8},{5,9},{6,10},{7,11},{8,4},{9,5},... | collective-permute-start | bytes 98312 | tf_op jit(solution)/shard_map/ppermute | solution.py:84
  64.2 8.1 %collective-permute-start.17 = (f32[32,256]{1,0:T(8,128)S(1)}, f32[32,256]{1,0:T(8,128)S(1)}, u32[]{:S(2)}, u32[]{:S(2)}) collective-permute-start(f32[32,256]{1,0:T(8,128)S(1)} %add.83.ra_ref), channel_id=1, source_target_pairs={{0,3},{1,2},{2,1},{3,0},{4,7},{5,6},{6,5},{7,4},{8,11},{9,10},{10,... | collective-permute-start | bytes 98312 | tf_op jit(solution)/shard_map/ppermute | solution.py:85
  78.4 6.8 %collective-permute-start.21 = (f32[64,256]{1,0:T(8,128)S(1)}, f32[64,256]{1,0:T(8,128)S(1)}, u32[]{:S(2)}, u32[]{:S(2)}) collective-permute-start(f32[64,256]{1,0:T(8,128)S(1)} %add.84), channel_id=1, source_target_pairs={{0,160},{16,176},{32,128},{48,144},{64,224},{80,240},{96,192},{112... | collective-permute-start | bytes 196616 | tf_op jit(solution)/shard_map/ppermute | solution.py:91
  81.0 6.5 %collective-permute-start.20 = (f32[64,256]{1,0:T(8,128)S(1)}, f32[64,256]{1,0:T(8,128)S(1)}, u32[]{:S(2)}, u32[]{:S(2)}) collective-permute-start(f32[64,256]{1,0:T(8,128)S(1)} %add.84), channel_id=1, source_target_pairs={{0,32},{16,48},{32,0},{48,16},{64,96},{80,112},{96,64},{112,80},{1... | collective-permute-start | bytes 196616 | tf_op jit(solution)/shard_map/ppermute | solution.py:91
  89.5 5.9 %collective-permute-start.22 = (f32[64,256]{1,0:T(8,128)S(1)}, f32[64,256]{1,0:T(8,128)S(1)}, u32[]{:S(2)}, u32[]{:S(2)}) collective-permute-start(f32[64,256]{1,0:T(8,128)S(1)} %add_add_fusion.1.ca_ref), channel_id=1, source_target_pairs={{0,96},{16,112},{32,64},{48,80},{64,32},{80,48},{96,0},{112,16},{1... | collective-permute-start | bytes 196616 | tf_op jit(solution)/shard_map/ppermute | solution.py:94
  99.4 7.2 %collective-permute-start.25 = (f32[32,256]{1,0:T(8,128)}, f32[32,256]{1,0:T(8,128)S(1)}, u32[]{:S(2)}, u32[]{:S(2)}) collective-permute-start(f32[32,256]{1,0:T(8,128)} %shard_map.79), channel_id=1, source_target_pairs={{0,5},{1,4},{2,7},{3,6},{4,1},{5,0},{6,3},{7,2},{8,13},{9,12},{10,... | collective-permute-start | bytes 98312 | tf_op jit(solution)/shard_map/ppermute | solution.py:82
  100.1 8.9 %collective-permute-start.24 = (f32[32,256]{1,0:T(8,128)}, f32[32,256]{1,0:T(8,128)S(1)}, u32[]{:S(2)}, u32[]{:S(2)}) collective-permute-start(f32[32,256]{1,0:T(8,128)} %shard_map.79), channel_id=1, source_target_pairs={{0,1},{1,0},{2,3},{3,2},{4,5},{5,4},{6,7},{7,6},{8,9},{9,8},{10,11... | collective-permute-start | bytes 98312 | tf_op jit(solution)/shard_map/ppermute | solution.py:82
  115.4 6.0 %collective-permute-start.27 = (f32[32,256]{1,0:T(8,128)S(1)}, f32[32,256]{1,0:T(8,128)S(1)}, u32[]{:S(2)}, u32[]{:S(2)}) collective-permute-start(f32[32,256]{1,0:T(8,128)S(1)} %add.91.ra_ref), channel_id=1, source_target_pairs={{0,3},{1,2},{2,1},{3,0},{4,7},{5,6},{6,5},{7,4},{8,11},{9,10},{10,... | collective-permute-start | bytes 98312 | tf_op jit(solution)/shard_map/ppermute | solution.py:85
  127.6 5.3 %collective-permute-start.31 = (f32[64,256]{1,0:T(8,128)S(1)}, f32[64,256]{1,0:T(8,128)S(1)}, u32[]{:S(2)}, u32[]{:S(2)}) collective-permute-start(f32[64,256]{1,0:T(8,128)S(1)} %add.92), channel_id=1, source_target_pairs={{0,160},{16,176},{32,128},{48,144},{64,224},{80,240},{96,192},{112... | collective-permute-start | bytes 196616 | tf_op jit(solution)/shard_map/ppermute | solution.py:91
  128.3 6.3 %collective-permute-start.30 = (f32[64,256]{1,0:T(8,128)S(1)}, f32[64,256]{1,0:T(8,128)S(1)}, u32[]{:S(2)}, u32[]{:S(2)}) collective-permute-start(f32[64,256]{1,0:T(8,128)S(1)} %add.92), channel_id=1, source_target_pairs={{0,32},{16,48},{32,0},{48,16},{64,96},{80,112},{96,64},{112,80},{1... | collective-permute-start | bytes 196616 | tf_op jit(solution)/shard_map/ppermute | solution.py:91
  136.6 5.6 %collective-permute-start.32 = (f32[64,256]{1,0:T(8,128)S(1)}, f32[64,256]{1,0:T(8,128)S(1)}, u32[]{:S(2)}, u32[]{:S(2)}) collective-permute-start(f32[64,256]{1,0:T(8,128)S(1)} %add_add_fusion.ca_ref), channel_id=1, source_target_pairs={{0,96},{16,112},{32,64},{48,80},{64,32},{80,48},{96,0},{112,16},{1... | collective-permute-start | bytes 196616 | tf_op jit(solution)/shard_map/ppermute | solution.py:94
  150.3 37.3 %collective-permute-start.38 = (bf16[8,64,1024]{2,1,0:T(8,128)(2,1)}, bf16[8,64,1024]{2,1,0:T(8,128)(2,1)S(1)}, u32[]{:S(2)}, u32[]{:S(2)}) collective-permute-start(bf16[8,64,1024]{2,1,0:T(8,128)(2,1)} %get-tuple-element.31), channel_id=1, source_target_pairs={{0,16},{16,0},{32,48},{48,32},{64,80},{80,64},{96,112},{112,96},{1... | collective-permute-start | bytes 3145736 | tf_op jit(solution)/shard_map/ppermute | solution.py:74
  150.4 12.8 %collective-permute-start.33 = (bf16[4,72,512]{2,1,0:T(8,128)(2,1)}, bf16[4,72,512]{2,1,0:T(8,128)(2,1)S(1)}, u32[]{:S(2)}, u32[]{:S(2)}) collective-permute-start(bf16[4,72,512]{2,1,0:T(8,128)(2,1)} %get-tuple-element.22), channel_id=1, source_target_pairs={{0,12},{1,13},{2,14},{3,15},{4,0},{5,1},{6,2},{7,3},{8,4},{9,5},{1... | collective-permute-start | bytes 884744 | tf_op jit(solution)/shard_map/ppermute | solution.py:58
  155.3 15.4 %collective-permute-start.34 = (bf16[4,72,512]{2,1,0:T(8,128)(2,1)}, bf16[4,72,512]{2,1,0:T(8,128)(2,1)S(1)}, u32[]{:S(2)}, u32[]{:S(2)}) collective-permute-start(bf16[4,72,512]{2,1,0:T(8,128)(2,1)} %get-tuple-element.23), channel_id=1, source_target_pairs={{0,8},{1,9},{2,10},{3,11},{4,12},{5,13},{6,14},{7,15},{8,0},{9,1},... | collective-permute-start | bytes 884744 | tf_op jit(solution)/shard_map/ppermute | solution.py:58
  157.1 14.3 %collective-permute-start.35 = (bf16[4,72,512]{2,1,0:T(8,128)(2,1)}, bf16[4,72,512]{2,1,0:T(8,128)(2,1)S(1)}, u32[]{:S(2)}, u32[]{:S(2)}) collective-permute-start(bf16[4,72,512]{2,1,0:T(8,128)(2,1)} %get-tuple-element.24), channel_id=1, source_target_pairs={{0,4},{1,5},{2,6},{3,7},{4,8},{5,9},{6,10},{7,11},{8,12},{9,13},{1... | collective-permute-start | bytes 884744 | tf_op jit(solution)/shard_map/ppermute | solution.py:58
  173.1 8.9 %collective-permute-start.36 = (bf16[2,72,512]{2,1,0:T(8,128)(2,1)}, bf16[2,72,512]{2,1,0:T(8,128)(2,1)S(1)}, u32[]{:S(2)}, u32[]{:S(2)}) collective-permute-start(bf16[2,72,512]{2,1,0:T(8,128)(2,1)} %get-tuple-element.26), channel_id=1, source_target_pairs={{0,3},{1,2},{2,1},{3,0},{4,7},{5,6},{6,5},{7,4},{8,11},{9,10},{10,... | collective-permute-start | bytes 442376 | tf_op jit(solution)/shard_map/ppermute | solution.py:66
  183.7 8.8 %collective-permute-start.37 = (bf16[1,72,512]{2,1,0:T(8,128)(2,1)}, bf16[1,72,512]{2,1,0:T(8,128)(2,1)S(1)}, u32[]{:S(2)}, u32[]{:S(2)}) collective-permute-start(bf16[1,72,512]{2,1,0:T(8,128)(2,1)} %get-tuple-element.28), channel_id=1, source_target_pairs={{0,1},{1,0},{2,3},{3,2},{4,5},{5,4},{6,7},{7,6},{8,9},{9,8},{10,11... | collective-permute-start | bytes 221192 | tf_op jit(solution)/shard_map/ppermute | solution.py:62
  189.0 9.3 %collective-permute-start.39 = (bf16[2,64,1024]{2,1,0:T(8,128)(2,1)S(1)}, bf16[2,64,1024]{2,1,0:T(8,128)(2,1)S(1)}, u32[]{:S(2)}, u32[]{:S(2)}) collective-permute-start(bf16[2,64,1024]{2,1,0:T(8,128)(2,1)S(1)} %get-tuple-element.32), channel_id=1, source_target_pairs={{0,96},{16,112},{32,0},{48,16},{64,32},{80,48},{96,64},{112,80},{1... | collective-permute-start | bytes 786440 | tf_op jit(solution)/shard_map/ppermute | solution.py:70
  190.9 12.0 %collective-permute-start.41 = (bf16[2,64,1024]{2,1,0:T(8,128)(2,1)S(1)}, bf16[2,64,1024]{2,1,0:T(8,128)(2,1)S(1)}, u32[]{:S(2)}, u32[]{:S(2)}) collective-permute-start(bf16[2,64,1024]{2,1,0:T(8,128)(2,1)S(1)} %get-tuple-element.33), channel_id=1, source_target_pairs={{0,32},{16,48},{32,64},{48,80},{64,96},{80,112},{96,0},{112,16},{1... | collective-permute-start | bytes 786440 | tf_op jit(solution)/shard_map/ppermute | solution.py:70
  191.1 11.8 %collective-permute-start.40 = (bf16[2,64,1024]{2,1,0:T(8,128)(2,1)S(1)}, bf16[2,64,1024]{2,1,0:T(8,128)(2,1)S(1)}, u32[]{:S(2)}, u32[]{:S(2)}) collective-permute-start(bf16[2,64,1024]{2,1,0:T(8,128)(2,1)S(1)} %get-tuple-element.34), channel_id=1, source_target_pairs={{0,64},{16,80},{32,96},{48,112},{64,0},{80,16},{96,32},{112,48},{1... | collective-permute-start | bytes 786440 | tf_op jit(solution)/shard_map/ppermute | solution.py:70
  (25 other events, 301.0 us)

commit v2 on v0

--- a/solution.py
+++ b/solution.py
@@ -62,6 +62,18 @@
     return lax.ppermute(a, "photo", photo_perm(same, shift(k)))
 
 
+def flip_z(a):
+    return lax.ppermute(a, "photo", photo_perm(same, flip))
+
+
+def across_z(a):
+    return lax.ppermute(a, "photo", photo_perm(same, lambda i: i ^ 2))
+
+
+def mirror_z(a):
+    return lax.ppermute(a, "photo", photo_perm(same, mirror))
+
+
 def shift_x(a, k):
     return lax.ppermute(a, "spec", spec_perm(same, shift(k), same))
 
@@ -75,10 +87,9 @@
 
 
 def sum_photo(a):
-    parts = [lax.ppermute(a, "photo", photo_perm(fy, fz)) for fy, fz in ((flip, same), (same, flip), (flip, flip))]
+    parts = [shift_y(a, k) for k in (1, 2, 3)]
     a = (a + parts[0]) + (parts[1] + parts[2])
-    a = a + lax.ppermute(a, "photo", photo_perm(mirror, same))
-    return (a, lax.ppermute(a, "photo", photo_perm(same, mirror)))
+    return [a] + [shift_z(a, k) for k in (1, 2, 3)]
 
 
 def sum_spec(a):
@@ -87,11 +98,12 @@
         lax.ppermute(a, "spec", spec_perm(fl, fx, same)) for fl, fx in ((flip, same), (same, flip), (flip, flip))
     ]
     a = (a + parts[0]) + (parts[1] + parts[2])
-    return (a, lax.ppermute(a, "spec", spec_perm(same, mirror, same)))
+    return [a, lax.ppermute(a, "spec", spec_perm(same, mirror, same))]
 
 
 def spec_slot(q, photo_id):
-    return (((photo_id >> 2) - (q >> 2)) & 3) * 4 + ((photo_id - q) & 3)
+    across = (photo_id ^ q) & 3
+    return (((photo_id >> 2) - (q >> 2)) & 3) * 4 + (across ^ (across >> 1))
 
 
 def photo_slot(q, spec_id):
@@ -171,14 +183,35 @@
     ]
 
 
+def column_start_kernel(pos_ref, *refs):
+    ys = refs[0:8]
+    n_ref, b_ref, yt_ref, sems = refs[8:]
+    copies = [pltpu.make_async_copy(ys[k], yt_ref.at[pl.ds(2 * k, 2)], sems.at[k]) for k in range(8)]
+    for copy in copies:
+        copy.start()
+    for copy in copies:
+        copy.wait()
+    for q in range(SLOTS):
+        slot = photo_slot(q, pos_ref[0])
+        mass = yt_ref[slot, F:EXT, :].astype(f32)
+        y = yt_ref[slot, 0:F, :].astype(f32)
+        weight = jnp.exp(jnp.sum(y * y, axis=0, keepdims=True) * -0.0625)
+        for k in range(4):
+            lanes = slice(k * TILE, (k + 1) * TILE)
+            n_ref[4 * q + k : 4 * q + k + 1, :] = mass[0:1, lanes]
+            b_ref[4 * q + k : 4 * q + k + 1, :] = weight[:, lanes]
+
+
 def first_kernel(index_ref, count_ref, pos_ref, *refs):
-    xs, ys = (refs[0:4], refs[4:12])
-    out_ref, m_ref, n_ref, g_hbm = refs[12:16]
+    xs, ys, b_ref = (refs[0:4], refs[4:12], refs[12])
+    out_ref, m_ref, g_hbm = refs[13:16]
     xt_ref, yt_ref, xr_ref, w_ref, acc_ref, g_ref, sems, g_sems = refs[16:]
     copies = piece_copies(xs, ys, xt_ref, yt_ref, sems)
     for copy in copies:
         copy.start()
     acc_ref[...] = jnp.zeros_like(acc_ref)
+    for column in range(TC):
+        w_ref[column] = high_low(b_ref[column : column + 1, :])
     for copy in copies:
         copy.wait()
 
@@ -190,23 +223,10 @@
 
     lax.fori_loop(0, SLOTS, turn_slot, 0)
 
-    def weigh(q, carry):
-        slot = photo_slot(q, pos_ref[1])
-        for k in range(4):
-            y = yt_ref[slot, 0:F, k * TILE : (k + 1) * TILE].astype(f32)
-            norm = jnp.sum(y * y, axis=0, keepdims=True)
-            w_ref[4 * q + k] = high_low(jnp.exp(norm * -0.0625))
-        return carry
-
-    lax.fori_loop(0, SLOTS, weigh, 0)
     for q in range(SLOTS):
         mass = xt_ref[spec_slot(q, pos_ref[0]), F:EXT, :].astype(f32)
         for k in range(2):
             m_ref[2 * q + k : 2 * q + k + 1, :] = mass[0:1, k * TILE : (k + 1) * TILE]
-    for q in range(SLOTS):
-        mass = yt_ref[photo_slot(q, pos_ref[1]), F:EXT, :].astype(f32)
-        for k in range(4):
-            n_ref[4 * q + k : 4 * q + k + 1, :] = mass[0:1, k * TILE : (k + 1) * TILE]
 
     def step(i, k, t, row, column):
         row_local = spec_slot(row >> 1, pos_ref[0]) * 2 + (row & 1)
@@ -231,10 +251,19 @@
     lax.fori_loop(0, turns_of(count_ref), sent, 0)
 
 
-def column_kernel(index_ref, count_ref, ra_ref, rb_ref, m_ref, g_hbm, out_ref, w_ref, acc_ref, g_ref, sems):
+def sum_of(refs):
+    total = refs[0][...]
+    for ref in refs[1:]:
+        total = total + ref[...]
+    return total
+
+
+def column_kernel(index_ref, count_ref, *refs):
+    r_refs = refs[0:4]
+    m_ref, g_hbm, out_ref, w_ref, acc_ref, g_ref, sems = refs[4:]
     start_tiles(count_ref, g_hbm, g_ref, sems)
     acc_ref[...] = jnp.zeros_like(acc_ref)
-    u = m_ref[...] / (ra_ref[...] + rb_ref[...])
+    u = m_ref[...] / sum_of(r_refs)
     for row in range(TR):
         w_ref[row] = high_low(u[row : row + 1, :])
 
@@ -259,7 +288,9 @@
     store_pairs(acc_ref, out_ref)
 
 
-def grad_kernel(index_ref, count_ref, pos_ref, ra_ref, rb_ref, ca_ref, cb_ref, m_ref, n_ref, g_hbm, *refs):
+def grad_kernel(index_ref, count_ref, pos_ref, *refs):
+    r_refs, c_refs, m_ref, n_ref, g_hbm = (refs[0:4], refs[4:6], *refs[6:9])
+    refs = refs[9:]
     xs, ys = (refs[0:4], refs[4:12])
     spec_outs, photo_outs, share_ref = (refs[12:16], refs[16:18], refs[18])
     xt_ref, yt_ref, u_ref, v_ref, wy_ref, vx_ref, spec_acc, photo_acc = refs[19:27]
@@ -268,8 +299,8 @@
     for copy in copies:
         copy.start()
     start_tiles(count_ref, g_hbm, g_ref, g_sems)
-    u_all = m_ref[...] / (ra_ref[...] + rb_ref[...])
-    total = ca_ref[...] + cb_ref[...]
+    u_all = m_ref[...] / sum_of(r_refs)
+    total = sum_of(c_refs)
     v_all = n_ref[...] / total
     both_all = v_all * total
     for q in range(SLOTS):
@@ -394,10 +425,12 @@
     x0 = jnp.concatenate([x_own, spec_mass.reshape(1, SB), x_pad])[None]
     y0 = jnp.concatenate([y_own, photo_mass.reshape(1, PB), y_pad])[None]
 
-    x_parts = [shift_z(x0, k) for k in (1, 2, 3)]
+    x_flip = flip_z(x0)
     y_low = swap_low(y0)
+    x0 = jnp.concatenate([x0, x_flip])
+    x_mirror = mirror_z(x0)
     y0 = jnp.concatenate([y0, y_low])
-    x0 = jnp.concatenate([x0] + x_parts)
+    x0 = jnp.concatenate([x0, x_mirror])
     ys = [y0] + [shift_x(y0, k) for k in (1, 2, 3)]
     xs = [x0] + [shift_y(x0, k) for k in (1, 2, 3)]
     ys = ys + [swap_core(y) for y in ys]
@@ -408,33 +441,37 @@
     column_acc = [pltpu.VMEM((TR, 16, TILE), bf16), pltpu.VMEM((TC, 16, TILE), f32)]
     blocks = [pltpu.VMEM((SLOTS, EXT, SB), bf16), pltpu.VMEM((SLOTS, EXT, PB), bf16)]
     piece_sems = pltpu.SemaphoreType.DMA((12,))
-    r, m, n, g = call(
-        first_kernel, [SMEM] * 3 + [ANY] * 12,
+    n, b = call(
+        column_start_kernel, [SMEM] + [ANY] * 8, [(VMEM, (TC, TILE), f32)] * 2,
+        [pltpu.VMEM((SLOTS, EXT, PB), bf16), pltpu.SemaphoreType.DMA((8,))], meta[2][1:], *ys,
+    )
+    r, m, g = call(
+        first_kernel, [SMEM] * 3 + [ANY] * 12 + [VMEM],
         [
-            (VMEM, (TR, TILE), f32), (VMEM, (TR, TILE), f32), (VMEM, (TC, TILE), f32),
+            (VMEM, (TR, TILE), f32), (VMEM, (TR, TILE), f32),
             (ANY, (TURNS, GROUP, TILE, TILE), bf16),
         ],
         blocks + [pltpu.VMEM((TR, TILE, F), bf16)] + row_acc + [tiles, piece_sems, tile_sems],
-        *meta, *xs, *ys,
+        *meta, *xs, *ys, b,
     )
     lists = meta[0:2]
 
-    def columns(ra, rb):
+    def columns(rs):
         return call(
-            column_kernel, [SMEM] * 2 + [VMEM] * 3 + [ANY], [(VMEM, (TC, TILE), f32)],
-            column_acc + [tiles, tile_sems], *lists, ra, rb, m, g,
+            column_kernel, [SMEM] * 2 + [VMEM] * 5 + [ANY], [(VMEM, (TC, TILE), f32)],
+            column_acc + [tiles, tile_sems], *lists, *rs, m, g,
         )[0]
 
-    ra, rb = in_vmem(sum_photo(r))
-    ca, cb = in_vmem(sum_spec(columns(ra, rb)))
+    rs = in_vmem(sum_photo(r))
+    cs = in_vmem(sum_spec(columns(rs)))
     (r,) = call(
         row_kernel, [SMEM] * 2 + [VMEM] * 3 + [ANY], [(VMEM, (TR, TILE), f32)],
-        row_acc + [tiles, tile_sems], *lists, ca, cb, n, g,
-    )
-    ra, rb = in_vmem(sum_photo(r))
-    ca, cb = in_vmem(sum_spec(columns(ra, rb)))
+        row_acc + [tiles, tile_sems], *lists, *cs, n, g,
+    )
+    rs = in_vmem(sum_photo(r))
+    cs = in_vmem(sum_spec(columns(rs)))
     *parts, share = call(
-        grad_kernel, [SMEM] * 3 + [VMEM] * 6 + [ANY] * 13,
+        grad_kernel, [SMEM] * 3 + [VMEM] * 8 + [ANY] * 13,
         [(ANY, (4, EXT, SB), bf16)] * 4 + [(ANY, (8, F, PB), bf16)] * 2 + [(VMEM, (4, 8, TILE), f32)],
         blocks
         + [
@@ -449,34 +486,34 @@
             tiles, piece_sems, tile_sems,
             pltpu.SemaphoreType.DMA((6,)),
         ],
-        *meta, ra, rb, ca, cb, m, n, g, *xs, *ys,
+        *meta, *rs, *cs, m, n, g, *xs, *ys,
     )
     share = share[:, 0, :].reshape(1, PB)
 
     spec_parts, photo_parts = (parts[0:4], parts[4:6])
     far = swap_core(photo_parts[1])
     y_parts = [shift_y(spec_parts[k], -k) for k in (1, 2, 3)]
-    photo_sums = [
-        photo_parts[0][2 * k : 2 * k + 2].astype(f32) + far[2 * k : 2 * k + 2].astype(f32) for k in range(4)
-    ]
-    x_parts = [shift_x(photo_sums[k].astype(bf16), -k) for k in (1, 2, 3)]
-    y_parts, x_parts = lax.optimization_barrier((y_parts, x_parts))
+    photo_sums = [photo_parts[0][2 * k : 2 * k + 2].astype(f32) + far[2 * k : 2 * k + 2].astype(f32) for k in range(4)]
+    x_parts = [total.astype(bf16) for total in photo_sums[1:]]
+    x_parts = [shift_x(part, -k) for k, part in zip((1, 2, 3), x_parts)]
+
     spec_sum, *z_parts = call(
-        relay_kernel, [VMEM] * 4,
-        [(VMEM, (EXT, SB), f32)] + [(VMEM, (EXT, SB), bf16)] * 3, [],
+        relay_kernel, [VMEM] * 4, [(VMEM, (EXT, SB), f32)] + [(VMEM, (EXT, SB), bf16)] * 3, [],
         spec_parts[0], *in_vmem(y_parts),
     )
-    z_parts = [shift_z(part, -k) for k, part in zip((1, 2, 3), z_parts)]
+    z_parts = [move(part) for move, part in zip((flip_z, mirror_z, across_z), z_parts)]
+    for part in z_parts:
+        spec_sum = spec_sum + part.astype(f32)
     photo_sum = photo_sums[0]
     for part in x_parts:
         photo_sum = photo_sum + part.astype(f32)
-    for part in z_parts:
-        spec_sum = spec_sum + part.astype(f32)
-    photo_sum = photo_sum[0] + swap_low(photo_sum[1].astype(bf16)).astype(f32)
+    photo_send = photo_sum[1].astype(bf16)
+    lowered = swap_low(photo_send)
+    photo_sum = photo_sum[0] + lowered.astype(f32)
+    grad_photo = (2.0 * (share * y_own.astype(f32) - photo_sum)).T[None]
     row_marginal = spec_sum[F : F + 1] + spec_sum[F + 1 : F + 2]
     grad_spec = 2.0 * (row_marginal * x_own.astype(f32) - spec_sum[0:F])
-    grad_photo = 2.0 * (share * y_own.astype(f32) - photo_sum)
-    return (grad_spec.T, grad_photo.T[None])
+    return (grad_spec.T, grad_photo)
 
 
 def solution(mesh):

time: 201 us -> 222 us (1.10)
  waiting for transfers between devices: 64.2 us -> 73.9 us
  starting transfers between devices: 89.1 us -> 96 us
    ppermute x6 -> x12, waiting for transfers between devices: 10.6 us -> 27.6 us  [shift_y(): return lax.ppermute(a, 'photo', photo_perm(shift(k), same))]
    ppermute x6 -> x12, starting transfers between devices: 11.7 us -> 26.4 us  [shift_y(): return lax.ppermute(a, 'photo', photo_perm(shift(k), same))]
    ppermute x12 -> x7, waiting for transfers between devices: 25.5 us -> 17.1 us  [the longest x2 6.94 us: mirror_z(): return lax.ppermute(a, 'photo', photo_perm(same, mirror))]
    ppermute x2, waiting for transfers between devices: 0.01 us -> 5.43 us  [swap_low(): return lax.ppermute(a, 'spec', spec_perm(flip, same, same))]
    ppermute x6, starting transfers between devices: 23.3 us -> 18.5 us  [shift_z(): return lax.ppermute(a, 'photo', photo_perm(same, shift(k)))]
    ppermute x6, starting transfers between devices: 10.2 us -> 7.14 us  [sum_spec(): lax.ppermute(a, 'spec', spec_perm(fl, fx, same))]
    ppermute x6, waiting for transfers between devices: 8.24 us -> 5.38 us  [shift_x(): return lax.ppermute(a, 'spec', spec_perm(same, shift(k), same))]
    ppermute x2, starting transfers between devices: 3.11 us -> 5.9 us  [swap_low(): return lax.ppermute(a, 'spec', spec_perm(flip, same, same))]
  transfers between devices with their start and end apart: 45 -> 46, of which waited for: 31 -> 28; matrix products, arithmetic and copies ran while one was open for 3% -> 3% of each run, Pallas kernels for 0% -> 2%
where the time goes in v2:
time: 222 us; the launch traced here: 218 us
  starting transfers between devices  96 us (43%)
  waiting for transfers between devices  73.9 us (33%)
  Pallas kernels  32.6 us (15%)
  other arithmetic  10.9 us (5%)
  local copies, waits for them, and re-layouts  2.96 us (1%)
    pallas_call x7, Pallas kernels, call(): pl.pallas_call(kernel, in_specs=in_specs, out_specs=[spec for spec, _, _...  32.6 us
    ppermute x12, waiting for transfers between devices, shift_y(): return lax.ppermute(a, 'photo', photo_perm(shift(k), same))  27.6 us
    ppermute x12, starting transfers between devices, shift_y(): return lax.ppermute(a, 'photo', photo_perm(shift(k), same))  26.4 us
    ppermute x6, starting transfers between devices, shift_z(): return lax.ppermute(a, 'photo', photo_perm(same, shift(k)))  18.5 us
    ppermute x2, starting transfers between devices, mirror_z(): return lax.ppermute(a, 'photo', photo_perm(same, mirror))  16.6 us
    ppermute x6, waiting for transfers between devices, shift_z(): return lax.ppermute(a, 'photo', photo_perm(same, shift(k)))  9.1 us
    ppermute x6, starting transfers between devices, shift_x(): return lax.ppermute(a, 'spec', spec_perm(same, shift(k), same))  8.48 us
    ppermute x6, starting transfers between devices, sum_spec(): lax.ppermute(a, 'spec', spec_perm(fl, fx, same))  7.14 us
  transfers between devices with their start and end apart: 46, of which 28 were waited for; matrix products, arithmetic and copies ran while one was open for 3% of the time, Pallas kernels for 2%

profile of v2, /device:TPU:8, one launch (start us, length us, event | category | flops | bytes accessed | tf_op | source)
XLA Modules:
  0.0 217.9 jit_solution(5405065580398859764)
XLA Ops:
  4.4 3.2 %collective-permute-done.5 = bf16[1,72,1024]{2,1,0:T(8,128)(2,1)S(1)} collective-permute-done((bf16[1,72,1024]{2,1,0:T(8,128)(2,1)S(1)}, bf16[1,72,1024]{2,1,0:T(8,128)(2,1)S(1)}, u32[]{:S(2)}, u32[]{:S(2)}) %collective-permute-start.5) | collective-permute-done | bytes 147488 | tf_op jit(solution)/shard_map/ppermute | solution.py:86
  7.6 2.8 %collective-permute-start.8 = (bf16[2,72,1024]{2,1,0:T(8,128)(2,1)S(1)}, bf16[2,72,1024]{2,1,0:T(8,128)(2,1)S(1)}, u32[]{:S(2)}, u32[]{:S(2)}) collective-permute-start(bf16[2,72,1024]{2,1,0:T(8,128)(2,1)S(1)} %pad_maximum_fusion.1.refs_0_.refs_4_.refs_13_), channel_id=1, source_target_pairs={{0,96},{16,112},{32,0},{48,16},{64,32},{80,48},{96,64},{112,80},{1... | collective-permute-start | bytes 884744 | tf_op jit(solution)/shard_map/ppermute | solution.py:78
  11.4 3.4 %collective-permute-start = (bf16[1,72,512]{2,1,0:T(8,128)(2,1)S(1)}, bf16[1,72,512]{2,1,0:T(8,128)(2,1)S(1)}, u32[]{:S(2)}, u32[]{:S(2)}) collective-permute-start(bf16[1,72,512]{2,1,0:T(8,128)(2,1)S(1)} %maximum_bitcast_fusion.1), channel_id=1, source_target_pairs={{0,1},{1,0},{2,3},{3,2},{4,5},{5,4},{6,7},{7,6},{8,9},{9,8},{10,11... | collective-permute-start | bytes 221192 | tf_op jit(solution)/shard_map/ppermute | solution.py:66
  17.1 11.4 %collective-permute-start.1 = (bf16[2,72,512]{2,1,0:T(8,128)(2,1)S(1)}, bf16[2,72,512]{2,1,0:T(8,128)(2,1)S(1)}, u32[]{:S(2)}, u32[]{:S(2)}) collective-permute-start(bf16[2,72,512]{2,1,0:T(8,128)(2,1)S(1)} %pad_maximum_fusion.2), channel_id=1, source_target_pairs={{0,3},{1,2},{2,1},{3,0},{4,7},{5,6},{6,5},{7,4},{8,11},{9,10},{10,... | collective-permute-start | bytes 442376 | tf_op jit(solution)/shard_map/ppermute | solution.py:74
  28.5 6.9 %collective-permute-done.1 = bf16[2,72,512]{2,1,0:T(8,128)(2,1)S(1)} collective-permute-done((bf16[2,72,512]{2,1,0:T(8,128)(2,1)S(1)}, bf16[2,72,512]{2,1,0:T(8,128)(2,1)S(1)}, u32[]{:S(2)}, u32[]{:S(2)}) %collective-permute-start.1) | collective-permute-done | bytes 147488 | tf_op jit(solution)/shard_map/ppermute | solution.py:74
  43.7 2.6 %shard_map.77 = (f32[64,256]{1,0:T(8,128)}, f32[64,256]{1,0:T(8,128)}) custom-call(s32[1]{0:T(128)} %bitcast.3.pos_ref, bf16[2,72,1024]{2,1,0:T(8,128)(2,1)} %copy-done, bf16[2,72,1024]{2,1,0:T(8,128)(2,1)} %copy-done.4, bf16[2,72,1024]{2,1,0:T(8,128)(2,1)} %copy-done.3, bf16[2,72,1024]{2,1,0:T(8,128)(2,1)} %copy-done.1, bf16[2,72,1024]{2,1,0:T(8,128)(2,1)} %copy-done.2, ...), custom_call_target="tpu_custom_call" | custom-call | tf_op jit(solution)/shard_map/pallas_call | solution.py:400
  46.4 5.0 %collective-permute-done.3.refs_2_.refs_11_ = bf16[4,72,512]{2,1,0:T(8,128)(2,1)S(1)} collective-permute-done((bf16[4,72,512]{2,1,0:T(8,128)(2,1)S(1)}, bf16[4,72,512]{2,1,0:T(8,128)(2,1)S(1)}, u32[]{:S(2)}, u32[]{:S(2)}) %collective-permute-start.3) | collective-permute-done | bytes 294944 | tf_op jit(solution)/shard_map/ppermute | solution.py:58
  53.6 8.6 %shard_map.78 = (f32[32,256]{1,0:T(8,128)}, f32[32,256]{1,0:T(8,128)}, bf16[12,8,256,256]{3,2,1,0:T(8,128)(2,1)}) custom-call(s32[96]{0:T(128)} %bitcast.42, s32[1]{0:T(128)} %bitcast.34.count_ref, s32[2]{0:T(128)} %pad_add_fusion.pos_ref, bf16[4,72,512]{2,1,0:T(8,128)(2,1)} %copy-done.8, bf16[4,72,512]{2,1,0:T(8,128)(2,1)} %collective-permute-done.2.refs_1_.refs_10_, ...), custom_call_target="tpu_custom_call" | custom-call | tf_op jit(solution)/shard_map/pallas_call | solution.py:400
  62.3 3.7 %collective-permute-start.15 = (f32[32,256]{1,0:T(8,128)}, f32[32,256]{1,0:T(8,128)S(1)}, u32[]{:S(2)}, u32[]{:S(2)}) collective-permute-start(f32[32,256]{1,0:T(8,128)} %get-tuple-element.19), channel_id=1, source_target_pairs={{0,12},{1,13},{2,14},{3,15},{4,0},{5,1},{6,2},{7,3},{8,4},{9,5},{1... | collective-permute-start | bytes 98312 | tf_op jit(solution)/shard_map/ppermute | solution.py:58
  73.3 8.7 %collective-permute-start.18 = (f32[32,256]{1,0:T(8,128)S(1)}, f32[32,256]{1,0:T(8,128)S(1)}, u32[]{:S(2)}, u32[]{:S(2)}) collective-permute-start(f32[32,256]{1,0:T(8,128)S(1)} %add_add_fusion.3.refs_0_), channel_id=1, source_target_pairs={{0,3},{1,0},{2,1},{3,2},{4,7},{5,4},{6,5},{7,6},{8,11},{9,8},{10,9... | collective-permute-start | bytes 98312 | tf_op jit(solution)/shard_map/ppermute | solution.py:62
  84.5 5.5 %collective-permute-done.17.refs_2_ = f32[32,256]{1,0:T(8,128)S(1)} collective-permute-done((f32[32,256]{1,0:T(8,128)S(1)}, f32[32,256]{1,0:T(8,128)S(1)}, u32[]{:S(2)}, u32[]{:S(2)}) %collective-permute-start.17) | collective-permute-done | bytes 32800 | tf_op jit(solution)/shard_map/ppermute | solution.py:62
  90.0 3.7 %shard_map.79 = f32[64,256]{1,0:T(8,128)} custom-call(s32[96]{0:T(128)} %bitcast.43, s32[1]{0:T(128)} %bitcast.35.count_ref, f32[32,256]{1,0:T(8,128)S(1)} %add_add_fusion.3.refs_0_, f32[32,256]{1,0:T(8,128)S(1)} %collective-permute-done.16.refs_1_, f32[32,256]{1,0:T(8,128)S(1)} %collective-permute-done.17.refs_2_, ...), custom_call_target="tpu_custom_call" | custom-call | tf_op jit(solution)/shard_map/pallas_call | solution.py:400
  102.0 3.2 %collective-permute-start.23 = (f32[64,256]{1,0:T(8,128)S(1)}, f32[64,256]{1,0:T(8,128)S(1)}, u32[]{:S(2)}, u32[]{:S(2)}) collective-permute-start(f32[64,256]{1,0:T(8,128)S(1)} %add_add_fusion.1.ca_ref), channel_id=1, source_target_pairs={{0,96},{16,112},{32,64},{48,80},{64,32},{80,48},{96,0},{112,16},{1... | collective-permute-start | bytes 196616 | tf_op jit(solution)/shard_map/ppermute | solution.py:101
  107.6 4.0 %shard_map.80 = f32[32,256]{1,0:T(8,128)} custom-call(s32[96]{0:T(128)} %bitcast.44, s32[1]{0:T(128)} %bitcast.36.count_ref, f32[64,256]{1,0:T(8,128)S(1)} %add_add_fusion.1.ca_ref, f32[64,256]{1,0:T(8,128)S(1)} %collective-permute-done.23.cb_ref, f32[64,256]{1,0:T(8,128)} %get-tuple-element.22.n_ref.refs_7_, ...), custom_call_target="tpu_custom_call" | custom-call | tf_op jit(solution)/shard_map/pallas_call | solution.py:400
  111.6 6.3 %collective-permute-start.26 = (f32[32,256]{1,0:T(8,128)}, f32[32,256]{1,0:T(8,128)S(1)}, u32[]{:S(2)}, u32[]{:S(2)}) collective-permute-start(f32[32,256]{1,0:T(8,128)} %shard_map.80), channel_id=1, source_target_pairs={{0,12},{1,13},{2,14},{3,15},{4,0},{5,1},{6,2},{7,3},{8,4},{9,5},{1... | collective-permute-start | bytes 98312 | tf_op jit(solution)/shard_map/ppermute | solution.py:58
  119.8 3.7 %collective-permute-done.25 = f32[32,256]{1,0:T(8,128)S(1)} collective-permute-done((f32[32,256]{1,0:T(8,128)}, f32[32,256]{1,0:T(8,128)S(1)}, u32[]{:S(2)}, u32[]{:S(2)}) %collective-permute-start.25) | collective-permute-done | bytes 32800 | tf_op jit(solution)/shard_map/ppermute | solution.py:58
  124.3 2.8 %collective-permute-start.29 = (f32[32,256]{1,0:T(8,128)S(1)}, f32[32,256]{1,0:T(8,128)S(1)}, u32[]{:S(2)}, u32[]{:S(2)}) collective-permute-start(f32[32,256]{1,0:T(8,128)S(1)} %add_add_fusion.2.refs_0_), channel_id=1, source_target_pairs={{0,3},{1,0},{2,1},{3,2},{4,7},{5,4},{6,5},{7,6},{8,11},{9,8},{10,9... | collective-permute-start | bytes 98312 | tf_op jit(solution)/shard_map/ppermute | solution.py:62
  128.8 2.8 %collective-permute-start.27 = (f32[32,256]{1,0:T(8,128)S(1)}, f32[32,256]{1,0:T(8,128)S(1)}, u32[]{:S(2)}, u32[]{:S(2)}) collective-permute-start(f32[32,256]{1,0:T(8,128)S(1)} %add_add_fusion.2.refs_0_), channel_id=1, source_target_pairs={{0,1},{1,2},{2,3},{3,0},{4,5},{5,6},{6,7},{7,4},{8,9},{9,10},{10,1... | collective-permute-start | bytes 98312 | tf_op jit(solution)/shard_map/ppermute | solution.py:62
  131.6 3.5 %collective-permute-done.28.refs_2_ = f32[32,256]{1,0:T(8,128)S(1)} collective-permute-done((f32[32,256]{1,0:T(8,128)S(1)}, f32[32,256]{1,0:T(8,128)S(1)}, u32[]{:S(2)}, u32[]{:S(2)}) %collective-permute-start.28) | collective-permute-done | bytes 32800 | tf_op jit(solution)/shard_map/ppermute | solution.py:62
  135.2 3.7 %shard_map.81 = f32[64,256]{1,0:T(8,128)} custom-call(s32[96]{0:T(128)} %bitcast.45, s32[1]{0:T(128)} %bitcast.37.count_ref, f32[32,256]{1,0:T(8,128)S(1)} %add_add_fusion.2.refs_0_, f32[32,256]{1,0:T(8,128)S(1)} %collective-permute-done.27.refs_1_, f32[32,256]{1,0:T(8,128)S(1)} %collective-permute-done.28.refs_2_, ...), custom_call_target="tpu_custom_call" | custom-call | tf_op jit(solution)/shard_map/pallas_call | solution.py:400
  141.4 3.2 %collective-permute-start.32 = (f32[64,256]{1,0:T(8,128)S(1)}, f32[64,256]{1,0:T(8,128)S(1)}, u32[]{:S(2)}, u32[]{:S(2)}) collective-permute-start(f32[64,256]{1,0:T(8,128)S(1)} %add.88), channel_id=1, source_target_pairs={{0,32},{16,48},{32,0},{48,16},{64,96},{80,112},{96,64},{112,80},{1... | collective-permute-start | bytes 196616 | tf_op jit(solution)/shard_map/ppermute | solution.py:98
  148.9 2.7 %collective-permute-start.34 = (f32[64,256]{1,0:T(8,128)S(1)}, f32[64,256]{1,0:T(8,128)S(1)}, u32[]{:S(2)}, u32[]{:S(2)}) collective-permute-start(f32[64,256]{1,0:T(8,128)S(1)} %add_add_fusion.refs_4_), channel_id=1, source_target_pairs={{0,96},{16,112},{32,64},{48,80},{64,32},{80,48},{96,0},{112,16},{1... | collective-permute-start | bytes 196616 | tf_op jit(solution)/shard_map/ppermute | solution.py:101
  151.6 3.1 %collective-permute-done.34.refs_5_ = f32[64,256]{1,0:T(8,128)S(1)} collective-permute-done((f32[64,256]{1,0:T(8,128)S(1)}, f32[64,256]{1,0:T(8,128)S(1)}, u32[]{:S(2)}, u32[]{:S(2)}) %collective-permute-start.34) | collective-permute-done | bytes 65568 | tf_op jit(solution)/shard_map/ppermute | solution.py:101
  154.7 8.1 %shard_map.82 = (bf16[4,72,512]{2,1,0:T(8,128)(2,1)}, bf16[4,72,512]{2,1,0:T(8,128)(2,1)}, bf16[4,72,512]{2,1,0:T(8,128)(2,1)}, bf16[4,72,512]{2,1,0:T(8,128)(2,...) custom-call(s32[96]{0:T(128)} %bitcast.46, s32[1]{0:T(128)} %bitcast.38.count_ref, ...), custom_call_target="tpu_custom_call" | custom-call | tf_op jit(solution)/shard_map/pallas_call | solution.py:400
  162.9 5.8 %collective-permute-start.35 = (bf16[4,72,512]{2,1,0:T(8,128)(2,1)}, bf16[4,72,512]{2,1,0:T(8,128)(2,1)S(1)}, u32[]{:S(2)}, u32[]{:S(2)}) collective-permute-start(bf16[4,72,512]{2,1,0:T(8,128)(2,1)} %get-tuple-element.24), channel_id=1, source_target_pairs={{0,12},{1,13},{2,14},{3,15},{4,0},{5,1},{6,2},{7,3},{8,4},{9,5},{1... | collective-permute-start | bytes 884744 | tf_op jit(solution)/shard_map/ppermute | solution.py:58
  171.1 5.4 %collective-permute-done.35.b_ref = bf16[4,72,512]{2,1,0:T(8,128)(2,1)S(1)} collective-permute-done((bf16[4,72,512]{2,1,0:T(8,128)(2,1)}, bf16[4,72,512]{2,1,0:T(8,128)(2,1)S(1)}, u32[]{:S(2)}, u32[]{:S(2)}) %collective-permute-start.35) | collective-permute-done | bytes 294944 | tf_op jit(solution)/shard_map/ppermute | solution.py:58
  176.5 6.2 %collective-permute-done.36.c_ref = bf16[4,72,512]{2,1,0:T(8,128)(2,1)S(1)} collective-permute-done((bf16[4,72,512]{2,1,0:T(8,128)(2,1)}, bf16[4,72,512]{2,1,0:T(8,128)(2,1)S(1)}, u32[]{:S(2)}, u32[]{:S(2)}) %collective-permute-start.36) | collective-permute-done | bytes 294944 | tf_op jit(solution)/shard_map/ppermute | solution.py:58
  185.1 3.1 %collective-permute-start.38 = (bf16[72,512]{1,0:T(8,128)(2,1)}, bf16[72,512]{1,0:T(8,128)(2,1)S(1)}, u32[]{:S(2)}, u32[]{:S(2)}) collective-permute-start(bf16[72,512]{1,0:T(8,128)(2,1)} %get-tuple-element.28), channel_id=1, source_target_pairs={{0,1},{1,0},{2,3},{3,2},{4,5},{5,4},{6,7},{7,6},{8,9},{9,8},{10,11... | collective-permute-start | bytes 221192 | tf_op jit(solution)/shard_map/ppermute | solution.py:66
  188.2 5.2 %collective-permute-start.39 = (bf16[72,512]{1,0:T(8,128)(2,1)}, bf16[72,512]{1,0:T(8,128)(2,1)S(1)}, u32[]{:S(2)}, u32[]{:S(2)}) collective-permute-start(bf16[72,512]{1,0:T(8,128)(2,1)} %get-tuple-element.29), channel_id=1, source_target_pairs={{0,3},{1,2},{2,1},{3,0},{4,7},{5,6},{6,5},{7,4},{8,11},{9,10},{10,... | collective-permute-start | bytes 221192 | tf_op jit(solution)/shard_map/ppermute | solution.py:74
  198.8 4.0 %collective-permute-done.40 = bf16[72,512]{1,0:T(8,128)(2,1)S(1)} collective-permute-done((bf16[72,512]{1,0:T(8,128)(2,1)}, bf16[72,512]{1,0:T(8,128)(2,1)S(1)}, u32[]{:S(2)}, u32[]{:S(2)}) %collective-permute-start.40) | collective-permute-done | bytes 73760 | tf_op jit(solution)/shard_map/ppermute | solution.py:70
  204.1 5.1 %collective-permute-done.44 = bf16[2,64,1024]{2,1,0:T(8,128)(2,1)S(1)} collective-permute-done((bf16[2,64,1024]{2,1,0:T(8,128)(2,1)S(1)}, bf16[2,64,1024]{2,1,0:T(8,128)(2,1)S(1)}, u32[]{:S(2)}, u32[]{:S(2)}) %collective-permute-start.44) | collective-permute-done | bytes 262176 | tf_op jit(solution)/shard_map/ppermute | solution.py:78
  210.3 3.9 %collective-permute-start.45 = (bf16[64,1024]{1,0:T(8,128)(2,1)S(1)}, bf16[64,1024]{1,0:T(8,128)(2,1)S(1)}, u32[]{:S(2)}, u32[]{:S(2)}) collective-permute-start(bf16[64,1024]{1,0:T(8,128)(2,1)S(1)} %fusion.4), channel_id=1, source_target_pairs={{0,128},{16,144},{32,160},{48,176},{64,192},{80,208},{96,224},{112... | collective-permute-start | bytes 393224 | tf_op jit(solution)/shard_map/ppermute | solution.py:86
  (116 shorter events, 64.8 us)
Async XLA Ops:
  1.7 5.9 %collective-permute-start.5 = (bf16[1,72,1024]{2,1,0:T(8,128)(2,1)S(1)}, bf16[1,72,1024]{2,1,0:T(8,128)(2,1)S(1)}, u32[]{:S(2)}, u32[]{:S(2)}) collective-permute-start(bf16[1,72,1024]{2,1,0:T(8,128)(2,1)S(1)} %maximum_bitcast_fusion), channel_id=1, source_target_pairs={{0,128},{16,144},{32,160},{48,176},{64,192},{80,208},{96,224},{112... | collective-permute-start | bytes 442376 | tf_op jit(solution)/shard_map/ppermute | solution.py:86
  7.6 8.8 %collective-permute-start.8 = (bf16[2,72,1024]{2,1,0:T(8,128)(2,1)S(1)}, bf16[2,72,1024]{2,1,0:T(8,128)(2,1)S(1)}, u32[]{:S(2)}, u32[]{:S(2)}) collective-permute-start(bf16[2,72,1024]{2,1,0:T(8,128)(2,1)S(1)} %pad_maximum_fusion.1.refs_0_.refs_4_.refs_13_), channel_id=1, source_target_pairs={{0,96},{16,112},{32,0},{48,16},{64,32},{80,48},{96,64},{112,80},{1... | collective-permute-start | bytes 884744 | tf_op jit(solution)/shard_map/ppermute | solution.py:78
  14.7 21.8 %collective-permute-start.9 = (bf16[2,72,1024]{2,1,0:T(8,128)(2,1)S(1)}, bf16[2,72,1024]{2,1,0:T(8,128)(2,1)S(1)}, u32[]{:S(2)}, u32[]{:S(2)}) collective-permute-start(bf16[2,72,1024]{2,1,0:T(8,128)(2,1)S(1)} %pad_maximum_fusion.1.refs_0_.refs_4_.refs_13_), channel_id=1, source_target_pairs={{0,16},{16,0},{32,48},{48,32},{64,80},{80,64},{96,112},{112,96},{1... | collective-permute-start | bytes 884744 | tf_op jit(solution)/shard_map/ppermute | solution.py:82
  14.7 21.2 %collective-permute-start.7 = (bf16[2,72,1024]{2,1,0:T(8,128)(2,1)S(1)}, bf16[2,72,1024]{2,1,0:T(8,128)(2,1)S(1)}, u32[]{:S(2)}, u32[]{:S(2)}) collective-permute-start(bf16[2,72,1024]{2,1,0:T(8,128)(2,1)S(1)} %pad_maximum_fusion.1.refs_0_.refs_4_.refs_13_), channel_id=1, source_target_pairs={{0,64},{16,80},{32,96},{48,112},{64,0},{80,16},{96,32},{112,48},{1... | collective-permute-start | bytes 884744 | tf_op jit(solution)/shard_map/ppermute | solution.py:78
  15.5 20.4 %collective-permute-start.6 = (bf16[2,72,1024]{2,1,0:T(8,128)(2,1)S(1)}, bf16[2,72,1024]{2,1,0:T(8,128)(2,1)S(1)}, u32[]{:S(2)}, u32[]{:S(2)}) collective-permute-start(bf16[2,72,1024]{2,1,0:T(8,128)(2,1)S(1)} %pad_maximum_fusion.1.refs_0_.refs_4_.refs_13_), channel_id=1, source_target_pairs={{0,32},{16,48},{32,64},{48,80},{64,96},{80,112},{96,0},{112,16},{1... | collective-permute-start | bytes 884744 | tf_op jit(solution)/shard_map/ppermute | solution.py:78
  16.4 22.7 %collective-permute-start.12 = (bf16[2,72,1024]{2,1,0:T(8,128)(2,1)S(1)}, bf16[2,72,1024]{2,1,0:T(8,128)(2,1)S(1)}, u32[]{:S(2)}, u32[]{:S(2)}) collective-permute-start(bf16[2,72,1024]{2,1,0:T(8,128)(2,1)S(1)} %collective-permute-done.8.refs_3_.refs_7_.refs_16_), channel_id=1, source_target_pairs={{0,16},{16,0},{32,48},{48,32},{64,80},{80,64},{96,112},{112,96},{1... | collective-permute-start | bytes 884744 | tf_op jit(solution)/shard_map/ppermute | solution.py:82
  17.1 18.3 %collective-permute-start.1 = (bf16[2,72,512]{2,1,0:T(8,128)(2,1)S(1)}, bf16[2,72,512]{2,1,0:T(8,128)(2,1)S(1)}, u32[]{:S(2)}, u32[]{:S(2)}) collective-permute-start(bf16[2,72,512]{2,1,0:T(8,128)(2,1)S(1)} %pad_maximum_fusion.2), channel_id=1, source_target_pairs={{0,3},{1,2},{2,1},{3,0},{4,7},{5,6},{6,5},{7,4},{8,11},{9,10},{10,... | collective-permute-start | bytes 442376 | tf_op jit(solution)/shard_map/ppermute | solution.py:74
  35.4 10.9 %collective-permute-start.4 = (bf16[4,72,512]{2,1,0:T(8,128)(2,1)S(1)}, bf16[4,72,512]{2,1,0:T(8,128)(2,1)S(1)}, u32[]{:S(2)}, u32[]{:S(2)}) collective-permute-start(bf16[4,72,512]{2,1,0:T(8,128)(2,1)S(1)} %pad_maximum_fusion.refs_0_.refs_9_), channel_id=1, source_target_pairs={{0,12},{1,13},{2,14},{3,15},{4,0},{5,1},{6,2},{7,3},{8,4},{9,5},{1... | collective-permute-start | bytes 884744 | tf_op jit(solution)/shard_map/ppermute | solution.py:58
  36.0 6.3 %collective-permute-start.11 = (bf16[2,72,1024]{2,1,0:T(8,128)(2,1)S(1)}, bf16[2,72,1024]{2,1,0:T(8,128)(2,1)S(1)}, u32[]{:S(2)}, u32[]{:S(2)}) collective-permute-start(bf16[2,72,1024]{2,1,0:T(8,128)(2,1)S(1)} %collective-permute-done.7.refs_2_.refs_6_.refs_15_), channel_id=1, source_target_pairs={{0,16},{16,0},{32,48},{48,32},{64,80},{80,64},{96,112},{112,96},{1... | collective-permute-start | bytes 884744 | tf_op jit(solution)/shard_map/ppermute | solution.py:82
  36.0 6.3 %collective-permute-start.10 = (bf16[2,72,1024]{2,1,0:T(8,128)(2,1)S(1)}, bf16[2,72,1024]{2,1,0:T(8,128)(2,1)S(1)}, u32[]{:S(2)}, u32[]{:S(2)}) collective-permute-start(bf16[2,72,1024]{2,1,0:T(8,128)(2,1)S(1)} %collective-permute-done.6.refs_1_.refs_5_.refs_14_), channel_id=1, source_target_pairs={{0,16},{16,0},{32,48},{48,32},{64,80},{80,64},{96,112},{112,96},{1... | collective-permute-start | bytes 884744 | tf_op jit(solution)/shard_map/ppermute | solution.py:82
  36.5 14.9 %collective-permute-start.3 = (bf16[4,72,512]{2,1,0:T(8,128)(2,1)S(1)}, bf16[4,72,512]{2,1,0:T(8,128)(2,1)S(1)}, u32[]{:S(2)}, u32[]{:S(2)}) collective-permute-start(bf16[4,72,512]{2,1,0:T(8,128)(2,1)S(1)} %pad_maximum_fusion.refs_0_.refs_9_), channel_id=1, source_target_pairs={{0,8},{1,9},{2,10},{3,11},{4,12},{5,13},{6,14},{7,15},{8,0},{9,1},... | collective-permute-start | bytes 884744 | tf_op jit(solution)/shard_map/ppermute | solution.py:58
  39.1 14.5 %collective-permute-start.2 = (bf16[4,72,512]{2,1,0:T(8,128)(2,1)S(1)}, bf16[4,72,512]{2,1,0:T(8,128)(2,1)}, u32[]{:S(2)}, u32[]{:S(2)}) collective-permute-start(bf16[4,72,512]{2,1,0:T(8,128)(2,1)S(1)} %pad_maximum_fusion.refs_0_.refs_9_), channel_id=1, source_target_pairs={{0,4},{1,5},{2,6},{3,7},{4,8},{5,9},{6,10},{7,11},{8,12},{9,13},{1... | collective-permute-start | bytes 884744 | tf_op jit(solution)/shard_map/ppermute | solution.py:58
  62.3 6.8 %collective-permute-start.15 = (f32[32,256]{1,0:T(8,128)}, f32[32,256]{1,0:T(8,128)S(1)}, u32[]{:S(2)}, u32[]{:S(2)}) collective-permute-start(f32[32,256]{1,0:T(8,128)} %get-tuple-element.19), channel_id=1, source_target_pairs={{0,12},{1,13},{2,14},{3,15},{4,0},{5,1},{6,2},{7,3},{8,4},{9,5},{1... | collective-permute-start | bytes 98312 | tf_op jit(solution)/shard_map/ppermute | solution.py:58
  73.3 11.2 %collective-permute-start.18 = (f32[32,256]{1,0:T(8,128)S(1)}, f32[32,256]{1,0:T(8,128)S(1)}, u32[]{:S(2)}, u32[]{:S(2)}) collective-permute-start(f32[32,256]{1,0:T(8,128)S(1)} %add_add_fusion.3.refs_0_), channel_id=1, source_target_pairs={{0,3},{1,0},{2,1},{3,2},{4,7},{5,4},{6,5},{7,6},{8,11},{9,8},{10,9... | collective-permute-start | bytes 98312 | tf_op jit(solution)/shard_map/ppermute | solution.py:62
  82.1 8.0 %collective-permute-start.17 = (f32[32,256]{1,0:T(8,128)S(1)}, f32[32,256]{1,0:T(8,128)S(1)}, u32[]{:S(2)}, u32[]{:S(2)}) collective-permute-start(f32[32,256]{1,0:T(8,128)S(1)} %add_add_fusion.3.refs_0_), channel_id=1, source_target_pairs={{0,2},{1,3},{2,0},{3,1},{4,6},{5,7},{6,4},{7,5},{8,10},{9,11},{10,... | collective-permute-start | bytes 98312 | tf_op jit(solution)/shard_map/ppermute | solution.py:62
  82.1 8.0 %collective-permute-start.16 = (f32[32,256]{1,0:T(8,128)S(1)}, f32[32,256]{1,0:T(8,128)S(1)}, u32[]{:S(2)}, u32[]{:S(2)}) collective-permute-start(f32[32,256]{1,0:T(8,128)S(1)} %add_add_fusion.3.refs_0_), channel_id=1, source_target_pairs={{0,1},{1,2},{2,3},{3,0},{4,5},{5,6},{6,7},{7,4},{8,9},{9,10},{10,1... | collective-permute-start | bytes 98312 | tf_op jit(solution)/shard_map/ppermute | solution.py:62
  111.6 8.2 %collective-permute-start.26 = (f32[32,256]{1,0:T(8,128)}, f32[32,256]{1,0:T(8,128)S(1)}, u32[]{:S(2)}, u32[]{:S(2)}) collective-permute-start(f32[32,256]{1,0:T(8,128)} %shard_map.80), channel_id=1, source_target_pairs={{0,12},{1,13},{2,14},{3,15},{4,0},{5,1},{6,2},{7,3},{8,4},{9,5},{1... | collective-permute-start | bytes 98312 | tf_op jit(solution)/shard_map/ppermute | solution.py:58
  124.3 7.3 %collective-permute-start.29 = (f32[32,256]{1,0:T(8,128)S(1)}, f32[32,256]{1,0:T(8,128)S(1)}, u32[]{:S(2)}, u32[]{:S(2)}) collective-permute-start(f32[32,256]{1,0:T(8,128)S(1)} %add_add_fusion.2.refs_0_), channel_id=1, source_target_pairs={{0,3},{1,0},{2,1},{3,2},{4,7},{5,4},{6,5},{7,6},{8,11},{9,8},{10,9... | collective-permute-start | bytes 98312 | tf_op jit(solution)/shard_map/ppermute | solution.py:62
  127.1 7.9 %collective-permute-start.28 = (f32[32,256]{1,0:T(8,128)S(1)}, f32[32,256]{1,0:T(8,128)S(1)}, u32[]{:S(2)}, u32[]{:S(2)}) collective-permute-start(f32[32,256]{1,0:T(8,128)S(1)} %add_add_fusion.2.refs_0_), channel_id=1, source_target_pairs={{0,2},{1,3},{2,0},{3,1},{4,6},{5,7},{6,4},{7,5},{8,10},{9,11},{10,... | collective-permute-start | bytes 98312 | tf_op jit(solution)/shard_map/ppermute | solution.py:62
  128.8 6.4 %collective-permute-start.27 = (f32[32,256]{1,0:T(8,128)S(1)}, f32[32,256]{1,0:T(8,128)S(1)}, u32[]{:S(2)}, u32[]{:S(2)}) collective-permute-start(f32[32,256]{1,0:T(8,128)S(1)} %add_add_fusion.2.refs_0_), channel_id=1, source_target_pairs={{0,1},{1,2},{2,3},{3,0},{4,5},{5,6},{6,7},{7,4},{8,9},{9,10},{10,1... | collective-permute-start | bytes 98312 | tf_op jit(solution)/shard_map/ppermute | solution.py:62
  141.4 6.4 %collective-permute-start.32 = (f32[64,256]{1,0:T(8,128)S(1)}, f32[64,256]{1,0:T(8,128)S(1)}, u32[]{:S(2)}, u32[]{:S(2)}) collective-permute-start(f32[64,256]{1,0:T(8,128)S(1)} %add.88), channel_id=1, source_target_pairs={{0,32},{16,48},{32,0},{48,16},{64,96},{80,112},{96,64},{112,80},{1... | collective-permute-start | bytes 196616 | tf_op jit(solution)/shard_map/ppermute | solution.py:98
  162.8 30.5 %collective-permute-start.41 = (bf16[8,64,1024]{2,1,0:T(8,128)(2,1)}, bf16[8,64,1024]{2,1,0:T(8,128)(2,1)S(1)}, u32[]{:S(2)}, u32[]{:S(2)}) collective-permute-start(bf16[8,64,1024]{2,1,0:T(8,128)(2,1)} %get-tuple-element.33), channel_id=1, source_target_pairs={{0,16},{16,0},{32,48},{48,32},{64,80},{80,64},{96,112},{112,96},{1... | collective-permute-start | bytes 3145736 | tf_op jit(solution)/shard_map/ppermute | solution.py:82
  162.9 13.5 %collective-permute-start.35 = (bf16[4,72,512]{2,1,0:T(8,128)(2,1)}, bf16[4,72,512]{2,1,0:T(8,128)(2,1)S(1)}, u32[]{:S(2)}, u32[]{:S(2)}) collective-permute-start(bf16[4,72,512]{2,1,0:T(8,128)(2,1)} %get-tuple-element.24), channel_id=1, source_target_pairs={{0,12},{1,13},{2,14},{3,15},{4,0},{5,1},{6,2},{7,3},{8,4},{9,5},{1... | collective-permute-start | bytes 884744 | tf_op jit(solution)/shard_map/ppermute | solution.py:58
  168.8 13.9 %collective-permute-start.36 = (bf16[4,72,512]{2,1,0:T(8,128)(2,1)}, bf16[4,72,512]{2,1,0:T(8,128)(2,1)S(1)}, u32[]{:S(2)}, u32[]{:S(2)}) collective-permute-start(bf16[4,72,512]{2,1,0:T(8,128)(2,1)} %get-tuple-element.25), channel_id=1, source_target_pairs={{0,8},{1,9},{2,10},{3,11},{4,12},{5,13},{6,14},{7,15},{8,0},{9,1},... | collective-permute-start | bytes 884744 | tf_op jit(solution)/shard_map/ppermute | solution.py:58
  168.9 14.5 %collective-permute-start.37 = (bf16[4,72,512]{2,1,0:T(8,128)(2,1)}, bf16[4,72,512]{2,1,0:T(8,128)(2,1)S(1)}, u32[]{:S(2)}, u32[]{:S(2)}) collective-permute-start(bf16[4,72,512]{2,1,0:T(8,128)(2,1)} %get-tuple-element.26), channel_id=1, source_target_pairs={{0,4},{1,5},{2,6},{3,7},{4,8},{5,9},{6,10},{7,11},{8,12},{9,13},{1... | collective-permute-start | bytes 884744 | tf_op jit(solution)/shard_map/ppermute | solution.py:58
  185.1 11.8 %collective-permute-start.38 = (bf16[72,512]{1,0:T(8,128)(2,1)}, bf16[72,512]{1,0:T(8,128)(2,1)S(1)}, u32[]{:S(2)}, u32[]{:S(2)}) collective-permute-start(bf16[72,512]{1,0:T(8,128)(2,1)} %get-tuple-element.28), channel_id=1, source_target_pairs={{0,1},{1,0},{2,3},{3,2},{4,5},{5,4},{6,7},{7,6},{8,9},{9,8},{10,11... | collective-permute-start | bytes 221192 | tf_op jit(solution)/shard_map/ppermute | solution.py:66
  188.2 10.6 %collective-permute-start.39 = (bf16[72,512]{1,0:T(8,128)(2,1)}, bf16[72,512]{1,0:T(8,128)(2,1)S(1)}, u32[]{:S(2)}, u32[]{:S(2)}) collective-permute-start(bf16[72,512]{1,0:T(8,128)(2,1)} %get-tuple-element.29), channel_id=1, source_target_pairs={{0,3},{1,2},{2,1},{3,0},{4,7},{5,6},{6,5},{7,4},{8,11},{9,10},{10,... | collective-permute-start | bytes 221192 | tf_op jit(solution)/shard_map/ppermute | solution.py:74
  193.4 9.4 %collective-permute-start.40 = (bf16[72,512]{1,0:T(8,128)(2,1)}, bf16[72,512]{1,0:T(8,128)(2,1)S(1)}, u32[]{:S(2)}, u32[]{:S(2)}) collective-permute-start(bf16[72,512]{1,0:T(8,128)(2,1)} %get-tuple-element.30), channel_id=1, source_target_pairs={{0,2},{1,3},{2,0},{3,1},{4,6},{5,7},{6,4},{7,5},{8,10},{9,11},{10,... | collective-permute-start | bytes 221192 | tf_op jit(solution)/shard_map/ppermute | solution.py:70
  194.8 9.3 %collective-permute-start.42 = (bf16[2,64,1024]{2,1,0:T(8,128)(2,1)S(1)}, bf16[2,64,1024]{2,1,0:T(8,128)(2,1)S(1)}, u32[]{:S(2)}, u32[]{:S(2)}) collective-permute-start(bf16[2,64,1024]{2,1,0:T(8,128)(2,1)S(1)} %get-tuple-element.34), channel_id=1, source_target_pairs={{0,96},{16,112},{32,0},{48,16},{64,32},{80,48},{96,64},{112,80},{1... | collective-permute-start | bytes 786440 | tf_op jit(solution)/shard_map/ppermute | solution.py:78
  195.6 13.5 %collective-permute-start.44 = (bf16[2,64,1024]{2,1,0:T(8,128)(2,1)S(1)}, bf16[2,64,1024]{2,1,0:T(8,128)(2,1)S(1)}, u32[]{:S(2)}, u32[]{:S(2)}) collective-permute-start(bf16[2,64,1024]{2,1,0:T(8,128)(2,1)S(1)} %get-tuple-element.35), channel_id=1, source_target_pairs={{0,32},{16,48},{32,64},{48,80},{64,96},{80,112},{96,0},{112,16},{1... | collective-permute-start | bytes 786440 | tf_op jit(solution)/shard_map/ppermute | solution.py:78
  196.9 12.2 %collective-permute-start.43 = (bf16[2,64,1024]{2,1,0:T(8,128)(2,1)S(1)}, bf16[2,64,1024]{2,1,0:T(8,128)(2,1)S(1)}, u32[]{:S(2)}, u32[]{:S(2)}) collective-permute-start(bf16[2,64,1024]{2,1,0:T(8,128)(2,1)S(1)} %get-tuple-element.36), channel_id=1, source_target_pairs={{0,64},{16,80},{32,96},{48,112},{64,0},{80,16},{96,32},{112,48},{1... | collective-permute-start | bytes 786440 | tf_op jit(solution)/shard_map/ppermute | solution.py:78
  210.3 6.8 %collective-permute-start.45 = (bf16[64,1024]{1,0:T(8,128)(2,1)S(1)}, bf16[64,1024]{1,0:T(8,128)(2,1)S(1)}, u32[]{:S(2)}, u32[]{:S(2)}) collective-permute-start(bf16[64,1024]{1,0:T(8,128)(2,1)S(1)} %fusion.4), channel_id=1, source_target_pairs={{0,128},{16,144},{32,160},{48,176},{64,192},{80,208},{96,224},{112... | collective-permute-start | bytes 393224 | tf_op jit(solution)/shard_map/ppermute | solution.py:86
  (27 other events, 331.2 us)

commit v3 on v2

--- a/solution.py
+++ b/solution.py
@@ -183,42 +183,45 @@
     ]
 
 
-def column_start_kernel(pos_ref, *refs):
-    ys = refs[0:8]
-    n_ref, b_ref, yt_ref, sems = refs[8:]
-    copies = [pltpu.make_async_copy(ys[k], yt_ref.at[pl.ds(2 * k, 2)], sems.at[k]) for k in range(8)]
-    for copy in copies:
-        copy.start()
-    for copy in copies:
-        copy.wait()
-    for q in range(SLOTS):
-        slot = photo_slot(q, pos_ref[0])
-        mass = yt_ref[slot, F:EXT, :].astype(f32)
-        y = yt_ref[slot, 0:F, :].astype(f32)
-        weight = jnp.exp(jnp.sum(y * y, axis=0, keepdims=True) * -0.0625)
-        for k in range(4):
-            lanes = slice(k * TILE, (k + 1) * TILE)
-            n_ref[4 * q + k : 4 * q + k + 1, :] = mass[0:1, lanes]
-            b_ref[4 * q + k : 4 * q + k + 1, :] = weight[:, lanes]
+def pack_kernel(x_ref, y_ref, x_mass_ref, y_mass_ref, x_out, y_out):
+    def rows(values):
+        sub = lax.broadcasted_iota(jnp.int32, (8, values[0].shape[1]), 0)
+        block = jnp.zeros(sub.shape, f32)
+        for i, value in enumerate(values):
+            block = jnp.where(sub == i, value, block)
+        return block.astype(bf16)
+
+    x_out[0, 0:F, :] = x_ref[...]
+    x_out[0, F:EXT, :] = rows([x_mass_ref[...].astype(f32)])
+    y = y_ref[...].astype(f32)
+    weight = jnp.exp(jnp.sum(y * y, axis=0, keepdims=True) * -0.0625)
+    high = weight.astype(bf16).astype(f32)
+    y_out[0, 0:F, :] = y_ref[...]
+    y_out[0, F:EXT, :] = rows([y_mass_ref[...].astype(f32), high, weight - high])
 
 
 def first_kernel(index_ref, count_ref, pos_ref, *refs):
-    xs, ys, b_ref = (refs[0:4], refs[4:12], refs[12])
-    out_ref, m_ref, g_hbm = refs[13:16]
+    xs, ys = (refs[0:4], refs[4:12])
+    out_ref, m_ref, n_ref, g_hbm = refs[12:16]
     xt_ref, yt_ref, xr_ref, w_ref, acc_ref, g_ref, sems, g_sems = refs[16:]
     copies = piece_copies(xs, ys, xt_ref, yt_ref, sems)
     for copy in copies:
         copy.start()
     acc_ref[...] = jnp.zeros_like(acc_ref)
-    for column in range(TC):
-        w_ref[column] = high_low(b_ref[column : column + 1, :])
     for copy in copies:
         copy.wait()
+    for q in range(SLOTS):
+        rows = yt_ref[photo_slot(q, pos_ref[1]), F:EXT, :].astype(f32)
+        for k in range(4):
+            lanes = slice(k * TILE, (k + 1) * TILE)
+            n_ref[4 * q + k : 4 * q + k + 1, :] = rows[0:1, lanes]
+            sub = lax.broadcasted_iota(jnp.int32, (16, TILE), 0)
+            pair = jnp.where(sub == 0, rows[1:2, lanes], jnp.where(sub == 1, rows[2:3, lanes], 0.0))
+            w_ref[4 * q + k] = pair.astype(bf16)
 
     def turn_slot(s, carry):
         for h in range(2):
-            x = xt_ref[s, 0:F, h * TILE : (h + 1) * TILE].astype(f32)
-            xr_ref[2 * s + h] = jnp.transpose(x).astype(bf16)
+            xr_ref[2 * s + h] = jnp.transpose(xt_ref[s, 0:F, h * TILE : (h + 1) * TILE])
         return carry
 
     lax.fori_loop(0, SLOTS, turn_slot, 0)
@@ -420,11 +423,10 @@
     )
     x_own = spec_feat.T
     y_own = photo_feat[0].T
-    x_pad = jnp.zeros((EXT - F - 1, SB), bf16)
-    y_pad = jnp.zeros((EXT - F - 1, PB), bf16)
-    x0 = jnp.concatenate([x_own, spec_mass.reshape(1, SB), x_pad])[None]
-    y0 = jnp.concatenate([y_own, photo_mass.reshape(1, PB), y_pad])[None]
-
+    x0, y0 = call(
+        pack_kernel, [VMEM] * 4, [(VMEM, (1, EXT, SB), bf16), (VMEM, (1, EXT, PB), bf16)], [],
+        x_own, y_own, spec_mass.reshape(1, SB), photo_mass.reshape(1, PB),
+    )
     x_flip = flip_z(x0)
     y_low = swap_low(y0)
     x0 = jnp.concatenate([x0, x_flip])
@@ -441,18 +443,14 @@
     column_acc = [pltpu.VMEM((TR, 16, TILE), bf16), pltpu.VMEM((TC, 16, TILE), f32)]
     blocks = [pltpu.VMEM((SLOTS, EXT, SB), bf16), pltpu.VMEM((SLOTS, EXT, PB), bf16)]
     piece_sems = pltpu.SemaphoreType.DMA((12,))
-    n, b = call(
-        column_start_kernel, [SMEM] + [ANY] * 8, [(VMEM, (TC, TILE), f32)] * 2,
-        [pltpu.VMEM((SLOTS, EXT, PB), bf16), pltpu.SemaphoreType.DMA((8,))], meta[2][1:], *ys,
-    )
-    r, m, g = call(
-        first_kernel, [SMEM] * 3 + [ANY] * 12 + [VMEM],
+    r, m, n, g = call(
+        first_kernel, [SMEM] * 3 + [ANY] * 12,
         [
-            (VMEM, (TR, TILE), f32), (VMEM, (TR, TILE), f32),
+            (VMEM, (TR, TILE), f32), (VMEM, (TR, TILE), f32), (VMEM, (TC, TILE), f32),
             (ANY, (TURNS, GROUP, TILE, TILE), bf16),
         ],
         blocks + [pltpu.VMEM((TR, TILE, F), bf16)] + row_acc + [tiles, piece_sems, tile_sems],
-        *meta, *xs, *ys, b,
+        *meta, *xs, *ys,
     )
     lists = meta[0:2]
 

time: 222 us -> 210 us (0.946)
  starting transfers between devices: 96 us -> 86.4 us
  waiting for transfers between devices: 73.9 us -> 71.6 us
    ppermute x6, waiting for transfers between devices: 5.38 us -> 16.6 us  [shift_x(): return lax.ppermute(a, 'spec', spec_perm(same, shift(k), same))]
    ppermute x2, starting transfers between devices: 16.6 us -> 9.22 us  [mirror_z(): return lax.ppermute(a, 'photo', photo_perm(same, mirror))]
    ppermute x2, waiting for transfers between devices: 6.94 us -> 0.16 us  [mirror_z(): return lax.ppermute(a, 'photo', photo_perm(same, mirror))]
    ppermute x12, waiting for transfers between devices: 27.6 us -> 23.4 us  [shift_y(): return lax.ppermute(a, 'photo', photo_perm(shift(k), same))]
    ppermute x6, starting transfers between devices: 18.5 us -> 14.6 us  [shift_z(): return lax.ppermute(a, 'photo', photo_perm(same, shift(k)))]
    ppermute x2, waiting for transfers between devices: 5.43 us -> 2.27 us  [swap_low(): return lax.ppermute(a, 'spec', spec_perm(flip, same, same))]
  transfers between devices with their start and end apart: 46 -> 46, of which waited for: 28 -> 29; matrix products, arithmetic and copies ran while one was open for 3% -> 4% of each run, Pallas kernels for 2% -> 1%
where the time goes in v3:
time: 210 us; the launch traced here: 205 us
  starting transfers between devices  86.4 us (41%)
  waiting for transfers between devices  71.6 us (34%)
  Pallas kernels  31.2 us (15%)
  other arithmetic  9.78 us (5%)
  local copies, waits for them, and re-layouts  4.78 us (2%)
    pallas_call x7, Pallas kernels, call(): pl.pallas_call(kernel, in_specs=in_specs, out_specs=[spec for spec, _, _...  31.2 us
    ppermute x12, starting transfers between devices, shift_y(): return lax.ppermute(a, 'photo', photo_perm(shift(k), same))  25.8 us
    ppermute x12, waiting for transfers between devices, shift_y(): return lax.ppermute(a, 'photo', photo_perm(shift(k), same))  23.4 us
    ppermute x6, waiting for transfers between devices, shift_x(): return lax.ppermute(a, 'spec', spec_perm(same, shift(k), same))  16.6 us
    ppermute x6, starting transfers between devices, shift_z(): return lax.ppermute(a, 'photo', photo_perm(same, shift(k)))  14.6 us
    ppermute x6, starting transfers between devices, shift_x(): return lax.ppermute(a, 'spec', spec_perm(same, shift(k), same))  9.27 us
    ppermute x6, starting transfers between devices, sum_spec(): lax.ppermute(a, 'spec', spec_perm(fl, fx, same))  9.25 us
    ppermute x2, starting transfers between devices, mirror_z(): return lax.ppermute(a, 'photo', photo_perm(same, mirror))  9.22 us
  transfers between devices with their start and end apart: 46, of which 29 were waited for; matrix products, arithmetic and copies ran while one was open for 4% of the time, Pallas kernels for 1%

profile of v3, /device:TPU:8, one launch (start us, length us, event | category | flops | bytes accessed | tf_op | source)
XLA Modules:
  0.0 205.4 jit_solution(5218004866308300086)
XLA Ops:
  3.5 3.3 %collective-permute-start = (bf16[1,72,512]{2,1,0:T(8,128)(2,1)}, bf16[1,72,512]{2,1,0:T(8,128)(2,1)S(1)}, u32[]{:S(2)}, u32[]{:S(2)}) collective-permute-start(bf16[1,72,512]{2,1,0:T(8,128)(2,1)} %get-tuple-element.19), channel_id=1, source_target_pairs={{0,1},{1,0},{2,3},{3,2},{4,5},{5,4},{6,7},{7,6},{8,9},{9,8},{10,11... | collective-permute-start | bytes 221192 | tf_op jit(solution)/shard_map/ppermute | solution.py:66
  11.5 5.6 %collective-permute-start.1 = (bf16[2,72,512]{2,1,0:T(8,128)(2,1)S(1)}, bf16[2,72,512]{2,1,0:T(8,128)(2,1)S(1)}, u32[]{:S(2)}, u32[]{:S(2)}) collective-permute-start(bf16[2,72,512]{2,1,0:T(8,128)(2,1)S(1)} %pad_maximum_fusion), channel_id=1, source_target_pairs={{0,3},{1,2},{2,1},{3,0},{4,7},{5,6},{6,5},{7,4},{8,11},{9,10},{10,... | collective-permute-start | bytes 442376 | tf_op jit(solution)/shard_map/ppermute | solution.py:74
  17.2 2.8 %collective-permute-start.8 = (bf16[2,72,1024]{2,1,0:T(8,128)(2,1)S(1)}, bf16[2,72,1024]{2,1,0:T(8,128)(2,1)S(1)}, u32[]{:S(2)}, u32[]{:S(2)}) collective-permute-start(bf16[2,72,1024]{2,1,0:T(8,128)(2,1)S(1)} %constant_dynamic-update-slice_fusion.3.refs_4_.refs_13_), channel_id=1, source_target_pairs={{0,96},{16,112},{32,0},{48,16},{64,32},{80,48},{96,64},{112,80},{1... | collective-permute-start | bytes 884744 | tf_op jit(solution)/shard_map/ppermute | solution.py:78
  25.0 8.2 %collective-permute-done.8.refs_7_.refs_16_ = bf16[2,72,1024]{2,1,0:T(8,128)(2,1)S(1)} collective-permute-done((bf16[2,72,1024]{2,1,0:T(8,128)(2,1)S(1)}, bf16[2,72,1024]{2,1,0:T(8,128)(2,1)S(1)}, u32[]{:S(2)}, u32[]{:S(2)}) %collective-permute-start.8) | collective-permute-done | bytes 294944 | tf_op jit(solution)/shard_map/ppermute | solution.py:78
  38.7 2.8 %collective-permute-done.2.refs_1_.refs_10_ = bf16[4,72,512]{2,1,0:T(8,128)(2,1)S(1)} collective-permute-done((bf16[4,72,512]{2,1,0:T(8,128)(2,1)S(1)}, bf16[4,72,512]{2,1,0:T(8,128)(2,1)S(1)}, u32[]{:S(2)}, u32[]{:S(2)}) %collective-permute-start.2) | collective-permute-done | bytes 294944 | tf_op jit(solution)/shard_map/ppermute | solution.py:58
  42.5 8.3 %shard_map.78 = (f32[32,256]{1,0:T(8,128)}, f32[32,256]{1,0:T(8,128)}, f32[64,256]{1,0:T(8,128)}, bf16[12,8,256,256]{3,2,1,0:T(8,128)(2,1)}) custom-call(s32[96]{0:T(128)} %bitcast.38, s32[1]{0:T(128)} %bitcast.30.count_ref, s32[2]{0:T(128)} %pad_add_fusion.pos_ref, bf16[4,72,512]{2,1,0:T(8,128)(2,1)} %copy-done.1, bf16[4,72,512]{2,1,0:T(8,128)(2,1)} %copy-done.8, ...), custom_call_target="tpu_custom_call" | custom-call | tf_op jit(solution)/shard_map/pallas_call | solution.py:403
  50.8 2.6 %collective-permute-start.15 = (f32[32,256]{1,0:T(8,128)}, f32[32,256]{1,0:T(8,128)S(1)}, u32[]{:S(2)}, u32[]{:S(2)}) collective-permute-start(f32[32,256]{1,0:T(8,128)} %get-tuple-element.21), channel_id=1, source_target_pairs={{0,12},{1,13},{2,14},{3,15},{4,0},{5,1},{6,2},{7,3},{8,4},{9,5},{1... | collective-permute-start | bytes 98312 | tf_op jit(solution)/shard_map/ppermute | solution.py:58
  53.4 3.7 %collective-permute-start.14 = (f32[32,256]{1,0:T(8,128)}, f32[32,256]{1,0:T(8,128)S(1)}, u32[]{:S(2)}, u32[]{:S(2)}) collective-permute-start(f32[32,256]{1,0:T(8,128)} %get-tuple-element.21), channel_id=1, source_target_pairs={{0,8},{1,9},{2,10},{3,11},{4,12},{5,13},{6,14},{7,15},{8,0},{9,1},... | collective-permute-start | bytes 98312 | tf_op jit(solution)/shard_map/ppermute | solution.py:58
  62.0 4.1 %collective-permute-start.18 = (f32[32,256]{1,0:T(8,128)S(1)}, f32[32,256]{1,0:T(8,128)S(1)}, u32[]{:S(2)}, u32[]{:S(2)}) collective-permute-start(f32[32,256]{1,0:T(8,128)S(1)} %add_add_fusion.3.refs_0_), channel_id=1, source_target_pairs={{0,3},{1,0},{2,1},{3,2},{4,7},{5,4},{6,5},{7,6},{8,11},{9,8},{10,9... | collective-permute-start | bytes 98312 | tf_op jit(solution)/shard_map/ppermute | solution.py:62
  66.9 2.8 %collective-permute-start.16 = (f32[32,256]{1,0:T(8,128)S(1)}, f32[32,256]{1,0:T(8,128)S(1)}, u32[]{:S(2)}, u32[]{:S(2)}) collective-permute-start(f32[32,256]{1,0:T(8,128)S(1)} %add_add_fusion.3.refs_0_), channel_id=1, source_target_pairs={{0,1},{1,2},{2,3},{3,0},{4,5},{5,6},{6,7},{7,4},{8,9},{9,10},{10,1... | collective-permute-start | bytes 98312 | tf_op jit(solution)/shard_map/ppermute | solution.py:62
  69.7 4.3 %collective-permute-done.17.refs_2_ = f32[32,256]{1,0:T(8,128)S(1)} collective-permute-done((f32[32,256]{1,0:T(8,128)S(1)}, f32[32,256]{1,0:T(8,128)S(1)}, u32[]{:S(2)}, u32[]{:S(2)}) %collective-permute-start.17) | collective-permute-done | bytes 32800 | tf_op jit(solution)/shard_map/ppermute | solution.py:62
  74.0 3.7 %shard_map.79 = f32[64,256]{1,0:T(8,128)} custom-call(s32[96]{0:T(128)} %bitcast.39, s32[1]{0:T(128)} %bitcast.31.count_ref, f32[32,256]{1,0:T(8,128)S(1)} %add_add_fusion.3.refs_0_, f32[32,256]{1,0:T(8,128)S(1)} %collective-permute-done.16.refs_1_, f32[32,256]{1,0:T(8,128)S(1)} %collective-permute-done.17.refs_2_, ...), custom_call_target="tpu_custom_call" | custom-call | tf_op jit(solution)/shard_map/pallas_call | solution.py:403
  81.9 3.9 %collective-permute-start.21 = (f32[64,256]{1,0:T(8,128)S(1)}, f32[64,256]{1,0:T(8,128)S(1)}, u32[]{:S(2)}, u32[]{:S(2)}) collective-permute-start(f32[64,256]{1,0:T(8,128)S(1)} %add.81), channel_id=1, source_target_pairs={{0,32},{16,48},{32,0},{48,16},{64,96},{80,112},{96,64},{112,80},{1... | collective-permute-start | bytes 196616 | tf_op jit(solution)/shard_map/ppermute | solution.py:98
  92.1 3.5 %collective-permute-done.23.cb_ref = f32[64,256]{1,0:T(8,128)S(1)} collective-permute-done((f32[64,256]{1,0:T(8,128)S(1)}, f32[64,256]{1,0:T(8,128)S(1)}, u32[]{:S(2)}, u32[]{:S(2)}) %collective-permute-start.23) | collective-permute-done | bytes 65568 | tf_op jit(solution)/shard_map/ppermute | solution.py:101
  95.6 4.0 %shard_map.80 = f32[32,256]{1,0:T(8,128)} custom-call(s32[96]{0:T(128)} %bitcast.40, s32[1]{0:T(128)} %bitcast.32.count_ref, f32[64,256]{1,0:T(8,128)S(1)} %add_add_fusion.1.ca_ref, f32[64,256]{1,0:T(8,128)S(1)} %collective-permute-done.23.cb_ref, f32[64,256]{1,0:T(8,128)} %get-tuple-element.24.n_ref.refs_7_, ...), custom_call_target="tpu_custom_call" | custom-call | tf_op jit(solution)/shard_map/pallas_call | solution.py:403
  99.7 5.5 %collective-permute-start.26 = (f32[32,256]{1,0:T(8,128)}, f32[32,256]{1,0:T(8,128)S(1)}, u32[]{:S(2)}, u32[]{:S(2)}) collective-permute-start(f32[32,256]{1,0:T(8,128)} %shard_map.80), channel_id=1, source_target_pairs={{0,12},{1,13},{2,14},{3,15},{4,0},{5,1},{6,2},{7,3},{8,4},{9,5},{1... | collective-permute-start | bytes 98312 | tf_op jit(solution)/shard_map/ppermute | solution.py:58
  107.1 3.7 %collective-permute-done.25 = f32[32,256]{1,0:T(8,128)S(1)} collective-permute-done((f32[32,256]{1,0:T(8,128)}, f32[32,256]{1,0:T(8,128)S(1)}, u32[]{:S(2)}, u32[]{:S(2)}) %collective-permute-start.25) | collective-permute-done | bytes 32800 | tf_op jit(solution)/shard_map/ppermute | solution.py:58
  115.7 2.8 %collective-permute-start.27 = (f32[32,256]{1,0:T(8,128)S(1)}, f32[32,256]{1,0:T(8,128)S(1)}, u32[]{:S(2)}, u32[]{:S(2)}) collective-permute-start(f32[32,256]{1,0:T(8,128)S(1)} %add_add_fusion.2.refs_0_), channel_id=1, source_target_pairs={{0,1},{1,2},{2,3},{3,0},{4,5},{5,6},{6,7},{7,4},{8,9},{9,10},{10,1... | collective-permute-start | bytes 98312 | tf_op jit(solution)/shard_map/ppermute | solution.py:62
  118.5 2.8 %collective-permute-done.28.refs_2_ = f32[32,256]{1,0:T(8,128)S(1)} collective-permute-done((f32[32,256]{1,0:T(8,128)S(1)}, f32[32,256]{1,0:T(8,128)S(1)}, u32[]{:S(2)}, u32[]{:S(2)}) %collective-permute-start.28) | collective-permute-done | bytes 32800 | tf_op jit(solution)/shard_map/ppermute | solution.py:62
  121.7 3.7 %shard_map.81 = f32[64,256]{1,0:T(8,128)} custom-call(s32[96]{0:T(128)} %bitcast.41, s32[1]{0:T(128)} %bitcast.33.count_ref, f32[32,256]{1,0:T(8,128)S(1)} %add_add_fusion.2.refs_0_, f32[32,256]{1,0:T(8,128)S(1)} %collective-permute-done.27.refs_1_, f32[32,256]{1,0:T(8,128)S(1)} %collective-permute-done.28.refs_2_, ...), custom_call_target="tpu_custom_call" | custom-call | tf_op jit(solution)/shard_map/pallas_call | solution.py:403
  128.0 3.5 %collective-permute-start.32 = (f32[64,256]{1,0:T(8,128)S(1)}, f32[64,256]{1,0:T(8,128)S(1)}, u32[]{:S(2)}, u32[]{:S(2)}) collective-permute-start(f32[64,256]{1,0:T(8,128)S(1)} %add.88), channel_id=1, source_target_pairs={{0,32},{16,48},{32,0},{48,16},{64,96},{80,112},{96,64},{112,80},{1... | collective-permute-start | bytes 196616 | tf_op jit(solution)/shard_map/ppermute | solution.py:98
  137.4 4.1 %collective-permute-done.34.refs_5_ = f32[64,256]{1,0:T(8,128)S(1)} collective-permute-done((f32[64,256]{1,0:T(8,128)S(1)}, f32[64,256]{1,0:T(8,128)S(1)}, u32[]{:S(2)}, u32[]{:S(2)}) %collective-permute-start.34) | collective-permute-done | bytes 65568 | tf_op jit(solution)/shard_map/ppermute | solution.py:101
  141.5 8.1 %shard_map.82 = (bf16[4,72,512]{2,1,0:T(8,128)(2,1)}, bf16[4,72,512]{2,1,0:T(8,128)(2,1)}, bf16[4,72,512]{2,1,0:T(8,128)(2,1)}, bf16[4,72,512]{2,1,0:T(8,128)(2,...) custom-call(s32[96]{0:T(128)} %bitcast.42, s32[1]{0:T(128)} %bitcast.34.count_ref, ...), custom_call_target="tpu_custom_call" | custom-call | tf_op jit(solution)/shard_map/pallas_call | solution.py:403
  149.7 6.1 %collective-permute-start.35 = (bf16[4,72,512]{2,1,0:T(8,128)(2,1)}, bf16[4,72,512]{2,1,0:T(8,128)(2,1)S(1)}, u32[]{:S(2)}, u32[]{:S(2)}) collective-permute-start(bf16[4,72,512]{2,1,0:T(8,128)(2,1)} %get-tuple-element.26), channel_id=1, source_target_pairs={{0,12},{1,13},{2,14},{3,15},{4,0},{5,1},{6,2},{7,3},{8,4},{9,5},{1... | collective-permute-start | bytes 884744 | tf_op jit(solution)/shard_map/ppermute | solution.py:58
  158.1 5.4 %collective-permute-done.35.b_ref = bf16[4,72,512]{2,1,0:T(8,128)(2,1)S(1)} collective-permute-done((bf16[4,72,512]{2,1,0:T(8,128)(2,1)}, bf16[4,72,512]{2,1,0:T(8,128)(2,1)S(1)}, u32[]{:S(2)}, u32[]{:S(2)}) %collective-permute-start.35) | collective-permute-done | bytes 294944 | tf_op jit(solution)/shard_map/ppermute | solution.py:58
  163.5 6.3 %collective-permute-done.36.c_ref = bf16[4,72,512]{2,1,0:T(8,128)(2,1)S(1)} collective-permute-done((bf16[4,72,512]{2,1,0:T(8,128)(2,1)}, bf16[4,72,512]{2,1,0:T(8,128)(2,1)S(1)}, u32[]{:S(2)}, u32[]{:S(2)}) %collective-permute-start.36) | collective-permute-done | bytes 294944 | tf_op jit(solution)/shard_map/ppermute | solution.py:58
  172.3 3.2 %collective-permute-start.38 = (bf16[72,512]{1,0:T(8,128)(2,1)}, bf16[72,512]{1,0:T(8,128)(2,1)S(1)}, u32[]{:S(2)}, u32[]{:S(2)}) collective-permute-start(bf16[72,512]{1,0:T(8,128)(2,1)} %get-tuple-element.30), channel_id=1, source_target_pairs={{0,1},{1,0},{2,3},{3,2},{4,5},{5,4},{6,7},{7,6},{8,9},{9,8},{10,11... | collective-permute-start | bytes 221192 | tf_op jit(solution)/shard_map/ppermute | solution.py:66
  175.4 3.6 %collective-permute-start.39 = (bf16[72,512]{1,0:T(8,128)(2,1)}, bf16[72,512]{1,0:T(8,128)(2,1)S(1)}, u32[]{:S(2)}, u32[]{:S(2)}) collective-permute-start(bf16[72,512]{1,0:T(8,128)(2,1)} %get-tuple-element.31), channel_id=1, source_target_pairs={{0,3},{1,2},{2,1},{3,0},{4,7},{5,6},{6,5},{7,4},{8,11},{9,10},{10,... | collective-permute-start | bytes 221192 | tf_op jit(solution)/shard_map/ppermute | solution.py:74
  182.8 2.6 %collective-permute-start.43 = (bf16[2,64,1024]{2,1,0:T(8,128)(2,1)S(1)}, bf16[2,64,1024]{2,1,0:T(8,128)(2,1)S(1)}, u32[]{:S(2)}, u32[]{:S(2)}) collective-permute-start(bf16[2,64,1024]{2,1,0:T(8,128)(2,1)S(1)} %get-tuple-element.38), channel_id=1, source_target_pairs={{0,64},{16,80},{32,96},{48,112},{64,0},{80,16},{96,32},{112,48},{1... | collective-permute-start | bytes 786440 | tf_op jit(solution)/shard_map/ppermute | solution.py:78
  185.4 2.7 %collective-permute-done.40 = bf16[72,512]{1,0:T(8,128)(2,1)S(1)} collective-permute-done((bf16[72,512]{1,0:T(8,128)(2,1)}, bf16[72,512]{1,0:T(8,128)(2,1)S(1)}, u32[]{:S(2)}, u32[]{:S(2)}) %collective-permute-start.40) | collective-permute-done | bytes 73760 | tf_op jit(solution)/shard_map/ppermute | solution.py:70
  191.6 3.8 %collective-permute-done.43 = bf16[2,64,1024]{2,1,0:T(8,128)(2,1)S(1)} collective-permute-done((bf16[2,64,1024]{2,1,0:T(8,128)(2,1)S(1)}, bf16[2,64,1024]{2,1,0:T(8,128)(2,1)S(1)}, u32[]{:S(2)}, u32[]{:S(2)}) %collective-permute-start.43) | collective-permute-done | bytes 262176 | tf_op jit(solution)/shard_map/ppermute | solution.py:78
  196.6 5.1 %collective-permute-start.45 = (bf16[64,1024]{1,0:T(8,128)(2,1)S(1)}, bf16[64,1024]{1,0:T(8,128)(2,1)S(1)}, u32[]{:S(2)}, u32[]{:S(2)}) collective-permute-start(bf16[64,1024]{1,0:T(8,128)(2,1)S(1)} %fusion.4), channel_id=1, source_target_pairs={{0,128},{16,144},{32,160},{48,176},{64,192},{80,208},{96,224},{112... | collective-permute-start | bytes 393224 | tf_op jit(solution)/shard_map/ppermute | solution.py:86
  (115 shorter events, 66.9 us)
Async XLA Ops:
  3.5 7.0 %collective-permute-start = (bf16[1,72,512]{2,1,0:T(8,128)(2,1)}, bf16[1,72,512]{2,1,0:T(8,128)(2,1)S(1)}, u32[]{:S(2)}, u32[]{:S(2)}) collective-permute-start(bf16[1,72,512]{2,1,0:T(8,128)(2,1)} %get-tuple-element.19), channel_id=1, source_target_pairs={{0,1},{1,0},{2,3},{3,2},{4,5},{5,4},{6,7},{7,6},{8,9},{9,8},{10,11... | collective-permute-start | bytes 221192 | tf_op jit(solution)/shard_map/ppermute | solution.py:66
  6.8 10.3 %collective-permute-start.5 = (bf16[1,72,1024]{2,1,0:T(8,128)(2,1)}, bf16[1,72,1024]{2,1,0:T(8,128)(2,1)S(1)}, u32[]{:S(2)}, u32[]{:S(2)}) collective-permute-start(bf16[1,72,1024]{2,1,0:T(8,128)(2,1)} %get-tuple-element.20), channel_id=1, source_target_pairs={{0,128},{16,144},{32,160},{48,176},{64,192},{80,208},{96,224},{112... | collective-permute-start | bytes 442376 | tf_op jit(solution)/shard_map/ppermute | solution.py:86
  11.5 10.4 %collective-permute-start.1 = (bf16[2,72,512]{2,1,0:T(8,128)(2,1)S(1)}, bf16[2,72,512]{2,1,0:T(8,128)(2,1)S(1)}, u32[]{:S(2)}, u32[]{:S(2)}) collective-permute-start(bf16[2,72,512]{2,1,0:T(8,128)(2,1)S(1)} %pad_maximum_fusion), channel_id=1, source_target_pairs={{0,3},{1,2},{2,1},{3,0},{4,7},{5,6},{6,5},{7,4},{8,11},{9,10},{10,... | collective-permute-start | bytes 442376 | tf_op jit(solution)/shard_map/ppermute | solution.py:74
  17.2 16.0 %collective-permute-start.8 = (bf16[2,72,1024]{2,1,0:T(8,128)(2,1)S(1)}, bf16[2,72,1024]{2,1,0:T(8,128)(2,1)S(1)}, u32[]{:S(2)}, u32[]{:S(2)}) collective-permute-start(bf16[2,72,1024]{2,1,0:T(8,128)(2,1)S(1)} %constant_dynamic-update-slice_fusion.3.refs_4_.refs_13_), channel_id=1, source_target_pairs={{0,96},{16,112},{32,0},{48,16},{64,32},{80,48},{96,64},{112,80},{1... | collective-permute-start | bytes 884744 | tf_op jit(solution)/shard_map/ppermute | solution.py:78
  20.0 14.8 %collective-permute-start.7 = (bf16[2,72,1024]{2,1,0:T(8,128)(2,1)S(1)}, bf16[2,72,1024]{2,1,0:T(8,128)(2,1)S(1)}, u32[]{:S(2)}, u32[]{:S(2)}) collective-permute-start(bf16[2,72,1024]{2,1,0:T(8,128)(2,1)S(1)} %constant_dynamic-update-slice_fusion.3.refs_4_.refs_13_), channel_id=1, source_target_pairs={{0,64},{16,80},{32,96},{48,112},{64,0},{80,16},{96,32},{112,48},{1... | collective-permute-start | bytes 884744 | tf_op jit(solution)/shard_map/ppermute | solution.py:78
  20.8 16.1 %collective-permute-start.6 = (bf16[2,72,1024]{2,1,0:T(8,128)(2,1)S(1)}, bf16[2,72,1024]{2,1,0:T(8,128)(2,1)S(1)}, u32[]{:S(2)}, u32[]{:S(2)}) collective-permute-start(bf16[2,72,1024]{2,1,0:T(8,128)(2,1)S(1)} %constant_dynamic-update-slice_fusion.3.refs_4_.refs_13_), channel_id=1, source_target_pairs={{0,32},{16,48},{32,64},{48,80},{64,96},{80,112},{96,0},{112,16},{1... | collective-permute-start | bytes 884744 | tf_op jit(solution)/shard_map/ppermute | solution.py:78
  21.9 15.0 %collective-permute-start.4 = (bf16[4,72,512]{2,1,0:T(8,128)(2,1)S(1)}, bf16[4,72,512]{2,1,0:T(8,128)(2,1)S(1)}, u32[]{:S(2)}, u32[]{:S(2)}) collective-permute-start(bf16[4,72,512]{2,1,0:T(8,128)(2,1)S(1)} %constant_dynamic-update-slice_fusion.refs_0_.refs_9_), channel_id=1, source_target_pairs={{0,12},{1,13},{2,14},{3,15},{4,0},{5,1},{6,2},{7,3},{8,4},{9,5},{1... | collective-permute-start | bytes 884744 | tf_op jit(solution)/shard_map/ppermute | solution.py:58
  22.4 16.3 %collective-permute-start.3 = (bf16[4,72,512]{2,1,0:T(8,128)(2,1)S(1)}, bf16[4,72,512]{2,1,0:T(8,128)(2,1)S(1)}, u32[]{:S(2)}, u32[]{:S(2)}) collective-permute-start(bf16[4,72,512]{2,1,0:T(8,128)(2,1)S(1)} %constant_dynamic-update-slice_fusion.refs_0_.refs_9_), channel_id=1, source_target_pairs={{0,8},{1,9},{2,10},{3,11},{4,12},{5,13},{6,14},{7,15},{8,0},{9,1},... | collective-permute-start | bytes 884744 | tf_op jit(solution)/shard_map/ppermute | solution.py:58
  33.2 8.3 %collective-permute-start.2 = (bf16[4,72,512]{2,1,0:T(8,128)(2,1)S(1)}, bf16[4,72,512]{2,1,0:T(8,128)(2,1)S(1)}, u32[]{:S(2)}, u32[]{:S(2)}) collective-permute-start(bf16[4,72,512]{2,1,0:T(8,128)(2,1)S(1)} %constant_dynamic-update-slice_fusion.refs_0_.refs_9_), channel_id=1, source_target_pairs={{0,4},{1,5},{2,6},{3,7},{4,8},{5,9},{6,10},{7,11},{8,12},{9,13},{1... | collective-permute-start | bytes 884744 | tf_op jit(solution)/shard_map/ppermute | solution.py:58
  34.8 6.7 %collective-permute-start.12 = (bf16[2,72,1024]{2,1,0:T(8,128)(2,1)S(1)}, bf16[2,72,1024]{2,1,0:T(8,128)(2,1)S(1)}, u32[]{:S(2)}, u32[]{:S(2)}) collective-permute-start(bf16[2,72,1024]{2,1,0:T(8,128)(2,1)S(1)} %collective-permute-done.8.refs_7_.refs_16_), channel_id=1, source_target_pairs={{0,16},{16,0},{32,48},{48,32},{64,80},{80,64},{96,112},{112,96},{1... | collective-permute-start | bytes 884744 | tf_op jit(solution)/shard_map/ppermute | solution.py:82
  50.8 7.0 %collective-permute-start.15 = (f32[32,256]{1,0:T(8,128)}, f32[32,256]{1,0:T(8,128)S(1)}, u32[]{:S(2)}, u32[]{:S(2)}) collective-permute-start(f32[32,256]{1,0:T(8,128)} %get-tuple-element.21), channel_id=1, source_target_pairs={{0,12},{1,13},{2,14},{3,15},{4,0},{5,1},{6,2},{7,3},{8,4},{9,5},{1... | collective-permute-start | bytes 98312 | tf_op jit(solution)/shard_map/ppermute | solution.py:58
  53.4 6.2 %collective-permute-start.14 = (f32[32,256]{1,0:T(8,128)}, f32[32,256]{1,0:T(8,128)S(1)}, u32[]{:S(2)}, u32[]{:S(2)}) collective-permute-start(f32[32,256]{1,0:T(8,128)} %get-tuple-element.21), channel_id=1, source_target_pairs={{0,8},{1,9},{2,10},{3,11},{4,12},{5,13},{6,14},{7,15},{8,0},{9,1},... | collective-permute-start | bytes 98312 | tf_op jit(solution)/shard_map/ppermute | solution.py:58
  62.0 7.7 %collective-permute-start.18 = (f32[32,256]{1,0:T(8,128)S(1)}, f32[32,256]{1,0:T(8,128)S(1)}, u32[]{:S(2)}, u32[]{:S(2)}) collective-permute-start(f32[32,256]{1,0:T(8,128)S(1)} %add_add_fusion.3.refs_0_), channel_id=1, source_target_pairs={{0,3},{1,0},{2,1},{3,2},{4,7},{5,4},{6,5},{7,6},{8,11},{9,8},{10,9... | collective-permute-start | bytes 98312 | tf_op jit(solution)/shard_map/ppermute | solution.py:62
  66.2 7.8 %collective-permute-start.17 = (f32[32,256]{1,0:T(8,128)S(1)}, f32[32,256]{1,0:T(8,128)S(1)}, u32[]{:S(2)}, u32[]{:S(2)}) collective-permute-start(f32[32,256]{1,0:T(8,128)S(1)} %add_add_fusion.3.refs_0_), channel_id=1, source_target_pairs={{0,2},{1,3},{2,0},{3,1},{4,6},{5,7},{6,4},{7,5},{8,10},{9,11},{10,... | collective-permute-start | bytes 98312 | tf_op jit(solution)/shard_map/ppermute | solution.py:62
  66.9 7.1 %collective-permute-start.16 = (f32[32,256]{1,0:T(8,128)S(1)}, f32[32,256]{1,0:T(8,128)S(1)}, u32[]{:S(2)}, u32[]{:S(2)}) collective-permute-start(f32[32,256]{1,0:T(8,128)S(1)} %add_add_fusion.3.refs_0_), channel_id=1, source_target_pairs={{0,1},{1,2},{2,3},{3,0},{4,5},{5,6},{6,7},{7,4},{8,9},{9,10},{10,1... | collective-permute-start | bytes 98312 | tf_op jit(solution)/shard_map/ppermute | solution.py:62
  81.9 6.2 %collective-permute-start.21 = (f32[64,256]{1,0:T(8,128)S(1)}, f32[64,256]{1,0:T(8,128)S(1)}, u32[]{:S(2)}, u32[]{:S(2)}) collective-permute-start(f32[64,256]{1,0:T(8,128)S(1)} %add.81), channel_id=1, source_target_pairs={{0,32},{16,48},{32,0},{48,16},{64,96},{80,112},{96,64},{112,80},{1... | collective-permute-start | bytes 196616 | tf_op jit(solution)/shard_map/ppermute | solution.py:98
  99.7 7.5 %collective-permute-start.26 = (f32[32,256]{1,0:T(8,128)}, f32[32,256]{1,0:T(8,128)S(1)}, u32[]{:S(2)}, u32[]{:S(2)}) collective-permute-start(f32[32,256]{1,0:T(8,128)} %shard_map.80), channel_id=1, source_target_pairs={{0,12},{1,13},{2,14},{3,15},{4,0},{5,1},{6,2},{7,3},{8,4},{9,5},{1... | collective-permute-start | bytes 98312 | tf_op jit(solution)/shard_map/ppermute | solution.py:58
  111.6 6.9 %collective-permute-start.29 = (f32[32,256]{1,0:T(8,128)S(1)}, f32[32,256]{1,0:T(8,128)S(1)}, u32[]{:S(2)}, u32[]{:S(2)}) collective-permute-start(f32[32,256]{1,0:T(8,128)S(1)} %add_add_fusion.2.refs_0_), channel_id=1, source_target_pairs={{0,3},{1,0},{2,1},{3,2},{4,7},{5,4},{6,5},{7,6},{8,11},{9,8},{10,9... | collective-permute-start | bytes 98312 | tf_op jit(solution)/shard_map/ppermute | solution.py:62
  113.5 7.8 %collective-permute-start.28 = (f32[32,256]{1,0:T(8,128)S(1)}, f32[32,256]{1,0:T(8,128)S(1)}, u32[]{:S(2)}, u32[]{:S(2)}) collective-permute-start(f32[32,256]{1,0:T(8,128)S(1)} %add_add_fusion.2.refs_0_), channel_id=1, source_target_pairs={{0,2},{1,3},{2,0},{3,1},{4,6},{5,7},{6,4},{7,5},{8,10},{9,11},{10,... | collective-permute-start | bytes 98312 | tf_op jit(solution)/shard_map/ppermute | solution.py:62
  115.7 6.0 %collective-permute-start.27 = (f32[32,256]{1,0:T(8,128)S(1)}, f32[32,256]{1,0:T(8,128)S(1)}, u32[]{:S(2)}, u32[]{:S(2)}) collective-permute-start(f32[32,256]{1,0:T(8,128)S(1)} %add_add_fusion.2.refs_0_), channel_id=1, source_target_pairs={{0,1},{1,2},{2,3},{3,0},{4,5},{5,6},{6,7},{7,4},{8,9},{9,10},{10,1... | collective-permute-start | bytes 98312 | tf_op jit(solution)/shard_map/ppermute | solution.py:62
  128.0 6.4 %collective-permute-start.32 = (f32[64,256]{1,0:T(8,128)S(1)}, f32[64,256]{1,0:T(8,128)S(1)}, u32[]{:S(2)}, u32[]{:S(2)}) collective-permute-start(f32[64,256]{1,0:T(8,128)S(1)} %add.88), channel_id=1, source_target_pairs={{0,32},{16,48},{32,0},{48,16},{64,96},{80,112},{96,64},{112,80},{1... | collective-permute-start | bytes 196616 | tf_op jit(solution)/shard_map/ppermute | solution.py:98
  149.6 29.6 %collective-permute-start.41 = (bf16[8,64,1024]{2,1,0:T(8,128)(2,1)}, bf16[8,64,1024]{2,1,0:T(8,128)(2,1)S(1)}, u32[]{:S(2)}, u32[]{:S(2)}) collective-permute-start(bf16[8,64,1024]{2,1,0:T(8,128)(2,1)} %get-tuple-element.35), channel_id=1, source_target_pairs={{0,16},{16,0},{32,48},{48,32},{64,80},{80,64},{96,112},{112,96},{1... | collective-permute-start | bytes 3145736 | tf_op jit(solution)/shard_map/ppermute | solution.py:82
  149.7 13.8 %collective-permute-start.35 = (bf16[4,72,512]{2,1,0:T(8,128)(2,1)}, bf16[4,72,512]{2,1,0:T(8,128)(2,1)S(1)}, u32[]{:S(2)}, u32[]{:S(2)}) collective-permute-start(bf16[4,72,512]{2,1,0:T(8,128)(2,1)} %get-tuple-element.26), channel_id=1, source_target_pairs={{0,12},{1,13},{2,14},{3,15},{4,0},{5,1},{6,2},{7,3},{8,4},{9,5},{1... | collective-permute-start | bytes 884744 | tf_op jit(solution)/shard_map/ppermute | solution.py:58
  155.8 14.1 %collective-permute-start.36 = (bf16[4,72,512]{2,1,0:T(8,128)(2,1)}, bf16[4,72,512]{2,1,0:T(8,128)(2,1)S(1)}, u32[]{:S(2)}, u32[]{:S(2)}) collective-permute-start(bf16[4,72,512]{2,1,0:T(8,128)(2,1)} %get-tuple-element.27), channel_id=1, source_target_pairs={{0,8},{1,9},{2,10},{3,11},{4,12},{5,13},{6,14},{7,15},{8,0},{9,1},... | collective-permute-start | bytes 884744 | tf_op jit(solution)/shard_map/ppermute | solution.py:58
  156.0 14.5 %collective-permute-start.37 = (bf16[4,72,512]{2,1,0:T(8,128)(2,1)}, bf16[4,72,512]{2,1,0:T(8,128)(2,1)S(1)}, u32[]{:S(2)}, u32[]{:S(2)}) collective-permute-start(bf16[4,72,512]{2,1,0:T(8,128)(2,1)} %get-tuple-element.28), channel_id=1, source_target_pairs={{0,4},{1,5},{2,6},{3,7},{4,8},{5,9},{6,10},{7,11},{8,12},{9,13},{1... | collective-permute-start | bytes 884744 | tf_op jit(solution)/shard_map/ppermute | solution.py:58
  172.3 10.5 %collective-permute-start.38 = (bf16[72,512]{1,0:T(8,128)(2,1)}, bf16[72,512]{1,0:T(8,128)(2,1)S(1)}, u32[]{:S(2)}, u32[]{:S(2)}) collective-permute-start(bf16[72,512]{1,0:T(8,128)(2,1)} %get-tuple-element.30), channel_id=1, source_target_pairs={{0,1},{1,0},{2,3},{3,2},{4,5},{5,4},{6,7},{7,6},{8,9},{9,8},{10,11... | collective-permute-start | bytes 221192 | tf_op jit(solution)/shard_map/ppermute | solution.py:66
  175.4 10.0 %collective-permute-start.39 = (bf16[72,512]{1,0:T(8,128)(2,1)}, bf16[72,512]{1,0:T(8,128)(2,1)S(1)}, u32[]{:S(2)}, u32[]{:S(2)}) collective-permute-start(bf16[72,512]{1,0:T(8,128)(2,1)} %get-tuple-element.31), channel_id=1, source_target_pairs={{0,3},{1,2},{2,1},{3,0},{4,7},{5,6},{6,5},{7,4},{8,11},{9,10},{10,... | collective-permute-start | bytes 221192 | tf_op jit(solution)/shard_map/ppermute | solution.py:74
  179.1 9.1 %collective-permute-start.40 = (bf16[72,512]{1,0:T(8,128)(2,1)}, bf16[72,512]{1,0:T(8,128)(2,1)S(1)}, u32[]{:S(2)}, u32[]{:S(2)}) collective-permute-start(bf16[72,512]{1,0:T(8,128)(2,1)} %get-tuple-element.32), channel_id=1, source_target_pairs={{0,2},{1,3},{2,0},{3,1},{4,6},{5,7},{6,4},{7,5},{8,10},{9,11},{10,... | collective-permute-start | bytes 221192 | tf_op jit(solution)/shard_map/ppermute | solution.py:70
  180.7 9.3 %collective-permute-start.42 = (bf16[2,64,1024]{2,1,0:T(8,128)(2,1)S(1)}, bf16[2,64,1024]{2,1,0:T(8,128)(2,1)S(1)}, u32[]{:S(2)}, u32[]{:S(2)}) collective-permute-start(bf16[2,64,1024]{2,1,0:T(8,128)(2,1)S(1)} %get-tuple-element.36), channel_id=1, source_target_pairs={{0,96},{16,112},{32,0},{48,16},{64,32},{80,48},{96,64},{112,80},{1... | collective-permute-start | bytes 786440 | tf_op jit(solution)/shard_map/ppermute | solution.py:78
  181.4 10.2 %collective-permute-start.44 = (bf16[2,64,1024]{2,1,0:T(8,128)(2,1)S(1)}, bf16[2,64,1024]{2,1,0:T(8,128)(2,1)S(1)}, u32[]{:S(2)}, u32[]{:S(2)}) collective-permute-start(bf16[2,64,1024]{2,1,0:T(8,128)(2,1)S(1)} %get-tuple-element.37), channel_id=1, source_target_pairs={{0,32},{16,48},{32,64},{48,80},{64,96},{80,112},{96,0},{112,16},{1... | collective-permute-start | bytes 786440 | tf_op jit(solution)/shard_map/ppermute | solution.py:78
  182.8 12.6 %collective-permute-start.43 = (bf16[2,64,1024]{2,1,0:T(8,128)(2,1)S(1)}, bf16[2,64,1024]{2,1,0:T(8,128)(2,1)S(1)}, u32[]{:S(2)}, u32[]{:S(2)}) collective-permute-start(bf16[2,64,1024]{2,1,0:T(8,128)(2,1)S(1)} %get-tuple-element.38), channel_id=1, source_target_pairs={{0,64},{16,80},{32,96},{48,112},{64,0},{80,16},{96,32},{112,48},{1... | collective-permute-start | bytes 786440 | tf_op jit(solution)/shard_map/ppermute | solution.py:78
  196.6 8.0 %collective-permute-start.45 = (bf16[64,1024]{1,0:T(8,128)(2,1)S(1)}, bf16[64,1024]{1,0:T(8,128)(2,1)S(1)}, u32[]{:S(2)}, u32[]{:S(2)}) collective-permute-start(bf16[64,1024]{1,0:T(8,128)(2,1)S(1)} %fusion.4), channel_id=1, source_target_pairs={{0,128},{16,144},{32,160},{48,176},{64,192},{80,208},{96,224},{112... | collective-permute-start | bytes 393224 | tf_op jit(solution)/shard_map/ppermute | solution.py:86
  (27 other events, 312.6 us)

commit v4 on v3

--- a/solution.py
+++ b/solution.py
@@ -183,21 +183,15 @@
     ]
 
 
-def pack_kernel(x_ref, y_ref, x_mass_ref, y_mass_ref, x_out, y_out):
-    def rows(values):
-        sub = lax.broadcasted_iota(jnp.int32, (8, values[0].shape[1]), 0)
-        block = jnp.zeros(sub.shape, f32)
-        for i, value in enumerate(values):
-            block = jnp.where(sub == i, value, block)
-        return block.astype(bf16)
-
-    x_out[0, 0:F, :] = x_ref[...]
-    x_out[0, F:EXT, :] = rows([x_mass_ref[...].astype(f32)])
+def pack_kernel(y_ref, mass_ref, out_ref):
     y = y_ref[...].astype(f32)
     weight = jnp.exp(jnp.sum(y * y, axis=0, keepdims=True) * -0.0625)
     high = weight.astype(bf16).astype(f32)
-    y_out[0, 0:F, :] = y_ref[...]
-    y_out[0, F:EXT, :] = rows([y_mass_ref[...].astype(f32), high, weight - high])
+    sub = lax.broadcasted_iota(jnp.int32, (8, PB), 0)
+    block = jnp.where(sub == 0, mass_ref[...].astype(f32), 0.0)
+    block = jnp.where(sub == 1, high, jnp.where(sub == 2, weight - high, block))
+    out_ref[0, 0:F, :] = y_ref[...]
+    out_ref[0, F:EXT, :] = block.astype(bf16)
 
 
 def first_kernel(index_ref, count_ref, pos_ref, *refs):
@@ -423,16 +417,16 @@
     )
     x_own = spec_feat.T
     y_own = photo_feat[0].T
-    x0, y0 = call(
-        pack_kernel, [VMEM] * 4, [(VMEM, (1, EXT, SB), bf16), (VMEM, (1, EXT, PB), bf16)], [],
-        x_own, y_own, spec_mass.reshape(1, SB), photo_mass.reshape(1, PB),
-    )
-    x_flip = flip_z(x0)
+    x_pad = jnp.zeros((EXT - F - 1, SB), bf16)
+    x0 = jnp.concatenate([x_own, spec_mass.reshape(1, SB), x_pad])[None]
+    (y0,) = call(
+        pack_kernel, [VMEM] * 2, [(VMEM, (1, EXT, PB), bf16)], [],
+        y_own, photo_mass.reshape(1, PB),
+    )
+    x_parts = [move(x0) for move in (flip_z, mirror_z, across_z)]
     y_low = swap_low(y0)
-    x0 = jnp.concatenate([x0, x_flip])
-    x_mirror = mirror_z(x0)
+    x0 = jnp.concatenate([x0] + x_parts)
     y0 = jnp.concatenate([y0, y_low])
-    x0 = jnp.concatenate([x0, x_mirror])
     ys = [y0] + [shift_x(y0, k) for k in (1, 2, 3)]
     xs = [x0] + [shift_y(x0, k) for k in (1, 2, 3)]
     ys = ys + [swap_core(y) for y in ys]

time: 210 us -> 207 us (0.986)
  starting transfers between devices: 86.4 us -> 80 us
  waiting for transfers between devices: 71.6 us -> 77.1 us
  local copies, waits for them, and re-layouts: 4.78 us -> 2.22 us
    ppermute x1 -> x2, starting transfers between devices: 0.18 us -> 7.37 us  [across_z(): return lax.ppermute(a, 'photo', photo_perm(same, lambda i: i ^ 2))]
    ppermute x2, starting transfers between devices: 9.22 us -> 3.48 us  [mirror_z(): return lax.ppermute(a, 'photo', photo_perm(same, mirror))]
    ppermute x6, waiting for transfers between devices: 16.6 us -> 11.8 us  [shift_x(): return lax.ppermute(a, 'spec', spec_perm(same, shift(k), same))]
    ppermute x2, waiting for transfers between devices: 0.16 us -> 3.01 us  [mirror_z(): return lax.ppermute(a, 'photo', photo_perm(same, mirror))]
    ppermute x2, starting transfers between devices: 6.99 us -> 4.83 us  [swap_low(): return lax.ppermute(a, 'spec', spec_perm(flip, same, same))]
  transfers between devices with their start and end apart: 46 -> 47, of which waited for: 29 -> 31; matrix products, arithmetic and copies ran while one was open for 4% -> 3% of each run, Pallas kernels for 1% -> 2%
where the time goes in v4:
time: 207 us; the launch traced here: 203 us
  starting transfers between devices  80 us (39%)
  waiting for transfers between devices  77.1 us (37%)
  Pallas kernels  31.2 us (15%)
  other arithmetic  10.8 us (5%)
  local copies, waits for them, and re-layouts  2.22 us (1%)
    pallas_call x7, Pallas kernels, call(): pl.pallas_call(kernel, in_specs=in_specs, out_specs=[spec for spec, _, _...  31.2 us
    ppermute x12, starting transfers between devices, shift_y(): return lax.ppermute(a, 'photo', photo_perm(shift(k), same))  25.7 us
    ppermute x12, waiting for transfers between devices, shift_y(): return lax.ppermute(a, 'photo', photo_perm(shift(k), same))  25 us
    ppermute x6, starting transfers between devices, shift_z(): return lax.ppermute(a, 'photo', photo_perm(same, shift(k)))  13.6 us
    ppermute x6, waiting for transfers between devices, shift_x(): return lax.ppermute(a, 'spec', spec_perm(same, shift(k), same))  11.8 us
    ppermute x2, waiting for transfers between devices, sum_spec(): return [a, lax.ppermute(a, 'spec', spec_perm(same, mirror, same))]  9.41 us
    ppermute x6, waiting for transfers between devices, shift_z(): return lax.ppermute(a, 'photo', photo_perm(same, shift(k)))  9.25 us
    ppermute x6, waiting for transfers between devices, sum_spec(): lax.ppermute(a, 'spec', spec_perm(fl, fx, same))  8.52 us
  transfers between devices with their start and end apart: 47, of which 31 were waited for; matrix products, arithmetic and copies ran while one was open for 3% of the time, Pallas kernels for 2%

profile of v4, /device:TPU:8, one launch (start us, length us, event | category | flops | bytes accessed | tf_op | source)
XLA Modules:
  0.0 203.0 jit_solution(2022005225169225183)
XLA Ops:
  2.3 7.3 %collective-permute-start.2 = (bf16[1,72,512]{2,1,0:T(8,128)(2,1)S(1)}, bf16[1,72,512]{2,1,0:T(8,128)(2,1)S(1)}, u32[]{:S(2)}, u32[]{:S(2)}) collective-permute-start(bf16[1,72,512]{2,1,0:T(8,128)(2,1)S(1)} %maximum_bitcast_fusion), channel_id=1, source_target_pairs={{0,2},{1,3},{2,0},{3,1},{4,6},{5,7},{6,4},{7,5},{8,10},{9,11},{10,... | collective-permute-start | bytes 221192 | tf_op jit(solution)/shard_map/ppermute | solution.py:70
  13.7 3.0 %collective-permute-done.1 = bf16[1,72,512]{2,1,0:T(8,128)(2,1)S(1)} collective-permute-done((bf16[1,72,512]{2,1,0:T(8,128)(2,1)S(1)}, bf16[1,72,512]{2,1,0:T(8,128)(2,1)S(1)}, u32[]{:S(2)}, u32[]{:S(2)}) %collective-permute-start.1) | collective-permute-done | bytes 73760 | tf_op jit(solution)/shard_map/ppermute | solution.py:74
  17.6 2.6 %collective-permute-start.4 = (bf16[4,72,512]{2,1,0:T(8,128)(2,1)S(1)}, bf16[4,72,512]{2,1,0:T(8,128)(2,1)S(1)}, u32[]{:S(2)}, u32[]{:S(2)}) collective-permute-start(bf16[4,72,512]{2,1,0:T(8,128)(2,1)S(1)} %pad_maximum_fusion.refs_0_.refs_9_), channel_id=1, source_target_pairs={{0,8},{1,9},{2,10},{3,11},{4,12},{5,13},{6,14},{7,15},{8,0},{9,1},... | collective-permute-start | bytes 884744 | tf_op jit(solution)/shard_map/ppermute | solution.py:58
  21.5 2.8 %collective-permute-start.9 = (bf16[2,72,1024]{2,1,0:T(8,128)(2,1)S(1)}, bf16[2,72,1024]{2,1,0:T(8,128)(2,1)S(1)}, u32[]{:S(2)}, u32[]{:S(2)}) collective-permute-start(bf16[2,72,1024]{2,1,0:T(8,128)(2,1)S(1)} %pad_maximum_fusion.1.refs_4_.refs_13_), channel_id=1, source_target_pairs={{0,96},{16,112},{32,0},{48,16},{64,32},{80,48},{96,64},{112,80},{1... | collective-permute-start | bytes 884744 | tf_op jit(solution)/shard_map/ppermute | solution.py:78
  28.6 4.8 %collective-permute-done.4.refs_2_.refs_11_ = bf16[4,72,512]{2,1,0:T(8,128)(2,1)S(1)} collective-permute-done((bf16[4,72,512]{2,1,0:T(8,128)(2,1)S(1)}, bf16[4,72,512]{2,1,0:T(8,128)(2,1)S(1)}, u32[]{:S(2)}, u32[]{:S(2)}) %collective-permute-start.4) | collective-permute-done | bytes 294944 | tf_op jit(solution)/shard_map/ppermute | solution.py:58
  33.4 2.8 %collective-permute-done.9.refs_7_.refs_16_ = bf16[2,72,1024]{2,1,0:T(8,128)(2,1)S(1)} collective-permute-done((bf16[2,72,1024]{2,1,0:T(8,128)(2,1)S(1)}, bf16[2,72,1024]{2,1,0:T(8,128)(2,1)S(1)}, u32[]{:S(2)}, u32[]{:S(2)}) %collective-permute-start.9) | collective-permute-done | bytes 294944 | tf_op jit(solution)/shard_map/ppermute | solution.py:78
  36.7 3.2 %collective-permute-done.7.refs_5_.refs_14_ = bf16[2,72,1024]{2,1,0:T(8,128)(2,1)S(1)} collective-permute-done((bf16[2,72,1024]{2,1,0:T(8,128)(2,1)S(1)}, bf16[2,72,1024]{2,1,0:T(8,128)(2,1)S(1)}, u32[]{:S(2)}, u32[]{:S(2)}) %collective-permute-start.7) | collective-permute-done | bytes 294944 | tf_op jit(solution)/shard_map/ppermute | solution.py:78
  42.2 8.3 %shard_map.78 = (f32[32,256]{1,0:T(8,128)}, f32[32,256]{1,0:T(8,128)}, f32[64,256]{1,0:T(8,128)}, bf16[12,8,256,256]{3,2,1,0:T(8,128)(2,1)}) custom-call(s32[96]{0:T(128)} %bitcast.40, s32[1]{0:T(128)} %bitcast.32.count_ref, s32[2]{0:T(128)} %pad_add_fusion.pos_ref, bf16[4,72,512]{2,1,0:T(8,128)(2,1)} %copy-done, bf16[4,72,512]{2,1,0:T(8,128)(2,1)} %copy-done.7, ...), custom_call_target="tpu_custom_call" | custom-call | tf_op jit(solution)/shard_map/pallas_call | solution.py:397
  50.6 3.0 %collective-permute-start.16 = (f32[32,256]{1,0:T(8,128)}, f32[32,256]{1,0:T(8,128)S(1)}, u32[]{:S(2)}, u32[]{:S(2)}) collective-permute-start(f32[32,256]{1,0:T(8,128)} %get-tuple-element.17), channel_id=1, source_target_pairs={{0,12},{1,13},{2,14},{3,15},{4,0},{5,1},{6,2},{7,3},{8,4},{9,5},{1... | collective-permute-start | bytes 98312 | tf_op jit(solution)/shard_map/ppermute | solution.py:58
  53.5 3.7 %collective-permute-start.15 = (f32[32,256]{1,0:T(8,128)}, f32[32,256]{1,0:T(8,128)S(1)}, u32[]{:S(2)}, u32[]{:S(2)}) collective-permute-start(f32[32,256]{1,0:T(8,128)} %get-tuple-element.17), channel_id=1, source_target_pairs={{0,8},{1,9},{2,10},{3,11},{4,12},{5,13},{6,14},{7,15},{8,0},{9,1},... | collective-permute-start | bytes 98312 | tf_op jit(solution)/shard_map/ppermute | solution.py:58
  62.3 5.5 %collective-permute-start.19 = (f32[32,256]{1,0:T(8,128)S(1)}, f32[32,256]{1,0:T(8,128)S(1)}, u32[]{:S(2)}, u32[]{:S(2)}) collective-permute-start(f32[32,256]{1,0:T(8,128)S(1)} %add_add_fusion.3.refs_0_), channel_id=1, source_target_pairs={{0,3},{1,0},{2,1},{3,2},{4,7},{5,4},{6,5},{7,6},{8,11},{9,8},{10,9... | collective-permute-start | bytes 98312 | tf_op jit(solution)/shard_map/ppermute | solution.py:62
  70.2 5.6 %collective-permute-done.18.refs_2_ = f32[32,256]{1,0:T(8,128)S(1)} collective-permute-done((f32[32,256]{1,0:T(8,128)S(1)}, f32[32,256]{1,0:T(8,128)S(1)}, u32[]{:S(2)}, u32[]{:S(2)}) %collective-permute-start.18) | collective-permute-done | bytes 32800 | tf_op jit(solution)/shard_map/ppermute | solution.py:62
  75.8 3.7 %shard_map.79 = f32[64,256]{1,0:T(8,128)} custom-call(s32[96]{0:T(128)} %bitcast.41, s32[1]{0:T(128)} %bitcast.33.count_ref, f32[32,256]{1,0:T(8,128)S(1)} %add_add_fusion.3.refs_0_, f32[32,256]{1,0:T(8,128)S(1)} %collective-permute-done.17.refs_1_, f32[32,256]{1,0:T(8,128)S(1)} %collective-permute-done.18.refs_2_, ...), custom_call_target="tpu_custom_call" | custom-call | tf_op jit(solution)/shard_map/pallas_call | solution.py:397
  82.4 3.4 %collective-permute-start.22 = (f32[64,256]{1,0:T(8,128)S(1)}, f32[64,256]{1,0:T(8,128)S(1)}, u32[]{:S(2)}, u32[]{:S(2)}) collective-permute-start(f32[64,256]{1,0:T(8,128)S(1)} %add.81), channel_id=1, source_target_pairs={{0,32},{16,48},{32,0},{48,16},{64,96},{80,112},{96,64},{112,80},{1... | collective-permute-start | bytes 196616 | tf_op jit(solution)/shard_map/ppermute | solution.py:98
  90.9 4.7 %collective-permute-done.24.cb_ref = f32[64,256]{1,0:T(8,128)S(1)} collective-permute-done((f32[64,256]{1,0:T(8,128)S(1)}, f32[64,256]{1,0:T(8,128)S(1)}, u32[]{:S(2)}, u32[]{:S(2)}) %collective-permute-start.24) | collective-permute-done | bytes 65568 | tf_op jit(solution)/shard_map/ppermute | solution.py:101
  95.6 4.0 %shard_map.80 = f32[32,256]{1,0:T(8,128)} custom-call(s32[96]{0:T(128)} %bitcast.42, s32[1]{0:T(128)} %bitcast.34.count_ref, f32[64,256]{1,0:T(8,128)S(1)} %add_add_fusion.1.ca_ref, f32[64,256]{1,0:T(8,128)S(1)} %collective-permute-done.24.cb_ref, f32[64,256]{1,0:T(8,128)} %get-tuple-element.20.n_ref.refs_7_, ...), custom_call_target="tpu_custom_call" | custom-call | tf_op jit(solution)/shard_map/pallas_call | solution.py:397
  99.6 5.5 %collective-permute-start.27 = (f32[32,256]{1,0:T(8,128)}, f32[32,256]{1,0:T(8,128)S(1)}, u32[]{:S(2)}, u32[]{:S(2)}) collective-permute-start(f32[32,256]{1,0:T(8,128)} %shard_map.80), channel_id=1, source_target_pairs={{0,12},{1,13},{2,14},{3,15},{4,0},{5,1},{6,2},{7,3},{8,4},{9,5},{1... | collective-permute-start | bytes 98312 | tf_op jit(solution)/shard_map/ppermute | solution.py:58
  107.1 3.7 %collective-permute-done.26 = f32[32,256]{1,0:T(8,128)S(1)} collective-permute-done((f32[32,256]{1,0:T(8,128)}, f32[32,256]{1,0:T(8,128)S(1)}, u32[]{:S(2)}, u32[]{:S(2)}) %collective-permute-start.26) | collective-permute-done | bytes 32800 | tf_op jit(solution)/shard_map/ppermute | solution.py:58
  114.5 2.8 %collective-permute-start.28 = (f32[32,256]{1,0:T(8,128)S(1)}, f32[32,256]{1,0:T(8,128)S(1)}, u32[]{:S(2)}, u32[]{:S(2)}) collective-permute-start(f32[32,256]{1,0:T(8,128)S(1)} %add_add_fusion.2.refs_0_), channel_id=1, source_target_pairs={{0,1},{1,2},{2,3},{3,0},{4,5},{5,6},{6,7},{7,4},{8,9},{9,10},{10,1... | collective-permute-start | bytes 98312 | tf_op jit(solution)/shard_map/ppermute | solution.py:62
  117.3 3.6 %collective-permute-done.29.refs_2_ = f32[32,256]{1,0:T(8,128)S(1)} collective-permute-done((f32[32,256]{1,0:T(8,128)S(1)}, f32[32,256]{1,0:T(8,128)S(1)}, u32[]{:S(2)}, u32[]{:S(2)}) %collective-permute-start.29) | collective-permute-done | bytes 32800 | tf_op jit(solution)/shard_map/ppermute | solution.py:62
  120.9 3.7 %shard_map.81 = f32[64,256]{1,0:T(8,128)} custom-call(s32[96]{0:T(128)} %bitcast.43, s32[1]{0:T(128)} %bitcast.35.count_ref, f32[32,256]{1,0:T(8,128)S(1)} %add_add_fusion.2.refs_0_, f32[32,256]{1,0:T(8,128)S(1)} %collective-permute-done.28.refs_1_, f32[32,256]{1,0:T(8,128)S(1)} %collective-permute-done.29.refs_2_, ...), custom_call_target="tpu_custom_call" | custom-call | tf_op jit(solution)/shard_map/pallas_call | solution.py:397
  127.2 3.7 %collective-permute-start.33 = (f32[64,256]{1,0:T(8,128)S(1)}, f32[64,256]{1,0:T(8,128)S(1)}, u32[]{:S(2)}, u32[]{:S(2)}) collective-permute-start(f32[64,256]{1,0:T(8,128)S(1)} %add.88), channel_id=1, source_target_pairs={{0,32},{16,48},{32,0},{48,16},{64,96},{80,112},{96,64},{112,80},{1... | collective-permute-start | bytes 196616 | tf_op jit(solution)/shard_map/ppermute | solution.py:98
  136.3 4.7 %collective-permute-done.35.refs_5_ = f32[64,256]{1,0:T(8,128)S(1)} collective-permute-done((f32[64,256]{1,0:T(8,128)S(1)}, f32[64,256]{1,0:T(8,128)S(1)}, u32[]{:S(2)}, u32[]{:S(2)}) %collective-permute-start.35) | collective-permute-done | bytes 65568 | tf_op jit(solution)/shard_map/ppermute | solution.py:101
  141.0 8.1 %shard_map.82 = (bf16[4,72,512]{2,1,0:T(8,128)(2,1)}, bf16[4,72,512]{2,1,0:T(8,128)(2,1)}, bf16[4,72,512]{2,1,0:T(8,128)(2,1)}, bf16[4,72,512]{2,1,0:T(8,128)(2,...) custom-call(s32[96]{0:T(128)} %bitcast.44, s32[1]{0:T(128)} %bitcast.36.count_ref, ...), custom_call_target="tpu_custom_call" | custom-call | tf_op jit(solution)/shard_map/pallas_call | solution.py:397
  149.2 4.6 %collective-permute-start.36 = (bf16[4,72,512]{2,1,0:T(8,128)(2,1)}, bf16[4,72,512]{2,1,0:T(8,128)(2,1)S(1)}, u32[]{:S(2)}, u32[]{:S(2)}) collective-permute-start(bf16[4,72,512]{2,1,0:T(8,128)(2,1)} %get-tuple-element.22), channel_id=1, source_target_pairs={{0,12},{1,13},{2,14},{3,15},{4,0},{5,1},{6,2},{7,3},{8,4},{9,5},{1... | collective-permute-start | bytes 884744 | tf_op jit(solution)/shard_map/ppermute | solution.py:58
  156.2 5.4 %collective-permute-done.36.b_ref = bf16[4,72,512]{2,1,0:T(8,128)(2,1)S(1)} collective-permute-done((bf16[4,72,512]{2,1,0:T(8,128)(2,1)}, bf16[4,72,512]{2,1,0:T(8,128)(2,1)S(1)}, u32[]{:S(2)}, u32[]{:S(2)}) %collective-permute-start.36) | collective-permute-done | bytes 294944 | tf_op jit(solution)/shard_map/ppermute | solution.py:58
  161.6 5.8 %collective-permute-done.37.c_ref = bf16[4,72,512]{2,1,0:T(8,128)(2,1)S(1)} collective-permute-done((bf16[4,72,512]{2,1,0:T(8,128)(2,1)}, bf16[4,72,512]{2,1,0:T(8,128)(2,1)S(1)}, u32[]{:S(2)}, u32[]{:S(2)}) %collective-permute-start.37) | collective-permute-done | bytes 294944 | tf_op jit(solution)/shard_map/ppermute | solution.py:58
  169.8 5.3 %collective-permute-start.39 = (bf16[72,512]{1,0:T(8,128)(2,1)}, bf16[72,512]{1,0:T(8,128)(2,1)S(1)}, u32[]{:S(2)}, u32[]{:S(2)}) collective-permute-start(bf16[72,512]{1,0:T(8,128)(2,1)} %get-tuple-element.26), channel_id=1, source_target_pairs={{0,1},{1,0},{2,3},{3,2},{4,5},{5,4},{6,7},{7,6},{8,9},{9,8},{10,11... | collective-permute-start | bytes 221192 | tf_op jit(solution)/shard_map/ppermute | solution.py:66
  175.1 3.5 %collective-permute-start.40 = (bf16[72,512]{1,0:T(8,128)(2,1)}, bf16[72,512]{1,0:T(8,128)(2,1)S(1)}, u32[]{:S(2)}, u32[]{:S(2)}) collective-permute-start(bf16[72,512]{1,0:T(8,128)(2,1)} %get-tuple-element.27), channel_id=1, source_target_pairs={{0,3},{1,2},{2,1},{3,0},{4,7},{5,6},{6,5},{7,4},{8,11},{9,10},{10,... | collective-permute-start | bytes 221192 | tf_op jit(solution)/shard_map/ppermute | solution.py:74
  183.4 4.0 %collective-permute-done.41 = bf16[72,512]{1,0:T(8,128)(2,1)S(1)} collective-permute-done((bf16[72,512]{1,0:T(8,128)(2,1)}, bf16[72,512]{1,0:T(8,128)(2,1)S(1)}, u32[]{:S(2)}, u32[]{:S(2)}) %collective-permute-start.41) | collective-permute-done | bytes 73760 | tf_op jit(solution)/shard_map/ppermute | solution.py:70
  189.3 5.0 %collective-permute-done.45 = bf16[2,64,1024]{2,1,0:T(8,128)(2,1)S(1)} collective-permute-done((bf16[2,64,1024]{2,1,0:T(8,128)(2,1)S(1)}, bf16[2,64,1024]{2,1,0:T(8,128)(2,1)S(1)}, u32[]{:S(2)}, u32[]{:S(2)}) %collective-permute-start.45) | collective-permute-done | bytes 262176 | tf_op jit(solution)/shard_map/ppermute | solution.py:78
  195.5 3.8 %collective-permute-start.46 = (bf16[64,1024]{1,0:T(8,128)(2,1)S(1)}, bf16[64,1024]{1,0:T(8,128)(2,1)S(1)}, u32[]{:S(2)}, u32[]{:S(2)}) collective-permute-start(bf16[64,1024]{1,0:T(8,128)(2,1)S(1)} %fusion.4), channel_id=1, source_target_pairs={{0,128},{16,144},{32,160},{48,176},{64,192},{80,208},{96,224},{112... | collective-permute-start | bytes 393224 | tf_op jit(solution)/shard_map/ppermute | solution.py:86
  (116 shorter events, 59.8 us)
Async XLA Ops:
  2.3 11.4 %collective-permute-start.2 = (bf16[1,72,512]{2,1,0:T(8,128)(2,1)S(1)}, bf16[1,72,512]{2,1,0:T(8,128)(2,1)S(1)}, u32[]{:S(2)}, u32[]{:S(2)}) collective-permute-start(bf16[1,72,512]{2,1,0:T(8,128)(2,1)S(1)} %maximum_bitcast_fusion), channel_id=1, source_target_pairs={{0,2},{1,3},{2,0},{3,1},{4,6},{5,7},{6,4},{7,5},{8,10},{9,11},{10,... | collective-permute-start | bytes 221192 | tf_op jit(solution)/shard_map/ppermute | solution.py:70
  9.6 7.1 %collective-permute-start.1 = (bf16[1,72,512]{2,1,0:T(8,128)(2,1)S(1)}, bf16[1,72,512]{2,1,0:T(8,128)(2,1)S(1)}, u32[]{:S(2)}, u32[]{:S(2)}) collective-permute-start(bf16[1,72,512]{2,1,0:T(8,128)(2,1)S(1)} %maximum_bitcast_fusion), channel_id=1, source_target_pairs={{0,3},{1,2},{2,1},{3,0},{4,7},{5,6},{6,5},{7,4},{8,11},{9,10},{10,... | collective-permute-start | bytes 221192 | tf_op jit(solution)/shard_map/ppermute | solution.py:74
  9.6 7.4 %collective-permute-start = (bf16[1,72,512]{2,1,0:T(8,128)(2,1)S(1)}, bf16[1,72,512]{2,1,0:T(8,128)(2,1)S(1)}, u32[]{:S(2)}, u32[]{:S(2)}) collective-permute-start(bf16[1,72,512]{2,1,0:T(8,128)(2,1)S(1)} %maximum_bitcast_fusion), channel_id=1, source_target_pairs={{0,1},{1,0},{2,3},{3,2},{4,5},{5,4},{6,7},{7,6},{8,9},{9,8},{10,11... | collective-permute-start | bytes 221192 | tf_op jit(solution)/shard_map/ppermute | solution.py:66
  12.7 7.9 %collective-permute-start.6 = (bf16[1,72,1024]{2,1,0:T(8,128)(2,1)}, bf16[1,72,1024]{2,1,0:T(8,128)(2,1)S(1)}, u32[]{:S(2)}, u32[]{:S(2)}) collective-permute-start(bf16[1,72,1024]{2,1,0:T(8,128)(2,1)} %shard_map.77), channel_id=1, source_target_pairs={{0,128},{16,144},{32,160},{48,176},{64,192},{80,208},{96,224},{112... | collective-permute-start | bytes 442376 | tf_op jit(solution)/shard_map/ppermute | solution.py:86
  17.1 9.0 %collective-permute-start.5 = (bf16[4,72,512]{2,1,0:T(8,128)(2,1)S(1)}, bf16[4,72,512]{2,1,0:T(8,128)(2,1)S(1)}, u32[]{:S(2)}, u32[]{:S(2)}) collective-permute-start(bf16[4,72,512]{2,1,0:T(8,128)(2,1)S(1)} %pad_maximum_fusion.refs_0_.refs_9_), channel_id=1, source_target_pairs={{0,12},{1,13},{2,14},{3,15},{4,0},{5,1},{6,2},{7,3},{8,4},{9,5},{1... | collective-permute-start | bytes 884744 | tf_op jit(solution)/shard_map/ppermute | solution.py:58
  17.6 15.8 %collective-permute-start.4 = (bf16[4,72,512]{2,1,0:T(8,128)(2,1)S(1)}, bf16[4,72,512]{2,1,0:T(8,128)(2,1)S(1)}, u32[]{:S(2)}, u32[]{:S(2)}) collective-permute-start(bf16[4,72,512]{2,1,0:T(8,128)(2,1)S(1)} %pad_maximum_fusion.refs_0_.refs_9_), channel_id=1, source_target_pairs={{0,8},{1,9},{2,10},{3,11},{4,12},{5,13},{6,14},{7,15},{8,0},{9,1},... | collective-permute-start | bytes 884744 | tf_op jit(solution)/shard_map/ppermute | solution.py:58
  21.5 14.7 %collective-permute-start.9 = (bf16[2,72,1024]{2,1,0:T(8,128)(2,1)S(1)}, bf16[2,72,1024]{2,1,0:T(8,128)(2,1)S(1)}, u32[]{:S(2)}, u32[]{:S(2)}) collective-permute-start(bf16[2,72,1024]{2,1,0:T(8,128)(2,1)S(1)} %pad_maximum_fusion.1.refs_4_.refs_13_), channel_id=1, source_target_pairs={{0,96},{16,112},{32,0},{48,16},{64,32},{80,48},{96,64},{112,80},{1... | collective-permute-start | bytes 884744 | tf_op jit(solution)/shard_map/ppermute | solution.py:78
  24.3 11.8 %collective-permute-start.8 = (bf16[2,72,1024]{2,1,0:T(8,128)(2,1)S(1)}, bf16[2,72,1024]{2,1,0:T(8,128)(2,1)S(1)}, u32[]{:S(2)}, u32[]{:S(2)}) collective-permute-start(bf16[2,72,1024]{2,1,0:T(8,128)(2,1)S(1)} %pad_maximum_fusion.1.refs_4_.refs_13_), channel_id=1, source_target_pairs={{0,64},{16,80},{32,96},{48,112},{64,0},{80,16},{96,32},{112,48},{1... | collective-permute-start | bytes 884744 | tf_op jit(solution)/shard_map/ppermute | solution.py:78
  25.1 14.7 %collective-permute-start.7 = (bf16[2,72,1024]{2,1,0:T(8,128)(2,1)S(1)}, bf16[2,72,1024]{2,1,0:T(8,128)(2,1)S(1)}, u32[]{:S(2)}, u32[]{:S(2)}) collective-permute-start(bf16[2,72,1024]{2,1,0:T(8,128)(2,1)S(1)} %pad_maximum_fusion.1.refs_4_.refs_13_), channel_id=1, source_target_pairs={{0,32},{16,48},{32,64},{48,80},{64,96},{80,112},{96,0},{112,16},{1... | collective-permute-start | bytes 884744 | tf_op jit(solution)/shard_map/ppermute | solution.py:78
  26.0 15.2 %collective-permute-start.3 = (bf16[4,72,512]{2,1,0:T(8,128)(2,1)S(1)}, bf16[4,72,512]{2,1,0:T(8,128)(2,1)S(1)}, u32[]{:S(2)}, u32[]{:S(2)}) collective-permute-start(bf16[4,72,512]{2,1,0:T(8,128)(2,1)S(1)} %pad_maximum_fusion.refs_0_.refs_9_), channel_id=1, source_target_pairs={{0,4},{1,5},{2,6},{3,7},{4,8},{5,9},{6,10},{7,11},{8,12},{9,13},{1... | collective-permute-start | bytes 884744 | tf_op jit(solution)/shard_map/ppermute | solution.py:58
  33.4 7.9 %collective-permute-start.10 = (bf16[2,72,1024]{2,1,0:T(8,128)(2,1)S(1)}, bf16[2,72,1024]{2,1,0:T(8,128)(2,1)S(1)}, u32[]{:S(2)}, u32[]{:S(2)}) collective-permute-start(bf16[2,72,1024]{2,1,0:T(8,128)(2,1)S(1)} %pad_maximum_fusion.1.refs_4_.refs_13_), channel_id=1, source_target_pairs={{0,16},{16,0},{32,48},{48,32},{64,80},{80,64},{96,112},{112,96},{1... | collective-permute-start | bytes 884744 | tf_op jit(solution)/shard_map/ppermute | solution.py:82
  50.6 7.3 %collective-permute-start.16 = (f32[32,256]{1,0:T(8,128)}, f32[32,256]{1,0:T(8,128)S(1)}, u32[]{:S(2)}, u32[]{:S(2)}) collective-permute-start(f32[32,256]{1,0:T(8,128)} %get-tuple-element.17), channel_id=1, source_target_pairs={{0,12},{1,13},{2,14},{3,15},{4,0},{5,1},{6,2},{7,3},{8,4},{9,5},{1... | collective-permute-start | bytes 98312 | tf_op jit(solution)/shard_map/ppermute | solution.py:58
  53.5 6.5 %collective-permute-start.15 = (f32[32,256]{1,0:T(8,128)}, f32[32,256]{1,0:T(8,128)S(1)}, u32[]{:S(2)}, u32[]{:S(2)}) collective-permute-start(f32[32,256]{1,0:T(8,128)} %get-tuple-element.17), channel_id=1, source_target_pairs={{0,8},{1,9},{2,10},{3,11},{4,12},{5,13},{6,14},{7,15},{8,0},{9,1},... | collective-permute-start | bytes 98312 | tf_op jit(solution)/shard_map/ppermute | solution.py:58
  62.3 7.9 %collective-permute-start.19 = (f32[32,256]{1,0:T(8,128)S(1)}, f32[32,256]{1,0:T(8,128)S(1)}, u32[]{:S(2)}, u32[]{:S(2)}) collective-permute-start(f32[32,256]{1,0:T(8,128)S(1)} %add_add_fusion.3.refs_0_), channel_id=1, source_target_pairs={{0,3},{1,0},{2,1},{3,2},{4,7},{5,4},{6,5},{7,6},{8,11},{9,8},{10,9... | collective-permute-start | bytes 98312 | tf_op jit(solution)/shard_map/ppermute | solution.py:62
  67.8 8.1 %collective-permute-start.18 = (f32[32,256]{1,0:T(8,128)S(1)}, f32[32,256]{1,0:T(8,128)S(1)}, u32[]{:S(2)}, u32[]{:S(2)}) collective-permute-start(f32[32,256]{1,0:T(8,128)S(1)} %add_add_fusion.3.refs_0_), channel_id=1, source_target_pairs={{0,2},{1,3},{2,0},{3,1},{4,6},{5,7},{6,4},{7,5},{8,10},{9,11},{10,... | collective-permute-start | bytes 98312 | tf_op jit(solution)/shard_map/ppermute | solution.py:62
  67.8 8.1 %collective-permute-start.17 = (f32[32,256]{1,0:T(8,128)S(1)}, f32[32,256]{1,0:T(8,128)S(1)}, u32[]{:S(2)}, u32[]{:S(2)}) collective-permute-start(f32[32,256]{1,0:T(8,128)S(1)} %add_add_fusion.3.refs_0_), channel_id=1, source_target_pairs={{0,1},{1,2},{2,3},{3,0},{4,5},{5,6},{6,7},{7,4},{8,9},{9,10},{10,1... | collective-permute-start | bytes 98312 | tf_op jit(solution)/shard_map/ppermute | solution.py:62
  82.4 6.2 %collective-permute-start.22 = (f32[64,256]{1,0:T(8,128)S(1)}, f32[64,256]{1,0:T(8,128)S(1)}, u32[]{:S(2)}, u32[]{:S(2)}) collective-permute-start(f32[64,256]{1,0:T(8,128)S(1)} %add.81), channel_id=1, source_target_pairs={{0,32},{16,48},{32,0},{48,16},{64,96},{80,112},{96,64},{112,80},{1... | collective-permute-start | bytes 196616 | tf_op jit(solution)/shard_map/ppermute | solution.py:98
  99.6 7.5 %collective-permute-start.27 = (f32[32,256]{1,0:T(8,128)}, f32[32,256]{1,0:T(8,128)S(1)}, u32[]{:S(2)}, u32[]{:S(2)}) collective-permute-start(f32[32,256]{1,0:T(8,128)} %shard_map.80), channel_id=1, source_target_pairs={{0,12},{1,13},{2,14},{3,15},{4,0},{5,1},{6,2},{7,3},{8,4},{9,5},{1... | collective-permute-start | bytes 98312 | tf_op jit(solution)/shard_map/ppermute | solution.py:58
  113.1 7.8 %collective-permute-start.29 = (f32[32,256]{1,0:T(8,128)S(1)}, f32[32,256]{1,0:T(8,128)S(1)}, u32[]{:S(2)}, u32[]{:S(2)}) collective-permute-start(f32[32,256]{1,0:T(8,128)S(1)} %add_add_fusion.2.refs_0_), channel_id=1, source_target_pairs={{0,2},{1,3},{2,0},{3,1},{4,6},{5,7},{6,4},{7,5},{8,10},{9,11},{10,... | collective-permute-start | bytes 98312 | tf_op jit(solution)/shard_map/ppermute | solution.py:62
  114.5 6.5 %collective-permute-start.28 = (f32[32,256]{1,0:T(8,128)S(1)}, f32[32,256]{1,0:T(8,128)S(1)}, u32[]{:S(2)}, u32[]{:S(2)}) collective-permute-start(f32[32,256]{1,0:T(8,128)S(1)} %add_add_fusion.2.refs_0_), channel_id=1, source_target_pairs={{0,1},{1,2},{2,3},{3,0},{4,5},{5,6},{6,7},{7,4},{8,9},{9,10},{10,1... | collective-permute-start | bytes 98312 | tf_op jit(solution)/shard_map/ppermute | solution.py:62
  127.2 6.6 %collective-permute-start.33 = (f32[64,256]{1,0:T(8,128)S(1)}, f32[64,256]{1,0:T(8,128)S(1)}, u32[]{:S(2)}, u32[]{:S(2)}) collective-permute-start(f32[64,256]{1,0:T(8,128)S(1)} %add.88), channel_id=1, source_target_pairs={{0,32},{16,48},{32,0},{48,16},{64,96},{80,112},{96,64},{112,80},{1... | collective-permute-start | bytes 196616 | tf_op jit(solution)/shard_map/ppermute | solution.py:98
  149.1 29.5 %collective-permute-start.42 = (bf16[8,64,1024]{2,1,0:T(8,128)(2,1)}, bf16[8,64,1024]{2,1,0:T(8,128)(2,1)S(1)}, u32[]{:S(2)}, u32[]{:S(2)}) collective-permute-start(bf16[8,64,1024]{2,1,0:T(8,128)(2,1)} %get-tuple-element.31), channel_id=1, source_target_pairs={{0,16},{16,0},{32,48},{48,32},{64,80},{80,64},{96,112},{112,96},{1... | collective-permute-start | bytes 3145736 | tf_op jit(solution)/shard_map/ppermute | solution.py:82
  149.2 12.4 %collective-permute-start.36 = (bf16[4,72,512]{2,1,0:T(8,128)(2,1)}, bf16[4,72,512]{2,1,0:T(8,128)(2,1)S(1)}, u32[]{:S(2)}, u32[]{:S(2)}) collective-permute-start(bf16[4,72,512]{2,1,0:T(8,128)(2,1)} %get-tuple-element.22), channel_id=1, source_target_pairs={{0,12},{1,13},{2,14},{3,15},{4,0},{5,1},{6,2},{7,3},{8,4},{9,5},{1... | collective-permute-start | bytes 884744 | tf_op jit(solution)/shard_map/ppermute | solution.py:58
  153.9 13.5 %collective-permute-start.37 = (bf16[4,72,512]{2,1,0:T(8,128)(2,1)}, bf16[4,72,512]{2,1,0:T(8,128)(2,1)S(1)}, u32[]{:S(2)}, u32[]{:S(2)}) collective-permute-start(bf16[4,72,512]{2,1,0:T(8,128)(2,1)} %get-tuple-element.23), channel_id=1, source_target_pairs={{0,8},{1,9},{2,10},{3,11},{4,12},{5,13},{6,14},{7,15},{8,0},{9,1},... | collective-permute-start | bytes 884744 | tf_op jit(solution)/shard_map/ppermute | solution.py:58
  153.9 14.2 %collective-permute-start.38 = (bf16[4,72,512]{2,1,0:T(8,128)(2,1)}, bf16[4,72,512]{2,1,0:T(8,128)(2,1)S(1)}, u32[]{:S(2)}, u32[]{:S(2)}) collective-permute-start(bf16[4,72,512]{2,1,0:T(8,128)(2,1)} %get-tuple-element.24), channel_id=1, source_target_pairs={{0,4},{1,5},{2,6},{3,7},{4,8},{5,9},{6,10},{7,11},{8,12},{9,13},{1... | collective-permute-start | bytes 884744 | tf_op jit(solution)/shard_map/ppermute | solution.py:58
  169.8 12.4 %collective-permute-start.39 = (bf16[72,512]{1,0:T(8,128)(2,1)}, bf16[72,512]{1,0:T(8,128)(2,1)S(1)}, u32[]{:S(2)}, u32[]{:S(2)}) collective-permute-start(bf16[72,512]{1,0:T(8,128)(2,1)} %get-tuple-element.26), channel_id=1, source_target_pairs={{0,1},{1,0},{2,3},{3,2},{4,5},{5,4},{6,7},{7,6},{8,9},{9,8},{10,11... | collective-permute-start | bytes 221192 | tf_op jit(solution)/shard_map/ppermute | solution.py:66
  175.1 8.4 %collective-permute-start.40 = (bf16[72,512]{1,0:T(8,128)(2,1)}, bf16[72,512]{1,0:T(8,128)(2,1)S(1)}, u32[]{:S(2)}, u32[]{:S(2)}) collective-permute-start(bf16[72,512]{1,0:T(8,128)(2,1)} %get-tuple-element.27), channel_id=1, source_target_pairs={{0,3},{1,2},{2,1},{3,0},{4,7},{5,6},{6,5},{7,4},{8,11},{9,10},{10,... | collective-permute-start | bytes 221192 | tf_op jit(solution)/shard_map/ppermute | solution.py:74
  178.5 8.9 %collective-permute-start.41 = (bf16[72,512]{1,0:T(8,128)(2,1)}, bf16[72,512]{1,0:T(8,128)(2,1)S(1)}, u32[]{:S(2)}, u32[]{:S(2)}) collective-permute-start(bf16[72,512]{1,0:T(8,128)(2,1)} %get-tuple-element.28), channel_id=1, source_target_pairs={{0,2},{1,3},{2,0},{3,1},{4,6},{5,7},{6,4},{7,5},{8,10},{9,11},{10,... | collective-permute-start | bytes 221192 | tf_op jit(solution)/shard_map/ppermute | solution.py:70
  180.1 9.3 %collective-permute-start.43 = (bf16[2,64,1024]{2,1,0:T(8,128)(2,1)S(1)}, bf16[2,64,1024]{2,1,0:T(8,128)(2,1)S(1)}, u32[]{:S(2)}, u32[]{:S(2)}) collective-permute-start(bf16[2,64,1024]{2,1,0:T(8,128)(2,1)S(1)} %get-tuple-element.32), channel_id=1, source_target_pairs={{0,96},{16,112},{32,0},{48,16},{64,32},{80,48},{96,64},{112,80},{1... | collective-permute-start | bytes 786440 | tf_op jit(solution)/shard_map/ppermute | solution.py:78
  180.1 14.1 %collective-permute-start.45 = (bf16[2,64,1024]{2,1,0:T(8,128)(2,1)S(1)}, bf16[2,64,1024]{2,1,0:T(8,128)(2,1)S(1)}, u32[]{:S(2)}, u32[]{:S(2)}) collective-permute-start(bf16[2,64,1024]{2,1,0:T(8,128)(2,1)S(1)} %get-tuple-element.33), channel_id=1, source_target_pairs={{0,32},{16,48},{32,64},{48,80},{64,96},{80,112},{96,0},{112,16},{1... | collective-permute-start | bytes 786440 | tf_op jit(solution)/shard_map/ppermute | solution.py:78
  182.2 12.1 %collective-permute-start.44 = (bf16[2,64,1024]{2,1,0:T(8,128)(2,1)S(1)}, bf16[2,64,1024]{2,1,0:T(8,128)(2,1)S(1)}, u32[]{:S(2)}, u32[]{:S(2)}) collective-permute-start(bf16[2,64,1024]{2,1,0:T(8,128)(2,1)S(1)} %get-tuple-element.34), channel_id=1, source_target_pairs={{0,64},{16,80},{32,96},{48,112},{64,0},{80,16},{96,32},{112,48},{1... | collective-permute-start | bytes 786440 | tf_op jit(solution)/shard_map/ppermute | solution.py:78
  195.5 6.8 %collective-permute-start.46 = (bf16[64,1024]{1,0:T(8,128)(2,1)S(1)}, bf16[64,1024]{1,0:T(8,128)(2,1)S(1)}, u32[]{:S(2)}, u32[]{:S(2)}) collective-permute-start(bf16[64,1024]{1,0:T(8,128)(2,1)S(1)} %fusion.4), channel_id=1, source_target_pairs={{0,128},{16,144},{32,160},{48,176},{64,192},{80,208},{96,224},{112... | collective-permute-start | bytes 393224 | tf_op jit(solution)/shard_map/ppermute | solution.py:86
  (28 other events, 303.3 us)

commit v5 on v4

--- a/solution.py
+++ b/solution.py
@@ -391,6 +391,11 @@
 SMEM = pl.BlockSpec(memory_space=pltpu.SMEM)
 VMEM = pl.BlockSpec(memory_space=pltpu.VMEM)
 ANY = pl.BlockSpec(memory_space=pl.ANY)
+KEPT = pl.BlockSpec(memory_space=pltpu.VMEM)
+
+
+def kept(shape, dtype):
+    return pltpu.VMEM(shape, dtype)
 
 
 def call(kernel, in_specs, outs, scratch, *args):
@@ -398,7 +403,7 @@
         kernel,
         in_specs=in_specs,
         out_specs=[spec for spec, _, _ in outs],
-        out_shape=[jax.ShapeDtypeStruct(s, d) for _, s, d in outs],
+        out_shape=[kept(s, d) if spec is KEPT else jax.ShapeDtypeStruct(s, d) for spec, s, d in outs],
         scratch_shapes=scratch,
     )(*args)
 
@@ -423,10 +428,12 @@
         pack_kernel, [VMEM] * 2, [(VMEM, (1, EXT, PB), bf16)], [],
         y_own, photo_mass.reshape(1, PB),
     )
-    x_parts = [move(x0) for move in (flip_z, mirror_z, across_z)]
+    x_flip = flip_z(x0)
     y_low = swap_low(y0)
-    x0 = jnp.concatenate([x0] + x_parts)
+    x0 = jnp.concatenate([x0, x_flip])
+    x_mirror = mirror_z(x0)
     y0 = jnp.concatenate([y0, y_low])
+    x0 = jnp.concatenate([x0, x_mirror])
     ys = [y0] + [shift_x(y0, k) for k in (1, 2, 3)]
     xs = [x0] + [shift_y(x0, k) for k in (1, 2, 3)]
     ys = ys + [swap_core(y) for y in ys]
@@ -440,24 +447,25 @@
     r, m, n, g = call(
         first_kernel, [SMEM] * 3 + [ANY] * 12,
         [
-            (VMEM, (TR, TILE), f32), (VMEM, (TR, TILE), f32), (VMEM, (TC, TILE), f32),
+            (KEPT, (TR, TILE), f32), (KEPT, (TR, TILE), f32), (KEPT, (TC, TILE), f32),
             (ANY, (TURNS, GROUP, TILE, TILE), bf16),
         ],
         blocks + [pltpu.VMEM((TR, TILE, F), bf16)] + row_acc + [tiles, piece_sems, tile_sems],
         *meta, *xs, *ys,
     )
+    m, n = in_vmem([m, n])
     lists = meta[0:2]
 
     def columns(rs):
         return call(
-            column_kernel, [SMEM] * 2 + [VMEM] * 5 + [ANY], [(VMEM, (TC, TILE), f32)],
+            column_kernel, [SMEM] * 2 + [VMEM] * 5 + [ANY], [(KEPT, (TC, TILE), f32)],
             column_acc + [tiles, tile_sems], *lists, *rs, m, g,
         )[0]
 
     rs = in_vmem(sum_photo(r))
     cs = in_vmem(sum_spec(columns(rs)))
     (r,) = call(
-        row_kernel, [SMEM] * 2 + [VMEM] * 3 + [ANY], [(VMEM, (TR, TILE), f32)],
+        row_kernel, [SMEM] * 2 + [VMEM] * 3 + [ANY], [(KEPT, (TR, TILE), f32)],
         row_acc + [tiles, tile_sems], *lists, *cs, n, g,
     )
     rs = in_vmem(sum_photo(r))
@@ -494,8 +502,6 @@
         spec_parts[0], *in_vmem(y_parts),
     )
     z_parts = [move(part) for move, part in zip((flip_z, mirror_z, across_z), z_parts)]
-    for part in z_parts:
-        spec_sum = spec_sum + part.astype(f32)
     photo_sum = photo_sums[0]
     for part in x_parts:
         photo_sum = photo_sum + part.astype(f32)
@@ -503,9 +509,11 @@
     lowered = swap_low(photo_send)
     photo_sum = photo_sum[0] + lowered.astype(f32)
     grad_photo = (2.0 * (share * y_own.astype(f32) - photo_sum)).T[None]
+    for part in z_parts:
+        spec_sum = spec_sum + part.astype(f32)
     row_marginal = spec_sum[F : F + 1] + spec_sum[F + 1 : F + 2]
-    grad_spec = 2.0 * (row_marginal * x_own.astype(f32) - spec_sum[0:F])
-    return (grad_spec.T, grad_photo)
+    grad_spec = (2.0 * (row_marginal * x_own.astype(f32) - spec_sum[0:F])).T
+    return (grad_spec, grad_photo)
 
 
 def solution(mesh):

time: 207 us -> 202 us (0.976)
  starting transfers between devices: 80 us -> 90.3 us
  waiting for transfers between devices: 77.1 us -> 68.2 us
  other arithmetic: 10.8 us -> 7.52 us
  Pallas kernels: 31.2 us -> 28.1 us
    ppermute x2 -> x1, starting transfers between devices: 7.37 us -> 0.58 us  [across_z(): return lax.ppermute(a, 'photo', photo_perm(same, lambda i: i ^ 2))]
    ppermute x2, starting transfers between devices: 3.48 us -> 10 us  [mirror_z(): return lax.ppermute(a, 'photo', photo_perm(same, mirror))]
    ppermute x6, starting transfers between devices: 13.6 us -> 19.8 us  [shift_z(): return lax.ppermute(a, 'photo', photo_perm(same, shift(k)))]
    ppermute x2, starting transfers between devices: 1.94 us -> 5.85 us  [sum_spec(): return [a, lax.ppermute(a, 'spec', spec_perm(same, mirror, same))]]
    ppermute x2, waiting for transfers between devices: 9.41 us -> 5.59 us  [sum_spec(): return [a, lax.ppermute(a, 'spec', spec_perm(same, mirror, same))]]
    ppermute x6, waiting for transfers between devices: 11.8 us -> 15 us  [shift_x(): return lax.ppermute(a, 'spec', spec_perm(same, shift(k), same))]
    pallas_call x7, Pallas kernels: 31.2 us -> 28.1 us  [call(): pl.pallas_call(kernel, in_specs=in_specs, out_specs=[spec for spec, _, _...]
    ppermute x6, waiting for transfers between devices: 9.25 us -> 6.43 us  [shift_z(): return lax.ppermute(a, 'photo', photo_perm(same, shift(k)))]
  transfers between devices with their start and end apart: 47 -> 46, of which waited for: 31 -> 31; matrix products, arithmetic and copies ran while one was open for 3% -> 3% of each run, Pallas kernels for 2% -> 2%
where the time goes in v5:
time: 202 us; the launch traced here: 198 us
  starting transfers between devices  90.3 us (45%)
  waiting for transfers between devices  68.2 us (34%)
  Pallas kernels  28.1 us (14%)
  other arithmetic  7.52 us (4%)
  local copies, waits for them, and re-layouts  2.4 us (1%)
    pallas_call x7, Pallas kernels, call(): pl.pallas_call(kernel, in_specs=in_specs, out_specs=[spec for spec, _, _...  28.1 us
    ppermute x12, starting transfers between devices, shift_y(): return lax.ppermute(a, 'photo', photo_perm(shift(k), same))  25.6 us
    ppermute x12, waiting for transfers between devices, shift_y(): return lax.ppermute(a, 'photo', photo_perm(shift(k), same))  24 us
    ppermute x6, starting transfers between devices, shift_z(): return lax.ppermute(a, 'photo', photo_perm(same, shift(k)))  19.8 us
    ppermute x6, waiting for transfers between devices, shift_x(): return lax.ppermute(a, 'spec', spec_perm(same, shift(k), same))  15 us
    ppermute x2, starting transfers between devices, mirror_z(): return lax.ppermute(a, 'photo', photo_perm(same, mirror))  10 us
    ppermute x6, starting transfers between devices, shift_x(): return lax.ppermute(a, 'spec', spec_perm(same, shift(k), same))  8.41 us
    ppermute x6, waiting for transfers between devices, sum_spec(): lax.ppermute(a, 'spec', spec_perm(fl, fx, same))  7.48 us
  transfers between devices with their start and end apart: 46, of which 31 were waited for; matrix products, arithmetic and copies ran while one was open for 3% of the time, Pallas kernels for 2%

profile of v5, /device:TPU:8, one launch (start us, length us, event | category | flops | bytes accessed | tf_op | source)
XLA Modules:
  0.0 198.2 jit_solution(8596870876782690827)
XLA Ops:
  2.3 3.4 %collective-permute-start = (bf16[1,72,512]{2,1,0:T(8,128)(2,1)S(1)}, bf16[1,72,512]{2,1,0:T(8,128)(2,1)S(1)}, u32[]{:S(2)}, u32[]{:S(2)}) collective-permute-start(bf16[1,72,512]{2,1,0:T(8,128)(2,1)S(1)} %maximum_bitcast_fusion), channel_id=1, source_target_pairs={{0,1},{1,0},{2,3},{3,2},{4,5},{5,4},{6,7},{7,6},{8,9},{9,8},{10,11... | collective-permute-start | bytes 221192 | tf_op jit(solution)/shard_map/ppermute | solution.py:66
  9.6 4.5 %collective-permute-start.1 = (bf16[2,72,512]{2,1,0:T(8,128)(2,1)S(1)}, bf16[2,72,512]{2,1,0:T(8,128)(2,1)S(1)}, u32[]{:S(2)}, u32[]{:S(2)}) collective-permute-start(bf16[2,72,512]{2,1,0:T(8,128)(2,1)S(1)} %pad_maximum_fusion.2), channel_id=1, source_target_pairs={{0,3},{1,2},{2,1},{3,0},{4,7},{5,6},{6,5},{7,4},{8,11},{9,10},{10,... | collective-permute-start | bytes 442376 | tf_op jit(solution)/shard_map/ppermute | solution.py:74
  15.1 2.8 %collective-permute-start.8 = (bf16[2,72,1024]{2,1,0:T(8,128)(2,1)S(1)}, bf16[2,72,1024]{2,1,0:T(8,128)(2,1)S(1)}, u32[]{:S(2)}, u32[]{:S(2)}) collective-permute-start(bf16[2,72,1024]{2,1,0:T(8,128)(2,1)S(1)} %pad_maximum_fusion.1.refs_4_.refs_13_), channel_id=1, source_target_pairs={{0,96},{16,112},{32,0},{48,16},{64,32},{80,48},{96,64},{112,80},{1... | collective-permute-start | bytes 884744 | tf_op jit(solution)/shard_map/ppermute | solution.py:78
  20.9 2.6 %collective-permute-start.3 = (bf16[4,72,512]{2,1,0:T(8,128)(2,1)S(1)}, bf16[4,72,512]{2,1,0:T(8,128)(2,1)S(1)}, u32[]{:S(2)}, u32[]{:S(2)}) collective-permute-start(bf16[4,72,512]{2,1,0:T(8,128)(2,1)S(1)} %pad_maximum_fusion.refs_0_.refs_9_), channel_id=1, source_target_pairs={{0,8},{1,9},{2,10},{3,11},{4,12},{5,13},{6,14},{7,15},{8,0},{9,1},... | collective-permute-start | bytes 884744 | tf_op jit(solution)/shard_map/ppermute | solution.py:58
  23.5 7.7 %collective-permute-done.8.refs_7_.refs_16_ = bf16[2,72,1024]{2,1,0:T(8,128)(2,1)S(1)} collective-permute-done((bf16[2,72,1024]{2,1,0:T(8,128)(2,1)S(1)}, bf16[2,72,1024]{2,1,0:T(8,128)(2,1)S(1)}, u32[]{:S(2)}, u32[]{:S(2)}) %collective-permute-start.8) | collective-permute-done | bytes 294944 | tf_op jit(solution)/shard_map/ppermute | solution.py:78
  36.6 2.9 %collective-permute-done.2.refs_1_.refs_10_ = bf16[4,72,512]{2,1,0:T(8,128)(2,1)S(1)} collective-permute-done((bf16[4,72,512]{2,1,0:T(8,128)(2,1)S(1)}, bf16[4,72,512]{2,1,0:T(8,128)(2,1)S(1)}, u32[]{:S(2)}, u32[]{:S(2)}) %collective-permute-start.2) | collective-permute-done | bytes 294944 | tf_op jit(solution)/shard_map/ppermute | solution.py:58
  40.4 7.7 %shard_map.78 = (f32[32,256]{1,0:T(8,128)S(1)}, f32[32,256]{1,0:T(8,128)S(1)}, f32[64,256]{1,0:T(8,128)S(1)}, bf16[12,8,256,256]{3,2,1,0:T(8,128)(2,1)}) custom-call(s32[96]{0:T(128)} %bitcast.40, s32[1]{0:T(128)} %bitcast.32.count_ref, s32[2]{0:T(128)} %pad_add_fusion.pos_ref, bf16[4,72,512]{2,1,0:T(8,128)(2,1)} %copy-done.1, ...), custom_call_target="tpu_custom_call" | custom-call | tf_op jit(solution)/shard_map/pallas_call | solution.py:402
  48.1 2.6 %collective-permute-start.15 = (f32[32,256]{1,0:T(8,128)S(1)}, f32[32,256]{1,0:T(8,128)S(1)}, u32[]{:S(2)}, u32[]{:S(2)}) collective-permute-start(f32[32,256]{1,0:T(8,128)S(1)} %get-tuple-element.17), channel_id=1, source_target_pairs={{0,12},{1,13},{2,14},{3,15},{4,0},{5,1},{6,2},{7,3},{8,4},{9,5},{1... | collective-permute-start | bytes 98312 | tf_op jit(solution)/shard_map/ppermute | solution.py:58
  50.7 3.7 %collective-permute-start.14 = (f32[32,256]{1,0:T(8,128)S(1)}, f32[32,256]{1,0:T(8,128)S(1)}, u32[]{:S(2)}, u32[]{:S(2)}) collective-permute-start(f32[32,256]{1,0:T(8,128)S(1)} %get-tuple-element.17), channel_id=1, source_target_pairs={{0,8},{1,9},{2,10},{3,11},{4,12},{5,13},{6,14},{7,15},{8,0},{9,1},... | collective-permute-start | bytes 98312 | tf_op jit(solution)/shard_map/ppermute | solution.py:58
  58.3 6.1 %collective-permute-start.18 = (f32[32,256]{1,0:T(8,128)S(1)}, f32[32,256]{1,0:T(8,128)S(1)}, u32[]{:S(2)}, u32[]{:S(2)}) collective-permute-start(f32[32,256]{1,0:T(8,128)S(1)} %add_add_fusion.3.refs_0_), channel_id=1, source_target_pairs={{0,3},{1,0},{2,1},{3,2},{4,7},{5,4},{6,5},{7,6},{8,11},{9,8},{10,9... | collective-permute-start | bytes 98312 | tf_op jit(solution)/shard_map/ppermute | solution.py:62
  66.8 2.8 %collective-permute-start.16 = (f32[32,256]{1,0:T(8,128)S(1)}, f32[32,256]{1,0:T(8,128)S(1)}, u32[]{:S(2)}, u32[]{:S(2)}) collective-permute-start(f32[32,256]{1,0:T(8,128)S(1)} %add_add_fusion.3.refs_0_), channel_id=1, source_target_pairs={{0,1},{1,2},{2,3},{3,0},{4,5},{5,6},{6,7},{7,4},{8,9},{9,10},{10,1... | collective-permute-start | bytes 98312 | tf_op jit(solution)/shard_map/ppermute | solution.py:62
  69.6 2.6 %collective-permute-done.17.refs_2_ = f32[32,256]{1,0:T(8,128)S(1)} collective-permute-done((f32[32,256]{1,0:T(8,128)S(1)}, f32[32,256]{1,0:T(8,128)S(1)}, u32[]{:S(2)}, u32[]{:S(2)}) %collective-permute-start.17) | collective-permute-done | bytes 32800 | tf_op jit(solution)/shard_map/ppermute | solution.py:62
  72.9 3.0 %shard_map.79 = f32[64,256]{1,0:T(8,128)S(1)} custom-call(s32[96]{0:T(128)} %bitcast.41, s32[1]{0:T(128)} %bitcast.33.count_ref, f32[32,256]{1,0:T(8,128)S(1)} %add_add_fusion.3.refs_0_, f32[32,256]{1,0:T(8,128)S(1)} %collective-permute-done.16.refs_1_, f32[32,256]{1,0:T(8,128)S(1)} %collective-permute-done.17.refs_2_, ...), custom_call_target="tpu_custom_call" | custom-call | tf_op jit(solution)/shard_map/pallas_call | solution.py:402
  84.8 3.4 %collective-permute-start.23 = (f32[64,256]{1,0:T(8,128)S(1)}, f32[64,256]{1,0:T(8,128)S(1)}, u32[]{:S(2)}, u32[]{:S(2)}) collective-permute-start(f32[64,256]{1,0:T(8,128)S(1)} %add_add_fusion.1.ca_ref), channel_id=1, source_target_pairs={{0,96},{16,112},{32,64},{48,80},{64,32},{80,48},{96,0},{112,16},{1... | collective-permute-start | bytes 196616 | tf_op jit(solution)/shard_map/ppermute | solution.py:101
  90.5 3.2 %shard_map.80 = f32[32,256]{1,0:T(8,128)S(1)} custom-call(s32[96]{0:T(128)} %bitcast.42, s32[1]{0:T(128)} %bitcast.34.count_ref, f32[64,256]{1,0:T(8,128)S(1)} %add_add_fusion.1.ca_ref, f32[64,256]{1,0:T(8,128)S(1)} %collective-permute-done.23.cb_ref, f32[64,256]{1,0:T(8,128)S(1)} %get-tuple-element.20.n_ref.refs_7_, ...), custom_call_target="tpu_custom_call" | custom-call | tf_op jit(solution)/shard_map/pallas_call | solution.py:402
  93.7 5.8 %collective-permute-start.26 = (f32[32,256]{1,0:T(8,128)S(1)}, f32[32,256]{1,0:T(8,128)S(1)}, u32[]{:S(2)}, u32[]{:S(2)}) collective-permute-start(f32[32,256]{1,0:T(8,128)S(1)} %shard_map.80), channel_id=1, source_target_pairs={{0,12},{1,13},{2,14},{3,15},{4,0},{5,1},{6,2},{7,3},{8,4},{9,5},{1... | collective-permute-start | bytes 98312 | tf_op jit(solution)/shard_map/ppermute | solution.py:58
  101.1 3.8 %collective-permute-done.25 = f32[32,256]{1,0:T(8,128)S(1)} collective-permute-done((f32[32,256]{1,0:T(8,128)S(1)}, f32[32,256]{1,0:T(8,128)S(1)}, u32[]{:S(2)}, u32[]{:S(2)}) %collective-permute-start.25) | collective-permute-done | bytes 32800 | tf_op jit(solution)/shard_map/ppermute | solution.py:58
  105.0 3.1 %collective-permute-start.29 = (f32[32,256]{1,0:T(8,128)S(1)}, f32[32,256]{1,0:T(8,128)S(1)}, u32[]{:S(2)}, u32[]{:S(2)}) collective-permute-start(f32[32,256]{1,0:T(8,128)S(1)} %add_add_fusion.2.refs_0_), channel_id=1, source_target_pairs={{0,3},{1,0},{2,1},{3,2},{4,7},{5,4},{6,5},{7,6},{8,11},{9,8},{10,9... | collective-permute-start | bytes 98312 | tf_op jit(solution)/shard_map/ppermute | solution.py:62
  108.1 2.6 %collective-permute-start.28 = (f32[32,256]{1,0:T(8,128)S(1)}, f32[32,256]{1,0:T(8,128)S(1)}, u32[]{:S(2)}, u32[]{:S(2)}) collective-permute-start(f32[32,256]{1,0:T(8,128)S(1)} %add_add_fusion.2.refs_0_), channel_id=1, source_target_pairs={{0,2},{1,3},{2,0},{3,1},{4,6},{5,7},{6,4},{7,5},{8,10},{9,11},{10,... | collective-permute-start | bytes 98312 | tf_op jit(solution)/shard_map/ppermute | solution.py:62
  110.7 2.8 %collective-permute-start.27 = (f32[32,256]{1,0:T(8,128)S(1)}, f32[32,256]{1,0:T(8,128)S(1)}, u32[]{:S(2)}, u32[]{:S(2)}) collective-permute-start(f32[32,256]{1,0:T(8,128)S(1)} %add_add_fusion.2.refs_0_), channel_id=1, source_target_pairs={{0,1},{1,2},{2,3},{3,0},{4,5},{5,6},{6,7},{7,4},{8,9},{9,10},{10,1... | collective-permute-start | bytes 98312 | tf_op jit(solution)/shard_map/ppermute | solution.py:62
  113.5 2.4 %collective-permute-done.28.refs_2_ = f32[32,256]{1,0:T(8,128)S(1)} collective-permute-done((f32[32,256]{1,0:T(8,128)S(1)}, f32[32,256]{1,0:T(8,128)S(1)}, u32[]{:S(2)}, u32[]{:S(2)}) %collective-permute-start.28) | collective-permute-done | bytes 32800 | tf_op jit(solution)/shard_map/ppermute | solution.py:62
  116.7 3.0 %shard_map.81 = f32[64,256]{1,0:T(8,128)S(1)} custom-call(s32[96]{0:T(128)} %bitcast.43, s32[1]{0:T(128)} %bitcast.35.count_ref, f32[32,256]{1,0:T(8,128)S(1)} %add_add_fusion.2.refs_0_, f32[32,256]{1,0:T(8,128)S(1)} %collective-permute-done.27.refs_1_, f32[32,256]{1,0:T(8,128)S(1)} %collective-permute-done.28.refs_2_, ...), custom_call_target="tpu_custom_call" | custom-call | tf_op jit(solution)/shard_map/pallas_call | solution.py:402
  128.1 2.4 %collective-permute-start.34 = (f32[64,256]{1,0:T(8,128)S(1)}, f32[64,256]{1,0:T(8,128)S(1)}, u32[]{:S(2)}, u32[]{:S(2)}) collective-permute-start(f32[64,256]{1,0:T(8,128)S(1)} %add_add_fusion.refs_4_), channel_id=1, source_target_pairs={{0,96},{16,112},{32,64},{48,80},{64,32},{80,48},{96,0},{112,16},{1... | collective-permute-start | bytes 196616 | tf_op jit(solution)/shard_map/ppermute | solution.py:101
  130.5 3.3 %collective-permute-done.34.refs_5_ = f32[64,256]{1,0:T(8,128)S(1)} collective-permute-done((f32[64,256]{1,0:T(8,128)S(1)}, f32[64,256]{1,0:T(8,128)S(1)}, u32[]{:S(2)}, u32[]{:S(2)}) %collective-permute-start.34) | collective-permute-done | bytes 65568 | tf_op jit(solution)/shard_map/ppermute | solution.py:101
  133.9 8.0 %shard_map.82 = (bf16[4,72,512]{2,1,0:T(8,128)(2,1)}, bf16[4,72,512]{2,1,0:T(8,128)(2,1)}, bf16[4,72,512]{2,1,0:T(8,128)(2,1)}, bf16[4,72,512]{2,1,0:T(8,128)(2,...) custom-call(s32[96]{0:T(128)} %bitcast.44, s32[1]{0:T(128)} %bitcast.36.count_ref, ...), custom_call_target="tpu_custom_call" | custom-call | tf_op jit(solution)/shard_map/pallas_call | solution.py:402
  141.9 5.6 %collective-permute-start.35 = (bf16[4,72,512]{2,1,0:T(8,128)(2,1)}, bf16[4,72,512]{2,1,0:T(8,128)(2,1)S(1)}, u32[]{:S(2)}, u32[]{:S(2)}) collective-permute-start(bf16[4,72,512]{2,1,0:T(8,128)(2,1)} %get-tuple-element.22), channel_id=1, source_target_pairs={{0,12},{1,13},{2,14},{3,15},{4,0},{5,1},{6,2},{7,3},{8,4},{9,5},{1... | collective-permute-start | bytes 884744 | tf_op jit(solution)/shard_map/ppermute | solution.py:58
  149.9 5.4 %collective-permute-done.35.b_ref = bf16[4,72,512]{2,1,0:T(8,128)(2,1)S(1)} collective-permute-done((bf16[4,72,512]{2,1,0:T(8,128)(2,1)}, bf16[4,72,512]{2,1,0:T(8,128)(2,1)S(1)}, u32[]{:S(2)}, u32[]{:S(2)}) %collective-permute-start.35) | collective-permute-done | bytes 294944 | tf_op jit(solution)/shard_map/ppermute | solution.py:58
  155.3 7.3 %collective-permute-done.36.c_ref = bf16[4,72,512]{2,1,0:T(8,128)(2,1)S(1)} collective-permute-done((bf16[4,72,512]{2,1,0:T(8,128)(2,1)}, bf16[4,72,512]{2,1,0:T(8,128)(2,1)S(1)}, u32[]{:S(2)}, u32[]{:S(2)}) %collective-permute-start.36) | collective-permute-done | bytes 294944 | tf_op jit(solution)/shard_map/ppermute | solution.py:58
  166.5 5.6 %collective-permute-start.39 = (bf16[72,512]{1,0:T(8,128)(2,1)}, bf16[72,512]{1,0:T(8,128)(2,1)S(1)}, u32[]{:S(2)}, u32[]{:S(2)}) collective-permute-start(bf16[72,512]{1,0:T(8,128)(2,1)} %get-tuple-element.27), channel_id=1, source_target_pairs={{0,3},{1,2},{2,1},{3,0},{4,7},{5,6},{6,5},{7,4},{8,11},{9,10},{10,... | collective-permute-start | bytes 221192 | tf_op jit(solution)/shard_map/ppermute | solution.py:74
  177.9 4.0 %collective-permute-done.40 = bf16[72,512]{1,0:T(8,128)(2,1)S(1)} collective-permute-done((bf16[72,512]{1,0:T(8,128)(2,1)}, bf16[72,512]{1,0:T(8,128)(2,1)S(1)}, u32[]{:S(2)}, u32[]{:S(2)}) %collective-permute-start.40) | collective-permute-done | bytes 73760 | tf_op jit(solution)/shard_map/ppermute | solution.py:70
  184.9 3.2 %collective-permute-done.43 = bf16[2,64,1024]{2,1,0:T(8,128)(2,1)S(1)} collective-permute-done((bf16[2,64,1024]{2,1,0:T(8,128)(2,1)S(1)}, bf16[2,64,1024]{2,1,0:T(8,128)(2,1)S(1)}, u32[]{:S(2)}, u32[]{:S(2)}) %collective-permute-start.43) | collective-permute-done | bytes 262176 | tf_op jit(solution)/shard_map/ppermute | solution.py:78
  189.3 5.2 %collective-permute-start.45 = (bf16[64,1024]{1,0:T(8,128)(2,1)S(1)}, bf16[64,1024]{1,0:T(8,128)(2,1)S(1)}, u32[]{:S(2)}, u32[]{:S(2)}) collective-permute-start(bf16[64,1024]{1,0:T(8,128)(2,1)S(1)} %fusion.4), channel_id=1, source_target_pairs={{0,128},{16,144},{32,160},{48,176},{64,192},{80,208},{96,224},{112... | collective-permute-start | bytes 393224 | tf_op jit(solution)/shard_map/ppermute | solution.py:86
  (115 shorter events, 64.1 us)
Async XLA Ops:
  2.3 7.3 %collective-permute-start = (bf16[1,72,512]{2,1,0:T(8,128)(2,1)S(1)}, bf16[1,72,512]{2,1,0:T(8,128)(2,1)S(1)}, u32[]{:S(2)}, u32[]{:S(2)}) collective-permute-start(bf16[1,72,512]{2,1,0:T(8,128)(2,1)S(1)} %maximum_bitcast_fusion), channel_id=1, source_target_pairs={{0,1},{1,0},{2,3},{3,2},{4,5},{5,4},{6,7},{7,6},{8,9},{9,8},{10,11... | collective-permute-start | bytes 221192 | tf_op jit(solution)/shard_map/ppermute | solution.py:66
  7.3 6.8 %collective-permute-start.5 = (bf16[1,72,1024]{2,1,0:T(8,128)(2,1)}, bf16[1,72,1024]{2,1,0:T(8,128)(2,1)S(1)}, u32[]{:S(2)}, u32[]{:S(2)}) collective-permute-start(bf16[1,72,1024]{2,1,0:T(8,128)(2,1)} %shard_map.77), channel_id=1, source_target_pairs={{0,128},{16,144},{32,160},{48,176},{64,192},{80,208},{96,224},{112... | collective-permute-start | bytes 442376 | tf_op jit(solution)/shard_map/ppermute | solution.py:86
  9.6 10.7 %collective-permute-start.1 = (bf16[2,72,512]{2,1,0:T(8,128)(2,1)S(1)}, bf16[2,72,512]{2,1,0:T(8,128)(2,1)S(1)}, u32[]{:S(2)}, u32[]{:S(2)}) collective-permute-start(bf16[2,72,512]{2,1,0:T(8,128)(2,1)S(1)} %pad_maximum_fusion.2), channel_id=1, source_target_pairs={{0,3},{1,2},{2,1},{3,0},{4,7},{5,6},{6,5},{7,4},{8,11},{9,10},{10,... | collective-permute-start | bytes 442376 | tf_op jit(solution)/shard_map/ppermute | solution.py:74
  15.0 5.9 %collective-permute-start.9 = (bf16[2,72,1024]{2,1,0:T(8,128)(2,1)S(1)}, bf16[2,72,1024]{2,1,0:T(8,128)(2,1)S(1)}, u32[]{:S(2)}, u32[]{:S(2)}) collective-permute-start(bf16[2,72,1024]{2,1,0:T(8,128)(2,1)S(1)} %pad_maximum_fusion.1.refs_4_.refs_13_), channel_id=1, source_target_pairs={{0,16},{16,0},{32,48},{48,32},{64,80},{80,64},{96,112},{112,96},{1... | collective-permute-start | bytes 884744 | tf_op jit(solution)/shard_map/ppermute | solution.py:82
  15.1 16.0 %collective-permute-start.8 = (bf16[2,72,1024]{2,1,0:T(8,128)(2,1)S(1)}, bf16[2,72,1024]{2,1,0:T(8,128)(2,1)S(1)}, u32[]{:S(2)}, u32[]{:S(2)}) collective-permute-start(bf16[2,72,1024]{2,1,0:T(8,128)(2,1)S(1)} %pad_maximum_fusion.1.refs_4_.refs_13_), channel_id=1, source_target_pairs={{0,96},{16,112},{32,0},{48,16},{64,32},{80,48},{96,64},{112,80},{1... | collective-permute-start | bytes 884744 | tf_op jit(solution)/shard_map/ppermute | solution.py:78
  18.0 14.8 %collective-permute-start.7 = (bf16[2,72,1024]{2,1,0:T(8,128)(2,1)S(1)}, bf16[2,72,1024]{2,1,0:T(8,128)(2,1)S(1)}, u32[]{:S(2)}, u32[]{:S(2)}) collective-permute-start(bf16[2,72,1024]{2,1,0:T(8,128)(2,1)S(1)} %pad_maximum_fusion.1.refs_4_.refs_13_), channel_id=1, source_target_pairs={{0,64},{16,80},{32,96},{48,112},{64,0},{80,16},{96,32},{112,48},{1... | collective-permute-start | bytes 884744 | tf_op jit(solution)/shard_map/ppermute | solution.py:78
  18.8 16.1 %collective-permute-start.6 = (bf16[2,72,1024]{2,1,0:T(8,128)(2,1)S(1)}, bf16[2,72,1024]{2,1,0:T(8,128)(2,1)S(1)}, u32[]{:S(2)}, u32[]{:S(2)}) collective-permute-start(bf16[2,72,1024]{2,1,0:T(8,128)(2,1)S(1)} %pad_maximum_fusion.1.refs_4_.refs_13_), channel_id=1, source_target_pairs={{0,32},{16,48},{32,64},{48,80},{64,96},{80,112},{96,0},{112,16},{1... | collective-permute-start | bytes 884744 | tf_op jit(solution)/shard_map/ppermute | solution.py:78
  20.4 14.5 %collective-permute-start.4 = (bf16[4,72,512]{2,1,0:T(8,128)(2,1)S(1)}, bf16[4,72,512]{2,1,0:T(8,128)(2,1)S(1)}, u32[]{:S(2)}, u32[]{:S(2)}) collective-permute-start(bf16[4,72,512]{2,1,0:T(8,128)(2,1)S(1)} %pad_maximum_fusion.refs_0_.refs_9_), channel_id=1, source_target_pairs={{0,12},{1,13},{2,14},{3,15},{4,0},{5,1},{6,2},{7,3},{8,4},{9,5},{1... | collective-permute-start | bytes 884744 | tf_op jit(solution)/shard_map/ppermute | solution.py:58
  20.9 15.7 %collective-permute-start.3 = (bf16[4,72,512]{2,1,0:T(8,128)(2,1)S(1)}, bf16[4,72,512]{2,1,0:T(8,128)(2,1)S(1)}, u32[]{:S(2)}, u32[]{:S(2)}) collective-permute-start(bf16[4,72,512]{2,1,0:T(8,128)(2,1)S(1)} %pad_maximum_fusion.refs_0_.refs_9_), channel_id=1, source_target_pairs={{0,8},{1,9},{2,10},{3,11},{4,12},{5,13},{6,14},{7,15},{8,0},{9,1},... | collective-permute-start | bytes 884744 | tf_op jit(solution)/shard_map/ppermute | solution.py:58
  31.2 8.3 %collective-permute-start.2 = (bf16[4,72,512]{2,1,0:T(8,128)(2,1)S(1)}, bf16[4,72,512]{2,1,0:T(8,128)(2,1)S(1)}, u32[]{:S(2)}, u32[]{:S(2)}) collective-permute-start(bf16[4,72,512]{2,1,0:T(8,128)(2,1)S(1)} %pad_maximum_fusion.refs_0_.refs_9_), channel_id=1, source_target_pairs={{0,4},{1,5},{2,6},{3,7},{4,8},{5,9},{6,10},{7,11},{8,12},{9,13},{1... | collective-permute-start | bytes 884744 | tf_op jit(solution)/shard_map/ppermute | solution.py:58
  32.8 6.7 %collective-permute-start.12 = (bf16[2,72,1024]{2,1,0:T(8,128)(2,1)S(1)}, bf16[2,72,1024]{2,1,0:T(8,128)(2,1)S(1)}, u32[]{:S(2)}, u32[]{:S(2)}) collective-permute-start(bf16[2,72,1024]{2,1,0:T(8,128)(2,1)S(1)} %collective-permute-done.8.refs_7_.refs_16_), channel_id=1, source_target_pairs={{0,16},{16,0},{32,48},{48,32},{64,80},{80,64},{96,112},{112,96},{1... | collective-permute-start | bytes 884744 | tf_op jit(solution)/shard_map/ppermute | solution.py:82
  48.1 6.8 %collective-permute-start.15 = (f32[32,256]{1,0:T(8,128)S(1)}, f32[32,256]{1,0:T(8,128)S(1)}, u32[]{:S(2)}, u32[]{:S(2)}) collective-permute-start(f32[32,256]{1,0:T(8,128)S(1)} %get-tuple-element.17), channel_id=1, source_target_pairs={{0,12},{1,13},{2,14},{3,15},{4,0},{5,1},{6,2},{7,3},{8,4},{9,5},{1... | collective-permute-start | bytes 98312 | tf_op jit(solution)/shard_map/ppermute | solution.py:58
  50.7 6.0 %collective-permute-start.14 = (f32[32,256]{1,0:T(8,128)S(1)}, f32[32,256]{1,0:T(8,128)S(1)}, u32[]{:S(2)}, u32[]{:S(2)}) collective-permute-start(f32[32,256]{1,0:T(8,128)S(1)} %get-tuple-element.17), channel_id=1, source_target_pairs={{0,8},{1,9},{2,10},{3,11},{4,12},{5,13},{6,14},{7,15},{8,0},{9,1},... | collective-permute-start | bytes 98312 | tf_op jit(solution)/shard_map/ppermute | solution.py:58
  58.3 11.3 %collective-permute-start.18 = (f32[32,256]{1,0:T(8,128)S(1)}, f32[32,256]{1,0:T(8,128)S(1)}, u32[]{:S(2)}, u32[]{:S(2)}) collective-permute-start(f32[32,256]{1,0:T(8,128)S(1)} %add_add_fusion.3.refs_0_), channel_id=1, source_target_pairs={{0,3},{1,0},{2,1},{3,2},{4,7},{5,4},{6,5},{7,6},{8,11},{9,8},{10,9... | collective-permute-start | bytes 98312 | tf_op jit(solution)/shard_map/ppermute | solution.py:62
  64.5 7.8 %collective-permute-start.17 = (f32[32,256]{1,0:T(8,128)S(1)}, f32[32,256]{1,0:T(8,128)S(1)}, u32[]{:S(2)}, u32[]{:S(2)}) collective-permute-start(f32[32,256]{1,0:T(8,128)S(1)} %add_add_fusion.3.refs_0_), channel_id=1, source_target_pairs={{0,2},{1,3},{2,0},{3,1},{4,6},{5,7},{6,4},{7,5},{8,10},{9,11},{10,... | collective-permute-start | bytes 98312 | tf_op jit(solution)/shard_map/ppermute | solution.py:62
  66.8 6.1 %collective-permute-start.16 = (f32[32,256]{1,0:T(8,128)S(1)}, f32[32,256]{1,0:T(8,128)S(1)}, u32[]{:S(2)}, u32[]{:S(2)}) collective-permute-start(f32[32,256]{1,0:T(8,128)S(1)} %add_add_fusion.3.refs_0_), channel_id=1, source_target_pairs={{0,1},{1,2},{2,3},{3,0},{4,5},{5,6},{6,7},{7,4},{8,9},{9,10},{10,1... | collective-permute-start | bytes 98312 | tf_op jit(solution)/shard_map/ppermute | solution.py:62
  93.7 7.4 %collective-permute-start.26 = (f32[32,256]{1,0:T(8,128)S(1)}, f32[32,256]{1,0:T(8,128)S(1)}, u32[]{:S(2)}, u32[]{:S(2)}) collective-permute-start(f32[32,256]{1,0:T(8,128)S(1)} %shard_map.80), channel_id=1, source_target_pairs={{0,12},{1,13},{2,14},{3,15},{4,0},{5,1},{6,2},{7,3},{8,4},{9,5},{1... | collective-permute-start | bytes 98312 | tf_op jit(solution)/shard_map/ppermute | solution.py:58
  105.0 8.5 %collective-permute-start.29 = (f32[32,256]{1,0:T(8,128)S(1)}, f32[32,256]{1,0:T(8,128)S(1)}, u32[]{:S(2)}, u32[]{:S(2)}) collective-permute-start(f32[32,256]{1,0:T(8,128)S(1)} %add_add_fusion.2.refs_0_), channel_id=1, source_target_pairs={{0,3},{1,0},{2,1},{3,2},{4,7},{5,4},{6,5},{7,6},{8,11},{9,8},{10,9... | collective-permute-start | bytes 98312 | tf_op jit(solution)/shard_map/ppermute | solution.py:62
  108.1 7.8 %collective-permute-start.28 = (f32[32,256]{1,0:T(8,128)S(1)}, f32[32,256]{1,0:T(8,128)S(1)}, u32[]{:S(2)}, u32[]{:S(2)}) collective-permute-start(f32[32,256]{1,0:T(8,128)S(1)} %add_add_fusion.2.refs_0_), channel_id=1, source_target_pairs={{0,2},{1,3},{2,0},{3,1},{4,6},{5,7},{6,4},{7,5},{8,10},{9,11},{10,... | collective-permute-start | bytes 98312 | tf_op jit(solution)/shard_map/ppermute | solution.py:62
  110.7 6.0 %collective-permute-start.27 = (f32[32,256]{1,0:T(8,128)S(1)}, f32[32,256]{1,0:T(8,128)S(1)}, u32[]{:S(2)}, u32[]{:S(2)}) collective-permute-start(f32[32,256]{1,0:T(8,128)S(1)} %add_add_fusion.2.refs_0_), channel_id=1, source_target_pairs={{0,1},{1,2},{2,3},{3,0},{4,5},{5,6},{6,7},{7,4},{8,9},{9,10},{10,1... | collective-permute-start | bytes 98312 | tf_op jit(solution)/shard_map/ppermute | solution.py:62
  121.4 5.9 %collective-permute-start.32 = (f32[64,256]{1,0:T(8,128)S(1)}, f32[64,256]{1,0:T(8,128)S(1)}, u32[]{:S(2)}, u32[]{:S(2)}) collective-permute-start(f32[64,256]{1,0:T(8,128)S(1)} %add.88), channel_id=1, source_target_pairs={{0,32},{16,48},{32,0},{48,16},{64,96},{80,112},{96,64},{112,80},{1... | collective-permute-start | bytes 196616 | tf_op jit(solution)/shard_map/ppermute | solution.py:98
  141.8 30.8 %collective-permute-start.41 = (bf16[8,64,1024]{2,1,0:T(8,128)(2,1)}, bf16[8,64,1024]{2,1,0:T(8,128)(2,1)S(1)}, u32[]{:S(2)}, u32[]{:S(2)}) collective-permute-start(bf16[8,64,1024]{2,1,0:T(8,128)(2,1)} %get-tuple-element.31), channel_id=1, source_target_pairs={{0,16},{16,0},{32,48},{48,32},{64,80},{80,64},{96,112},{112,96},{1... | collective-permute-start | bytes 3145736 | tf_op jit(solution)/shard_map/ppermute | solution.py:82
  141.9 13.3 %collective-permute-start.35 = (bf16[4,72,512]{2,1,0:T(8,128)(2,1)}, bf16[4,72,512]{2,1,0:T(8,128)(2,1)S(1)}, u32[]{:S(2)}, u32[]{:S(2)}) collective-permute-start(bf16[4,72,512]{2,1,0:T(8,128)(2,1)} %get-tuple-element.22), channel_id=1, source_target_pairs={{0,12},{1,13},{2,14},{3,15},{4,0},{5,1},{6,2},{7,3},{8,4},{9,5},{1... | collective-permute-start | bytes 884744 | tf_op jit(solution)/shard_map/ppermute | solution.py:58
  147.5 15.0 %collective-permute-start.36 = (bf16[4,72,512]{2,1,0:T(8,128)(2,1)}, bf16[4,72,512]{2,1,0:T(8,128)(2,1)S(1)}, u32[]{:S(2)}, u32[]{:S(2)}) collective-permute-start(bf16[4,72,512]{2,1,0:T(8,128)(2,1)} %get-tuple-element.23), channel_id=1, source_target_pairs={{0,8},{1,9},{2,10},{3,11},{4,12},{5,13},{6,14},{7,15},{8,0},{9,1},... | collective-permute-start | bytes 884744 | tf_op jit(solution)/shard_map/ppermute | solution.py:58
  148.7 14.5 %collective-permute-start.37 = (bf16[4,72,512]{2,1,0:T(8,128)(2,1)}, bf16[4,72,512]{2,1,0:T(8,128)(2,1)S(1)}, u32[]{:S(2)}, u32[]{:S(2)}) collective-permute-start(bf16[4,72,512]{2,1,0:T(8,128)(2,1)} %get-tuple-element.24), channel_id=1, source_target_pairs={{0,4},{1,5},{2,6},{3,7},{4,8},{5,9},{6,10},{7,11},{8,12},{9,13},{1... | collective-permute-start | bytes 884744 | tf_op jit(solution)/shard_map/ppermute | solution.py:58
  164.9 11.2 %collective-permute-start.38 = (bf16[72,512]{1,0:T(8,128)(2,1)}, bf16[72,512]{1,0:T(8,128)(2,1)S(1)}, u32[]{:S(2)}, u32[]{:S(2)}) collective-permute-start(bf16[72,512]{1,0:T(8,128)(2,1)} %get-tuple-element.26), channel_id=1, source_target_pairs={{0,1},{1,0},{2,3},{3,2},{4,5},{5,4},{6,7},{7,6},{8,9},{9,8},{10,11... | collective-permute-start | bytes 221192 | tf_op jit(solution)/shard_map/ppermute | solution.py:66
  166.5 11.4 %collective-permute-start.39 = (bf16[72,512]{1,0:T(8,128)(2,1)}, bf16[72,512]{1,0:T(8,128)(2,1)S(1)}, u32[]{:S(2)}, u32[]{:S(2)}) collective-permute-start(bf16[72,512]{1,0:T(8,128)(2,1)} %get-tuple-element.27), channel_id=1, source_target_pairs={{0,3},{1,2},{2,1},{3,0},{4,7},{5,6},{6,5},{7,4},{8,11},{9,10},{10,... | collective-permute-start | bytes 221192 | tf_op jit(solution)/shard_map/ppermute | solution.py:74
  172.0 9.9 %collective-permute-start.40 = (bf16[72,512]{1,0:T(8,128)(2,1)}, bf16[72,512]{1,0:T(8,128)(2,1)S(1)}, u32[]{:S(2)}, u32[]{:S(2)}) collective-permute-start(bf16[72,512]{1,0:T(8,128)(2,1)} %get-tuple-element.28), channel_id=1, source_target_pairs={{0,2},{1,3},{2,0},{3,1},{4,6},{5,7},{6,4},{7,5},{8,10},{9,11},{10,... | collective-permute-start | bytes 221192 | tf_op jit(solution)/shard_map/ppermute | solution.py:70
  174.0 9.3 %collective-permute-start.42 = (bf16[2,64,1024]{2,1,0:T(8,128)(2,1)S(1)}, bf16[2,64,1024]{2,1,0:T(8,128)(2,1)S(1)}, u32[]{:S(2)}, u32[]{:S(2)}) collective-permute-start(bf16[2,64,1024]{2,1,0:T(8,128)(2,1)S(1)} %get-tuple-element.32), channel_id=1, source_target_pairs={{0,96},{16,112},{32,0},{48,16},{64,32},{80,48},{96,64},{112,80},{1... | collective-permute-start | bytes 786440 | tf_op jit(solution)/shard_map/ppermute | solution.py:78
  174.3 10.6 %collective-permute-start.44 = (bf16[2,64,1024]{2,1,0:T(8,128)(2,1)S(1)}, bf16[2,64,1024]{2,1,0:T(8,128)(2,1)S(1)}, u32[]{:S(2)}, u32[]{:S(2)}) collective-permute-start(bf16[2,64,1024]{2,1,0:T(8,128)(2,1)S(1)} %get-tuple-element.33), channel_id=1, source_target_pairs={{0,32},{16,48},{32,64},{48,80},{64,96},{80,112},{96,0},{112,16},{1... | collective-permute-start | bytes 786440 | tf_op jit(solution)/shard_map/ppermute | solution.py:78
  176.1 11.9 %collective-permute-start.43 = (bf16[2,64,1024]{2,1,0:T(8,128)(2,1)S(1)}, bf16[2,64,1024]{2,1,0:T(8,128)(2,1)S(1)}, u32[]{:S(2)}, u32[]{:S(2)}) collective-permute-start(bf16[2,64,1024]{2,1,0:T(8,128)(2,1)S(1)} %get-tuple-element.34), channel_id=1, source_target_pairs={{0,64},{16,80},{32,96},{48,112},{64,0},{80,16},{96,32},{112,48},{1... | collective-permute-start | bytes 786440 | tf_op jit(solution)/shard_map/ppermute | solution.py:78
  189.3 8.2 %collective-permute-start.45 = (bf16[64,1024]{1,0:T(8,128)(2,1)S(1)}, bf16[64,1024]{1,0:T(8,128)(2,1)S(1)}, u32[]{:S(2)}, u32[]{:S(2)}) collective-permute-start(bf16[64,1024]{1,0:T(8,128)(2,1)S(1)} %fusion.4), channel_id=1, source_target_pairs={{0,128},{16,144},{32,160},{48,176},{64,192},{80,208},{96,224},{112... | collective-permute-start | bytes 393224 | tf_op jit(solution)/shard_map/ppermute | solution.py:86
  (27 other events, 307.1 us)

commit v6 on v5

--- a/solution.py
+++ b/solution.py
@@ -291,7 +291,7 @@
     xs, ys = (refs[0:4], refs[4:12])
     spec_outs, photo_outs, share_ref = (refs[12:16], refs[16:18], refs[18])
     xt_ref, yt_ref, u_ref, v_ref, wy_ref, vx_ref, spec_acc, photo_acc = refs[19:27]
-    spec_ref, photo_ref, g_ref, sems, g_sems, out_sems = refs[27:]
+    g_ref, sems, g_sems = refs[27:]
     copies = piece_copies(xs, ys, xt_ref, yt_ref, sems)
     for copy in copies:
         copy.start()
@@ -347,33 +347,34 @@
 
     over_tiles(index_ref, count_ref, wait_tiles(g_hbm, g_ref, g_sems), step, nothing)
 
-    def store_y(s, carry):
-        for k in range(4):
-            v = v_ref[4 * s + k][0:1, :]
-            photo_ref[s, :, k * TILE : (k + 1) * TILE] = (photo_acc[4 * s + k] * v).astype(bf16)
-        return carry
-
-    def store_x(s, carry):
-        for k in range(2):
-            lanes = slice(k * TILE, (k + 1) * TILE)
-            u = u_ref[2 * s + k][0:1, :]
-            both = spec_acc[2 * s + k]
-            spec_ref[s, 0:F, lanes] = (both[0:F, :] * u).astype(bf16)
-            total = jnp.broadcast_to((both[F : F + 1, :] + both[F + 1 : F + 2, :]) * u, (8, TILE))
-            spec_ref[s, F:EXT, lanes] = high_low_rows(total)
-        return carry
-
-    sends = []
-    for h in (1, 0):
-        lax.fori_loop(8 * h, 8 * h + 8, store_y, 0)
-        sends.append(pltpu.make_async_copy(photo_ref.at[pl.ds(8 * h, 8)], photo_outs[h], out_sems.at[4 + h]))
-        sends[-1].start()
+    def store_y(h):
+        def store(j, carry):
+            for k in range(4):
+                tile = 32 * h + 4 * j + k
+                v = v_ref[tile][0:1, :]
+                photo_outs[h][j, :, k * TILE : (k + 1) * TILE] = (photo_acc[tile] * v).astype(bf16)
+            return carry
+
+        lax.fori_loop(0, 8, store, 0)
+
+    def store_x(h):
+        def store(j, carry):
+            for k in range(2):
+                lanes = slice(k * TILE, (k + 1) * TILE)
+                tile = 8 * h + 2 * j + k
+                u = u_ref[tile][0:1, :]
+                both = spec_acc[tile]
+                spec_outs[h][j, 0:F, lanes] = (both[0:F, :] * u).astype(bf16)
+                total = jnp.broadcast_to((both[F : F + 1, :] + both[F + 1 : F + 2, :]) * u, (8, TILE))
+                spec_outs[h][j, F:EXT, lanes] = high_low_rows(total)
+            return carry
+
+        lax.fori_loop(0, 4, store, 0)
+
+    for h in range(2):
+        store_y(h)
     for h in range(4):
-        lax.fori_loop(4 * h, 4 * h + 4, store_x, 0)
-        sends.append(pltpu.make_async_copy(spec_ref.at[pl.ds(4 * h, 4)], spec_outs[h], out_sems.at[h]))
-        sends[-1].start()
-    for send in sends:
-        send.wait()
+        store_x(h)
 
 
 def relay_kernel(a_ref, b_ref, c_ref, d_ref, own_ref, *send_refs):
@@ -405,6 +406,7 @@
         out_specs=[spec for spec, _, _ in outs],
         out_shape=[kept(s, d) if spec is KEPT else jax.ShapeDtypeStruct(s, d) for spec, s, d in outs],
         scratch_shapes=scratch,
+        compiler_params=pltpu.CompilerParams(vmem_limit_bytes=40 << 20),
     )(*args)
 
 
@@ -425,7 +427,7 @@
     x_pad = jnp.zeros((EXT - F - 1, SB), bf16)
     x0 = jnp.concatenate([x_own, spec_mass.reshape(1, SB), x_pad])[None]
     (y0,) = call(
-        pack_kernel, [VMEM] * 2, [(VMEM, (1, EXT, PB), bf16)], [],
+        pack_kernel, [VMEM] * 2, [(KEPT, (1, EXT, PB), bf16)], [],
         y_own, photo_mass.reshape(1, PB),
     )
     x_flip = flip_z(x0)
@@ -472,7 +474,7 @@
     cs = in_vmem(sum_spec(columns(rs)))
     *parts, share = call(
         grad_kernel, [SMEM] * 3 + [VMEM] * 8 + [ANY] * 13,
-        [(ANY, (4, EXT, SB), bf16)] * 4 + [(ANY, (8, F, PB), bf16)] * 2 + [(VMEM, (4, 8, TILE), f32)],
+        [(KEPT, (4, EXT, SB), bf16)] * 4 + [(KEPT, (8, F, PB), bf16)] * 2 + [(KEPT, (4, 8, TILE), f32)],
         blocks
         + [
             pltpu.VMEM((TR, 8, TILE), f32),
@@ -481,10 +483,7 @@
             pltpu.VMEM((TR, F, TILE), bf16),
             pltpu.VMEM((TR, WROWS, TILE), f32),
             pltpu.VMEM((TC, F, TILE), f32),
-            pltpu.VMEM((SLOTS, EXT, SB), bf16),
-            pltpu.VMEM((SLOTS, F, PB), bf16),
             tiles, piece_sems, tile_sems,
-            pltpu.SemaphoreType.DMA((6,)),
         ],
         *meta, *rs, *cs, m, n, g, *xs, *ys,
     )
@@ -498,7 +497,7 @@
     x_parts = [shift_x(part, -k) for k, part in zip((1, 2, 3), x_parts)]
 
     spec_sum, *z_parts = call(
-        relay_kernel, [VMEM] * 4, [(VMEM, (EXT, SB), f32)] + [(VMEM, (EXT, SB), bf16)] * 3, [],
+        relay_kernel, [VMEM] * 4, [(KEPT, (EXT, SB), f32)] + [(KEPT, (EXT, SB), bf16)] * 3, [],
         spec_parts[0], *in_vmem(y_parts),
     )
     z_parts = [move(part) for move, part in zip((flip_z, mirror_z, across_z), z_parts)]

time: 202 us -> 205 us (1.015)
  local copies, waits for them, and re-layouts: 2.4 us -> 16.8 us
  Pallas kernels: 28.1 us -> 18 us
  other arithmetic: 7.52 us -> 3.15 us
    unnamed x26 -> x16, local copies, waits for them, and re-layouts: 0.86 us -> 16 us
    pallas_call x7, Pallas kernels: 28.1 us -> 18 us  [call(): pl.pallas_call(kernel, in_specs=in_specs, out_specs=[spec for spec, _, _...]
  transfers between devices with their start and end apart: 46 -> 46, of which waited for: 31 -> 32; matrix products, arithmetic and copies ran while one was open for 3% -> 1% of each run, Pallas kernels for 2% -> 0%
where the time goes in v6:
time: 205 us; the launch traced here: 201 us
  starting transfers between devices  91.7 us (45%)
  waiting for transfers between devices  70 us (34%)
  Pallas kernels  18 us (9%)
  local copies, waits for them, and re-layouts  16.8 us (8%)
  other arithmetic  3.15 us (2%)
    ppermute x12, starting transfers between devices, shift_y(): return lax.ppermute(a, 'photo', photo_perm(shift(k), same))  26.2 us
    ppermute x12, waiting for transfers between devices, shift_y(): return lax.ppermute(a, 'photo', photo_perm(shift(k), same))  24.9 us
    ppermute x6, starting transfers between devices, shift_z(): return lax.ppermute(a, 'photo', photo_perm(same, shift(k)))  20.4 us
    pallas_call x7, Pallas kernels, call(): pl.pallas_call(kernel, in_specs=in_specs, out_specs=[spec for spec, _, _...  18 us
    unnamed x16, local copies, waits for them, and re-layouts  16 us
    ppermute x6, waiting for transfers between devices, shift_x(): return lax.ppermute(a, 'spec', spec_perm(same, shift(k), same))  14.5 us
    ppermute x2, starting transfers between devices, mirror_z(): return lax.ppermute(a, 'photo', photo_perm(same, mirror))  10.1 us
    ppermute x6, starting transfers between devices, shift_x(): return lax.ppermute(a, 'spec', spec_perm(same, shift(k), same))  8.36 us
  transfers between devices with their start and end apart: 46, of which 32 were waited for; matrix products, arithmetic and copies ran while one was open for 1% of the time, Pallas kernels for 0%

profile of v6, /device:TPU:8, one launch (start us, length us, event | category | flops | bytes accessed | tf_op | source)
XLA Modules:
  0.0 201.2 jit_solution(17330821640883182958)
XLA Ops:
  2.3 3.4 %collective-permute-start = (bf16[1,72,512]{2,1,0:T(8,128)(2,1)S(1)}, bf16[1,72,512]{2,1,0:T(8,128)(2,1)S(1)}, u32[]{:S(2)}, u32[]{:S(2)}) collective-permute-start(bf16[1,72,512]{2,1,0:T(8,128)(2,1)S(1)} %maximum_bitcast_fusion), channel_id=1, source_target_pairs={{0,1},{1,0},{2,3},{3,2},{4,5},{5,4},{6,7},{7,6},{8,9},{9,8},{10,11... | collective-permute-start | bytes 221192 | tf_op jit(solution)/shard_map/ppermute | solution.py:66
  9.6 4.5 %collective-permute-start.1 = (bf16[2,72,512]{2,1,0:T(8,128)(2,1)S(1)}, bf16[2,72,512]{2,1,0:T(8,128)(2,1)S(1)}, u32[]{:S(2)}, u32[]{:S(2)}) collective-permute-start(bf16[2,72,512]{2,1,0:T(8,128)(2,1)S(1)} %pad_maximum_fusion.2), channel_id=1, source_target_pairs={{0,3},{1,2},{2,1},{3,0},{4,7},{5,6},{6,5},{7,4},{8,11},{9,10},{10,... | collective-permute-start | bytes 442376 | tf_op jit(solution)/shard_map/ppermute | solution.py:74
  14.2 2.8 %collective-permute-start.8 = (bf16[2,72,1024]{2,1,0:T(8,128)(2,1)S(1)}, bf16[2,72,1024]{2,1,0:T(8,128)(2,1)S(1)}, u32[]{:S(2)}, u32[]{:S(2)}) collective-permute-start(bf16[2,72,1024]{2,1,0:T(8,128)(2,1)S(1)} %pad_maximum_fusion.1.refs_4_.refs_13_), channel_id=1, source_target_pairs={{0,96},{16,112},{32,0},{48,16},{64,32},{80,48},{96,64},{112,80},{1... | collective-permute-start | bytes 884744 | tf_op jit(solution)/shard_map/ppermute | solution.py:78
  20.8 2.6 %collective-permute-start.3 = (bf16[4,72,512]{2,1,0:T(8,128)(2,1)S(1)}, bf16[4,72,512]{2,1,0:T(8,128)(2,1)S(1)}, u32[]{:S(2)}, u32[]{:S(2)}) collective-permute-start(bf16[4,72,512]{2,1,0:T(8,128)(2,1)S(1)} %pad_maximum_fusion.refs_0_.refs_9_), channel_id=1, source_target_pairs={{0,8},{1,9},{2,10},{3,11},{4,12},{5,13},{6,14},{7,15},{8,0},{9,1},... | collective-permute-start | bytes 884744 | tf_op jit(solution)/shard_map/ppermute | solution.py:58
  23.4 6.9 %collective-permute-done.8.refs_7_.refs_16_ = bf16[2,72,1024]{2,1,0:T(8,128)(2,1)S(1)} collective-permute-done((bf16[2,72,1024]{2,1,0:T(8,128)(2,1)S(1)}, bf16[2,72,1024]{2,1,0:T(8,128)(2,1)S(1)}, u32[]{:S(2)}, u32[]{:S(2)}) %collective-permute-start.8) | collective-permute-done | bytes 294944 | tf_op jit(solution)/shard_map/ppermute | solution.py:78
  36.0 2.5 %collective-permute-done.2.refs_1_.refs_10_ = bf16[4,72,512]{2,1,0:T(8,128)(2,1)S(1)} collective-permute-done((bf16[4,72,512]{2,1,0:T(8,128)(2,1)S(1)}, bf16[4,72,512]{2,1,0:T(8,128)(2,1)S(1)}, u32[]{:S(2)}, u32[]{:S(2)}) %collective-permute-start.2) | collective-permute-done | bytes 294944 | tf_op jit(solution)/shard_map/ppermute | solution.py:58
  39.2 6.4 %shard_map.78 = (f32[32,256]{1,0:T(8,128)S(1)}, f32[32,256]{1,0:T(8,128)S(1)}, f32[64,256]{1,0:T(8,128)S(1)}, bf16[12,8,256,256]{3,2,1,0:T(8,128)(2,1)}) custom-call(s32[96]{0:T(128)S(1)} %bitcast.38, s32[1]{0:T(128)} %bitcast.32.count_ref, s32[2]{0:T(128)S(1)} %pad_add_fusion.pos_ref, bf16[4,72,512]{2,1,0:T(8,128)(2,1)S(1)} %pad_maximum_fusion.refs_0_.refs_9_, ...), custom_call_target="tpu_custom_call" | custom-call | tf_op jit(solution)/shard_map/pallas_call | solution.py:403
  45.6 2.6 %collective-permute-start.15 = (f32[32,256]{1,0:T(8,128)S(1)}, f32[32,256]{1,0:T(8,128)S(1)}, u32[]{:S(2)}, u32[]{:S(2)}) collective-permute-start(f32[32,256]{1,0:T(8,128)S(1)} %get-tuple-element.17), channel_id=1, source_target_pairs={{0,12},{1,13},{2,14},{3,15},{4,0},{5,1},{6,2},{7,3},{8,4},{9,5},{1... | collective-permute-start | bytes 98312 | tf_op jit(solution)/shard_map/ppermute | solution.py:58
  48.2 3.7 %collective-permute-start.14 = (f32[32,256]{1,0:T(8,128)S(1)}, f32[32,256]{1,0:T(8,128)S(1)}, u32[]{:S(2)}, u32[]{:S(2)}) collective-permute-start(f32[32,256]{1,0:T(8,128)S(1)} %get-tuple-element.17), channel_id=1, source_target_pairs={{0,8},{1,9},{2,10},{3,11},{4,12},{5,13},{6,14},{7,15},{8,0},{9,1},... | collective-permute-start | bytes 98312 | tf_op jit(solution)/shard_map/ppermute | solution.py:58
  55.9 6.0 %collective-permute-start.18 = (f32[32,256]{1,0:T(8,128)S(1)}, f32[32,256]{1,0:T(8,128)S(1)}, u32[]{:S(2)}, u32[]{:S(2)}) collective-permute-start(f32[32,256]{1,0:T(8,128)S(1)} %add_add_fusion.3.refs_0_), channel_id=1, source_target_pairs={{0,3},{1,0},{2,1},{3,2},{4,7},{5,4},{6,5},{7,6},{8,11},{9,8},{10,9... | collective-permute-start | bytes 98312 | tf_op jit(solution)/shard_map/ppermute | solution.py:62
  64.2 2.8 %collective-permute-start.16 = (f32[32,256]{1,0:T(8,128)S(1)}, f32[32,256]{1,0:T(8,128)S(1)}, u32[]{:S(2)}, u32[]{:S(2)}) collective-permute-start(f32[32,256]{1,0:T(8,128)S(1)} %add_add_fusion.3.refs_0_), channel_id=1, source_target_pairs={{0,1},{1,2},{2,3},{3,0},{4,5},{5,6},{6,7},{7,4},{8,9},{9,10},{10,1... | collective-permute-start | bytes 98312 | tf_op jit(solution)/shard_map/ppermute | solution.py:62
  67.1 2.6 %collective-permute-done.17.refs_2_ = f32[32,256]{1,0:T(8,128)S(1)} collective-permute-done((f32[32,256]{1,0:T(8,128)S(1)}, f32[32,256]{1,0:T(8,128)S(1)}, u32[]{:S(2)}, u32[]{:S(2)}) %collective-permute-start.17) | collective-permute-done | bytes 32800 | tf_op jit(solution)/shard_map/ppermute | solution.py:62
  70.3 4.6 %copy-done = bf16[12,8,256,256]{3,2,1,0:T(8,128)(2,1)S(1)} copy-done((bf16[12,8,256,256]{3,2,1,0:T(8,128)(2,1)S(1)}, bf16[12,8,256,256]{3,2,1,0:T(8,128)(2,1)}, u32[]{:S(2)}) %copy-start) | copy-done | bytes 12582936
  85.7 3.4 %collective-permute-start.23 = (f32[64,256]{1,0:T(8,128)S(1)}, f32[64,256]{1,0:T(8,128)S(1)}, u32[]{:S(2)}, u32[]{:S(2)}) collective-permute-start(f32[64,256]{1,0:T(8,128)S(1)} %add_add_fusion.1.ca_ref), channel_id=1, source_target_pairs={{0,96},{16,112},{32,64},{48,80},{64,32},{80,48},{96,0},{112,16},{1... | collective-permute-start | bytes 196616 | tf_op jit(solution)/shard_map/ppermute | solution.py:101
  91.4 4.6 %copy-done.1 = bf16[12,8,256,256]{3,2,1,0:T(8,128)(2,1)S(1)} copy-done((bf16[12,8,256,256]{3,2,1,0:T(8,128)(2,1)S(1)}, bf16[12,8,256,256]{3,2,1,0:T(8,128)(2,1)}, u32[]{:S(2)}) %copy-start.1) | copy-done | bytes 12582936
  98.2 6.0 %collective-permute-start.26 = (f32[32,256]{1,0:T(8,128)S(1)}, f32[32,256]{1,0:T(8,128)S(1)}, u32[]{:S(2)}, u32[]{:S(2)}) collective-permute-start(f32[32,256]{1,0:T(8,128)S(1)} %shard_map.80), channel_id=1, source_target_pairs={{0,12},{1,13},{2,14},{3,15},{4,0},{5,1},{6,2},{7,3},{8,4},{9,5},{1... | collective-permute-start | bytes 98312 | tf_op jit(solution)/shard_map/ppermute | solution.py:58
  105.8 3.8 %collective-permute-done.25 = f32[32,256]{1,0:T(8,128)S(1)} collective-permute-done((f32[32,256]{1,0:T(8,128)S(1)}, f32[32,256]{1,0:T(8,128)S(1)}, u32[]{:S(2)}, u32[]{:S(2)}) %collective-permute-start.25) | collective-permute-done | bytes 32800 | tf_op jit(solution)/shard_map/ppermute | solution.py:58
  109.6 3.7 %collective-permute-start.29 = (f32[32,256]{1,0:T(8,128)S(1)}, f32[32,256]{1,0:T(8,128)S(1)}, u32[]{:S(2)}, u32[]{:S(2)}) collective-permute-start(f32[32,256]{1,0:T(8,128)S(1)} %add_add_fusion.2.refs_0_), channel_id=1, source_target_pairs={{0,3},{1,0},{2,1},{3,2},{4,7},{5,4},{6,5},{7,6},{8,11},{9,8},{10,9... | collective-permute-start | bytes 98312 | tf_op jit(solution)/shard_map/ppermute | solution.py:62
  113.3 2.7 %collective-permute-start.28 = (f32[32,256]{1,0:T(8,128)S(1)}, f32[32,256]{1,0:T(8,128)S(1)}, u32[]{:S(2)}, u32[]{:S(2)}) collective-permute-start(f32[32,256]{1,0:T(8,128)S(1)} %add_add_fusion.2.refs_0_), channel_id=1, source_target_pairs={{0,2},{1,3},{2,0},{3,1},{4,6},{5,7},{6,4},{7,5},{8,10},{9,11},{10,... | collective-permute-start | bytes 98312 | tf_op jit(solution)/shard_map/ppermute | solution.py:62
  116.0 2.8 %collective-permute-start.27 = (f32[32,256]{1,0:T(8,128)S(1)}, f32[32,256]{1,0:T(8,128)S(1)}, u32[]{:S(2)}, u32[]{:S(2)}) collective-permute-start(f32[32,256]{1,0:T(8,128)S(1)} %add_add_fusion.2.refs_0_), channel_id=1, source_target_pairs={{0,1},{1,2},{2,3},{3,0},{4,5},{5,6},{6,7},{7,4},{8,9},{9,10},{10,1... | collective-permute-start | bytes 98312 | tf_op jit(solution)/shard_map/ppermute | solution.py:62
  122.1 4.6 %copy-done.2 = bf16[12,8,256,256]{3,2,1,0:T(8,128)(2,1)S(1)} copy-done((bf16[12,8,256,256]{3,2,1,0:T(8,128)(2,1)S(1)}, bf16[12,8,256,256]{3,2,1,0:T(8,128)(2,1)}, u32[]{:S(2)}) %copy-start.2) | copy-done | bytes 12582936
  130.1 2.4 %collective-permute-start.32 = (f32[64,256]{1,0:T(8,128)S(1)}, f32[64,256]{1,0:T(8,128)S(1)}, u32[]{:S(2)}, u32[]{:S(2)}) collective-permute-start(f32[64,256]{1,0:T(8,128)S(1)} %add.88), channel_id=1, source_target_pairs={{0,32},{16,48},{32,0},{48,16},{64,96},{80,112},{96,64},{112,80},{1... | collective-permute-start | bytes 196616 | tf_op jit(solution)/shard_map/ppermute | solution.py:98
  136.8 2.6 %collective-permute-start.34 = (f32[64,256]{1,0:T(8,128)S(1)}, f32[64,256]{1,0:T(8,128)S(1)}, u32[]{:S(2)}, u32[]{:S(2)}) collective-permute-start(f32[64,256]{1,0:T(8,128)S(1)} %add_add_fusion.refs_4_), channel_id=1, source_target_pairs={{0,96},{16,112},{32,64},{48,80},{64,32},{80,48},{96,0},{112,16},{1... | collective-permute-start | bytes 196616 | tf_op jit(solution)/shard_map/ppermute | solution.py:101
  139.4 3.2 %collective-permute-done.34.refs_5_ = f32[64,256]{1,0:T(8,128)S(1)} collective-permute-done((f32[64,256]{1,0:T(8,128)S(1)}, f32[64,256]{1,0:T(8,128)S(1)}, u32[]{:S(2)}, u32[]{:S(2)}) %collective-permute-start.34) | collective-permute-done | bytes 65568 | tf_op jit(solution)/shard_map/ppermute | solution.py:101
  142.6 5.5 %shard_map.82 = (bf16[4,72,512]{2,1,0:T(8,128)(2,1)S(1)}, bf16[4,72,512]{2,1,0:T(8,128)(2,1)S(1)}, bf16[4,72,512]{2,1,0:T(8,128)(2,1)S(1)}, bf16[4,72,512]{2,1,0...) custom-call(s32[96]{0:T(128)S(1)} %bitcast.42, ...), custom_call_target="tpu_custom_call" | custom-call | tf_op jit(solution)/shard_map/pallas_call | solution.py:403
  148.2 6.1 %collective-permute-start.35 = (bf16[4,72,512]{2,1,0:T(8,128)(2,1)S(1)}, bf16[4,72,512]{2,1,0:T(8,128)(2,1)S(1)}, u32[]{:S(2)}, u32[]{:S(2)}) collective-permute-start(bf16[4,72,512]{2,1,0:T(8,128)(2,1)S(1)} %get-tuple-element.22), channel_id=1, source_target_pairs={{0,12},{1,13},{2,14},{3,15},{4,0},{5,1},{6,2},{7,3},{8,4},{9,5},{1... | collective-permute-start | bytes 884744 | tf_op jit(solution)/shard_map/ppermute | solution.py:58
  155.9 5.8 %collective-permute-done.35.b_ref = bf16[4,72,512]{2,1,0:T(8,128)(2,1)S(1)} collective-permute-done((bf16[4,72,512]{2,1,0:T(8,128)(2,1)S(1)}, bf16[4,72,512]{2,1,0:T(8,128)(2,1)S(1)}, u32[]{:S(2)}, u32[]{:S(2)}) %collective-permute-start.35) | collective-permute-done | bytes 294944 | tf_op jit(solution)/shard_map/ppermute | solution.py:58
  161.7 7.3 %collective-permute-done.36.c_ref = bf16[4,72,512]{2,1,0:T(8,128)(2,1)S(1)} collective-permute-done((bf16[4,72,512]{2,1,0:T(8,128)(2,1)S(1)}, bf16[4,72,512]{2,1,0:T(8,128)(2,1)S(1)}, u32[]{:S(2)}, u32[]{:S(2)}) %collective-permute-start.36) | collective-permute-done | bytes 294944 | tf_op jit(solution)/shard_map/ppermute | solution.py:58
  171.3 5.6 %collective-permute-start.39 = (bf16[72,512]{1,0:T(8,128)(2,1)S(1)}, bf16[72,512]{1,0:T(8,128)(2,1)S(1)}, u32[]{:S(2)}, u32[]{:S(2)}) collective-permute-start(bf16[72,512]{1,0:T(8,128)(2,1)S(1)} %get-tuple-element.27), channel_id=1, source_target_pairs={{0,3},{1,2},{2,1},{3,0},{4,7},{5,6},{6,5},{7,4},{8,11},{9,10},{10,... | collective-permute-start | bytes 221192 | tf_op jit(solution)/shard_map/ppermute | solution.py:74
  181.8 4.8 %collective-permute-done.40 = bf16[72,512]{1,0:T(8,128)(2,1)S(1)} collective-permute-done((bf16[72,512]{1,0:T(8,128)(2,1)S(1)}, bf16[72,512]{1,0:T(8,128)(2,1)S(1)}, u32[]{:S(2)}, u32[]{:S(2)}) %collective-permute-start.40) | collective-permute-done | bytes 73760 | tf_op jit(solution)/shard_map/ppermute | solution.py:70
  188.4 3.8 %collective-permute-done.43 = bf16[2,64,1024]{2,1,0:T(8,128)(2,1)S(1)} collective-permute-done((bf16[2,64,1024]{2,1,0:T(8,128)(2,1)S(1)}, bf16[2,64,1024]{2,1,0:T(8,128)(2,1)S(1)}, u32[]{:S(2)}, u32[]{:S(2)}) %collective-permute-start.43) | collective-permute-done | bytes 262176 | tf_op jit(solution)/shard_map/ppermute | solution.py:78
  192.4 5.0 %collective-permute-start.45 = (bf16[64,1024]{1,0:T(8,128)(2,1)S(1)}, bf16[64,1024]{1,0:T(8,128)(2,1)S(1)}, u32[]{:S(2)}, u32[]{:S(2)}) collective-permute-start(bf16[64,1024]{1,0:T(8,128)(2,1)S(1)} %fusion.4), channel_id=1, source_target_pairs={{0,128},{16,144},{32,160},{48,176},{64,192},{80,208},{96,224},{112... | collective-permute-start | bytes 393224 | tf_op jit(solution)/shard_map/ppermute | solution.py:86
  (105 shorter events, 64.6 us)
Async XLA Ops:
  2.3 7.3 %collective-permute-start = (bf16[1,72,512]{2,1,0:T(8,128)(2,1)S(1)}, bf16[1,72,512]{2,1,0:T(8,128)(2,1)S(1)}, u32[]{:S(2)}, u32[]{:S(2)}) collective-permute-start(bf16[1,72,512]{2,1,0:T(8,128)(2,1)S(1)} %maximum_bitcast_fusion), channel_id=1, source_target_pairs={{0,1},{1,0},{2,3},{3,2},{4,5},{5,4},{6,7},{7,6},{8,9},{9,8},{10,11... | collective-permute-start | bytes 221192 | tf_op jit(solution)/shard_map/ppermute | solution.py:66
  7.3 6.8 %collective-permute-start.5 = (bf16[1,72,1024]{2,1,0:T(8,128)(2,1)S(1)}, bf16[1,72,1024]{2,1,0:T(8,128)(2,1)S(1)}, u32[]{:S(2)}, u32[]{:S(2)}) collective-permute-start(bf16[1,72,1024]{2,1,0:T(8,128)(2,1)S(1)} %shard_map.77), channel_id=1, source_target_pairs={{0,128},{16,144},{32,160},{48,176},{64,192},{80,208},{96,224},{112... | collective-permute-start | bytes 442376 | tf_op jit(solution)/shard_map/ppermute | solution.py:86
  9.6 10.6 %collective-permute-start.1 = (bf16[2,72,512]{2,1,0:T(8,128)(2,1)S(1)}, bf16[2,72,512]{2,1,0:T(8,128)(2,1)S(1)}, u32[]{:S(2)}, u32[]{:S(2)}) collective-permute-start(bf16[2,72,512]{2,1,0:T(8,128)(2,1)S(1)} %pad_maximum_fusion.2), channel_id=1, source_target_pairs={{0,3},{1,2},{2,1},{3,0},{4,7},{5,6},{6,5},{7,4},{8,11},{9,10},{10,... | collective-permute-start | bytes 442376 | tf_op jit(solution)/shard_map/ppermute | solution.py:74
  14.1 6.7 %collective-permute-start.9 = (bf16[2,72,1024]{2,1,0:T(8,128)(2,1)S(1)}, bf16[2,72,1024]{2,1,0:T(8,128)(2,1)S(1)}, u32[]{:S(2)}, u32[]{:S(2)}) collective-permute-start(bf16[2,72,1024]{2,1,0:T(8,128)(2,1)S(1)} %pad_maximum_fusion.1.refs_4_.refs_13_), channel_id=1, source_target_pairs={{0,16},{16,0},{32,48},{48,32},{64,80},{80,64},{96,112},{112,96},{1... | collective-permute-start | bytes 884744 | tf_op jit(solution)/shard_map/ppermute | solution.py:82
  14.2 16.0 %collective-permute-start.8 = (bf16[2,72,1024]{2,1,0:T(8,128)(2,1)S(1)}, bf16[2,72,1024]{2,1,0:T(8,128)(2,1)S(1)}, u32[]{:S(2)}, u32[]{:S(2)}) collective-permute-start(bf16[2,72,1024]{2,1,0:T(8,128)(2,1)S(1)} %pad_maximum_fusion.1.refs_4_.refs_13_), channel_id=1, source_target_pairs={{0,96},{16,112},{32,0},{48,16},{64,32},{80,48},{96,64},{112,80},{1... | collective-permute-start | bytes 884744 | tf_op jit(solution)/shard_map/ppermute | solution.py:78
  17.0 14.8 %collective-permute-start.7 = (bf16[2,72,1024]{2,1,0:T(8,128)(2,1)S(1)}, bf16[2,72,1024]{2,1,0:T(8,128)(2,1)S(1)}, u32[]{:S(2)}, u32[]{:S(2)}) collective-permute-start(bf16[2,72,1024]{2,1,0:T(8,128)(2,1)S(1)} %pad_maximum_fusion.1.refs_4_.refs_13_), channel_id=1, source_target_pairs={{0,64},{16,80},{32,96},{48,112},{64,0},{80,16},{96,32},{112,48},{1... | collective-permute-start | bytes 884744 | tf_op jit(solution)/shard_map/ppermute | solution.py:78
  17.8 16.1 %collective-permute-start.6 = (bf16[2,72,1024]{2,1,0:T(8,128)(2,1)S(1)}, bf16[2,72,1024]{2,1,0:T(8,128)(2,1)S(1)}, u32[]{:S(2)}, u32[]{:S(2)}) collective-permute-start(bf16[2,72,1024]{2,1,0:T(8,128)(2,1)S(1)} %pad_maximum_fusion.1.refs_4_.refs_13_), channel_id=1, source_target_pairs={{0,32},{16,48},{32,64},{48,80},{64,96},{80,112},{96,0},{112,16},{1... | collective-permute-start | bytes 884744 | tf_op jit(solution)/shard_map/ppermute | solution.py:78
  20.3 13.7 %collective-permute-start.4 = (bf16[4,72,512]{2,1,0:T(8,128)(2,1)S(1)}, bf16[4,72,512]{2,1,0:T(8,128)(2,1)S(1)}, u32[]{:S(2)}, u32[]{:S(2)}) collective-permute-start(bf16[4,72,512]{2,1,0:T(8,128)(2,1)S(1)} %pad_maximum_fusion.refs_0_.refs_9_), channel_id=1, source_target_pairs={{0,12},{1,13},{2,14},{3,15},{4,0},{5,1},{6,2},{7,3},{8,4},{9,5},{1... | collective-permute-start | bytes 884744 | tf_op jit(solution)/shard_map/ppermute | solution.py:58
  20.8 15.2 %collective-permute-start.3 = (bf16[4,72,512]{2,1,0:T(8,128)(2,1)S(1)}, bf16[4,72,512]{2,1,0:T(8,128)(2,1)S(1)}, u32[]{:S(2)}, u32[]{:S(2)}) collective-permute-start(bf16[4,72,512]{2,1,0:T(8,128)(2,1)S(1)} %pad_maximum_fusion.refs_0_.refs_9_), channel_id=1, source_target_pairs={{0,8},{1,9},{2,10},{3,11},{4,12},{5,13},{6,14},{7,15},{8,0},{9,1},... | collective-permute-start | bytes 884744 | tf_op jit(solution)/shard_map/ppermute | solution.py:58
  30.2 8.3 %collective-permute-start.2 = (bf16[4,72,512]{2,1,0:T(8,128)(2,1)S(1)}, bf16[4,72,512]{2,1,0:T(8,128)(2,1)S(1)}, u32[]{:S(2)}, u32[]{:S(2)}) collective-permute-start(bf16[4,72,512]{2,1,0:T(8,128)(2,1)S(1)} %pad_maximum_fusion.refs_0_.refs_9_), channel_id=1, source_target_pairs={{0,4},{1,5},{2,6},{3,7},{4,8},{5,9},{6,10},{7,11},{8,12},{9,13},{1... | collective-permute-start | bytes 884744 | tf_op jit(solution)/shard_map/ppermute | solution.py:58
  31.8 6.7 %collective-permute-start.12 = (bf16[2,72,1024]{2,1,0:T(8,128)(2,1)S(1)}, bf16[2,72,1024]{2,1,0:T(8,128)(2,1)S(1)}, u32[]{:S(2)}, u32[]{:S(2)}) collective-permute-start(bf16[2,72,1024]{2,1,0:T(8,128)(2,1)S(1)} %collective-permute-done.8.refs_7_.refs_16_), channel_id=1, source_target_pairs={{0,16},{16,0},{32,48},{48,32},{64,80},{80,64},{96,112},{112,96},{1... | collective-permute-start | bytes 884744 | tf_op jit(solution)/shard_map/ppermute | solution.py:82
  45.6 6.8 %collective-permute-start.15 = (f32[32,256]{1,0:T(8,128)S(1)}, f32[32,256]{1,0:T(8,128)S(1)}, u32[]{:S(2)}, u32[]{:S(2)}) collective-permute-start(f32[32,256]{1,0:T(8,128)S(1)} %get-tuple-element.17), channel_id=1, source_target_pairs={{0,12},{1,13},{2,14},{3,15},{4,0},{5,1},{6,2},{7,3},{8,4},{9,5},{1... | collective-permute-start | bytes 98312 | tf_op jit(solution)/shard_map/ppermute | solution.py:58
  48.2 6.2 %collective-permute-start.14 = (f32[32,256]{1,0:T(8,128)S(1)}, f32[32,256]{1,0:T(8,128)S(1)}, u32[]{:S(2)}, u32[]{:S(2)}) collective-permute-start(f32[32,256]{1,0:T(8,128)S(1)} %get-tuple-element.17), channel_id=1, source_target_pairs={{0,8},{1,9},{2,10},{3,11},{4,12},{5,13},{6,14},{7,15},{8,0},{9,1},... | collective-permute-start | bytes 98312 | tf_op jit(solution)/shard_map/ppermute | solution.py:58
  55.9 11.2 %collective-permute-start.18 = (f32[32,256]{1,0:T(8,128)S(1)}, f32[32,256]{1,0:T(8,128)S(1)}, u32[]{:S(2)}, u32[]{:S(2)}) collective-permute-start(f32[32,256]{1,0:T(8,128)S(1)} %add_add_fusion.3.refs_0_), channel_id=1, source_target_pairs={{0,3},{1,0},{2,1},{3,2},{4,7},{5,4},{6,5},{7,6},{8,11},{9,8},{10,9... | collective-permute-start | bytes 98312 | tf_op jit(solution)/shard_map/ppermute | solution.py:62
  61.8 7.8 %collective-permute-start.17 = (f32[32,256]{1,0:T(8,128)S(1)}, f32[32,256]{1,0:T(8,128)S(1)}, u32[]{:S(2)}, u32[]{:S(2)}) collective-permute-start(f32[32,256]{1,0:T(8,128)S(1)} %add_add_fusion.3.refs_0_), channel_id=1, source_target_pairs={{0,2},{1,3},{2,0},{3,1},{4,6},{5,7},{6,4},{7,5},{8,10},{9,11},{10,... | collective-permute-start | bytes 98312 | tf_op jit(solution)/shard_map/ppermute | solution.py:62
  64.2 6.0 %collective-permute-start.16 = (f32[32,256]{1,0:T(8,128)S(1)}, f32[32,256]{1,0:T(8,128)S(1)}, u32[]{:S(2)}, u32[]{:S(2)}) collective-permute-start(f32[32,256]{1,0:T(8,128)S(1)} %add_add_fusion.3.refs_0_), channel_id=1, source_target_pairs={{0,1},{1,2},{2,3},{3,0},{4,5},{5,6},{6,7},{7,4},{8,9},{9,10},{10,1... | collective-permute-start | bytes 98312 | tf_op jit(solution)/shard_map/ppermute | solution.py:62
  98.2 7.6 %collective-permute-start.26 = (f32[32,256]{1,0:T(8,128)S(1)}, f32[32,256]{1,0:T(8,128)S(1)}, u32[]{:S(2)}, u32[]{:S(2)}) collective-permute-start(f32[32,256]{1,0:T(8,128)S(1)} %shard_map.80), channel_id=1, source_target_pairs={{0,12},{1,13},{2,14},{3,15},{4,0},{5,1},{6,2},{7,3},{8,4},{9,5},{1... | collective-permute-start | bytes 98312 | tf_op jit(solution)/shard_map/ppermute | solution.py:58
  109.6 9.2 %collective-permute-start.29 = (f32[32,256]{1,0:T(8,128)S(1)}, f32[32,256]{1,0:T(8,128)S(1)}, u32[]{:S(2)}, u32[]{:S(2)}) collective-permute-start(f32[32,256]{1,0:T(8,128)S(1)} %add_add_fusion.2.refs_0_), channel_id=1, source_target_pairs={{0,3},{1,0},{2,1},{3,2},{4,7},{5,4},{6,5},{7,6},{8,11},{9,8},{10,9... | collective-permute-start | bytes 98312 | tf_op jit(solution)/shard_map/ppermute | solution.py:62
  113.3 7.8 %collective-permute-start.28 = (f32[32,256]{1,0:T(8,128)S(1)}, f32[32,256]{1,0:T(8,128)S(1)}, u32[]{:S(2)}, u32[]{:S(2)}) collective-permute-start(f32[32,256]{1,0:T(8,128)S(1)} %add_add_fusion.2.refs_0_), channel_id=1, source_target_pairs={{0,2},{1,3},{2,0},{3,1},{4,6},{5,7},{6,4},{7,5},{8,10},{9,11},{10,... | collective-permute-start | bytes 98312 | tf_op jit(solution)/shard_map/ppermute | solution.py:62
  116.0 6.0 %collective-permute-start.27 = (f32[32,256]{1,0:T(8,128)S(1)}, f32[32,256]{1,0:T(8,128)S(1)}, u32[]{:S(2)}, u32[]{:S(2)}) collective-permute-start(f32[32,256]{1,0:T(8,128)S(1)} %add_add_fusion.2.refs_0_), channel_id=1, source_target_pairs={{0,1},{1,2},{2,3},{3,0},{4,5},{5,6},{6,7},{7,4},{8,9},{9,10},{10,1... | collective-permute-start | bytes 98312 | tf_op jit(solution)/shard_map/ppermute | solution.py:62
  130.1 6.0 %collective-permute-start.32 = (f32[64,256]{1,0:T(8,128)S(1)}, f32[64,256]{1,0:T(8,128)S(1)}, u32[]{:S(2)}, u32[]{:S(2)}) collective-permute-start(f32[64,256]{1,0:T(8,128)S(1)} %add.88), channel_id=1, source_target_pairs={{0,32},{16,48},{32,0},{48,16},{64,96},{80,112},{96,64},{112,80},{1... | collective-permute-start | bytes 196616 | tf_op jit(solution)/shard_map/ppermute | solution.py:98
  148.1 29.6 %collective-permute-start.41 = (bf16[8,64,1024]{2,1,0:T(8,128)(2,1)S(1)}, bf16[8,64,1024]{2,1,0:T(8,128)(2,1)S(1)}, u32[]{:S(2)}, u32[]{:S(2)}) collective-permute-start(bf16[8,64,1024]{2,1,0:T(8,128)(2,1)S(1)} %get-tuple-element.31), channel_id=1, source_target_pairs={{0,16},{16,0},{32,48},{48,32},{64,80},{80,64},{96,112},{112,96},{1... | collective-permute-start | bytes 3145736 | tf_op jit(solution)/shard_map/ppermute | solution.py:82
  148.2 13.5 %collective-permute-start.35 = (bf16[4,72,512]{2,1,0:T(8,128)(2,1)S(1)}, bf16[4,72,512]{2,1,0:T(8,128)(2,1)S(1)}, u32[]{:S(2)}, u32[]{:S(2)}) collective-permute-start(bf16[4,72,512]{2,1,0:T(8,128)(2,1)S(1)} %get-tuple-element.22), channel_id=1, source_target_pairs={{0,12},{1,13},{2,14},{3,15},{4,0},{5,1},{6,2},{7,3},{8,4},{9,5},{1... | collective-permute-start | bytes 884744 | tf_op jit(solution)/shard_map/ppermute | solution.py:58
  154.3 14.7 %collective-permute-start.36 = (bf16[4,72,512]{2,1,0:T(8,128)(2,1)S(1)}, bf16[4,72,512]{2,1,0:T(8,128)(2,1)S(1)}, u32[]{:S(2)}, u32[]{:S(2)}) collective-permute-start(bf16[4,72,512]{2,1,0:T(8,128)(2,1)S(1)} %get-tuple-element.23), channel_id=1, source_target_pairs={{0,8},{1,9},{2,10},{3,11},{4,12},{5,13},{6,14},{7,15},{8,0},{9,1},... | collective-permute-start | bytes 884744 | tf_op jit(solution)/shard_map/ppermute | solution.py:58
  155.4 14.3 %collective-permute-start.37 = (bf16[4,72,512]{2,1,0:T(8,128)(2,1)S(1)}, bf16[4,72,512]{2,1,0:T(8,128)(2,1)S(1)}, u32[]{:S(2)}, u32[]{:S(2)}) collective-permute-start(bf16[4,72,512]{2,1,0:T(8,128)(2,1)S(1)} %get-tuple-element.24), channel_id=1, source_target_pairs={{0,4},{1,5},{2,6},{3,7},{4,8},{5,9},{6,10},{7,11},{8,12},{9,13},{1... | collective-permute-start | bytes 884744 | tf_op jit(solution)/shard_map/ppermute | solution.py:58
  169.8 10.3 %collective-permute-start.38 = (bf16[72,512]{1,0:T(8,128)(2,1)S(1)}, bf16[72,512]{1,0:T(8,128)(2,1)S(1)}, u32[]{:S(2)}, u32[]{:S(2)}) collective-permute-start(bf16[72,512]{1,0:T(8,128)(2,1)S(1)} %get-tuple-element.26), channel_id=1, source_target_pairs={{0,1},{1,0},{2,3},{3,2},{4,5},{5,4},{6,7},{7,6},{8,9},{9,8},{10,11... | collective-permute-start | bytes 221192 | tf_op jit(solution)/shard_map/ppermute | solution.py:66
  171.3 10.5 %collective-permute-start.39 = (bf16[72,512]{1,0:T(8,128)(2,1)S(1)}, bf16[72,512]{1,0:T(8,128)(2,1)S(1)}, u32[]{:S(2)}, u32[]{:S(2)}) collective-permute-start(bf16[72,512]{1,0:T(8,128)(2,1)S(1)} %get-tuple-element.27), channel_id=1, source_target_pairs={{0,3},{1,2},{2,1},{3,0},{4,7},{5,6},{6,5},{7,4},{8,11},{9,10},{10,... | collective-permute-start | bytes 221192 | tf_op jit(solution)/shard_map/ppermute | solution.py:74
  176.9 9.7 %collective-permute-start.40 = (bf16[72,512]{1,0:T(8,128)(2,1)S(1)}, bf16[72,512]{1,0:T(8,128)(2,1)S(1)}, u32[]{:S(2)}, u32[]{:S(2)}) collective-permute-start(bf16[72,512]{1,0:T(8,128)(2,1)S(1)} %get-tuple-element.28), channel_id=1, source_target_pairs={{0,2},{1,3},{2,0},{3,1},{4,6},{5,7},{6,4},{7,5},{8,10},{9,11},{10,... | collective-permute-start | bytes 221192 | tf_op jit(solution)/shard_map/ppermute | solution.py:70
  178.0 9.3 %collective-permute-start.42 = (bf16[2,64,1024]{2,1,0:T(8,128)(2,1)S(1)}, bf16[2,64,1024]{2,1,0:T(8,128)(2,1)S(1)}, u32[]{:S(2)}, u32[]{:S(2)}) collective-permute-start(bf16[2,64,1024]{2,1,0:T(8,128)(2,1)S(1)} %get-tuple-element.32), channel_id=1, source_target_pairs={{0,96},{16,112},{32,0},{48,16},{64,32},{80,48},{96,64},{112,80},{1... | collective-permute-start | bytes 786440 | tf_op jit(solution)/shard_map/ppermute | solution.py:78
  178.1 10.3 %collective-permute-start.44 = (bf16[2,64,1024]{2,1,0:T(8,128)(2,1)S(1)}, bf16[2,64,1024]{2,1,0:T(8,128)(2,1)S(1)}, u32[]{:S(2)}, u32[]{:S(2)}) collective-permute-start(bf16[2,64,1024]{2,1,0:T(8,128)(2,1)S(1)} %get-tuple-element.33), channel_id=1, source_target_pairs={{0,32},{16,48},{32,64},{48,80},{64,96},{80,112},{96,0},{112,16},{1... | collective-permute-start | bytes 786440 | tf_op jit(solution)/shard_map/ppermute | solution.py:78
  180.1 12.1 %collective-permute-start.43 = (bf16[2,64,1024]{2,1,0:T(8,128)(2,1)S(1)}, bf16[2,64,1024]{2,1,0:T(8,128)(2,1)S(1)}, u32[]{:S(2)}, u32[]{:S(2)}) collective-permute-start(bf16[2,64,1024]{2,1,0:T(8,128)(2,1)S(1)} %get-tuple-element.34), channel_id=1, source_target_pairs={{0,64},{16,80},{32,96},{48,112},{64,0},{80,16},{96,32},{112,48},{1... | collective-permute-start | bytes 786440 | tf_op jit(solution)/shard_map/ppermute | solution.py:78
  192.4 8.0 %collective-permute-start.45 = (bf16[64,1024]{1,0:T(8,128)(2,1)S(1)}, bf16[64,1024]{1,0:T(8,128)(2,1)S(1)}, u32[]{:S(2)}, u32[]{:S(2)}) collective-permute-start(bf16[64,1024]{1,0:T(8,128)(2,1)S(1)} %fusion.4), channel_id=1, source_target_pairs={{0,128},{16,144},{32,160},{48,176},{64,192},{80,208},{96,224},{112... | collective-permute-start | bytes 393224 | tf_op jit(solution)/shard_map/ppermute | solution.py:86
  (22 other events, 218.7 us)

commit v7 on v6

--- a/solution.py
+++ b/solution.py
@@ -140,34 +140,16 @@
     return (count_ref[0] + GROUP - 1) // GROUP
 
 
-def over_tiles(index_ref, count_ref, before, step, after):
+def over_tiles(index_ref, count_ref, step):
     last = count_ref[0] - 1
 
     def turn(i, carry):
-        before(i)
         for k in range(GROUP):
             row, column = entry_of(index_ref, i * GROUP + k, last)
             step(i, k, i * GROUP + k, row, column)
-        after(i)
         return carry
 
     lax.fori_loop(0, turns_of(count_ref), turn, 0)
-
-
-def start_tiles(count_ref, g_hbm, g_ref, sems):
-    def turn(i, carry):
-        pltpu.make_async_copy(g_hbm.at[i], g_ref.at[i], sems.at[i]).start()
-        return carry
-
-    lax.fori_loop(0, turns_of(count_ref), turn, 0)
-
-
-def wait_tiles(g_hbm, g_ref, sems):
-    return lambda i: pltpu.make_async_copy(g_hbm.at[i], g_ref.at[i], sems.at[i]).wait()
-
-
-def nothing(i):
-    pass
 
 
 def store_pairs(acc_ref, out_ref):
@@ -196,8 +178,8 @@
 
 def first_kernel(index_ref, count_ref, pos_ref, *refs):
     xs, ys = (refs[0:4], refs[4:12])
-    out_ref, m_ref, n_ref, g_hbm = refs[12:16]
-    xt_ref, yt_ref, xr_ref, w_ref, acc_ref, g_ref, sems, g_sems = refs[16:]
+    out_ref, m_ref, n_ref, g_ref = refs[12:16]
+    xt_ref, yt_ref, xr_ref, w_ref, acc_ref, sems = refs[16:]
     copies = piece_copies(xs, ys, xt_ref, yt_ref, sems)
     for copy in copies:
         copy.start()
@@ -235,17 +217,8 @@
         g_ref[i, k] = g
         acc_ref[row] += contract_last(live(w_ref[column], t, count_ref), g)
 
-    def send(i):
-        pltpu.make_async_copy(g_ref.at[i], g_hbm.at[i], g_sems.at[i]).start()
-
-    over_tiles(index_ref, count_ref, nothing, step, send)
+    over_tiles(index_ref, count_ref, step)
     store_pairs(acc_ref, out_ref)
-
-    def sent(i, carry):
-        pltpu.make_async_copy(g_ref.at[i], g_hbm.at[i], g_sems.at[i]).wait()
-        return carry
-
-    lax.fori_loop(0, turns_of(count_ref), sent, 0)
 
 
 def sum_of(refs):
@@ -257,8 +230,7 @@
 
 def column_kernel(index_ref, count_ref, *refs):
     r_refs = refs[0:4]
-    m_ref, g_hbm, out_ref, w_ref, acc_ref, g_ref, sems = refs[4:]
-    start_tiles(count_ref, g_hbm, g_ref, sems)
+    m_ref, g_ref, out_ref, w_ref, acc_ref = refs[4:]
     acc_ref[...] = jnp.zeros_like(acc_ref)
     u = m_ref[...] / sum_of(r_refs)
     for row in range(TR):
@@ -267,12 +239,11 @@
     def step(i, k, t, row, column):
         acc_ref[column] += jnp.dot(live(w_ref[row], t, count_ref), g_ref[i, k], preferred_element_type=f32)
 
-    over_tiles(index_ref, count_ref, wait_tiles(g_hbm, g_ref, sems), step, nothing)
+    over_tiles(index_ref, count_ref, step)
     store_pairs(acc_ref, out_ref)
 
 
-def row_kernel(index_ref, count_ref, ca_ref, cb_ref, n_ref, g_hbm, out_ref, w_ref, acc_ref, g_ref, sems):
-    start_tiles(count_ref, g_hbm, g_ref, sems)
+def row_kernel(index_ref, count_ref, ca_ref, cb_ref, n_ref, g_ref, out_ref, w_ref, acc_ref):
     acc_ref[...] = jnp.zeros_like(acc_ref)
     v = n_ref[...] / (ca_ref[...] + cb_ref[...])
     for column in range(TC):
@@ -281,21 +252,20 @@
     def step(i, k, t, row, column):
         acc_ref[row] += contract_last(live(w_ref[column], t, count_ref), g_ref[i, k])
 
-    over_tiles(index_ref, count_ref, wait_tiles(g_hbm, g_ref, sems), step, nothing)
+    over_tiles(index_ref, count_ref, step)
     store_pairs(acc_ref, out_ref)
 
 
 def grad_kernel(index_ref, count_ref, pos_ref, *refs):
-    r_refs, c_refs, m_ref, n_ref, g_hbm = (refs[0:4], refs[4:6], *refs[6:9])
+    r_refs, c_refs, m_ref, n_ref, g_ref = (refs[0:4], refs[4:6], *refs[6:9])
     refs = refs[9:]
     xs, ys = (refs[0:4], refs[4:12])
     spec_outs, photo_outs, share_ref = (refs[12:16], refs[16:18], refs[18])
     xt_ref, yt_ref, u_ref, v_ref, wy_ref, vx_ref, spec_acc, photo_acc = refs[19:27]
-    g_ref, sems, g_sems = refs[27:]
+    (sems,) = refs[27:]
     copies = piece_copies(xs, ys, xt_ref, yt_ref, sems)
     for copy in copies:
         copy.start()
-    start_tiles(count_ref, g_hbm, g_ref, g_sems)
     u_all = m_ref[...] / sum_of(r_refs)
     total = sum_of(c_refs)
     v_all = n_ref[...] / total
@@ -345,7 +315,7 @@
         spec_acc[row_local] += contract_last(live(wy_ref[column_local], t, count_ref), g)
         photo_acc[column_local] += jnp.dot(live(vx_ref[row_local], t, count_ref), g, preferred_element_type=f32)
 
-    over_tiles(index_ref, count_ref, wait_tiles(g_hbm, g_ref, g_sems), step, nothing)
+    over_tiles(index_ref, count_ref, step)
 
     def store_y(h):
         def store(j, carry):
@@ -406,7 +376,7 @@
         out_specs=[spec for spec, _, _ in outs],
         out_shape=[kept(s, d) if spec is KEPT else jax.ShapeDtypeStruct(s, d) for spec, s, d in outs],
         scratch_shapes=scratch,
-        compiler_params=pltpu.CompilerParams(vmem_limit_bytes=40 << 20),
+        compiler_params=pltpu.CompilerParams(vmem_limit_bytes=18 << 20),
     )(*args)
 
 
@@ -440,8 +410,6 @@
     xs = [x0] + [shift_y(x0, k) for k in (1, 2, 3)]
     ys = ys + [swap_core(y) for y in ys]
 
-    tiles = pltpu.VMEM((TURNS, GROUP, TILE, TILE), bf16)
-    tile_sems = pltpu.SemaphoreType.DMA((TURNS,))
     row_acc = [pltpu.VMEM((TC, 16, TILE), bf16), pltpu.VMEM((TR, 16, TILE), f32)]
     column_acc = [pltpu.VMEM((TR, 16, TILE), bf16), pltpu.VMEM((TC, 16, TILE), f32)]
     blocks = [pltpu.VMEM((SLOTS, EXT, SB), bf16), pltpu.VMEM((SLOTS, EXT, PB), bf16)]
@@ -450,30 +418,30 @@
         first_kernel, [SMEM] * 3 + [ANY] * 12,
         [
             (KEPT, (TR, TILE), f32), (KEPT, (TR, TILE), f32), (KEPT, (TC, TILE), f32),
-            (ANY, (TURNS, GROUP, TILE, TILE), bf16),
+            (KEPT, (TURNS, GROUP, TILE, TILE), bf16),
         ],
-        blocks + [pltpu.VMEM((TR, TILE, F), bf16)] + row_acc + [tiles, piece_sems, tile_sems],
+        blocks + [pltpu.VMEM((TR, TILE, F), bf16)] + row_acc + [piece_sems],
         *meta, *xs, *ys,
     )
-    m, n = in_vmem([m, n])
+    m, n, g = in_vmem([m, n, g])
     lists = meta[0:2]
 
     def columns(rs):
         return call(
-            column_kernel, [SMEM] * 2 + [VMEM] * 5 + [ANY], [(KEPT, (TC, TILE), f32)],
-            column_acc + [tiles, tile_sems], *lists, *rs, m, g,
+            column_kernel, [SMEM] * 2 + [VMEM] * 6, [(KEPT, (TC, TILE), f32)],
+            column_acc, *lists, *rs, m, g,
         )[0]
 
     rs = in_vmem(sum_photo(r))
     cs = in_vmem(sum_spec(columns(rs)))
     (r,) = call(
-        row_kernel, [SMEM] * 2 + [VMEM] * 3 + [ANY], [(KEPT, (TR, TILE), f32)],
-        row_acc + [tiles, tile_sems], *lists, *cs, n, g,
+        row_kernel, [SMEM] * 2 + [VMEM] * 4, [(KEPT, (TR, TILE), f32)],
+        row_acc, *lists, *cs, n, g,
     )
     rs = in_vmem(sum_photo(r))
     cs = in_vmem(sum_spec(columns(rs)))
     *parts, share = call(
-        grad_kernel, [SMEM] * 3 + [VMEM] * 8 + [ANY] * 13,
+        grad_kernel, [SMEM] * 3 + [VMEM] * 9 + [ANY] * 12,
         [(KEPT, (4, EXT, SB), bf16)] * 4 + [(KEPT, (8, F, PB), bf16)] * 2 + [(KEPT, (4, 8, TILE), f32)],
         blocks
         + [
@@ -483,7 +451,7 @@
             pltpu.VMEM((TR, F, TILE), bf16),
             pltpu.VMEM((TR, WROWS, TILE), f32),
             pltpu.VMEM((TC, F, TILE), f32),
-            tiles, piece_sems, tile_sems,
+            piece_sems,
         ],
         *meta, *rs, *cs, m, n, g, *xs, *ys,
     )

time: 205 us -> 187 us (0.912)
  local copies, waits for them, and re-layouts: 16.8 us -> 3.04 us
  starting transfers between devices: 91.7 us -> 89 us
  Pallas kernels: 18 us -> 15.9 us
    unnamed x16 -> x10, local copies, waits for them, and re-layouts: 16 us -> 2.25 us
    pallas_call x7, Pallas kernels: 18 us -> 15.9 us  [call(): pl.pallas_call(kernel, in_specs=in_specs, out_specs=[spec for spec, _, _...]
  transfers between devices with their start and end apart: 46 -> 46, of which waited for: 32 -> 31; matrix products, arithmetic and copies ran while one was open for 1% -> 1% of each run, Pallas kernels for 0% -> 0%
where the time goes in v7:
time: 187 us; the launch traced here: 183 us
  starting transfers between devices  89 us (48%)
  waiting for transfers between devices  70.8 us (38%)
  Pallas kernels  15.9 us (9%)
  other arithmetic  3.13 us (2%)
  local copies, waits for them, and re-layouts  3.04 us (2%)
    ppermute x12, waiting for transfers between devices, shift_y(): return lax.ppermute(a, 'photo', photo_perm(shift(k), same))  25.1 us
    ppermute x12, starting transfers between devices, shift_y(): return lax.ppermute(a, 'photo', photo_perm(shift(k), same))  24.3 us
    ppermute x6, starting transfers between devices, shift_z(): return lax.ppermute(a, 'photo', photo_perm(same, shift(k)))  19.7 us
    pallas_call x7, Pallas kernels, call(): pl.pallas_call(kernel, in_specs=in_specs, out_specs=[spec for spec, _, _...  15.9 us
    ppermute x6, waiting for transfers between devices, shift_x(): return lax.ppermute(a, 'spec', spec_perm(same, shift(k), same))  14.3 us
    ppermute x2, starting transfers between devices, mirror_z(): return lax.ppermute(a, 'photo', photo_perm(same, mirror))  10.1 us
    ppermute x6, starting transfers between devices, shift_x(): return lax.ppermute(a, 'spec', spec_perm(same, shift(k), same))  8.47 us
    ppermute x6, waiting for transfers between devices, sum_spec(): lax.ppermute(a, 'spec', spec_perm(fl, fx, same))  7.74 us
  transfers between devices with their start and end apart: 46, of which 31 were waited for; matrix products, arithmetic and copies ran while one was open for 1% of the time, Pallas kernels for 0%

profile of v7, /device:TPU:8, one launch (start us, length us, event | category | flops | bytes accessed | tf_op | source)
XLA Modules:
  0.0 183.4 jit_solution(1522604072274294371)
XLA Ops:
  2.3 3.4 %collective-permute-start = (bf16[1,72,512]{2,1,0:T(8,128)(2,1)S(1)}, bf16[1,72,512]{2,1,0:T(8,128)(2,1)S(1)}, u32[]{:S(2)}, u32[]{:S(2)}) collective-permute-start(bf16[1,72,512]{2,1,0:T(8,128)(2,1)S(1)} %maximum_bitcast_fusion), channel_id=1, source_target_pairs={{0,1},{1,0},{2,3},{3,2},{4,5},{5,4},{6,7},{7,6},{8,9},{9,8},{10,11... | collective-permute-start | bytes 221192 | tf_op jit(solution)/shard_map/ppermute | solution.py:66
  9.6 4.5 %collective-permute-start.1 = (bf16[2,72,512]{2,1,0:T(8,128)(2,1)S(1)}, bf16[2,72,512]{2,1,0:T(8,128)(2,1)S(1)}, u32[]{:S(2)}, u32[]{:S(2)}) collective-permute-start(bf16[2,72,512]{2,1,0:T(8,128)(2,1)S(1)} %pad_maximum_fusion.2), channel_id=1, source_target_pairs={{0,3},{1,2},{2,1},{3,0},{4,7},{5,6},{6,5},{7,4},{8,11},{9,10},{10,... | collective-permute-start | bytes 442376 | tf_op jit(solution)/shard_map/ppermute | solution.py:74
  14.2 2.8 %collective-permute-start.8 = (bf16[2,72,1024]{2,1,0:T(8,128)(2,1)S(1)}, bf16[2,72,1024]{2,1,0:T(8,128)(2,1)S(1)}, u32[]{:S(2)}, u32[]{:S(2)}) collective-permute-start(bf16[2,72,1024]{2,1,0:T(8,128)(2,1)S(1)} %pad_maximum_fusion.1.refs_4_.refs_13_), channel_id=1, source_target_pairs={{0,96},{16,112},{32,0},{48,16},{64,32},{80,48},{96,64},{112,80},{1... | collective-permute-start | bytes 884744 | tf_op jit(solution)/shard_map/ppermute | solution.py:78
  20.8 2.6 %collective-permute-start.3 = (bf16[4,72,512]{2,1,0:T(8,128)(2,1)S(1)}, bf16[4,72,512]{2,1,0:T(8,128)(2,1)S(1)}, u32[]{:S(2)}, u32[]{:S(2)}) collective-permute-start(bf16[4,72,512]{2,1,0:T(8,128)(2,1)S(1)} %pad_maximum_fusion.refs_0_.refs_9_), channel_id=1, source_target_pairs={{0,8},{1,9},{2,10},{3,11},{4,12},{5,13},{6,14},{7,15},{8,0},{9,1},... | collective-permute-start | bytes 884744 | tf_op jit(solution)/shard_map/ppermute | solution.py:58
  23.4 6.9 %collective-permute-done.8.refs_7_.refs_16_ = bf16[2,72,1024]{2,1,0:T(8,128)(2,1)S(1)} collective-permute-done((bf16[2,72,1024]{2,1,0:T(8,128)(2,1)S(1)}, bf16[2,72,1024]{2,1,0:T(8,128)(2,1)S(1)}, u32[]{:S(2)}, u32[]{:S(2)}) %collective-permute-start.8) | collective-permute-done | bytes 294944 | tf_op jit(solution)/shard_map/ppermute | solution.py:78
  36.0 2.5 %collective-permute-done.2.refs_1_.refs_10_ = bf16[4,72,512]{2,1,0:T(8,128)(2,1)S(1)} collective-permute-done((bf16[4,72,512]{2,1,0:T(8,128)(2,1)S(1)}, bf16[4,72,512]{2,1,0:T(8,128)(2,1)S(1)}, u32[]{:S(2)}, u32[]{:S(2)}) %collective-permute-start.2) | collective-permute-done | bytes 294944 | tf_op jit(solution)/shard_map/ppermute | solution.py:58
  39.2 5.4 %shard_map.78 = (f32[32,256]{1,0:T(8,128)S(1)}, f32[32,256]{1,0:T(8,128)S(1)}, f32[64,256]{1,0:T(8,128)S(1)}, bf16[12,8,256,256]{3,2,1,0:T(8,128)(2,1)S(1)}) custom-call(s32[96]{0:T(128)S(1)} %bitcast.38, s32[1]{0:T(128)} %bitcast.32.count_ref, s32[2]{0:T(128)S(1)} %pad_add_fusion.pos_ref, bf16[4,72,512]{2,1,0:T(8,128)(2,1)S(1)} %pad_maximum_fusion.refs_0_.refs_9_, ...), custom_call_target="tpu_custom_call" | custom-call | tf_op jit(solution)/shard_map/pallas_call | solution.py:373
  44.7 2.6 %collective-permute-start.15 = (f32[32,256]{1,0:T(8,128)S(1)}, f32[32,256]{1,0:T(8,128)S(1)}, u32[]{:S(2)}, u32[]{:S(2)}) collective-permute-start(f32[32,256]{1,0:T(8,128)S(1)} %get-tuple-element.17), channel_id=1, source_target_pairs={{0,12},{1,13},{2,14},{3,15},{4,0},{5,1},{6,2},{7,3},{8,4},{9,5},{1... | collective-permute-start | bytes 98312 | tf_op jit(solution)/shard_map/ppermute | solution.py:58
  47.3 3.7 %collective-permute-start.14 = (f32[32,256]{1,0:T(8,128)S(1)}, f32[32,256]{1,0:T(8,128)S(1)}, u32[]{:S(2)}, u32[]{:S(2)}) collective-permute-start(f32[32,256]{1,0:T(8,128)S(1)} %get-tuple-element.17), channel_id=1, source_target_pairs={{0,8},{1,9},{2,10},{3,11},{4,12},{5,13},{6,14},{7,15},{8,0},{9,1},... | collective-permute-start | bytes 98312 | tf_op jit(solution)/shard_map/ppermute | solution.py:58
  54.9 6.0 %collective-permute-start.18 = (f32[32,256]{1,0:T(8,128)S(1)}, f32[32,256]{1,0:T(8,128)S(1)}, u32[]{:S(2)}, u32[]{:S(2)}) collective-permute-start(f32[32,256]{1,0:T(8,128)S(1)} %add_add_fusion.3.refs_0_), channel_id=1, source_target_pairs={{0,3},{1,0},{2,1},{3,2},{4,7},{5,4},{6,5},{7,6},{8,11},{9,8},{10,9... | collective-permute-start | bytes 98312 | tf_op jit(solution)/shard_map/ppermute | solution.py:62
  60.9 2.4 %collective-permute-start.17 = (f32[32,256]{1,0:T(8,128)S(1)}, f32[32,256]{1,0:T(8,128)S(1)}, u32[]{:S(2)}, u32[]{:S(2)}) collective-permute-start(f32[32,256]{1,0:T(8,128)S(1)} %add_add_fusion.3.refs_0_), channel_id=1, source_target_pairs={{0,2},{1,3},{2,0},{3,1},{4,6},{5,7},{6,4},{7,5},{8,10},{9,11},{10,... | collective-permute-start | bytes 98312 | tf_op jit(solution)/shard_map/ppermute | solution.py:62
  63.3 2.8 %collective-permute-start.16 = (f32[32,256]{1,0:T(8,128)S(1)}, f32[32,256]{1,0:T(8,128)S(1)}, u32[]{:S(2)}, u32[]{:S(2)}) collective-permute-start(f32[32,256]{1,0:T(8,128)S(1)} %add_add_fusion.3.refs_0_), channel_id=1, source_target_pairs={{0,1},{1,2},{2,3},{3,0},{4,5},{5,6},{6,7},{7,4},{8,9},{9,10},{10,1... | collective-permute-start | bytes 98312 | tf_op jit(solution)/shard_map/ppermute | solution.py:62
  66.1 2.6 %collective-permute-done.17.refs_2_ = f32[32,256]{1,0:T(8,128)S(1)} collective-permute-done((f32[32,256]{1,0:T(8,128)S(1)}, f32[32,256]{1,0:T(8,128)S(1)}, u32[]{:S(2)}, u32[]{:S(2)}) %collective-permute-start.17) | collective-permute-done | bytes 32800 | tf_op jit(solution)/shard_map/ppermute | solution.py:62
  79.9 3.5 %collective-permute-start.23 = (f32[64,256]{1,0:T(8,128)S(1)}, f32[64,256]{1,0:T(8,128)S(1)}, u32[]{:S(2)}, u32[]{:S(2)}) collective-permute-start(f32[64,256]{1,0:T(8,128)S(1)} %add_add_fusion.1.ca_ref), channel_id=1, source_target_pairs={{0,96},{16,112},{32,64},{48,80},{64,32},{80,48},{96,0},{112,16},{1... | collective-permute-start | bytes 196616 | tf_op jit(solution)/shard_map/ppermute | solution.py:101
  87.5 5.3 %collective-permute-start.26 = (f32[32,256]{1,0:T(8,128)S(1)}, f32[32,256]{1,0:T(8,128)S(1)}, u32[]{:S(2)}, u32[]{:S(2)}) collective-permute-start(f32[32,256]{1,0:T(8,128)S(1)} %shard_map.80), channel_id=1, source_target_pairs={{0,12},{1,13},{2,14},{3,15},{4,0},{5,1},{6,2},{7,3},{8,4},{9,5},{1... | collective-permute-start | bytes 98312 | tf_op jit(solution)/shard_map/ppermute | solution.py:58
  94.4 3.8 %collective-permute-done.25 = f32[32,256]{1,0:T(8,128)S(1)} collective-permute-done((f32[32,256]{1,0:T(8,128)S(1)}, f32[32,256]{1,0:T(8,128)S(1)}, u32[]{:S(2)}, u32[]{:S(2)}) %collective-permute-start.25) | collective-permute-done | bytes 32800 | tf_op jit(solution)/shard_map/ppermute | solution.py:58
  98.2 3.2 %collective-permute-start.29 = (f32[32,256]{1,0:T(8,128)S(1)}, f32[32,256]{1,0:T(8,128)S(1)}, u32[]{:S(2)}, u32[]{:S(2)}) collective-permute-start(f32[32,256]{1,0:T(8,128)S(1)} %add_add_fusion.2.refs_0_), channel_id=1, source_target_pairs={{0,3},{1,0},{2,1},{3,2},{4,7},{5,4},{6,5},{7,6},{8,11},{9,8},{10,9... | collective-permute-start | bytes 98312 | tf_op jit(solution)/shard_map/ppermute | solution.py:62
  101.4 2.5 %collective-permute-start.28 = (f32[32,256]{1,0:T(8,128)S(1)}, f32[32,256]{1,0:T(8,128)S(1)}, u32[]{:S(2)}, u32[]{:S(2)}) collective-permute-start(f32[32,256]{1,0:T(8,128)S(1)} %add_add_fusion.2.refs_0_), channel_id=1, source_target_pairs={{0,2},{1,3},{2,0},{3,1},{4,6},{5,7},{6,4},{7,5},{8,10},{9,11},{10,... | collective-permute-start | bytes 98312 | tf_op jit(solution)/shard_map/ppermute | solution.py:62
  103.9 2.8 %collective-permute-start.27 = (f32[32,256]{1,0:T(8,128)S(1)}, f32[32,256]{1,0:T(8,128)S(1)}, u32[]{:S(2)}, u32[]{:S(2)}) collective-permute-start(f32[32,256]{1,0:T(8,128)S(1)} %add_add_fusion.2.refs_0_), channel_id=1, source_target_pairs={{0,1},{1,2},{2,3},{3,0},{4,5},{5,6},{6,7},{7,4},{8,9},{9,10},{10,1... | collective-permute-start | bytes 98312 | tf_op jit(solution)/shard_map/ppermute | solution.py:62
  106.7 2.5 %collective-permute-done.28.refs_2_ = f32[32,256]{1,0:T(8,128)S(1)} collective-permute-done((f32[32,256]{1,0:T(8,128)S(1)}, f32[32,256]{1,0:T(8,128)S(1)}, u32[]{:S(2)}, u32[]{:S(2)}) %collective-permute-start.28) | collective-permute-done | bytes 32800 | tf_op jit(solution)/shard_map/ppermute | solution.py:62
  113.3 2.6 %collective-permute-start.32 = (f32[64,256]{1,0:T(8,128)S(1)}, f32[64,256]{1,0:T(8,128)S(1)}, u32[]{:S(2)}, u32[]{:S(2)}) collective-permute-start(f32[64,256]{1,0:T(8,128)S(1)} %add.88), channel_id=1, source_target_pairs={{0,32},{16,48},{32,0},{48,16},{64,96},{80,112},{96,64},{112,80},{1... | collective-permute-start | bytes 196616 | tf_op jit(solution)/shard_map/ppermute | solution.py:98
  120.1 2.3 %collective-permute-start.34 = (f32[64,256]{1,0:T(8,128)S(1)}, f32[64,256]{1,0:T(8,128)S(1)}, u32[]{:S(2)}, u32[]{:S(2)}) collective-permute-start(f32[64,256]{1,0:T(8,128)S(1)} %add_add_fusion.refs_4_), channel_id=1, source_target_pairs={{0,96},{16,112},{32,64},{48,80},{64,32},{80,48},{96,0},{112,16},{1... | collective-permute-start | bytes 196616 | tf_op jit(solution)/shard_map/ppermute | solution.py:101
  122.4 3.5 %collective-permute-done.34.refs_5_ = f32[64,256]{1,0:T(8,128)S(1)} collective-permute-done((f32[64,256]{1,0:T(8,128)S(1)}, f32[64,256]{1,0:T(8,128)S(1)}, u32[]{:S(2)}, u32[]{:S(2)}) %collective-permute-start.34) | collective-permute-done | bytes 65568 | tf_op jit(solution)/shard_map/ppermute | solution.py:101
  125.9 5.4 %shard_map.82 = (bf16[4,72,512]{2,1,0:T(8,128)(2,1)S(1)}, bf16[4,72,512]{2,1,0:T(8,128)(2,1)S(1)}, bf16[4,72,512]{2,1,0:T(8,128)(2,1)S(1)}, bf16[4,72,512]{2,1,0...) custom-call(s32[96]{0:T(128)S(1)} %bitcast.42, ...), custom_call_target="tpu_custom_call" | custom-call | tf_op jit(solution)/shard_map/pallas_call | solution.py:373
  131.4 4.9 %collective-permute-start.35 = (bf16[4,72,512]{2,1,0:T(8,128)(2,1)S(1)}, bf16[4,72,512]{2,1,0:T(8,128)(2,1)S(1)}, u32[]{:S(2)}, u32[]{:S(2)}) collective-permute-start(bf16[4,72,512]{2,1,0:T(8,128)(2,1)S(1)} %get-tuple-element.22), channel_id=1, source_target_pairs={{0,12},{1,13},{2,14},{3,15},{4,0},{5,1},{6,2},{7,3},{8,4},{9,5},{1... | collective-permute-start | bytes 884744 | tf_op jit(solution)/shard_map/ppermute | solution.py:58
  137.9 5.8 %collective-permute-done.35.b_ref = bf16[4,72,512]{2,1,0:T(8,128)(2,1)S(1)} collective-permute-done((bf16[4,72,512]{2,1,0:T(8,128)(2,1)S(1)}, bf16[4,72,512]{2,1,0:T(8,128)(2,1)S(1)}, u32[]{:S(2)}, u32[]{:S(2)}) %collective-permute-start.35) | collective-permute-done | bytes 294944 | tf_op jit(solution)/shard_map/ppermute | solution.py:58
  143.7 7.5 %collective-permute-done.36.c_ref = bf16[4,72,512]{2,1,0:T(8,128)(2,1)S(1)} collective-permute-done((bf16[4,72,512]{2,1,0:T(8,128)(2,1)S(1)}, bf16[4,72,512]{2,1,0:T(8,128)(2,1)S(1)}, u32[]{:S(2)}, u32[]{:S(2)}) %collective-permute-start.36) | collective-permute-done | bytes 294944 | tf_op jit(solution)/shard_map/ppermute | solution.py:58
  153.6 5.7 %collective-permute-start.39 = (bf16[72,512]{1,0:T(8,128)(2,1)S(1)}, bf16[72,512]{1,0:T(8,128)(2,1)S(1)}, u32[]{:S(2)}, u32[]{:S(2)}) collective-permute-start(bf16[72,512]{1,0:T(8,128)(2,1)S(1)} %get-tuple-element.27), channel_id=1, source_target_pairs={{0,3},{1,2},{2,1},{3,0},{4,7},{5,6},{6,5},{7,4},{8,11},{9,10},{10,... | collective-permute-start | bytes 221192 | tf_op jit(solution)/shard_map/ppermute | solution.py:74
  164.1 4.8 %collective-permute-done.40 = bf16[72,512]{1,0:T(8,128)(2,1)S(1)} collective-permute-done((bf16[72,512]{1,0:T(8,128)(2,1)S(1)}, bf16[72,512]{1,0:T(8,128)(2,1)S(1)}, u32[]{:S(2)}, u32[]{:S(2)}) %collective-permute-start.40) | collective-permute-done | bytes 73760 | tf_op jit(solution)/shard_map/ppermute | solution.py:70
  169.4 5.0 %collective-permute-done.44 = bf16[2,64,1024]{2,1,0:T(8,128)(2,1)S(1)} collective-permute-done((bf16[2,64,1024]{2,1,0:T(8,128)(2,1)S(1)}, bf16[2,64,1024]{2,1,0:T(8,128)(2,1)S(1)}, u32[]{:S(2)}, u32[]{:S(2)}) %collective-permute-start.44) | collective-permute-done | bytes 262176 | tf_op jit(solution)/shard_map/ppermute | solution.py:78
  174.6 5.1 %collective-permute-start.45 = (bf16[64,1024]{1,0:T(8,128)(2,1)S(1)}, bf16[64,1024]{1,0:T(8,128)(2,1)S(1)}, u32[]{:S(2)}, u32[]{:S(2)}) collective-permute-start(bf16[64,1024]{1,0:T(8,128)(2,1)S(1)} %fusion.4), channel_id=1, source_target_pairs={{0,128},{16,144},{32,160},{48,176},{64,192},{80,208},{96,224},{112... | collective-permute-start | bytes 393224 | tf_op jit(solution)/shard_map/ppermute | solution.py:86
  180.3 2.3 %collective-permute-done.45 = bf16[64,1024]{1,0:T(8,128)(2,1)S(1)} collective-permute-done((bf16[64,1024]{1,0:T(8,128)(2,1)S(1)}, bf16[64,1024]{1,0:T(8,128)(2,1)S(1)}, u32[]{:S(2)}, u32[]{:S(2)}) %collective-permute-start.45) | collective-permute-done | bytes 131104 | tf_op jit(solution)/shard_map/ppermute | solution.py:86
  (99 shorter events, 55.3 us)
Async XLA Ops:
  2.3 7.3 %collective-permute-start = (bf16[1,72,512]{2,1,0:T(8,128)(2,1)S(1)}, bf16[1,72,512]{2,1,0:T(8,128)(2,1)S(1)}, u32[]{:S(2)}, u32[]{:S(2)}) collective-permute-start(bf16[1,72,512]{2,1,0:T(8,128)(2,1)S(1)} %maximum_bitcast_fusion), channel_id=1, source_target_pairs={{0,1},{1,0},{2,3},{3,2},{4,5},{5,4},{6,7},{7,6},{8,9},{9,8},{10,11... | collective-permute-start | bytes 221192 | tf_op jit(solution)/shard_map/ppermute | solution.py:66
  7.3 6.8 %collective-permute-start.5 = (bf16[1,72,1024]{2,1,0:T(8,128)(2,1)S(1)}, bf16[1,72,1024]{2,1,0:T(8,128)(2,1)S(1)}, u32[]{:S(2)}, u32[]{:S(2)}) collective-permute-start(bf16[1,72,1024]{2,1,0:T(8,128)(2,1)S(1)} %shard_map.77), channel_id=1, source_target_pairs={{0,128},{16,144},{32,160},{48,176},{64,192},{80,208},{96,224},{112... | collective-permute-start | bytes 442376 | tf_op jit(solution)/shard_map/ppermute | solution.py:86
  9.6 10.6 %collective-permute-start.1 = (bf16[2,72,512]{2,1,0:T(8,128)(2,1)S(1)}, bf16[2,72,512]{2,1,0:T(8,128)(2,1)S(1)}, u32[]{:S(2)}, u32[]{:S(2)}) collective-permute-start(bf16[2,72,512]{2,1,0:T(8,128)(2,1)S(1)} %pad_maximum_fusion.2), channel_id=1, source_target_pairs={{0,3},{1,2},{2,1},{3,0},{4,7},{5,6},{6,5},{7,4},{8,11},{9,10},{10,... | collective-permute-start | bytes 442376 | tf_op jit(solution)/shard_map/ppermute | solution.py:74
  14.1 6.7 %collective-permute-start.9 = (bf16[2,72,1024]{2,1,0:T(8,128)(2,1)S(1)}, bf16[2,72,1024]{2,1,0:T(8,128)(2,1)S(1)}, u32[]{:S(2)}, u32[]{:S(2)}) collective-permute-start(bf16[2,72,1024]{2,1,0:T(8,128)(2,1)S(1)} %pad_maximum_fusion.1.refs_4_.refs_13_), channel_id=1, source_target_pairs={{0,16},{16,0},{32,48},{48,32},{64,80},{80,64},{96,112},{112,96},{1... | collective-permute-start | bytes 884744 | tf_op jit(solution)/shard_map/ppermute | solution.py:82
  14.2 16.0 %collective-permute-start.8 = (bf16[2,72,1024]{2,1,0:T(8,128)(2,1)S(1)}, bf16[2,72,1024]{2,1,0:T(8,128)(2,1)S(1)}, u32[]{:S(2)}, u32[]{:S(2)}) collective-permute-start(bf16[2,72,1024]{2,1,0:T(8,128)(2,1)S(1)} %pad_maximum_fusion.1.refs_4_.refs_13_), channel_id=1, source_target_pairs={{0,96},{16,112},{32,0},{48,16},{64,32},{80,48},{96,64},{112,80},{1... | collective-permute-start | bytes 884744 | tf_op jit(solution)/shard_map/ppermute | solution.py:78
  17.0 14.8 %collective-permute-start.7 = (bf16[2,72,1024]{2,1,0:T(8,128)(2,1)S(1)}, bf16[2,72,1024]{2,1,0:T(8,128)(2,1)S(1)}, u32[]{:S(2)}, u32[]{:S(2)}) collective-permute-start(bf16[2,72,1024]{2,1,0:T(8,128)(2,1)S(1)} %pad_maximum_fusion.1.refs_4_.refs_13_), channel_id=1, source_target_pairs={{0,64},{16,80},{32,96},{48,112},{64,0},{80,16},{96,32},{112,48},{1... | collective-permute-start | bytes 884744 | tf_op jit(solution)/shard_map/ppermute | solution.py:78
  17.8 16.1 %collective-permute-start.6 = (bf16[2,72,1024]{2,1,0:T(8,128)(2,1)S(1)}, bf16[2,72,1024]{2,1,0:T(8,128)(2,1)S(1)}, u32[]{:S(2)}, u32[]{:S(2)}) collective-permute-start(bf16[2,72,1024]{2,1,0:T(8,128)(2,1)S(1)} %pad_maximum_fusion.1.refs_4_.refs_13_), channel_id=1, source_target_pairs={{0,32},{16,48},{32,64},{48,80},{64,96},{80,112},{96,0},{112,16},{1... | collective-permute-start | bytes 884744 | tf_op jit(solution)/shard_map/ppermute | solution.py:78
  20.3 13.7 %collective-permute-start.4 = (bf16[4,72,512]{2,1,0:T(8,128)(2,1)S(1)}, bf16[4,72,512]{2,1,0:T(8,128)(2,1)S(1)}, u32[]{:S(2)}, u32[]{:S(2)}) collective-permute-start(bf16[4,72,512]{2,1,0:T(8,128)(2,1)S(1)} %pad_maximum_fusion.refs_0_.refs_9_), channel_id=1, source_target_pairs={{0,12},{1,13},{2,14},{3,15},{4,0},{5,1},{6,2},{7,3},{8,4},{9,5},{1... | collective-permute-start | bytes 884744 | tf_op jit(solution)/shard_map/ppermute | solution.py:58
  20.8 15.2 %collective-permute-start.3 = (bf16[4,72,512]{2,1,0:T(8,128)(2,1)S(1)}, bf16[4,72,512]{2,1,0:T(8,128)(2,1)S(1)}, u32[]{:S(2)}, u32[]{:S(2)}) collective-permute-start(bf16[4,72,512]{2,1,0:T(8,128)(2,1)S(1)} %pad_maximum_fusion.refs_0_.refs_9_), channel_id=1, source_target_pairs={{0,8},{1,9},{2,10},{3,11},{4,12},{5,13},{6,14},{7,15},{8,0},{9,1},... | collective-permute-start | bytes 884744 | tf_op jit(solution)/shard_map/ppermute | solution.py:58
  30.2 8.3 %collective-permute-start.2 = (bf16[4,72,512]{2,1,0:T(8,128)(2,1)S(1)}, bf16[4,72,512]{2,1,0:T(8,128)(2,1)S(1)}, u32[]{:S(2)}, u32[]{:S(2)}) collective-permute-start(bf16[4,72,512]{2,1,0:T(8,128)(2,1)S(1)} %pad_maximum_fusion.refs_0_.refs_9_), channel_id=1, source_target_pairs={{0,4},{1,5},{2,6},{3,7},{4,8},{5,9},{6,10},{7,11},{8,12},{9,13},{1... | collective-permute-start | bytes 884744 | tf_op jit(solution)/shard_map/ppermute | solution.py:58
  31.8 6.7 %collective-permute-start.12 = (bf16[2,72,1024]{2,1,0:T(8,128)(2,1)S(1)}, bf16[2,72,1024]{2,1,0:T(8,128)(2,1)S(1)}, u32[]{:S(2)}, u32[]{:S(2)}) collective-permute-start(bf16[2,72,1024]{2,1,0:T(8,128)(2,1)S(1)} %collective-permute-done.8.refs_7_.refs_16_), channel_id=1, source_target_pairs={{0,16},{16,0},{32,48},{48,32},{64,80},{80,64},{96,112},{112,96},{1... | collective-permute-start | bytes 884744 | tf_op jit(solution)/shard_map/ppermute | solution.py:82
  44.7 6.8 %collective-permute-start.15 = (f32[32,256]{1,0:T(8,128)S(1)}, f32[32,256]{1,0:T(8,128)S(1)}, u32[]{:S(2)}, u32[]{:S(2)}) collective-permute-start(f32[32,256]{1,0:T(8,128)S(1)} %get-tuple-element.17), channel_id=1, source_target_pairs={{0,12},{1,13},{2,14},{3,15},{4,0},{5,1},{6,2},{7,3},{8,4},{9,5},{1... | collective-permute-start | bytes 98312 | tf_op jit(solution)/shard_map/ppermute | solution.py:58
  47.3 6.2 %collective-permute-start.14 = (f32[32,256]{1,0:T(8,128)S(1)}, f32[32,256]{1,0:T(8,128)S(1)}, u32[]{:S(2)}, u32[]{:S(2)}) collective-permute-start(f32[32,256]{1,0:T(8,128)S(1)} %get-tuple-element.17), channel_id=1, source_target_pairs={{0,8},{1,9},{2,10},{3,11},{4,12},{5,13},{6,14},{7,15},{8,0},{9,1},... | collective-permute-start | bytes 98312 | tf_op jit(solution)/shard_map/ppermute | solution.py:58
  54.9 11.2 %collective-permute-start.18 = (f32[32,256]{1,0:T(8,128)S(1)}, f32[32,256]{1,0:T(8,128)S(1)}, u32[]{:S(2)}, u32[]{:S(2)}) collective-permute-start(f32[32,256]{1,0:T(8,128)S(1)} %add_add_fusion.3.refs_0_), channel_id=1, source_target_pairs={{0,3},{1,0},{2,1},{3,2},{4,7},{5,4},{6,5},{7,6},{8,11},{9,8},{10,9... | collective-permute-start | bytes 98312 | tf_op jit(solution)/shard_map/ppermute | solution.py:62
  60.9 7.8 %collective-permute-start.17 = (f32[32,256]{1,0:T(8,128)S(1)}, f32[32,256]{1,0:T(8,128)S(1)}, u32[]{:S(2)}, u32[]{:S(2)}) collective-permute-start(f32[32,256]{1,0:T(8,128)S(1)} %add_add_fusion.3.refs_0_), channel_id=1, source_target_pairs={{0,2},{1,3},{2,0},{3,1},{4,6},{5,7},{6,4},{7,5},{8,10},{9,11},{10,... | collective-permute-start | bytes 98312 | tf_op jit(solution)/shard_map/ppermute | solution.py:62
  63.3 6.1 %collective-permute-start.16 = (f32[32,256]{1,0:T(8,128)S(1)}, f32[32,256]{1,0:T(8,128)S(1)}, u32[]{:S(2)}, u32[]{:S(2)}) collective-permute-start(f32[32,256]{1,0:T(8,128)S(1)} %add_add_fusion.3.refs_0_), channel_id=1, source_target_pairs={{0,1},{1,2},{2,3},{3,0},{4,5},{5,6},{6,7},{7,4},{8,9},{9,10},{10,1... | collective-permute-start | bytes 98312 | tf_op jit(solution)/shard_map/ppermute | solution.py:62
  87.5 6.9 %collective-permute-start.26 = (f32[32,256]{1,0:T(8,128)S(1)}, f32[32,256]{1,0:T(8,128)S(1)}, u32[]{:S(2)}, u32[]{:S(2)}) collective-permute-start(f32[32,256]{1,0:T(8,128)S(1)} %shard_map.80), channel_id=1, source_target_pairs={{0,12},{1,13},{2,14},{3,15},{4,0},{5,1},{6,2},{7,3},{8,4},{9,5},{1... | collective-permute-start | bytes 98312 | tf_op jit(solution)/shard_map/ppermute | solution.py:58
  98.2 8.5 %collective-permute-start.29 = (f32[32,256]{1,0:T(8,128)S(1)}, f32[32,256]{1,0:T(8,128)S(1)}, u32[]{:S(2)}, u32[]{:S(2)}) collective-permute-start(f32[32,256]{1,0:T(8,128)S(1)} %add_add_fusion.2.refs_0_), channel_id=1, source_target_pairs={{0,3},{1,0},{2,1},{3,2},{4,7},{5,4},{6,5},{7,6},{8,11},{9,8},{10,9... | collective-permute-start | bytes 98312 | tf_op jit(solution)/shard_map/ppermute | solution.py:62
  101.4 7.8 %collective-permute-start.28 = (f32[32,256]{1,0:T(8,128)S(1)}, f32[32,256]{1,0:T(8,128)S(1)}, u32[]{:S(2)}, u32[]{:S(2)}) collective-permute-start(f32[32,256]{1,0:T(8,128)S(1)} %add_add_fusion.2.refs_0_), channel_id=1, source_target_pairs={{0,2},{1,3},{2,0},{3,1},{4,6},{5,7},{6,4},{7,5},{8,10},{9,11},{10,... | collective-permute-start | bytes 98312 | tf_op jit(solution)/shard_map/ppermute | solution.py:62
  103.9 6.0 %collective-permute-start.27 = (f32[32,256]{1,0:T(8,128)S(1)}, f32[32,256]{1,0:T(8,128)S(1)}, u32[]{:S(2)}, u32[]{:S(2)}) collective-permute-start(f32[32,256]{1,0:T(8,128)S(1)} %add_add_fusion.2.refs_0_), channel_id=1, source_target_pairs={{0,1},{1,2},{2,3},{3,0},{4,5},{5,6},{6,7},{7,4},{8,9},{9,10},{10,1... | collective-permute-start | bytes 98312 | tf_op jit(solution)/shard_map/ppermute | solution.py:62
  113.3 6.1 %collective-permute-start.32 = (f32[64,256]{1,0:T(8,128)S(1)}, f32[64,256]{1,0:T(8,128)S(1)}, u32[]{:S(2)}, u32[]{:S(2)}) collective-permute-start(f32[64,256]{1,0:T(8,128)S(1)} %add.88), channel_id=1, source_target_pairs={{0,32},{16,48},{32,0},{48,16},{64,96},{80,112},{96,64},{112,80},{1... | collective-permute-start | bytes 196616 | tf_op jit(solution)/shard_map/ppermute | solution.py:98
  131.3 28.5 %collective-permute-start.41 = (bf16[8,64,1024]{2,1,0:T(8,128)(2,1)S(1)}, bf16[8,64,1024]{2,1,0:T(8,128)(2,1)S(1)}, u32[]{:S(2)}, u32[]{:S(2)}) collective-permute-start(bf16[8,64,1024]{2,1,0:T(8,128)(2,1)S(1)} %get-tuple-element.31), channel_id=1, source_target_pairs={{0,16},{16,0},{32,48},{48,32},{64,80},{80,64},{96,112},{112,96},{1... | collective-permute-start | bytes 3145736 | tf_op jit(solution)/shard_map/ppermute | solution.py:82
  131.4 12.3 %collective-permute-start.35 = (bf16[4,72,512]{2,1,0:T(8,128)(2,1)S(1)}, bf16[4,72,512]{2,1,0:T(8,128)(2,1)S(1)}, u32[]{:S(2)}, u32[]{:S(2)}) collective-permute-start(bf16[4,72,512]{2,1,0:T(8,128)(2,1)S(1)} %get-tuple-element.22), channel_id=1, source_target_pairs={{0,12},{1,13},{2,14},{3,15},{4,0},{5,1},{6,2},{7,3},{8,4},{9,5},{1... | collective-permute-start | bytes 884744 | tf_op jit(solution)/shard_map/ppermute | solution.py:58
  136.3 14.9 %collective-permute-start.36 = (bf16[4,72,512]{2,1,0:T(8,128)(2,1)S(1)}, bf16[4,72,512]{2,1,0:T(8,128)(2,1)S(1)}, u32[]{:S(2)}, u32[]{:S(2)}) collective-permute-start(bf16[4,72,512]{2,1,0:T(8,128)(2,1)S(1)} %get-tuple-element.23), channel_id=1, source_target_pairs={{0,8},{1,9},{2,10},{3,11},{4,12},{5,13},{6,14},{7,15},{8,0},{9,1},... | collective-permute-start | bytes 884744 | tf_op jit(solution)/shard_map/ppermute | solution.py:58
  137.6 14.3 %collective-permute-start.37 = (bf16[4,72,512]{2,1,0:T(8,128)(2,1)S(1)}, bf16[4,72,512]{2,1,0:T(8,128)(2,1)S(1)}, u32[]{:S(2)}, u32[]{:S(2)}) collective-permute-start(bf16[4,72,512]{2,1,0:T(8,128)(2,1)S(1)} %get-tuple-element.24), channel_id=1, source_target_pairs={{0,4},{1,5},{2,6},{3,7},{4,8},{5,9},{6,10},{7,11},{8,12},{9,13},{1... | collective-permute-start | bytes 884744 | tf_op jit(solution)/shard_map/ppermute | solution.py:58
  152.0 10.2 %collective-permute-start.38 = (bf16[72,512]{1,0:T(8,128)(2,1)S(1)}, bf16[72,512]{1,0:T(8,128)(2,1)S(1)}, u32[]{:S(2)}, u32[]{:S(2)}) collective-permute-start(bf16[72,512]{1,0:T(8,128)(2,1)S(1)} %get-tuple-element.26), channel_id=1, source_target_pairs={{0,1},{1,0},{2,3},{3,2},{4,5},{5,4},{6,7},{7,6},{8,9},{9,8},{10,11... | collective-permute-start | bytes 221192 | tf_op jit(solution)/shard_map/ppermute | solution.py:66
  153.6 10.5 %collective-permute-start.39 = (bf16[72,512]{1,0:T(8,128)(2,1)S(1)}, bf16[72,512]{1,0:T(8,128)(2,1)S(1)}, u32[]{:S(2)}, u32[]{:S(2)}) collective-permute-start(bf16[72,512]{1,0:T(8,128)(2,1)S(1)} %get-tuple-element.27), channel_id=1, source_target_pairs={{0,3},{1,2},{2,1},{3,0},{4,7},{5,6},{6,5},{7,4},{8,11},{9,10},{10,... | collective-permute-start | bytes 221192 | tf_op jit(solution)/shard_map/ppermute | solution.py:74
  159.2 9.7 %collective-permute-start.40 = (bf16[72,512]{1,0:T(8,128)(2,1)S(1)}, bf16[72,512]{1,0:T(8,128)(2,1)S(1)}, u32[]{:S(2)}, u32[]{:S(2)}) collective-permute-start(bf16[72,512]{1,0:T(8,128)(2,1)S(1)} %get-tuple-element.28), channel_id=1, source_target_pairs={{0,2},{1,3},{2,0},{3,1},{4,6},{5,7},{6,4},{7,5},{8,10},{9,11},{10,... | collective-permute-start | bytes 221192 | tf_op jit(solution)/shard_map/ppermute | solution.py:70
  160.1 9.3 %collective-permute-start.42 = (bf16[2,64,1024]{2,1,0:T(8,128)(2,1)S(1)}, bf16[2,64,1024]{2,1,0:T(8,128)(2,1)S(1)}, u32[]{:S(2)}, u32[]{:S(2)}) collective-permute-start(bf16[2,64,1024]{2,1,0:T(8,128)(2,1)S(1)} %get-tuple-element.32), channel_id=1, source_target_pairs={{0,96},{16,112},{32,0},{48,16},{64,32},{80,48},{96,64},{112,80},{1... | collective-permute-start | bytes 786440 | tf_op jit(solution)/shard_map/ppermute | solution.py:78
  160.9 13.5 %collective-permute-start.44 = (bf16[2,64,1024]{2,1,0:T(8,128)(2,1)S(1)}, bf16[2,64,1024]{2,1,0:T(8,128)(2,1)S(1)}, u32[]{:S(2)}, u32[]{:S(2)}) collective-permute-start(bf16[2,64,1024]{2,1,0:T(8,128)(2,1)S(1)} %get-tuple-element.33), channel_id=1, source_target_pairs={{0,32},{16,48},{32,64},{48,80},{64,96},{80,112},{96,0},{112,16},{1... | collective-permute-start | bytes 786440 | tf_op jit(solution)/shard_map/ppermute | solution.py:78
  162.2 12.1 %collective-permute-start.43 = (bf16[2,64,1024]{2,1,0:T(8,128)(2,1)S(1)}, bf16[2,64,1024]{2,1,0:T(8,128)(2,1)S(1)}, u32[]{:S(2)}, u32[]{:S(2)}) collective-permute-start(bf16[2,64,1024]{2,1,0:T(8,128)(2,1)S(1)} %get-tuple-element.34), channel_id=1, source_target_pairs={{0,64},{16,80},{32,96},{48,112},{64,0},{80,16},{96,32},{112,48},{1... | collective-permute-start | bytes 786440 | tf_op jit(solution)/shard_map/ppermute | solution.py:78
  174.6 8.0 %collective-permute-start.45 = (bf16[64,1024]{1,0:T(8,128)(2,1)S(1)}, bf16[64,1024]{1,0:T(8,128)(2,1)S(1)}, u32[]{:S(2)}, u32[]{:S(2)}) collective-permute-start(bf16[64,1024]{1,0:T(8,128)(2,1)S(1)} %fusion.4), channel_id=1, source_target_pairs={{0,128},{16,144},{32,160},{48,176},{64,192},{80,208},{96,224},{112... | collective-permute-start | bytes 393224 | tf_op jit(solution)/shard_map/ppermute | solution.py:86
  (19 other events, 203.5 us)
